TPU v7x, 256 devices: a whole 4x4x8 slice. The times are simulated.
256 devices in a mesh: dom: 64 (over x, z, core), feat: 4 (over y).
Axes of the slice: x: 4, y: 4, z: 8, core: 2. Of those that a mesh axis runs over, the one named last changes fastest.
Arguments:
- features: bfloat16 [98304, 1024], P('dom', 'feat'), may hold values from -6 to 6
- first_self: bfloat16 [1024, 256], P('feat'), may hold values from -0.1875 to 0.1875
- first_neighbor: bfloat16 [1024, 256], P('feat'), may hold values from -0.1875 to 0.1875
- first_bias: float32 [256], replicated, may hold values from -3 to 3
- second_self: bfloat16 [256, 256], replicated, may hold values from -0.375 to 0.375
- second_neighbor: bfloat16 [256, 256], replicated, may hold values from -0.375 to 0.375
- send_rows: int32 [64, 2048], P('dom'), may hold values from 0 to 1535
- arrive_count: int32 [64, 64], P('dom'), may hold values from 1 to 32, as said below
- self_slot: int32 [32768], P('dom'), may hold values from 0 to 2047, as said below
- neighbor_slot: int32 [32768, 25], P('dom'), may hold values from 0 to 2047, as said below
- degree: int32 [32768], P('dom'), may hold values from 1 to 25
- seed_self: int32 [8192], P('dom'), may hold values from 0 to 511
- seed_neighbor: int32 [8192, 10], P('dom'), may hold values from 0 to 511
- cotangent: bfloat16 [8192, 256], P('dom'), may hold values from -0.25 to 0.25
Outputs:
- seed_embedding: bfloat16 [8192, 256], P('dom')
- grad_first_self: float32 [1024, 256], P('feat')
- grad_first_neighbor: float32 [1024, 256], P('feat')
- grad_second_self: float32 [256, 256], replicated
- grad_second_neighbor: float32 [256, 256], replicated
Inputs may be any that keep to these rules, and one draw needn't show every extreme that they name: `arrive_count`: some owner receives 32 filled slots from every source in every draw. `self_slot`: each entry names slot s * 32 + k of its owner's received slots, with k < arrive_count[owner, s]; the owner that receives 32 filled slots from every source has a mid node at each end of the range. `neighbor_slot`: each entry names slot s * 32 + k of its owner's received slots, with k < arrive_count[owner, s]; the owner that receives 32 filled slots from every source has a mid node at each end of the range.
All inputs are finite; a program needn't handle non-finite values.
Results may differ from a plain program's by a relative error of at most 0.017.
Values may be sent and summed in bfloat16 or wider, within the bound.
No kernel may reach another device: no remote copies, remote signals or barrier semaphores. Data moves between devices by JAX's collectives and lax.ppermute only.
A program may use at most 128 MiB of HBM per device.

v0:
```python
import jax
import jax.numpy as jnp
from jax import lax
from jax.sharding import PartitionSpec as P


def column_blocks(weight_self, weight_near, slices):
    rows_in, hidden = weight_self.shape
    block_width = hidden // slices
    paired = jnp.stack(
        [
            weight_self.reshape(rows_in, slices, block_width),
            weight_near.reshape(rows_in, slices, block_width),
        ],
        axis=2,
    )
    return paired.reshape(rows_in, 2 * hidden)


def split_blocks(blocked, slices):
    rows_total = blocked.shape[0]
    shaped = blocked.reshape(rows_total, slices, 2, blocked.shape[1] // (2 * slices))
    return (shaped[:, :, 0, :].reshape(rows_total, -1), shaped[:, :, 1, :].reshape(rows_total, -1))


def inner_rows(left_rows, right_rows):
    return lax.dot_general(
        left_rows, right_rows, (((0,), (0,)), ((), ())), preferred_element_type=jnp.float32
    )


def right_transposed(left_rows, right_rows):
    return lax.dot_general(
        left_rows, right_rows, (((1,), (1,)), ((), ())), preferred_element_type=jnp.float32
    )


def layer_one(self_table, near_table, self_slot, neighbor_slot, degree, bias_part):
    self_rows = jnp.take(self_table, self_slot, axis=0).astype(jnp.float32)
    near_rows = jnp.take(near_table, neighbor_slot, axis=0).astype(jnp.float32)
    live_mask = lax.broadcasted_iota(jnp.int32, neighbor_slot.shape, 1) < degree[:, None]
    near_mean = (
        jnp.sum(jnp.where(live_mask[:, :, None], near_rows, 0.0), axis=1)
        / degree.astype(jnp.float32)[:, None]
    )
    pre = self_rows + near_mean + bias_part[None, :]
    sigma = jax.nn.sigmoid(pre)
    active = (pre * sigma).astype(jnp.bfloat16)
    slope = (sigma * (1.0 + pre * (1.0 - sigma))).astype(jnp.bfloat16)
    return (active, slope)


def source_partials(features, paired, flat_rows, peer_count):
    partial_value = jnp.dot(features, paired, preferred_element_type=jnp.float32).astype(
        jnp.bfloat16
    )
    return jnp.take(partial_value, flat_rows, axis=0).reshape(peer_count, -1, paired.shape[1])


def per_device(
    features,
    first_self,
    first_neighbor,
    first_bias,
    second_self,
    second_neighbor,
    send_rows,
    arrive_count,
    self_slot,
    neighbor_slot,
    degree,
    seed_self,
    seed_neighbor,
    cotangent,
):
    peer_count = lax.axis_size("dom")
    slices = lax.axis_size("feat")
    rows_in, hidden = first_self.shape
    block_width = hidden // slices
    paired = column_blocks(first_self, first_neighbor, slices)
    flat_rows = send_rows.reshape(-1)
    capacity = flat_rows.shape[0] // peer_count
    slot_total = peer_count * capacity
    valid_mask = (
        lax.broadcasted_iota(jnp.int32, (peer_count, capacity), 1)
        < arrive_count.reshape(peer_count, 1)
    ).reshape(slot_total, 1)
    outgoing = source_partials(features, paired, flat_rows, peer_count)
    incoming = lax.all_to_all(outgoing, "dom", split_axis=0, concat_axis=0, tiled=True)
    summed = lax.psum(incoming.astype(jnp.float32).astype(jnp.bfloat16), "feat")
    slot_table = summed.reshape(slot_total, 2 * hidden) * valid_mask.astype(jnp.bfloat16)
    table_self, table_near = split_blocks(slot_table, slices)
    active, slope = layer_one(table_self, table_near, self_slot, neighbor_slot, degree, first_bias)
    fan_two = seed_neighbor.shape[1]
    seed_count = seed_self.shape[0]
    mid_count = active.shape[0]
    seed_rows = jnp.take(active, seed_self, axis=0)
    seed_mean = (
        jnp.sum(jnp.take(active, seed_neighbor, axis=0).astype(jnp.float32), axis=1) / fan_two
    ).astype(jnp.bfloat16)
    seed_embedding = (
        jnp.dot(seed_rows, second_self, preferred_element_type=jnp.float32)
        + jnp.dot(seed_mean, second_neighbor, preferred_element_type=jnp.float32)
    ).astype(jnp.bfloat16)
    grad_second_self = inner_rows(seed_rows, cotangent)
    grad_second_neighbor = inner_rows(seed_mean, cotangent)
    back_self = right_transposed(cotangent, second_self)
    back_near = right_transposed(cotangent, second_neighbor) / fan_two
    spread = jnp.broadcast_to(back_near[:, None, :], (seed_count, fan_two, hidden)).reshape(
        -1, hidden
    )
    grad_active = jnp.zeros((mid_count, hidden), jnp.float32).at[seed_self].add(back_self)
    grad_active = grad_active.at[seed_neighbor.reshape(-1)].add(spread)
    grad_pre = grad_active * slope.astype(jnp.float32)
    live_mask = lax.broadcasted_iota(jnp.int32, neighbor_slot.shape, 1) < degree[:, None]
    near_share = jnp.where(
        live_mask[:, :, None], grad_pre[:, None, :] / degree.astype(jnp.float32)[:, None, None], 0.0
    )
    grad_self_slots = jnp.zeros((slot_total, hidden), jnp.float32).at[self_slot].add(grad_pre)
    grad_near_slots = (
        jnp.zeros((slot_total, hidden), jnp.float32)
        .at[neighbor_slot.reshape(-1)]
        .add(near_share.reshape(-1, hidden))
    )
    grad_blocked = jnp.stack(
        [
            grad_self_slots.reshape(slot_total, slices, block_width),
            grad_near_slots.reshape(slot_total, slices, block_width),
        ],
        axis=2,
    ).reshape(slot_total, 2 * hidden)
    grad_table = (grad_blocked * valid_mask.astype(jnp.float32)).astype(jnp.bfloat16)
    returned = lax.all_to_all(
        grad_table.reshape(peer_count, capacity, 2 * hidden),
        "dom",
        split_axis=0,
        concat_axis=0,
        tiled=True,
    )
    grad_both = inner_rows(
        jnp.take(features, flat_rows, axis=0), returned.reshape(slot_total, 2 * hidden)
    )
    grad_first_self, grad_first_neighbor = split_blocks(grad_both, slices)
    grad_first_self, grad_first_neighbor, grad_second_self, grad_second_neighbor = lax.psum(
        (grad_first_self, grad_first_neighbor, grad_second_self, grad_second_neighbor), "dom"
    )
    return (
        seed_embedding,
        grad_first_self,
        grad_first_neighbor,
        grad_second_self,
        grad_second_neighbor,
    )


def solution(mesh):
    in_specs = (
        P("dom", "feat"),
        P("feat", None),
        P("feat", None),
        P(),
        P(),
        P(),
        P("dom", None),
        P("dom", None),
        P("dom"),
        P("dom", None),
        P("dom"),
        P("dom"),
        P("dom", None),
        P("dom", None),
    )
    out_specs = (P("dom", None), P("feat", None), P("feat", None), P(), P())
    return jax.shard_map(
        per_device, mesh=mesh, in_specs=in_specs, out_specs=out_specs, check_vma=False
    )
```

profile of v0, /device:TPU:1, one launch (start us, length us, event | category | flops | bytes accessed | tf_op | source)
XLA Modules:
  0.0 690.7 jit_solution(11119431915029062679)
XLA Ops:
  8.0 1.0 copy.45
  9.0 1.0 copy.46
  10.1 1.8 fusion.4
  11.9 1.7 copy.48
  14.9 9.2 %gather_fusion = bf16[2048,512]{1,0:T(8,128)(2,1)} fusion(bf16[1536,512]{1,0:T(8,128)(2,1)S(1)} %copy.48, s32[2048]{0:T(1024)S(1)} %broadcast_clamp_fusion), kind=kCustom, calls=%fused_computation | custom fusion | bytes 4202496 | tf_op jit(solution)/shard_map/jit(_take)/gather | solution.py:57
  24.0 2.8 broadcast_select_fusion
  26.9 13.0 %all-to-all-start = ((bf16[64,32,512]{2,1,0:T(8,128)(2,1)}), bf16[64,32,512]{2,1,0:T(8,128)(2,1)S(1)}, u32[]{:S(2)}, u32[]{:S(2)}) async-start(bf16[64,32,512]{2,1,0:T(8,128)(2,1)} %broadcast_select_fusion), calls=%async_computation | async-start | bytes 4194304 | tf_op jit(solution)/shard_map/all_to_all | solution.py:89
  42.4 48.7 %all-to-all-done = bf16[64,32,512]{2,1,0:T(8,128)(2,1)S(1)} async-done(((bf16[64,32,512]{2,1,0:T(8,128)(2,1)}), bf16[64,32,512]{2,1,0:T(8,128)(2,1)S(1)}, u32[]{:S(2)}, u32[]{:S(2)}) %all-to-all-start) | async-done | bytes 2097184 | tf_op jit(solution)/shard_map/all_to_all | solution.py:89
  91.1 3.6 reshape.237
  96.1 1.4 reshape.305
  97.7 1.2 convert_element_type.65
  101.1 1.4 scatter_custom_fusion
  102.5 9.8 %scatter_fusion = f32[512,256]{1,0:T(8,128)S(1)} fusion(f32[512,256]{1,0:T(8,128)S(1)} %scatter_custom_fusion, s32[1280]{0:T(1024)S(1)} %fusion.23, f32[1280,256]{1,0:T(8,128)} %reshape.305), kind=kCustom, calls=%fused_computation.7 | custom fusion | flops 327680 | bytes 3937280 | tf_op jit(solution)/shard_map/scatter-add | solution.py:113
  113.7 75.8 %all-reduce.4.cloned.1.call-done = bf16[2048,4,2,64]{3,2,1,0:T(2,128)(2,1)} async-done(((bf16[2048,4,2,64]{3,2,1,0:T(2,128)(2,1)}), bf16[2048,4,2,64]{3,2,1,0:T(2,128)(2,1)}) %all-reduce.4.cloned.1.call-update) | async-done | bytes 2097168 | tf_op jit(solution)/shard_map/psum | solution.py:90
  189.5 8.4 %broadcast_multiply_fusion = bf16[2048,4,2,64]{3,2,1,0:T(2,128)(2,1)S(1)} fusion(bf16[2048,4,2,64]{3,2,1,0:T(2,128)(2,1)} %all-reduce.4.cloned.1.call-done, bf16[2048]{0:T(1024)(128)(2,1)S(1)} %copy-done.16), kind=kLoop, calls=%fused_computation.19 | loop fusion | flops 1048576 | bytes 4198400 | tf_op jit(solution)/shard_map/mul | solution.py:91
  197.9 7.0 %fusion.29 = (bf16[2048,4,1,64]{3,2,1,0:T(2,128)(2,1)}, bf16[2048,4,1,64]{3,2,1,0:T(2,128)(2,1)}) fusion(bf16[2048,4,2,64]{3,2,1,0:T(2,128)(2,1)S(1)} %broadcast_multiply_fusion), kind=kLoop, calls=%fused_computation.78 | loop fusion | bytes 4194304 | tf_op jit(solution)/shard_map/slice | solution.py:23
  204.9 10.3 %copy.52 = bf16[2048,4,1,64]{0,3,1,2:T(8,128)(2,1)} copy(bf16[2048,4,1,64]{3,2,1,0:T(2,128)(2,1)} %get-tuple-element.10) | data formatting | bytes 2097152 | tf_op jit(solution)/shard_map/slice | solution.py:23
  215.2 1.5 copy.54
  216.7 36.0 %gather_fusion.2 = bf16[12800,256]{1,0:T(8,128)(2,1)} fusion(bf16[2048,256]{1,0:T(8,128)(2,1)S(1)} %copy.54, s32[13312]{0:T(1024)S(1)} %pad_clamp_fusion), kind=kCustom, calls=%fused_computation.2 | custom fusion | bytes 13158400 | tf_op jit(solution)/shard_map/jit(_take)/gather | solution.py:40
  252.7 11.1 %reshape.262 = bf16[512,25,256]{2,1,0:T(8,128)(2,1)} reshape(bf16[12800,256]{1,0:T(8,128)(2,1)} %gather_fusion.2) | data formatting | bytes 13107200 | tf_op jit(solution)/shard_map/jit(_take)/gather | solution.py:40
  263.8 10.3 %copy.49 = bf16[2048,4,1,64]{0,3,1,2:T(8,128)(2,1)} copy(bf16[2048,4,1,64]{3,2,1,0:T(2,128)(2,1)} %get-tuple-element.9) | data formatting | bytes 2097152 | tf_op jit(solution)/shard_map/slice | solution.py:23
  274.1 1.5 copy.50
  275.6 6.9 %select_reduce_fusion = f32[512,256]{1,0:T(8,128)S(1)} fusion(bf16[512,25,256]{2,1,0:T(8,128)(2,1)} %reshape.262, pred[512,25]{1,0:T(8,128)(4,1)S(1)} %copy.51, pred[512,25]{1,0:T(8,128)(4,1)S(1)} %iota_compare_fusion), kind=kLoop, calls=%fused_computation.10 | loop fusion | flops 12976128 | bytes 7103488 | tf_op jit(solution)/shard_map/reduce_sum | solution.py:43
  282.6 2.0 gather_fusion.1
  284.5 1.1 fusion.14
  285.6 5.2 scatter_custom_fusion.2
  290.8 7.1 %broadcast_in_dim.144 = f32[512,25,256]{2,1,0:T(8,128)} broadcast(f32[512,256]{1,0:T(8,128)S(1)} %get-tuple-element.11), dimensions={0,2} | broadcast | bytes 13631488 | tf_op jit(solution)/shard_map/jit(_where)/broadcast_in_dim | solution.py:116
  297.9 16.1 %broadcast_in_dim.145 = f32[12800,256]{1,0:T(8,128)} reshape(f32[512,25,256]{2,1,0:T(8,128)} %broadcast_in_dim.144) | data formatting | bytes 26214400 | tf_op jit(solution)/shard_map/jit(_where)/broadcast_in_dim | solution.py:116
  314.0 78.0 %scatter_custom_fusion.3 = f32[2048,256]{1,0:T(8,128)} fusion(s32[12800]{0:T(1024)} %fusion.17, f32[12800,256]{1,0:T(8,128)} %broadcast_in_dim.145, f32[]{:T(128)} %constant.76.clone.1, pred[12800]{0:T(1024)(128)(4,1)S(1)} %copy-done.14), kind=kCustom, calls=%fused_computation.11 | custom fusion | flops 6553600 | bytes 15218176 | tf_op jit(solution)/shard_map/scatter-add | solution.py:123
  392.0 3.1 copy.60
  395.1 1.8 copy.58
  396.9 4.7 pad_maximum_fusion
  401.6 12.2 %copy.61 = f32[2048,4,2,64]{3,2,1,0:T(2,128)} copy(f32[2048,4,2,64]{0,3,1,2:T(8,128)} %pad_maximum_fusion) | data formatting | bytes 8388608 | tf_op jit(solution)/shard_map/stack | solution.py:125
  413.8 10.8 %reshape.242 = f32[64,32,512]{2,1,0:T(8,128)} reshape(f32[2048,4,2,64]{3,2,1,0:T(2,128)} %copy.61) | data formatting | bytes 8388608 | tf_op jit(solution)/shard_map/reshape | solution.py:131
  424.5 3.9 multiply_convert_fusion
  428.4 10.8 %all-to-all-start.1 = ((bf16[64,32,512]{2,1,0:T(8,128)(2,1)}), bf16[64,32,512]{2,1,0:T(8,128)(2,1)S(1)}, u32[]{:S(2)}, u32[]{:S(2)}) async-start(bf16[64,32,512]{2,1,0:T(8,128)(2,1)} %multiply_convert_fusion), calls=%async_computation.1 | async-start | bytes 4194304 | tf_op jit(solution)/shard_map/all_to_all | solution.py:133
  439.5 9.0 %gather_fusion.5 = bf16[2048,256]{1,0:T(8,128)(2,1)} fusion(bf16[1536,256]{1,0:T(8,128)(2,1)S(1)} %copy-done, s32[2048]{0:T(1024)S(1)} %copy-done.13), kind=kCustom, calls=%fused_computation.5 | custom fusion | bytes 2105344 | tf_op jit(solution)/shard_map/jit(_take)/gather | solution.py:141
  449.9 4.7 gather_fusion.4
  454.5 2.1 reshape.278
  456.7 1.8 convert_reduce_fusion
  460.4 30.0 %all-to-all-done.1 = bf16[64,32,512]{2,1,0:T(8,128)(2,1)S(1)} async-done(((bf16[64,32,512]{2,1,0:T(8,128)(2,1)}), bf16[64,32,512]{2,1,0:T(8,128)(2,1)S(1)}, u32[]{:S(2)}, u32[]{:S(2)}) %all-to-all-start.1) | async-done | bytes 2097184 | tf_op jit(solution)/shard_map/all_to_all | solution.py:133
  490.5 2.5 copy.62
  492.9 2.8 fusion.6
  498.5 178.7 %all-reduce.6.cloned.1.call-done = (f32[256,256]{1,0:T(8,128)}, f32[256,256]{1,0:T(8,128)}, f32[256,256]{1,0:T(8,128)}, f32[256,256]{1,0:T(8,128)}) async-done(((f32[256,256]{1,0:T(8,128)}, f32[256,256]{1,0:T(8,128)}, f32[256,256]{1,0:T(8,128)}, f32[256,256]{1,0:T(8,128)}), (f32[256,256]{1,0:T(8,128)}, f32[256,256]{1,0:T(8,128)}, f32[256,256]{1,0:T(8,128)}, ...) | async-done | bytes 1048592 | tf_op jit(solution)/shard_map/psum | solution.py:144
  677.2 1.7 copy.72
  678.9 1.7 copy.73
  680.6 1.7 copy.74
  682.2 1.7 copy.75
  (104 shorter events, 15.9 us)
Async XLA Ops:
  7.2 2.9 copy-start
  8.0 6.9 copy-start.12
  10.0 4.0 copy-start.11
  24.0 15.9 %copy-start.21 = (s32[1,64]{1,0:T(1,128)S(1)}, s32[1,64]{1,0:T(1,128)}, u32[]{:S(2)}) copy-start(s32[1,64]{1,0:T(1,128)} %param.21) | copy-start | bytes 772
  24.0 17.2 %copy-start.3 = (s32[512,25]{0,1:T(8,128)S(1)}, s32[512,25]{0,1:T(8,128)}, u32[]{:S(2)}) copy-start(s32[512,25]{0,1:T(8,128)} %param.23) | copy-start | bytes 153604
  26.9 64.2 %all-to-all-start = ((bf16[64,32,512]{2,1,0:T(8,128)(2,1)}), bf16[64,32,512]{2,1,0:T(8,128)(2,1)S(1)}, u32[]{:S(2)}, u32[]{:S(2)}) async-start(bf16[64,32,512]{2,1,0:T(8,128)(2,1)} %broadcast_select_fusion), calls=%async_computation | async-start | bytes 4194304 | tf_op jit(solution)/shard_map/all_to_all | solution.py:89
  39.9 149.7 %all-reduce.4.cloned.1.call-start = ((), (), s32[]{:S(2)}) async-start(), calls=%async_computation.2 | async-start | bytes 8388608 | tf_op jit(solution)/shard_map/psum | solution.py:90
  94.7 0.8 copy-start.2
  94.7 0.9 copy-start.6
  94.8 2.7 copy-start.10
  95.7 5.2 copy-start.4
  95.9 5.0 copy-start.24
  100.9 1.6 copy-start.22
  102.5 9.8 %copy-start.18 = (s32[512]{0:T(512)S(1)}, s32[512]{0:T(512)}, u32[]{:S(2)}) copy-start(s32[512]{0:T(512)} %param.22) | copy-start | bytes 6148
  102.5 11.2 %copy-start.8 = (s32[12800]{0:T(1024)S(1)}, s32[12800]{0:T(1024)}, u32[]{:S(2)}) copy-start(s32[12800]{0:T(1024)} %reshape.263) | copy-start | bytes 153604
  102.5 87.0 %copy-start.16 = (bf16[2048]{0:T(1024)(128)(2,1)S(1)}, bf16[2048]{0:T(1024)(128)(2,1)}, u32[]{:S(2)}) copy-start(bf16[2048]{0:T(1024)(128)(2,1)} %reshape.244) | copy-start | bytes 12292
  112.4 85.6 %copy-start.17 = (s32[512]{0:T(512)}, s32[512]{0:T(512)S(1)}, u32[]{:S(2)}) copy-start(s32[512]{0:T(512)S(1)} %compare_select_fusion.7) | copy-start | bytes 6148
  282.6 3.1 copy-start.15
  282.6 3.1 copy-start.19
  282.6 3.1 copy-start.20
  297.9 16.1 %copy-start.14 = (pred[12800]{0:T(1024)(128)(4,1)S(1)}, pred[12800]{0:T(1024)(128)(4,1)}, u32[]{:S(2)}) copy-start(pred[12800]{0:T(1024)(128)(4,1)} %lt.155) | copy-start | bytes 38404
  392.0 3.1 copy-start.1
  413.8 10.8 %copy-start.9 = (f32[64,32]{1,0:T(8,128)S(1)}, f32[64,32]{1,0:T(8,128)}, u32[]{:S(2)}) copy-start(f32[64,32]{1,0:T(8,128)} %get-tuple-element.15) | copy-start | bytes 24580
  428.4 11.1 %copy-start.13 = (s32[2048]{0:T(1024)S(1)}, s32[2048]{0:T(1024)}, u32[]{:S(2)}) copy-start(s32[2048]{0:T(1024)} %copy-done.12) | copy-start | bytes 24580
  428.4 62.0 %all-to-all-start.1 = ((bf16[64,32,512]{2,1,0:T(8,128)(2,1)}), bf16[64,32,512]{2,1,0:T(8,128)(2,1)S(1)}, u32[]{:S(2)}, u32[]{:S(2)}) async-start(bf16[64,32,512]{2,1,0:T(8,128)(2,1)} %multiply_convert_fusion), calls=%async_computation.1 | async-start | bytes 4194304 | tf_op jit(solution)/shard_map/all_to_all | solution.py:133
  439.2 9.7 %copy-start.23 = (s32[128]{0:T(128)S(1)}, s32[128]{0:T(128)}, u32[]{:S(2)}) copy-start(s32[128]{0:T(128)} %copy-done.22) | copy-start | bytes 1540
  439.2 9.8 %copy-start.25 = (s32[128]{0:T(128)S(1)}, s32[128]{0:T(128)}, u32[]{:S(2)}) copy-start(s32[128]{0:T(128)} %param.25) | copy-start | bytes 1540
  439.2 238.0 %all-reduce.6.cloned.1.call-start = ((), (), s32[]{:S(2)}) async-start(), calls=%async_computation.3 | async-start | bytes 2097152 | tf_op jit(solution)/shard_map/psum | solution.py:144
  492.9 4.5 copy-start.5
  492.9 4.7 copy-start.7
Sparse Core Ops, SparseCore 0:
  94.9 94.5 all-reduce.3
  497.6 179.6 all-reduce.5
where the time goes:
time: 693 us; the launch traced here: 691 us
  waiting for transfers between devices  333 us (48%)
  local copies, waits for them, and re-layouts  181 us (26%)
  other arithmetic  130 us (19%)
  starting transfers between devices  24.1 us (3%)
  between operations  14.6 us (2%)
  matrix products  7.82 us (1%)
    psum x1, waiting for transfers between devices, per_device(): lax.psum((grad_first_self, grad_first_neighbor, grad_second_self, grad_se...  179 us
    scatter-add x1, other arithmetic, per_device(): grad_near_slots = jnp.zeros((slot_total, hidden), jnp.float32).at[neighbo...  78 us
    psum x1, waiting for transfers between devices, per_device(): summed = lax.psum(incoming.astype(jnp.float32).astype(jnp.bfloat16), 'feat')  75.8 us
    all_to_all x1, waiting for transfers between devices, per_device(): lax.all_to_all(outgoing, 'dom', split_axis=0, concat_axis=0, tiled=True)  48.7 us
    gather x2, local copies, waits for them, and re-layouts, layer_one(): near_rows = jnp.take(near_table, neighbor_slot, axis=0).astype(jnp.float32)  47.1 us
    all_to_all x1, waiting for transfers between devices, per_device(): lax.all_to_all(grad_table.reshape(peer_count, capacity, 2 * hidden), 'dom...  30 us
    broadcast_in_dim x2, local copies, waits for them, and re-layouts, per_device(): jnp.where(live_mask[:, :, None], grad_pre[:, None, :] / degree.astype(jnp...  23.2 us
    slice x2, local copies, waits for them, and re-layouts, split_blocks(): shaped[:, :, 0, :].reshape(rows_total, -1)  17.3 us
  transfers between devices with their start and end apart: 4, of which 4 were waited for; matrix products, arithmetic and copies ran while one was open for 6% of the time, Pallas kernels for 0%

commit v1 on v0

v1 whole, which is shorter than its diff:
```python
import jax
import jax.numpy as jnp
from jax import lax
from jax.experimental import pallas as pl
from jax.experimental.pallas import tpu as pltpu
from jax.sharding import PartitionSpec as P

BF16 = jnp.bfloat16
F32 = jnp.float32
I32 = jnp.int32


def dot(left, right, left_dim=1, right_dim=0):
    return lax.dot_general(
        left, right, (((left_dim,), (right_dim,)), ((), ())), preferred_element_type=F32
    )


def call(body, outs, args, name, flops=0, moved=0, vmem=None, scratch=()):
    specs = [pl.BlockSpec(memory_space=pltpu.VMEM) for _ in args]
    out_specs = [pl.BlockSpec(memory_space=pltpu.VMEM) for _ in outs]
    return pl.pallas_call(
        body,
        out_shape=[jax.ShapeDtypeStruct(shape, dtype) for shape, dtype in outs],
        in_specs=specs,
        out_specs=out_specs,
        scratch_shapes=scratch,
        name=name,
        compiler_params=pltpu.CompilerParams(vmem_limit_bytes=vmem or (24 << 20)),
        cost_estimate=pl.CostEstimate(flops=flops, bytes_accessed=moved, transcendentals=0),
    )(*args)


def project_body(x_ref, self_ref, near_ref, out_ref):
    slices, rows, width = out_ref.shape
    half = width // 2
    step = rows // 4
    for at in range(slices):
        weight = jnp.concatenate(
            [self_ref[:, at * half : (at + 1) * half], near_ref[:, at * half : (at + 1) * half]],
            axis=1,
        )
        for piece in range(4):
            span = pl.ds(piece * step, step)
            out_ref[at, span, :] = dot(x_ref[span, :], weight).astype(BF16)


def pick_tables_body(column_ref, row_ref, x_ref, pick_ref, spread_ref, xt_ref):
    slots, rows = pick_ref.shape
    step = 128

    def fill_pick(at, carry):
        span = pl.ds(pl.multiple_of(at * step, step), step)
        lane = lax.broadcasted_iota(I32, (step, rows), 1)
        pick_ref[span, :] = jnp.where(column_ref[span, :] == lane, 1.0, 0.0).astype(BF16)
        return carry

    lax.fori_loop(0, slots // step, fill_pick, 0)

    def fill_spread(at, carry):
        span = pl.ds(pl.multiple_of(at * step, step), step)
        line = lax.broadcasted_iota(I32, (step, slots), 0) + at * step
        spread_ref[span, :] = jnp.where(row_ref[...] == line, 1.0, 0.0).astype(BF16)
        return carry

    lax.fori_loop(0, rows // step, fill_spread, 0)
    xt_ref[...] = x_ref[...].T


def count_tables_body(
    self_ref, near_ref, degree_ref, seed_ref, seed_near_ref,
    self_table, near_table, seed_table, seed_near_table, live_ref,
):
    slots, mids = near_table.shape
    fan = near_ref.shape[0]
    step = 32
    live = lax.broadcasted_iota(I32, (fan, mids), 0) < degree_ref[...]
    live_ref[...] = jnp.where(live, near_ref[...], -1)

    def fill(at, carry):
        span = pl.ds(pl.multiple_of(at * step, step), step)
        line = lax.broadcasted_iota(I32, (step, mids), 0) + at * step
        total = jnp.zeros((step, mids), F32)
        for j in range(fan):
            total = total + jnp.where(live_ref[j : j + 1, :] == line, 1.0, 0.0)
        near_table[span, :] = total.astype(BF16)
        self_table[span, :] = jnp.where(self_ref[...] == line, 1.0, 0.0).astype(BF16)
        return carry

    lax.fori_loop(0, slots // step, fill, 0)
    seeds = seed_table.shape[1]
    line = lax.broadcasted_iota(I32, (mids, seeds), 0)
    seed_table[...] = jnp.where(seed_ref[...] == line, 1.0, 0.0).astype(BF16)
    total = jnp.zeros((mids, seeds), F32)
    for j in range(seed_near_ref.shape[0]):
        total = total + jnp.where(seed_near_ref[j : j + 1, :] == line, 1.0, 0.0)
    seed_near_table[...] = total.astype(BF16)


def send_body(parts_ref, pick_ref, out_ref):
    slices = parts_ref.shape[0]
    total = parts_ref[0].astype(F32)
    for at in range(1, slices):
        total = total + parts_ref[at].astype(F32)
    total = total.astype(BF16)
    slots = pick_ref.shape[0]
    step = slots // 8
    for piece in range(8):
        span = pl.ds(piece * step, step)
        out_ref[span, :] = dot(pick_ref[span, :], total).astype(BF16)


def owner_body(
    fan_two,
    slot_ref, mask_ref, self_table, near_table, degree_ref, bias_ref, seed_table, seed_near_table,
    second_self_ref, second_near_ref, cotangent_ref, grad_ref, seeds_ref,
):
    half = bias_ref.shape[0]
    degree = degree_ref[...].astype(F32)
    table = slot_ref[...] * mask_ref[...]
    own = dot(table, self_table[...], 0, 0)[:half]
    near = dot(table, near_table[...], 0, 0)[half:]
    pre = own + near / degree + bias_ref[...]
    sigma = 1.0 / (1.0 + jnp.exp(-pre))
    active = (pre * sigma).astype(BF16)
    slope = (sigma * (1.0 + pre * (1.0 - sigma))).astype(BF16).astype(F32)
    seeds_ref[:half, :] = dot(active, seed_table[...]).astype(BF16)
    seeds_ref[half:, :] = (dot(active, seed_near_table[...]) / fan_two).astype(BF16)
    back_self = dot(second_self_ref[...], cotangent_ref[...], 1, 1)
    back_near = dot(second_near_ref[...], cotangent_ref[...], 1, 1) / fan_two

    def spread(back, picks):
        high = back.astype(BF16)
        low = (back - high.astype(F32)).astype(BF16)
        both = dot(jnp.concatenate([high, low], axis=0), picks, 1, 1)
        return both[:half] + both[half:]

    grad_active = spread(back_self, seed_table[...]) + spread(back_near, seed_near_table[...])
    grad_pre = grad_active * slope
    nothing = jnp.zeros(grad_pre.shape, BF16)
    for_self = jnp.concatenate([grad_pre.astype(BF16), nothing], axis=0)
    for_near = jnp.concatenate([nothing, (grad_pre / degree).astype(BF16)], axis=0)
    slots = slot_ref.shape[0]
    step = slots // 4
    for piece in range(4):
        span = pl.ds(piece * step, step)
        grad = dot(self_table[span, :], for_self, 1, 1) + dot(near_table[span, :], for_near, 1, 1)
        grad_ref[span, :] = grad.astype(BF16) * mask_ref[span, :]


def seeds_body(seeds_ref, second_self_ref, second_near_ref, cotangent_ref, out_ref, grad_ref):
    slices, both, seeds = seeds_ref.shape
    half = both // 2
    tiles = grad_ref.shape[0] // 2
    per = tiles // slices
    total = jnp.zeros(out_ref.shape, F32)
    cotangent = cotangent_ref[...]
    for at in range(slices):
        rows = pl.ds(at * half, half)
        total = total + dot(seeds_ref[at, :half, :], second_self_ref[rows, :], 0, 0)
        total = total + dot(seeds_ref[at, half:, :], second_near_ref[rows, :], 0, 0)
        grad = dot(seeds_ref[at], cotangent)
        shaped = (per,) + grad_ref.shape[1:]
        grad_ref[pl.ds(at * per, per)] = grad[:half].reshape(shaped).astype(BF16)
        grad_ref[pl.ds(tiles + at * per, per)] = grad[half:].reshape(shaped).astype(BF16)
    out_ref[...] = total.astype(BF16)


def gather_body(returned_ref, spread_ref, out_ref):
    rows = spread_ref.shape[0]
    step = rows // 6
    for piece in range(6):
        span = pl.ds(piece * step, step)
        value = dot(spread_ref[span, :], returned_ref[...]).astype(BF16)
        for at in range(out_ref.shape[0]):
            out_ref[at, span, :] = value


def weight_body(xt_ref, grads_ref, out_ref):
    slices, rows, width = grads_ref.shape
    half = width // 2
    tiles = out_ref.shape[0] // 2
    pieces = [dot(xt_ref[...], grads_ref[at]) for at in range(slices)]
    own = jnp.concatenate([piece[:, :half] for piece in pieces], axis=1)
    near = jnp.concatenate([piece[:, half:] for piece in pieces], axis=1)
    shaped = (tiles,) + out_ref.shape[1:]
    out_ref[pl.ds(0, tiles)] = own.reshape(shaped).astype(BF16)
    out_ref[pl.ds(tiles, tiles)] = near.reshape(shaped).astype(BF16)


def sum_body(first_ref, second_ref, out_ref):
    first = jnp.sum(first_ref[...].astype(F32), axis=0)
    second = jnp.sum(second_ref[...].astype(F32), axis=0)
    both = jnp.concatenate([first, second], axis=0).astype(BF16)
    out_ref[...] = jnp.broadcast_to(both[None], out_ref.shape)


def finish_body(all_ref, first_self_ref, first_near_ref, second_self_ref, second_near_ref):
    peers, tall, width = all_ref.shape
    lines = tall // 2
    tiles = peers // 2
    value = all_ref[...].astype(F32)
    first_self_ref[...] = value[:tiles, :lines].reshape(tiles * lines, width)
    first_near_ref[...] = value[tiles:, :lines].reshape(tiles * lines, width)
    second_self_ref[...] = value[:tiles, lines:].reshape(tiles * lines, width)
    second_near_ref[...] = value[tiles:, lines:].reshape(tiles * lines, width)


def exchange(value, axis):
    return lax.all_to_all(value, axis, split_axis=0, concat_axis=0, tiled=True)


def per_device(
    features,
    first_self,
    first_neighbor,
    first_bias,
    second_self,
    second_neighbor,
    send_rows,
    arrive_count,
    self_slot,
    neighbor_slot,
    degree,
    seed_self,
    seed_neighbor,
    cotangent,
):
    peers = lax.axis_size("dom")
    slices = lax.axis_size("feat")
    rows, slice_cols = features.shape
    hidden = first_self.shape[1]
    half = hidden // slices
    width = 2 * half
    slots = send_rows.shape[1]
    capacity = slots // peers
    mids, fan = neighbor_slot.shape
    seeds, fan_two = seed_neighbor.shape
    out_cols = second_self.shape[1]
    lines = hidden * 2 // peers

    (parts,) = call(
        project_body, [((slices, rows, width), BF16)], (features, first_self, first_neighbor),
        "project", 2 * rows * slice_cols * 2 * hidden, rows * (slice_cols + 2 * hidden) * 2,
    )
    parts = exchange(parts, "feat")

    pick, spread, features_t = call(
        pick_tables_body,
        [((slots, rows), BF16), ((rows, slots), BF16), ((slice_cols, rows), BF16)],
        (send_rows.reshape(slots, 1), send_rows, features), "pick_tables",
        0, 4 * rows * slots, 48 << 20,
    )
    self_table, near_table, seed_table, seed_near_table = call(
        count_tables_body,
        [((slots, mids), BF16), ((slots, mids), BF16), ((mids, seeds), BF16), ((mids, seeds), BF16)],
        (
            self_slot.reshape(1, mids), neighbor_slot.T, degree.reshape(1, mids),
            seed_self.reshape(1, seeds), seed_neighbor.T,
        ),
        "count_tables", 0, 16 * slots * mids, scratch=[pltpu.VMEM((fan, mids), I32)],
    )
    mask = jnp.broadcast_to(
        (
            lax.broadcasted_iota(I32, (peers, capacity, width), 1)
            < arrive_count.reshape(peers, 1, 1)
        ),
        (peers, capacity, width),
    ).astype(BF16).reshape(slots, width)
    mine = lax.axis_index("feat") * half
    bias = lax.dynamic_slice(first_bias.reshape(hidden, 1), (mine, 0), (half, 1))
    second_self_part = lax.dynamic_slice(second_self, (mine, 0), (half, out_cols))
    second_near_part = lax.dynamic_slice(second_neighbor, (mine, 0), (half, out_cols))

    (outgoing,) = call(
        send_body, [((slots, width), BF16)], (parts, pick), "send",
        2 * slots * rows * width, 2 * slots * rows,
    )
    incoming = exchange(outgoing.reshape(peers, capacity, width), "dom").reshape(slots, width)

    grad_table, own_seeds = call(
        lambda *refs: owner_body(fan_two, *refs),
        [((slots, width), BF16), ((width, seeds), BF16)],
        (
            incoming, mask, self_table, near_table, degree.reshape(1, mids), bias, seed_table,
            seed_near_table, second_self_part, second_near_part, cotangent,
        ),
        "owner", 8 * slots * mids * width, 4 * slots * mids,
    )
    returned = exchange(grad_table.reshape(peers, capacity, width), "dom").reshape(slots, width)

    all_seeds = exchange(
        jnp.broadcast_to(own_seeds[None], (slices, width, seeds)), "feat"
    )
    seed_embedding, grad_second = call(
        seeds_body, [((seeds, out_cols), BF16), ((peers, lines, out_cols), BF16)],
        (all_seeds, second_self, second_neighbor, cotangent), "seeds",
        8 * seeds * hidden * out_cols, 2 * slots * width,
    )

    (row_grads,) = call(
        gather_body, [((slices, rows, width), BF16)], (returned, spread), "gather",
        2 * slots * rows * width, 2 * slots * rows,
    )
    row_grads = exchange(row_grads, "feat")
    grad_second = exchange(grad_second, "dom")
    (grad_first,) = call(
        weight_body, [((peers, lines, hidden), BF16)], (features_t, row_grads), "weight",
        2 * rows * slice_cols * 2 * hidden, 2 * rows * (slice_cols + 2 * hidden),
    )
    grad_first = exchange(grad_first, "dom")
    (summed,) = call(
        sum_body, [((peers, 2 * lines, hidden), BF16)], (grad_first, grad_second), "sum",
        0, 4 * peers * lines * hidden,
    )
    summed = exchange(summed, "dom")
    grad_first_self, grad_first_neighbor, grad_second_self, grad_second_neighbor = call(
        finish_body, [((slice_cols, hidden), F32)] * 2 + [((hidden, out_cols), F32)] * 2,
        (summed,), "finish", 0, 8 * peers * lines * hidden,
    )
    return (
        seed_embedding,
        grad_first_self,
        grad_first_neighbor,
        grad_second_self,
        grad_second_neighbor,
    )


def solution(mesh):
    in_specs = (
        P("dom", "feat"),
        P("feat", None),
        P("feat", None),
        P(),
        P(),
        P(),
        P("dom", None),
        P("dom", None),
        P("dom"),
        P("dom", None),
        P("dom"),
        P("dom"),
        P("dom", None),
        P("dom", None),
    )
    out_specs = (P("dom", None), P("feat", None), P("feat", None), P(), P())
    return jax.shard_map(
        per_device, mesh=mesh, in_specs=in_specs, out_specs=out_specs, check_vma=False
    )
```

time: 693 us -> 191 us (0.28)
  waiting for transfers between devices: 333 us -> 44.2 us
  local copies, waits for them, and re-layouts: 181 us -> 14.1 us
  other arithmetic: 130 us -> 0.07 us
  blocking collectives: 0 us -> 64.4 us
  Pallas kernels: 0 us -> 32.3 us
  between operations: 14.6 us -> 0.87 us
  starting transfers between devices: 24.1 us -> 34.4 us
  matrix products: 7.82 us -> 0 us
    psum x2 -> x0, waiting for transfers between devices: 255 us -> none  [the longest x1 179 us: per_device(): lax.psum((grad_first_self, grad_first_neighbor, grad_second_self, grad_se...]
    scatter-add x4 -> x0, other arithmetic: 94.4 us -> none  [the longest x1 78 us: per_device(): grad_near_slots = jnp.zeros((slot_total, hidden), jnp.float32).at[neighbo...]
    gather x8 -> x0, local copies, waits for them, and re-layouts: 74.9 us -> none  [the longest x2 47.1 us: layer_one(): near_rows = jnp.take(near_table, neighbor_slot, axis=0).astype(jnp.float32)]
    all_to_all x0 -> x3, blocking collectives: none -> 64.4 us  [exchange(): return lax.all_to_all(value, axis, split_axis=0, concat_axis=0, tiled=True)]
    all_to_all x2 -> x5, waiting for transfers between devices: 78.7 us -> 44.2 us  [exchange(): return lax.all_to_all(value, axis, split_axis=0, concat_axis=0, tiled=True)]
    pallas_call x0 -> x10, Pallas kernels: none -> 32.3 us  [call(): pl.pallas_call(body, out_shape=[jax.ShapeDtypeStruct(shape, dtype) for sh...]
    slice x4 -> x0, local copies, waits for them, and re-layouts: 27.6 us -> none  [the longest x2 17.3 us: split_blocks(): shaped[:, :, 0, :].reshape(rows_total, -1)]
    broadcast_in_dim x5 -> x1, local copies, waits for them, and re-layouts: 24.3 us -> 0.67 us  [per_device(): jnp.broadcast_to(own_seeds[None], (slices, width, seeds))]
  transfers between devices with their start and end apart: 4 -> 5, of which waited for: 4 -> 4; matrix products, arithmetic and copies ran while one was open for 6% -> 0% of each run, Pallas kernels for 0% -> 13%
where the time goes in v1:
time: 191 us; the launch traced here: 190 us
  blocking collectives  64.4 us (34%)
  waiting for transfers between devices  44.2 us (23%)
  starting transfers between devices  34.4 us (18%)
  Pallas kernels  32.3 us (17%)
  local copies, waits for them, and re-layouts  14.1 us (7%)
    all_to_all x3, blocking collectives, exchange(): return lax.all_to_all(value, axis, split_axis=0, concat_axis=0, tiled=True)  64.4 us
    all_to_all x5, waiting for transfers between devices, exchange(): return lax.all_to_all(value, axis, split_axis=0, concat_axis=0, tiled=True)  44.2 us
    all_to_all x5, starting transfers between devices, exchange(): return lax.all_to_all(value, axis, split_axis=0, concat_axis=0, tiled=True)  34.4 us
    pallas_call x10, Pallas kernels, call(): pl.pallas_call(body, out_shape=[jax.ShapeDtypeStruct(shape, dtype) for sh...  32.3 us
    unnamed x42, local copies, waits for them, and re-layouts  12.4 us
  transfers between devices with their start and end apart: 5, of which 4 were waited for; matrix products, arithmetic and copies ran while one was open for 0% of the time, Pallas kernels for 13%

profile of v1, /device:TPU:1, one launch (start us, length us, event | category | flops | bytes accessed | tf_op | source)
XLA Modules:
  0.0 190.2 jit_solution(3138576608016017553)
XLA Ops:
  0.6 0.0 copy-start
  0.6 0.0 copy-start.3
  0.7 1.1 copy-done.3
  1.8 0.9 copy-done.12
  2.7 0.9 copy-done.13
  3.6 2.2 %project.1 = bf16[4,1536,128]{2,1,0:T(8,128)(2,1)} custom-call(bf16[1536,256]{1,0:T(8,128)(2,1)S(1)} %copy-done.3, bf16[256,256]{1,0:T(8,128)(2,1)S(1)} %copy-done.12, bf16[256,256]{1,0:T(8,128)(2,1)S(1)} %copy-done.13), custom_call_target="tpu_custom_call" | custom-call | flops 402653184 | bytes 2359296 | tf_op jit(solution)/shard_map/project/pallas_call | solution.py:22
  5.8 5.1 %all-to-all-start = ((bf16[4,1536,128]{2,1,0:T(8,128)(2,1)}), bf16[4,1536,128]{2,1,0:T(8,128)(2,1)S(1)}, u32[]{:S(2)}, u32[]{:S(2)}) async-start(bf16[4,1536,128]{2,1,0:T(8,128)(2,1)} %project.1), calls=%async_computation | async-start | bytes 3145728 | tf_op jit(solution)/shard_map/all_to_all | solution.py:210
  10.9 0.0 copy-done.15
  10.9 0.4 copy.20.column_ref
  11.3 7.7 %pick_tables.1 = (bf16[2048,1536]{1,0:T(8,128)(2,1)}, bf16[1536,2048]{1,0:T(8,128)(2,1)}, bf16[256,1536]{1,0:T(8,128)(2,1)S(1)}) custom-call(s32[2048,1]{1,0:T(8,128)S(1)} %copy.20.column_ref, s32[1,2048]{1,0:T(1,128)S(1)} %copy-done.15, bf16[1536,256]{1,0:T(8,128)(2,1)S(1)} %copy-done.4), custom_call_target="tpu_custom_call" | custom-call | bytes 12582912 | tf_op jit(solution)/shard_map/pick_tables/pallas_call | solution.py:22
  19.0 0.9 copy-done.7
  19.9 10.0 %all-to-all-done.parts_ref = bf16[4,1536,128]{2,1,0:T(8,128)(2,1)S(1)} async-done(((bf16[4,1536,128]{2,1,0:T(8,128)(2,1)}), bf16[4,1536,128]{2,1,0:T(8,128)(2,1)S(1)}, u32[]{:S(2)}, u32[]{:S(2)}) %all-to-all-start) | async-done | bytes 1572896 | tf_op jit(solution)/shard_map/all_to_all | solution.py:210
  29.9 2.8 %copy-done.2 = bf16[2048,1536]{1,0:T(8,128)(2,1)S(1)} copy-done((bf16[2048,1536]{1,0:T(8,128)(2,1)S(1)}, bf16[2048,1536]{1,0:T(8,128)(2,1)}, u32[]{:S(2)}) %copy-start.2) | copy-done | bytes 6291480
  32.7 0.0 copy-start.18
  32.7 0.0 copy-start.19
  32.7 0.0 copy-start.10
  32.8 0.0 copy-start.11
  32.8 0.0 copy-start.9
  32.8 2.7 %send.1 = bf16[2048,128]{1,0:T(8,128)(2,1)} custom-call(bf16[4,1536,128]{2,1,0:T(8,128)(2,1)S(1)} %all-to-all-done.parts_ref, bf16[2048,1536]{1,0:T(8,128)(2,1)S(1)} %copy-done.2), custom_call_target="tpu_custom_call" | custom-call | flops 805306368 | bytes 6291456 | tf_op jit(solution)/shard_map/send/pallas_call | solution.py:22
  35.5 14.2 %all-to-all-start.1 = ((bf16[64,32,128]{2,1,0:T(8,128)(2,1)}), bf16[64,32,128]{2,1,0:T(8,128)(2,1)S(1)}, u32[]{:S(2)}, u32[]{:S(2)}) async-start(bf16[64,32,128]{2,1,0:T(8,128)(2,1)} %bitcast.1), calls=%async_computation.1 | async-start | bytes 1048576 | tf_op jit(solution)/shard_map/all_to_all | solution.py:210
  49.7 0.1 fusion
  49.7 0.1 reshape.54
  49.8 0.1 dynamic-slice_bitcast_fusion
  49.9 0.1 copy.21.refs_5_
  50.1 11.0 %count_tables.1 = (bf16[2048,512]{1,0:T(8,128)(2,1)S(1)}, bf16[2048,512]{1,0:T(8,128)(2,1)S(1)}, bf16[512,128]{1,0:T(8,128)(2,1)S(1)}, bf16[512,128]{1,0:T(8,128)(2,1)S(1)}) custom-call(s32[1,512]{1,0:T(1,128)S(1)} %bitcast.21, s32[25,512]{1,0:T(8,128)S(1)} %bitcast.16, s32[1,512]{1,0:T(1,128)S(1)} %bitcast.18, s32[1,128]{1,0:T(1,128)S(1)} %bitcast.22, ...), custom_call_target="tpu_custom_call" | custom-call | bytes 16777216 | tf_op jit(solution)/shard_map/count_tables/pallas_call | solution.py:22
  61.1 0.0 copy-start.5
  61.1 1.4 copy-done.5
  62.5 0.0 copy-done.11
  62.5 4.5 %all-to-all-done.1 = bf16[64,32,128]{2,1,0:T(8,128)(2,1)S(1)} async-done(((bf16[64,32,128]{2,1,0:T(8,128)(2,1)}), bf16[64,32,128]{2,1,0:T(8,128)(2,1)S(1)}, u32[]{:S(2)}, u32[]{:S(2)}) %all-to-all-start.1) | async-done | bytes 524320 | tf_op jit(solution)/shard_map/all_to_all | solution.py:210
  67.0 0.3 iota.10.refs_1_
  67.3 1.6 copy-done.6
  68.9 2.4 %owner.1 = (bf16[2048,128]{1,0:T(8,128)(2,1)S(1)}, bf16[128,128]{1,0:T(8,128)(2,1)S(1)}) custom-call(bf16[2048,128]{1,0:T(8,128)(2,1)S(1)} %bitcast.13, bf16[2048,128]{1,0:T(8,128)(2,1)S(1)} %iota.10.refs_1_, bf16[2048,512]{1,0:T(8,128)(2,1)S(1)} %get-tuple-element.21.refs_2_, bf16[2048,512]{1,0:T(8,128)(2,1)S(1)} %copy-done.6, s32[1,512]{1,0:T(1,128)S(1)} %bitcast.19, ...), custom_call_target="tpu_custom_call" | custom-call | flops 1073741824 | bytes 4194304 | tf_op jit(solution)/shard_map/owner/pallas_call | solution.py:22
  71.3 23.4 %all_to_all.40 = bf16[64,32,128]{2,1,0:T(8,128)(2,1)S(1)} all-to-all(bf16[64,32,128]{2,1,0:T(8,128)(2,1)S(1)} %bitcast.15), channel_id=1, replica_groups=mesh['dom'=64,'feat'=4] {'dom'}, dimensions={0} | all-to-all | bytes 1048576 | tf_op jit(solution)/shard_map/all_to_all | solution.py:210
  94.7 0.7 broadcast_in_dim.2
  95.4 3.3 %all-to-all-start.2 = ((bf16[4,128,128]{2,1,0:T(8,128)(2,1)}), bf16[4,128,128]{2,1,0:T(8,128)(2,1)S(1)}, u32[]{:S(2)}, u32[]{:S(2)}) async-start(bf16[4,128,128]{2,1,0:T(8,128)(2,1)} %broadcast_in_dim.2), calls=%async_computation.2 | async-start | bytes 262144 | tf_op jit(solution)/shard_map/all_to_all | solution.py:210
  98.7 2.8 %copy-done.1 = bf16[1536,2048]{1,0:T(8,128)(2,1)S(1)} copy-done((bf16[1536,2048]{1,0:T(8,128)(2,1)S(1)}, bf16[1536,2048]{1,0:T(8,128)(2,1)}, u32[]{:S(2)}) %copy-start.1) | copy-done | bytes 6291480
  101.5 3.0 %gather.1 = bf16[4,1536,128]{2,1,0:T(8,128)(2,1)} custom-call(bf16[2048,128]{1,0:T(8,128)(2,1)S(1)} %bitcast.14, bf16[1536,2048]{1,0:T(8,128)(2,1)S(1)} %copy-done.1), custom_call_target="tpu_custom_call" | custom-call | flops 805306368 | bytes 6291456 | tf_op jit(solution)/shard_map/gather/pallas_call | solution.py:22
  104.5 0.0 all-to-all-done.2.seeds_ref
  104.5 4.3 %all-to-all-start.4 = ((bf16[4,1536,128]{2,1,0:T(8,128)(2,1)}), bf16[4,1536,128]{2,1,0:T(8,128)(2,1)S(1)}, u32[]{:S(2)}, u32[]{:S(2)}) async-start(bf16[4,1536,128]{2,1,0:T(8,128)(2,1)} %gather.1), calls=%async_computation.4 | async-start | bytes 3145728 | tf_op jit(solution)/shard_map/all_to_all | solution.py:210
  108.9 1.1 seeds.1
  110.0 18.8 %all-to-all-done.4.grads_ref = bf16[4,1536,128]{2,1,0:T(8,128)(2,1)S(1)} async-done(((bf16[4,1536,128]{2,1,0:T(8,128)(2,1)}), bf16[4,1536,128]{2,1,0:T(8,128)(2,1)S(1)}, u32[]{:S(2)}, u32[]{:S(2)}) %all-to-all-start.4) | async-done | bytes 1572896 | tf_op jit(solution)/shard_map/all_to_all | solution.py:210
  128.7 7.4 %all-to-all-start.6 = ((bf16[64,8,256]{2,1,0:T(8,128)(2,1)}), bf16[64,8,256]{2,1,0:T(8,128)(2,1)S(1)}, u32[]{:S(2)}, u32[]{:S(2)}) async-start(bf16[64,8,256]{2,1,0:T(8,128)(2,1)} %get-tuple-element.30), calls=%async_computation.6 | async-start | bytes 524288 | tf_op jit(solution)/shard_map/all_to_all | solution.py:210
  136.2 1.0 weight.1
  137.2 10.9 %all-to-all-done.6.second_ref = bf16[64,8,256]{2,1,0:T(8,128)(2,1)S(1)} async-done(((bf16[64,8,256]{2,1,0:T(8,128)(2,1)}), bf16[64,8,256]{2,1,0:T(8,128)(2,1)S(1)}, u32[]{:S(2)}, u32[]{:S(2)}) %all-to-all-start.6) | async-done | bytes 262176 | tf_op jit(solution)/shard_map/all_to_all | solution.py:210
  148.2 17.8 %all_to_all.41.first_ref = bf16[64,8,256]{2,1,0:T(8,128)(2,1)S(1)} all-to-all(bf16[64,8,256]{2,1,0:T(8,128)(2,1)S(1)} %weight.1), channel_id=1, replica_groups=mesh['dom'=64,'feat'=4] {'dom'}, dimensions={0} | all-to-all | bytes 524288 | tf_op jit(solution)/shard_map/all_to_all | solution.py:210
  166.0 0.1 sum.1
  166.1 23.2 %all_to_all.42.all_ref = bf16[64,16,256]{2,1,0:T(8,128)(2,1)S(1)} all-to-all(bf16[64,16,256]{2,1,0:T(8,128)(2,1)S(1)} %sum.1), channel_id=1, replica_groups=mesh['dom'=64,'feat'=4] {'dom'}, dimensions={0} | all-to-all | bytes 1048576 | tf_op jit(solution)/shard_map/all_to_all | solution.py:210
  189.2 1.0 finish.1
  (25 shorter events, 0.0 us)
Async XLA Ops:
  0.6 49.2 %copy-start = (f32[256]{0:T(256)S(1)}, f32[256]{0:T(256)}, u32[]{:S(2)}) copy-start(f32[256]{0:T(256)} %param.17) | copy-start | bytes 3076
  0.6 1.1 copy-start.3
  1.8 0.9 copy-start.12
  2.7 0.9 copy-start.13
  5.8 5.2 %copy-start.15 = (s32[1,2048]{1,0:T(1,128)S(1)}, s32[1,2048]{1,0:T(1,128)}, u32[]{:S(2)}) copy-start(s32[1,2048]{1,0:T(1,128)} %row_ref.1) | copy-start | bytes 24580
  5.8 5.5 %copy-start.4 = (bf16[1536,256]{1,0:T(8,128)(2,1)S(1)}, bf16[1536,256]{1,0:T(8,128)(2,1)}, u32[]{:S(2)}) copy-start(bf16[1536,256]{1,0:T(8,128)(2,1)} %x_ref.3) | copy-start | bytes 2359300
  5.8 24.1 %all-to-all-start = ((bf16[4,1536,128]{2,1,0:T(8,128)(2,1)}), bf16[4,1536,128]{2,1,0:T(8,128)(2,1)S(1)}, u32[]{:S(2)}, u32[]{:S(2)}) async-start(bf16[4,1536,128]{2,1,0:T(8,128)(2,1)} %project.1), calls=%async_computation | async-start | bytes 3145728 | tf_op jit(solution)/shard_map/all_to_all | solution.py:210
  19.0 0.9 copy-start.7
  29.9 2.8 %copy-start.2 = (bf16[2048,1536]{1,0:T(8,128)(2,1)S(1)}, bf16[2048,1536]{1,0:T(8,128)(2,1)}, u32[]{:S(2)}) copy-start(bf16[2048,1536]{1,0:T(8,128)(2,1)} %get-tuple-element.20.pick_ref) | copy-start | bytes 18874372
  32.7 16.9 %copy-start.20 = (s32[1,64]{1,0:T(1,128)S(1)}, s32[1,64]{1,0:T(1,128)}, u32[]{:S(2)}) copy-start(s32[1,64]{1,0:T(1,128)} %param.21) | copy-start | bytes 772
  32.7 17.3 %copy-start.14 = (s32[512,25]{0,1:T(8,128)S(1)}, s32[512,25]{0,1:T(8,128)}, u32[]{:S(2)}) copy-start(s32[512,25]{0,1:T(8,128)} %param.23) | copy-start | bytes 153604
  32.7 17.3 %copy-start.16 = (s32[512]{0:T(512)S(1)}, s32[512]{0:T(512)}, u32[]{:S(2)}) copy-start(s32[512]{0:T(512)} %param.24) | copy-start | bytes 6148
  32.7 17.3 %copy-start.17 = (s32[128,10]{0,1:T(8,128)S(1)}, s32[128,10]{0,1:T(8,128)}, u32[]{:S(2)}) copy-start(s32[128,10]{0,1:T(8,128)} %param.26) | copy-start | bytes 15364
  32.7 17.3 %copy-start.18 = (s32[512]{0:T(512)S(1)}, s32[512]{0:T(512)}, u32[]{:S(2)}) copy-start(s32[512]{0:T(512)} %param.22) | copy-start | bytes 6148
  32.7 17.3 %copy-start.19 = (s32[128]{0:T(128)S(1)}, s32[128]{0:T(128)}, u32[]{:S(2)}) copy-start(s32[128]{0:T(128)} %param.25) | copy-start | bytes 1540
  32.7 29.7 %copy-start.10 = (bf16[256,256]{1,0:T(8,128)(2,1)S(1)}, bf16[256,256]{1,0:T(8,128)(2,1)}, u32[]{:S(2)}) copy-start(bf16[256,256]{1,0:T(8,128)(2,1)} %second_near_ref.1) | copy-start | bytes 393220
  32.8 29.7 %copy-start.11 = (bf16[256,256]{1,0:T(8,128)(2,1)S(1)}, bf16[256,256]{1,0:T(8,128)(2,1)}, u32[]{:S(2)}) copy-start(bf16[256,256]{1,0:T(8,128)(2,1)} %second_self_ref.1) | copy-start | bytes 393220
  32.8 34.5 %copy-start.9 = (bf16[128,256]{1,0:T(8,128)(2,1)S(1)}, bf16[128,256]{1,0:T(8,128)(2,1)}, u32[]{:S(2)}) copy-start(bf16[128,256]{1,0:T(8,128)(2,1)} %cotangent_ref.1) | copy-start | bytes 196612
  35.5 31.5 %all-to-all-start.1 = ((bf16[64,32,128]{2,1,0:T(8,128)(2,1)}), bf16[64,32,128]{2,1,0:T(8,128)(2,1)S(1)}, u32[]{:S(2)}, u32[]{:S(2)}) async-start(bf16[64,32,128]{2,1,0:T(8,128)(2,1)} %bitcast.1), calls=%async_computation.1 | async-start | bytes 1048576 | tf_op jit(solution)/shard_map/all_to_all | solution.py:210
  61.1 1.4 copy-start.5
  67.3 1.6 copy-start.6
  95.4 9.1 %all-to-all-start.2 = ((bf16[4,128,128]{2,1,0:T(8,128)(2,1)}), bf16[4,128,128]{2,1,0:T(8,128)(2,1)S(1)}, u32[]{:S(2)}, u32[]{:S(2)}) async-start(bf16[4,128,128]{2,1,0:T(8,128)(2,1)} %broadcast_in_dim.2), calls=%async_computation.2 | async-start | bytes 262144 | tf_op jit(solution)/shard_map/all_to_all | solution.py:210
  98.7 2.8 %copy-start.1 = (bf16[1536,2048]{1,0:T(8,128)(2,1)S(1)}, bf16[1536,2048]{1,0:T(8,128)(2,1)}, u32[]{:S(2)}) copy-start(bf16[1536,2048]{1,0:T(8,128)(2,1)} %get-tuple-element.29.spread_ref) | copy-start | bytes 18874372
  104.5 31.6 %copy-start.8 = (bf16[256,1536]{1,0:T(8,128)(2,1)S(1)}, bf16[256,1536]{1,0:T(8,128)(2,1)}, u32[]{:S(2)}) copy-start(bf16[256,1536]{1,0:T(8,128)(2,1)} %copy-done.7) | copy-start | bytes 2359300
  104.5 24.2 %all-to-all-start.4 = ((bf16[4,1536,128]{2,1,0:T(8,128)(2,1)}), bf16[4,1536,128]{2,1,0:T(8,128)(2,1)S(1)}, u32[]{:S(2)}, u32[]{:S(2)}) async-start(bf16[4,1536,128]{2,1,0:T(8,128)(2,1)} %gather.1), calls=%async_computation.4 | async-start | bytes 3145728 | tf_op jit(solution)/shard_map/all_to_all | solution.py:210
  128.7 19.4 %all-to-all-start.6 = ((bf16[64,8,256]{2,1,0:T(8,128)(2,1)}), bf16[64,8,256]{2,1,0:T(8,128)(2,1)S(1)}, u32[]{:S(2)}, u32[]{:S(2)}) async-start(bf16[64,8,256]{2,1,0:T(8,128)(2,1)} %get-tuple-element.30), calls=%async_computation.6 | async-start | bytes 524288 | tf_op jit(solution)/shard_map/all_to_all | solution.py:210

commit v2 on v1

v2 whole, which is shorter than its diff:
```python
import functools

import jax
import jax.numpy as jnp
from jax import lax
from jax.experimental import pallas as pl
from jax.experimental.pallas import tpu as pltpu
from jax.sharding import PartitionSpec as P

BF16 = jnp.bfloat16
F32 = jnp.float32
I32 = jnp.int32


def dot(left, right, left_dim=1, right_dim=0):
    return lax.dot_general(
        left, right, (((left_dim,), (right_dim,)), ((), ())), preferred_element_type=F32
    )


def call(body, outs, args, name, flops=0, moved=0, vmem=16, scratch=(), scalars=0):
    specs = [
        pl.BlockSpec(memory_space=pltpu.SMEM if at < scalars else pltpu.VMEM)
        for at in range(len(args))
    ]
    out_specs = [pl.BlockSpec(memory_space=pltpu.VMEM) for _ in outs]
    return pl.pallas_call(
        body,
        out_shape=[jax.ShapeDtypeStruct(shape, dtype) for shape, dtype in outs],
        in_specs=specs,
        out_specs=out_specs,
        scratch_shapes=scratch,
        name=name,
        compiler_params=pltpu.CompilerParams(vmem_limit_bytes=vmem << 20),
        cost_estimate=pl.CostEstimate(flops=flops, bytes_accessed=moved, transcendentals=0),
    )(*args)


def pick_body(row_ref, x_ref, self_ref, near_ref, out_ref, weight_ref, slices):
    rows = x_ref.shape[0]
    half = self_ref.shape[1] // slices
    for at in range(slices):
        span = slice(at * half, (at + 1) * half)
        weight_ref[:, 2 * at * half : 2 * (at + 1) * half] = jnp.concatenate(
            [self_ref[:, span], near_ref[:, span]], axis=1
        )
    step = 128
    lane = lax.broadcasted_iota(I32, (step, step), 1)

    def fill(at, carry):
        start = pl.multiple_of(at * step, step)
        wanted = jnp.broadcast_to(row_ref[:, pl.ds(start, step)], (step, step)).T
        picks = jnp.concatenate(
            [
                jnp.where(wanted == lane + low, 1.0, 0.0).astype(BF16)
                for low in range(0, rows, step)
            ],
            axis=1,
        )
        out_ref[pl.ds(start, step), :] = dot(picks, x_ref[...]).astype(BF16)
        return carry

    lax.fori_loop(0, out_ref.shape[0] // step, fill, 0, unroll=4)


def count_body(
    self_ref, near_ref, degree_ref, seed_ref, seed_near_ref,
    self_table, near_table, seed_table, seed_near_table, live_ref,
    capacity, per,
):
    slots, mids = near_table.shape
    fan = near_ref.shape[0]
    quarter = slots * per // capacity
    deep = capacity.bit_length() - 1
    low = per.bit_length() - 1

    def placed(slot):
        return (
            ((slot >> low) & (capacity // per - 1)) * quarter
            + (slot >> deep) * per
            + (slot & (per - 1))
        )

    step = 32
    live = lax.broadcasted_iota(I32, (fan, mids), 0) < degree_ref[...]
    live_ref[...] = jnp.where(live, placed(near_ref[...]), -1)
    own = placed(self_ref[...])

    def fill(at, carry):
        span = pl.ds(pl.multiple_of(at * step, step), step)
        line = lax.broadcasted_iota(I32, (step, mids), 0) + at * step
        total = jnp.zeros((step, mids), F32)
        for j in range(fan):
            total = total + jnp.where(live_ref[j : j + 1, :] == line, 1.0, 0.0)
        near_table[span, :] = total.astype(BF16)
        self_table[span, :] = jnp.where(own == line, 1.0, 0.0).astype(BF16)
        return carry

    lax.fori_loop(0, slots // step, fill, 0)
    seeds = seed_table.shape[1]
    line = lax.broadcasted_iota(I32, (mids, seeds), 0)
    seed_table[...] = jnp.where(seed_ref[...] == line, 1.0, 0.0).astype(BF16)
    total = jnp.zeros((mids, seeds), F32)
    for j in range(seed_near_ref.shape[0]):
        total = total + jnp.where(seed_near_ref[j : j + 1, :] == line, 1.0, 0.0)
    seed_near_table[...] = total.astype(BF16)


def slot_rows(x_ref, at):
    peers, _, per, cols = x_ref.shape
    return x_ref[:, at].astype(F32).reshape(peers * per, cols).astype(BF16)


def project_body(me_ref, x_ref, *refs):
    weight_refs, out_ref = refs[:-1], refs[-1]
    slices, _, width = out_ref.shape
    total = None
    for shift, weight_ref in enumerate(weight_refs):
        at = lax.rem(me_ref[0] + slices - shift, slices)
        part = dot(slot_rows(x_ref, at), weight_ref[...])
        total = part if total is None else total + part
    total = total.astype(BF16)
    for at in range(slices):
        out_ref[at] = total[:, at * width : (at + 1) * width]


def turn_body(x_ref, out_ref):
    cols = x_ref.shape[3]
    for at in range(x_ref.shape[1]):
        out_ref[at * cols : (at + 1) * cols, :] = slot_rows(x_ref, at).T


def owner_body(
    me_ref, slot_ref, mask_ref, self_table, near_table, degree_ref, bias_ref, seed_table,
    seed_near_table, second_self_ref, second_near_ref, cotangent_ref, grad_ref, seeds_ref,
    fan_two,
):
    slots, width = slot_ref.shape
    half = width // 2
    mine = pl.ds(pl.multiple_of(me_ref[0] * half, half), half)
    degree = degree_ref[...].astype(F32)
    table = slot_ref[...] * mask_ref[...]
    own = dot(table, self_table[...], 0, 0)[:half]
    near = dot(table, near_table[...], 0, 0)[half:]
    pre = own + near / degree + bias_ref[mine, :]
    sigma = 1.0 / (1.0 + jnp.exp(-pre))
    active = (pre * sigma).astype(BF16)
    slope = (sigma * (1.0 + pre * (1.0 - sigma))).astype(BF16).astype(F32)
    seeds_ref[:half, :] = dot(active, seed_table[...]).astype(BF16)
    seeds_ref[half:, :] = (dot(active, seed_near_table[...]) / fan_two).astype(BF16)
    back_self = dot(second_self_ref[mine, :], cotangent_ref[...], 1, 1)
    back_near = dot(second_near_ref[mine, :], cotangent_ref[...], 1, 1) / fan_two

    def spread(back, picks):
        high = back.astype(BF16)
        low = (back - high.astype(F32)).astype(BF16)
        both = dot(jnp.concatenate([high, low], axis=0), picks, 1, 1)
        return both[:half] + both[half:]

    grad_active = spread(back_self, seed_table[...]) + spread(back_near, seed_near_table[...])
    grad_pre = grad_active * slope
    nothing = jnp.zeros(grad_pre.shape, BF16)
    for_self = jnp.concatenate([grad_pre.astype(BF16), nothing], axis=0)
    for_near = jnp.concatenate([nothing, (grad_pre / degree).astype(BF16)], axis=0)
    step = slots // 4
    for piece in range(4):
        span = pl.ds(piece * step, step)
        grad = dot(self_table[span, :], for_self, 1, 1) + dot(near_table[span, :], for_near, 1, 1)
        grad_ref[span, :] = grad.astype(BF16) * mask_ref[span, :]


def seeds_body(me_ref, second_self_ref, second_near_ref, cotangent_ref, *refs):
    seeds_refs, (out_ref, grad_ref) = refs[:-2], refs[-2:]
    slices = len(seeds_refs)
    half = seeds_refs[0].shape[0] // 2
    tiles = grad_ref.shape[0] // 2
    per = tiles // slices
    shaped = (per,) + grad_ref.shape[1:]
    total = jnp.zeros(out_ref.shape, F32)
    cotangent = cotangent_ref[...]
    for shift, seeds_ref in enumerate(seeds_refs):
        at = lax.rem(me_ref[0] + slices - shift, slices)
        rows = pl.ds(pl.multiple_of(at * half, half), half)
        total = total + dot(seeds_ref[:half, :], second_self_ref[rows, :], 0, 0)
        total = total + dot(seeds_ref[half:, :], second_near_ref[rows, :], 0, 0)
        grad = dot(seeds_ref[...], cotangent)
        grad_ref[pl.ds(at * per, per)] = grad[:half].reshape(shaped).astype(BF16)
        grad_ref[pl.ds(tiles + at * per, per)] = grad[half:].reshape(shaped).astype(BF16)
    out_ref[...] = total.astype(BF16)


def weight_body(xt_ref, grads_ref, out_ref):
    slices, step = out_ref.shape[:2]
    grads = jnp.concatenate([grads_ref[at] for at in range(slices)], axis=1)
    for at in range(slices):
        out_ref[at] = dot(xt_ref[pl.ds(at * step, step), :], grads).astype(BF16)


def merge_body(parts_ref, second_ref, out_ref):
    slices, _, cols = parts_ref.shape
    width = cols // slices
    half = width // 2
    tiles = out_ref.shape[0] // 2
    lines = out_ref.shape[1] // 2
    total = jnp.sum(parts_ref[...].astype(F32), axis=0)
    for side in range(2):
        part = jnp.concatenate(
            [
                total[:, at * width + side * half : at * width + (side + 1) * half]
                for at in range(slices)
            ],
            axis=1,
        )
        shaped = (tiles, lines, part.shape[1])
        out_ref[pl.ds(side * tiles, tiles), :lines] = part.reshape(shaped).astype(BF16)
    out_ref[:, lines:] = second_ref[...]


def sum_body(parts_ref, out_ref):
    total = jnp.sum(parts_ref[...].astype(F32), axis=0).astype(BF16)
    out_ref[...] = jnp.broadcast_to(total[None], out_ref.shape)


def finish_body(all_ref, first_self_ref, first_near_ref, second_self_ref, second_near_ref):
    peers, tall, width = all_ref.shape
    lines = tall // 2
    tiles = peers // 2
    value = all_ref[...].astype(F32)
    first_self_ref[...] = value[:tiles, :lines].reshape(tiles * lines, width)
    first_near_ref[...] = value[tiles:, :lines].reshape(tiles * lines, width)
    second_self_ref[...] = value[:tiles, lines:].reshape(tiles * lines, width)
    second_near_ref[...] = value[tiles:, lines:].reshape(tiles * lines, width)


def exchange(value, axis):
    return lax.all_to_all(value, axis, split_axis=0, concat_axis=0, tiled=True)


def per_device(
    features,
    first_self,
    first_neighbor,
    first_bias,
    second_self,
    second_neighbor,
    send_rows,
    arrive_count,
    self_slot,
    neighbor_slot,
    degree,
    seed_self,
    seed_neighbor,
    cotangent,
):
    peers = lax.axis_size("dom")
    slices = lax.axis_size("feat")
    rows, slice_cols = features.shape
    hidden = first_self.shape[1]
    half = hidden // slices
    width = 2 * half
    slots = send_rows.shape[1]
    capacity = slots // peers
    per = capacity // slices
    quarter = slots // slices
    mids, fan = neighbor_slot.shape
    seeds, fan_two = seed_neighbor.shape
    out_cols = second_self.shape[1]
    lines = 2 * hidden // peers
    me = lax.axis_index("feat").astype(I32).reshape(1)

    def around(value):
        return [value] + [
            lax.ppermute(value, "feat", [(at, (at + shift) % slices) for at in range(slices)])
            for shift in range(1, slices)
        ]

    picked, weight = call(
        functools.partial(pick_body, slices=slices),
        [((slots, slice_cols), BF16), ((slice_cols, 2 * hidden), BF16)],
        (send_rows, features, first_self, first_neighbor), "pick",
        2 * slots * rows * slice_cols, 2 * slots * rows,
    )
    routed = exchange(picked.reshape(peers * slices, per, slice_cols), ("dom", "feat"))
    routed = routed.reshape(peers, slices, per, slice_cols)
    weights = around(weight)

    self_table, near_table, seed_table, seed_near_table = call(
        functools.partial(count_body, capacity=capacity, per=per),
        [((slots, mids), BF16), ((slots, mids), BF16), ((mids, seeds), BF16), ((mids, seeds), BF16)],
        (
            self_slot.reshape(1, mids), neighbor_slot.T, degree.reshape(1, mids),
            seed_self.reshape(1, seeds), seed_neighbor.T,
        ),
        "count", 0, 16 * slots * mids, scratch=[pltpu.VMEM((fan, mids), I32)],
    )
    slot_at = lax.broadcasted_iota(I32, (slices, peers, per, width), 0) * per
    slot_at = slot_at + lax.broadcasted_iota(I32, (slices, peers, per, width), 2)
    mask = (slot_at < arrive_count.reshape(1, peers, 1, 1)).astype(BF16).reshape(slots, width)
    bias = first_bias.reshape(hidden, 1)

    routed, seed_table = lax.optimization_barrier((routed, seed_table))

    (projected,) = call(
        project_body, [((slices, quarter, width), BF16)], (me, routed, *weights), "project",
        2 * quarter * slices * slice_cols * 2 * hidden, 4 * quarter * slices * slice_cols,
        scalars=1,
    )
    table = exchange(projected, "feat").reshape(slots, width)
    (turned,) = call(
        turn_body, [((slices * slice_cols, quarter), BF16)], (routed,), "turn",
        0, 8 * quarter * slices * slice_cols,
    )

    grad_table, own_seeds = call(
        functools.partial(owner_body, fan_two=fan_two),
        [((slots, width), BF16), ((width, seeds), BF16)],
        (
            me, table, mask, self_table, near_table, degree.reshape(1, mids), bias, seed_table,
            seed_near_table, second_self, second_neighbor, cotangent,
        ),
        "owner", 8 * slots * mids * width, 4 * slots * mids, scalars=1,
    )
    grads = exchange(grad_table.reshape(slices, quarter, width), "feat")
    seed_embedding, grad_second = call(
        seeds_body, [((seeds, out_cols), BF16), ((peers, lines, out_cols), BF16)],
        (me, second_self, second_neighbor, cotangent, *around(own_seeds)), "seeds",
        8 * seeds * hidden * out_cols, 2 * slots * width, scalars=1,
    )
    (partials,) = call(
        weight_body, [((slices, slice_cols, 2 * hidden), BF16)], (turned, grads), "weight",
        2 * quarter * slices * slice_cols * 2 * hidden, 4 * quarter * slices * slice_cols,
    )
    partials = exchange(partials, "feat")
    (merged,) = call(
        merge_body, [((peers, 2 * lines, hidden), BF16)], (partials, grad_second), "merge",
        0, 8 * peers * lines * hidden,
    )
    merged = exchange(merged, "dom")
    (summed,) = call(
        sum_body, [((peers, 2 * lines, hidden), BF16)], (merged,), "sum",
        0, 8 * peers * lines * hidden,
    )
    summed = exchange(summed, "dom")
    grad_first_self, grad_first_neighbor, grad_second_self, grad_second_neighbor = call(
        finish_body, [((slice_cols, hidden), F32)] * 2 + [((hidden, out_cols), F32)] * 2,
        (summed,), "finish", 0, 8 * peers * lines * hidden,
    )
    return (
        seed_embedding,
        grad_first_self,
        grad_first_neighbor,
        grad_second_self,
        grad_second_neighbor,
    )


def solution(mesh):
    in_specs = (
        P("dom", "feat"),
        P("feat", None),
        P("feat", None),
        P(),
        P(),
        P(),
        P("dom", None),
        P("dom", None),
        P("dom"),
        P("dom", None),
        P("dom"),
        P("dom"),
        P("dom", None),
        P("dom", None),
    )
    out_specs = (P("dom", None), P("feat", None), P("feat", None), P(), P())
    return jax.shard_map(
        per_device, mesh=mesh, in_specs=in_specs, out_specs=out_specs, check_vma=False
    )
```

time: 191 us -> 159 us (0.83)
  blocking collectives: 64.4 us -> 49.3 us
  Pallas kernels: 32.3 us -> 23.9 us
  waiting for transfers between devices: 44.2 us -> 37.8 us
  local copies, waits for them, and re-layouts: 14.1 us -> 10.1 us
    all_to_all x5 -> x4, waiting for transfers between devices: 44.2 us -> 29.2 us  [exchange(): return lax.all_to_all(value, axis, split_axis=0, concat_axis=0, tiled=True)]
    all_to_all x3 -> x2, blocking collectives: 64.4 us -> 49.3 us  [exchange(): return lax.all_to_all(value, axis, split_axis=0, concat_axis=0, tiled=True)]
    ppermute x0 -> x6, starting transfers between devices: none -> 10 us  [around(): lax.ppermute(value, 'feat', [(at, (at + shift) % slices) for at in range(...]
    ppermute x0 -> x6, waiting for transfers between devices: none -> 8.62 us  [around(): lax.ppermute(value, 'feat', [(at, (at + shift) % slices) for at in range(...]
    pallas_call x10, Pallas kernels: 32.3 us -> 23.9 us  [call(): pl.pallas_call(body, out_shape=[jax.ShapeDtypeStruct(shape, dtype) for sh...]
    all_to_all x5 -> x4, starting transfers between devices: 34.4 us -> 26.1 us  [exchange(): return lax.all_to_all(value, axis, split_axis=0, concat_axis=0, tiled=True)]
    unnamed x42 -> x36, local copies, waits for them, and re-layouts: 12.4 us -> 9.51 us
  transfers between devices with their start and end apart: 5 -> 10, of which waited for: 4 -> 5; matrix products, arithmetic and copies ran while one was open for 0% -> 0% of each run, Pallas kernels for 13% -> 8%
where the time goes in v2:
time: 159 us; the launch traced here: 158 us
  blocking collectives  49.3 us (31%)
  waiting for transfers between devices  37.8 us (24%)
  starting transfers between devices  36.2 us (23%)
  Pallas kernels  23.9 us (15%)
  local copies, waits for them, and re-layouts  10.1 us (6%)
    all_to_all x2, blocking collectives, exchange(): return lax.all_to_all(value, axis, split_axis=0, concat_axis=0, tiled=True)  49.3 us
    all_to_all x4, waiting for transfers between devices, exchange(): return lax.all_to_all(value, axis, split_axis=0, concat_axis=0, tiled=True)  29.2 us
    all_to_all x4, starting transfers between devices, exchange(): return lax.all_to_all(value, axis, split_axis=0, concat_axis=0, tiled=True)  26.1 us
    pallas_call x10, Pallas kernels, call(): pl.pallas_call(body, out_shape=[jax.ShapeDtypeStruct(shape, dtype) for sh...  23.9 us
    ppermute x6, starting transfers between devices, around(): lax.ppermute(value, 'feat', [(at, (at + shift) % slices) for at in range(...  10 us
    unnamed x36, local copies, waits for them, and re-layouts  9.51 us
    ppermute x6, waiting for transfers between devices, around(): lax.ppermute(value, 'feat', [(at, (at + shift) % slices) for at in range(...  8.62 us
  transfers between devices with their start and end apart: 10, of which 5 were waited for; matrix products, arithmetic and copies ran while one was open for 0% of the time, Pallas kernels for 8%

profile of v2, /device:TPU:1, one launch (start us, length us, event | category | flops | bytes accessed | tf_op | source)
XLA Modules:
  0.0 158.2 jit_solution(16012588163436245720)
XLA Ops:
  0.6 1.1 copy-done.12
  1.8 0.9 copy-done.13
  2.7 0.9 copy-done.14
  3.6 0.7 copy-done.15
  4.3 3.7 %pick.1 = (bf16[2048,256]{1,0:T(8,128)(2,1)}, bf16[256,512]{1,0:T(8,128)(2,1)S(1)}) custom-call(s32[1,2048]{1,0:T(1,128)S(1)} %copy-done.15, bf16[1536,256]{1,0:T(8,128)(2,1)S(1)} %copy-done.12, bf16[256,256]{1,0:T(8,128)(2,1)S(1)} %copy-done.13, bf16[256,256]{1,0:T(8,128)(2,1)S(1)} %copy-done.14), custom_call_target="tpu_custom_call" | custom-call | flops 1610612736 | bytes 6291456 | tf_op jit(solution)/shard_map/pick/pallas_call | solution.py:27
  8.0 0.0 copy-start.11
  8.0 15.7 %all-to-all-start = ((bf16[256,8,256]{2,1,0:T(8,128)(2,1)}), bf16[256,8,256]{2,1,0:T(8,128)(2,1)S(1)}, u32[]{:S(2)}, u32[]{:S(2)}) async-start(bf16[256,8,256]{2,1,0:T(8,128)(2,1)} %bitcast.1), calls=%async_computation | async-start | bytes 2097152 | tf_op jit(solution)/shard_map/all_to_all | solution.py:236
  23.7 0.0 copy-start.17
  23.7 0.0 copy-start.16
  23.7 1.5 collective-permute-start
  25.2 2.4 %collective-permute-start.1 = (bf16[256,512]{1,0:T(8,128)(2,1)S(1)}, bf16[256,512]{1,0:T(8,128)(2,1)S(1)}, u32[]{:S(2)}, u32[]{:S(2)}) collective-permute-start(bf16[256,512]{1,0:T(8,128)(2,1)S(1)} %get-tuple-element.24.refs_0_), channel_id=1, source_target_pairs={{0,2},{1,3},{2,0},{3,1},{4,6},{5,7},{6,4},{7,5},{8,10},{9,11},{10,... | collective-permute-start | bytes 786440 | tf_op jit(solution)/shard_map/ppermute | solution.py:273
  27.6 1.1 collective-permute-start.2
  28.8 11.1 %count.1 = (bf16[2048,512]{1,0:T(8,128)(2,1)S(1)}, bf16[2048,512]{1,0:T(8,128)(2,1)S(1)}, bf16[512,128]{1,0:T(8,128)(2,1)S(1)}, bf16[512,128]{1,0:T(8,128)(2,1)S(1)}) custom-call(s32[1,512]{1,0:T(1,128)S(1)} %bitcast.19, s32[25,512]{1,0:T(8,128)S(1)} %bitcast.15, s32[1,512]{1,0:T(1,128)S(1)} %bitcast.16, s32[1,128]{1,0:T(1,128)S(1)} %bitcast.20, ...), custom_call_target="tpu_custom_call" | custom-call | bytes 16777216 | tf_op jit(solution)/shard_map/count/pallas_call | solution.py:27
  39.9 1.3 copy-done
  41.2 1.3 copy-done.2
  42.5 13.6 %all-to-all-done = bf16[256,8,256]{2,1,0:T(8,128)(2,1)S(1)} async-done(((bf16[256,8,256]{2,1,0:T(8,128)(2,1)}), bf16[256,8,256]{2,1,0:T(8,128)(2,1)S(1)}, u32[]{:S(2)}, u32[]{:S(2)}) %all-to-all-start) | async-done | bytes 1048608 | tf_op jit(solution)/shard_map/all_to_all | solution.py:236
  56.2 0.0 collective-permute-done.refs_1_
  56.2 0.0 collective-permute-done.1.refs_2_
  56.2 0.0 collective-permute-done.2.refs_3_
  56.2 0.0 copy-start.4
  56.2 0.0 copy-start.5
  56.2 0.0 copy-start.6
  56.2 1.5 project.1
  57.7 3.5 %all-to-all-start.1 = ((bf16[4,512,128]{2,1,0:T(8,128)(2,1)}), bf16[4,512,128]{2,1,0:T(8,128)(2,1)S(1)}, u32[]{:S(2)}, u32[]{:S(2)}) async-start(bf16[4,512,128]{2,1,0:T(8,128)(2,1)} %project.1), calls=%async_computation.1 | async-start | bytes 1048576 | tf_op jit(solution)/shard_map/all_to_all | solution.py:236
  61.2 0.1 fusion
  61.3 0.1 reshape.57
  61.5 0.1 copy.19.bias_ref
  61.6 8.3 %all-to-all-done.1 = bf16[4,512,128]{2,1,0:T(8,128)(2,1)S(1)} async-done(((bf16[4,512,128]{2,1,0:T(8,128)(2,1)}), bf16[4,512,128]{2,1,0:T(8,128)(2,1)S(1)}, u32[]{:S(2)}, u32[]{:S(2)}) %all-to-all-start.1) | async-done | bytes 524320 | tf_op jit(solution)/shard_map/all_to_all | solution.py:236
  69.9 0.3 lt.18.mask_ref
  70.3 1.6 copy-done.1
  71.9 1.6 %copy-done.3 = bf16[2048,512]{1,0:T(8,128)(2,1)S(1)} copy-done((bf16[2048,512]{1,0:T(8,128)(2,1)S(1)}, bf16[2048,512]{1,0:T(8,128)(2,1)}, u32[]{:S(2)}) %copy-start.3) | copy-done | bytes 2097176
  73.5 3.2 %owner.1 = (bf16[2048,128]{1,0:T(8,128)(2,1)}, bf16[128,128]{1,0:T(8,128)(2,1)S(1)}) custom-call(s32[1]{0:T(128)} %bitcast.me_ref, bf16[2048,128]{1,0:T(8,128)(2,1)S(1)} %bitcast.14, bf16[2048,128]{1,0:T(8,128)(2,1)S(1)} %lt.18.mask_ref, bf16[2048,512]{1,0:T(8,128)(2,1)S(1)} %copy-done.1, bf16[2048,512]{1,0:T(8,128)(2,1)S(1)} %copy-done.3, ...), custom_call_target="tpu_custom_call" | custom-call | flops 1073741824 | bytes 4194304 | tf_op jit(solution)/shard_map/owner/pallas_call | solution.py:27
  76.7 3.5 %all-to-all-start.2 = ((bf16[4,512,128]{2,1,0:T(8,128)(2,1)}), bf16[4,512,128]{2,1,0:T(8,128)(2,1)S(1)}, u32[]{:S(2)}, u32[]{:S(2)}) async-start(bf16[4,512,128]{2,1,0:T(8,128)(2,1)} %bitcast.11), calls=%async_computation.2 | async-start | bytes 1048576 | tf_op jit(solution)/shard_map/all_to_all | solution.py:236
  80.2 0.3 turn.1.xt_ref
  80.5 7.2 %all-to-all-done.2.grads_ref = bf16[4,512,128]{2,1,0:T(8,128)(2,1)S(1)} async-done(((bf16[4,512,128]{2,1,0:T(8,128)(2,1)}), bf16[4,512,128]{2,1,0:T(8,128)(2,1)S(1)}, u32[]{:S(2)}, u32[]{:S(2)}) %all-to-all-start.2) | async-done | bytes 524320 | tf_op jit(solution)/shard_map/all_to_all | solution.py:236
  87.7 1.7 %weight.1 = bf16[4,256,512]{2,1,0:T(8,128)(2,1)} custom-call(bf16[1024,512]{1,0:T(8,128)(2,1)S(1)} %turn.1.xt_ref, bf16[4,512,128]{2,1,0:T(8,128)(2,1)S(1)} %all-to-all-done.2.grads_ref), custom_call_target="tpu_custom_call" | custom-call | flops 536870912 | bytes 2097152 | tf_op jit(solution)/shard_map/weight/pallas_call | solution.py:27
  89.4 3.5 %all-to-all-start.3 = ((bf16[4,256,512]{2,1,0:T(8,128)(2,1)}), bf16[4,256,512]{2,1,0:T(8,128)(2,1)S(1)}, u32[]{:S(2)}, u32[]{:S(2)}) async-start(bf16[4,256,512]{2,1,0:T(8,128)(2,1)} %weight.1), calls=%async_computation.3 | async-start | bytes 2097152 | tf_op jit(solution)/shard_map/all_to_all | solution.py:236
  92.9 1.4 collective-permute-start.3
  94.3 2.4 %collective-permute-start.4 = (bf16[128,128]{1,0:T(8,128)(2,1)S(1)}, bf16[128,128]{1,0:T(8,128)(2,1)S(1)}, u32[]{:S(2)}, u32[]{:S(2)}) collective-permute-start(bf16[128,128]{1,0:T(8,128)(2,1)S(1)} %get-tuple-element.29.refs_0_), channel_id=1, source_target_pairs={{0,2},{1,3},{2,0},{3,1},{4,6},{5,7},{6,4},{7,5},{8,10},{9,11},{10,... | collective-permute-start | bytes 98312 | tf_op jit(solution)/shard_map/ppermute | solution.py:273
  96.7 1.2 collective-permute-start.5
  97.9 4.5 %collective-permute-done.3.refs_1_ = bf16[128,128]{1,0:T(8,128)(2,1)S(1)} collective-permute-done((bf16[128,128]{1,0:T(8,128)(2,1)S(1)}, bf16[128,128]{1,0:T(8,128)(2,1)S(1)}, u32[]{:S(2)}, u32[]{:S(2)}) %collective-permute-start.3) | collective-permute-done | bytes 32800 | tf_op jit(solution)/shard_map/ppermute | solution.py:273
  102.4 4.1 %collective-permute-done.4.refs_2_ = bf16[128,128]{1,0:T(8,128)(2,1)S(1)} collective-permute-done((bf16[128,128]{1,0:T(8,128)(2,1)S(1)}, bf16[128,128]{1,0:T(8,128)(2,1)S(1)}, u32[]{:S(2)}, u32[]{:S(2)}) %collective-permute-start.4) | collective-permute-done | bytes 32800 | tf_op jit(solution)/shard_map/ppermute | solution.py:273
  106.5 1.0 seeds.1
  107.5 0.2 merge.1
  107.8 25.9 %all_to_all.30.parts_ref = bf16[64,16,256]{2,1,0:T(8,128)(2,1)S(1)} all-to-all(bf16[64,16,256]{2,1,0:T(8,128)(2,1)S(1)} %merge.1), channel_id=1, replica_groups=mesh['dom'=64,'feat'=4] {'dom'}, dimensions={0} | all-to-all | bytes 1048576 | tf_op jit(solution)/shard_map/all_to_all | solution.py:236
  133.7 0.1 sum.1
  133.8 23.4 %all_to_all.31.all_ref = bf16[64,16,256]{2,1,0:T(8,128)(2,1)S(1)} all-to-all(bf16[64,16,256]{2,1,0:T(8,128)(2,1)S(1)} %sum.1), channel_id=1, replica_groups=mesh['dom'=64,'feat'=4] {'dom'}, dimensions={0} | all-to-all | bytes 1048576 | tf_op jit(solution)/shard_map/all_to_all | solution.py:236
  157.2 1.0 finish.1
  (25 shorter events, 0.1 us)
Async XLA Ops:
  0.6 1.1 copy-start.12
  1.8 0.9 copy-start.13
  2.7 0.9 copy-start.14
  3.6 0.7 copy-start.15
  8.0 20.8 %copy-start.7 = (s32[512,25]{0,1:T(8,128)S(1)}, s32[512,25]{0,1:T(8,128)}, u32[]{:S(2)}) copy-start(s32[512,25]{0,1:T(8,128)} %param.23) | copy-start | bytes 153604
  8.0 20.8 %copy-start.8 = (s32[512]{0:T(512)S(1)}, s32[512]{0:T(512)}, u32[]{:S(2)}) copy-start(s32[512]{0:T(512)} %param.24) | copy-start | bytes 6148
  8.0 20.8 %copy-start.9 = (s32[128,10]{0,1:T(8,128)S(1)}, s32[128,10]{0,1:T(8,128)}, u32[]{:S(2)}) copy-start(s32[128,10]{0,1:T(8,128)} %param.26) | copy-start | bytes 15364
  8.0 20.8 %copy-start.10 = (s32[512]{0:T(512)S(1)}, s32[512]{0:T(512)}, u32[]{:S(2)}) copy-start(s32[512]{0:T(512)} %param.22) | copy-start | bytes 6148
  8.0 20.8 %copy-start.11 = (s32[128]{0:T(128)S(1)}, s32[128]{0:T(128)}, u32[]{:S(2)}) copy-start(s32[128]{0:T(128)} %param.25) | copy-start | bytes 1540
  8.0 48.1 %all-to-all-start = ((bf16[256,8,256]{2,1,0:T(8,128)(2,1)}), bf16[256,8,256]{2,1,0:T(8,128)(2,1)S(1)}, u32[]{:S(2)}, u32[]{:S(2)}) async-start(bf16[256,8,256]{2,1,0:T(8,128)(2,1)} %bitcast.1), calls=%async_computation | async-start | bytes 2097152 | tf_op jit(solution)/shard_map/all_to_all | solution.py:236
  23.7 37.5 %copy-start.17 = (s32[1,64]{1,0:T(1,128)S(1)}, s32[1,64]{1,0:T(1,128)}, u32[]{:S(2)}) copy-start(s32[1,64]{1,0:T(1,128)} %param.21) | copy-start | bytes 772
  23.7 37.7 %copy-start.16 = (f32[256]{0:T(256)S(1)}, f32[256]{0:T(256)}, u32[]{:S(2)}) copy-start(f32[256]{0:T(256)} %param.17) | copy-start | bytes 3076
  23.7 32.4 %collective-permute-start = (bf16[256,512]{1,0:T(8,128)(2,1)S(1)}, bf16[256,512]{1,0:T(8,128)(2,1)S(1)}, u32[]{:S(2)}, u32[]{:S(2)}) collective-permute-start(bf16[256,512]{1,0:T(8,128)(2,1)S(1)} %get-tuple-element.24.refs_0_), channel_id=1, source_target_pairs={{0,1},{1,2},{2,3},{3,0},{4,5},{5,6},{6,7},{7,4},{8,9},{9,10},{10,1... | collective-permute-start | bytes 786440 | tf_op jit(solution)/shard_map/ppermute | solution.py:273
  25.2 31.0 %collective-permute-start.1 = (bf16[256,512]{1,0:T(8,128)(2,1)S(1)}, bf16[256,512]{1,0:T(8,128)(2,1)S(1)}, u32[]{:S(2)}, u32[]{:S(2)}) collective-permute-start(bf16[256,512]{1,0:T(8,128)(2,1)S(1)} %get-tuple-element.24.refs_0_), channel_id=1, source_target_pairs={{0,2},{1,3},{2,0},{3,1},{4,6},{5,7},{6,4},{7,5},{8,10},{9,11},{10,... | collective-permute-start | bytes 786440 | tf_op jit(solution)/shard_map/ppermute | solution.py:273
  27.6 28.5 %collective-permute-start.2 = (bf16[256,512]{1,0:T(8,128)(2,1)S(1)}, bf16[256,512]{1,0:T(8,128)(2,1)S(1)}, u32[]{:S(2)}, u32[]{:S(2)}) collective-permute-start(bf16[256,512]{1,0:T(8,128)(2,1)S(1)} %get-tuple-element.24.refs_0_), channel_id=1, source_target_pairs={{0,3},{1,0},{2,1},{3,2},{4,7},{5,4},{6,5},{7,6},{8,11},{9,8},{10,9... | collective-permute-start | bytes 786440 | tf_op jit(solution)/shard_map/ppermute | solution.py:273
  39.9 1.3 copy-start
  41.2 1.3 copy-start.2
  56.2 14.1 %copy-start.4 = (bf16[256,256]{1,0:T(8,128)(2,1)S(1)}, bf16[256,256]{1,0:T(8,128)(2,1)}, u32[]{:S(2)}) copy-start(bf16[256,256]{1,0:T(8,128)(2,1)} %second_self_ref.3) | copy-start | bytes 393220
  56.2 14.1 %copy-start.5 = (bf16[256,256]{1,0:T(8,128)(2,1)S(1)}, bf16[256,256]{1,0:T(8,128)(2,1)}, u32[]{:S(2)}) copy-start(bf16[256,256]{1,0:T(8,128)(2,1)} %second_near_ref.3) | copy-start | bytes 393220
  56.2 14.1 %copy-start.6 = (bf16[128,256]{1,0:T(8,128)(2,1)S(1)}, bf16[128,256]{1,0:T(8,128)(2,1)}, u32[]{:S(2)}) copy-start(bf16[128,256]{1,0:T(8,128)(2,1)} %cotangent_ref.3) | copy-start | bytes 196612
  57.7 12.2 %all-to-all-start.1 = ((bf16[4,512,128]{2,1,0:T(8,128)(2,1)}), bf16[4,512,128]{2,1,0:T(8,128)(2,1)S(1)}, u32[]{:S(2)}, u32[]{:S(2)}) async-start(bf16[4,512,128]{2,1,0:T(8,128)(2,1)} %project.1), calls=%async_computation.1 | async-start | bytes 1048576 | tf_op jit(solution)/shard_map/all_to_all | solution.py:236
  70.3 1.6 %copy-start.1 = (bf16[2048,512]{1,0:T(8,128)(2,1)S(1)}, bf16[2048,512]{1,0:T(8,128)(2,1)}, u32[]{:S(2)}) copy-start(bf16[2048,512]{1,0:T(8,128)(2,1)} %copy-done) | copy-start | bytes 6291460
  71.9 1.6 %copy-start.3 = (bf16[2048,512]{1,0:T(8,128)(2,1)S(1)}, bf16[2048,512]{1,0:T(8,128)(2,1)}, u32[]{:S(2)}) copy-start(bf16[2048,512]{1,0:T(8,128)(2,1)} %copy-done.2) | copy-start | bytes 6291460
  76.7 11.0 %all-to-all-start.2 = ((bf16[4,512,128]{2,1,0:T(8,128)(2,1)}), bf16[4,512,128]{2,1,0:T(8,128)(2,1)S(1)}, u32[]{:S(2)}, u32[]{:S(2)}) async-start(bf16[4,512,128]{2,1,0:T(8,128)(2,1)} %bitcast.11), calls=%async_computation.2 | async-start | bytes 1048576 | tf_op jit(solution)/shard_map/all_to_all | solution.py:236
  89.4 18.2 %all-to-all-start.3 = ((bf16[4,256,512]{2,1,0:T(8,128)(2,1)}), bf16[4,256,512]{2,1,0:T(8,128)(2,1)S(1)}, u32[]{:S(2)}, u32[]{:S(2)}) async-start(bf16[4,256,512]{2,1,0:T(8,128)(2,1)} %weight.1), calls=%async_computation.3 | async-start | bytes 2097152 | tf_op jit(solution)/shard_map/all_to_all | solution.py:236
  92.9 9.5 %collective-permute-start.3 = (bf16[128,128]{1,0:T(8,128)(2,1)S(1)}, bf16[128,128]{1,0:T(8,128)(2,1)S(1)}, u32[]{:S(2)}, u32[]{:S(2)}) collective-permute-start(bf16[128,128]{1,0:T(8,128)(2,1)S(1)} %get-tuple-element.29.refs_0_), channel_id=1, source_target_pairs={{0,1},{1,2},{2,3},{3,0},{4,5},{5,6},{6,7},{7,4},{8,9},{9,10},{10,1... | collective-permute-start | bytes 98312 | tf_op jit(solution)/shard_map/ppermute | solution.py:273
  94.3 12.2 %collective-permute-start.4 = (bf16[128,128]{1,0:T(8,128)(2,1)S(1)}, bf16[128,128]{1,0:T(8,128)(2,1)S(1)}, u32[]{:S(2)}, u32[]{:S(2)}) collective-permute-start(bf16[128,128]{1,0:T(8,128)(2,1)S(1)} %get-tuple-element.29.refs_0_), channel_id=1, source_target_pairs={{0,2},{1,3},{2,0},{3,1},{4,6},{5,7},{6,4},{7,5},{8,10},{9,11},{10,... | collective-permute-start | bytes 98312 | tf_op jit(solution)/shard_map/ppermute | solution.py:273
  96.7 9.8 %collective-permute-start.5 = (bf16[128,128]{1,0:T(8,128)(2,1)S(1)}, bf16[128,128]{1,0:T(8,128)(2,1)S(1)}, u32[]{:S(2)}, u32[]{:S(2)}) collective-permute-start(bf16[128,128]{1,0:T(8,128)(2,1)S(1)} %get-tuple-element.29.refs_0_), channel_id=1, source_target_pairs={{0,3},{1,0},{2,1},{3,2},{4,7},{5,4},{6,5},{7,6},{8,11},{9,8},{10,9... | collective-permute-start | bytes 98312 | tf_op jit(solution)/shard_map/ppermute | solution.py:273

commit v3 on v2

v3 whole, which is shorter than its diff:
```python
import functools

import jax
import jax.numpy as jnp
from jax import lax
from jax.experimental import pallas as pl
from jax.experimental.pallas import tpu as pltpu
from jax.sharding import Mesh
from jax.sharding import PartitionSpec as P

BF16 = jnp.bfloat16
F32 = jnp.float32
I32 = jnp.int32
AXES = ("x", "z", "core", "feat")


def dot(left, right, left_dim=1, right_dim=0):
    return lax.dot_general(
        left, right, (((left_dim,), (right_dim,)), ((), ())), preferred_element_type=F32
    )


def call(body, outs, args, name, flops=0, moved=0, vmem=16, scratch=(), scalars=0):
    specs = [
        pl.BlockSpec(memory_space=pltpu.SMEM if at < scalars else pltpu.VMEM)
        for at in range(len(args))
    ]
    out_specs = [pl.BlockSpec(memory_space=pltpu.VMEM) for _ in outs]
    return pl.pallas_call(
        body,
        out_shape=[jax.ShapeDtypeStruct(shape, dtype) for shape, dtype in outs],
        in_specs=specs,
        out_specs=out_specs,
        scratch_shapes=scratch,
        name=name,
        compiler_params=pltpu.CompilerParams(vmem_limit_bytes=vmem << 20),
        cost_estimate=pl.CostEstimate(flops=flops, bytes_accessed=moved, transcendentals=0),
    )(*args)


def pick_body(row_ref, x_ref, self_ref, near_ref, out_ref, weight_ref, slices):
    rows = x_ref.shape[0]
    half = self_ref.shape[1] // slices
    for at in range(slices):
        span = slice(at * half, (at + 1) * half)
        weight_ref[:, 2 * at * half : 2 * (at + 1) * half] = jnp.concatenate(
            [self_ref[:, span], near_ref[:, span]], axis=1
        )
    step = 128
    lane = lax.broadcasted_iota(I32, (step, step), 1)

    def fill(at, carry):
        start = pl.multiple_of(at * step, step)
        wanted = jnp.broadcast_to(row_ref[:, pl.ds(start, step)], (step, step)).T
        picks = jnp.concatenate(
            [
                jnp.where(wanted == lane + low, 1.0, 0.0).astype(BF16)
                for low in range(0, rows, step)
            ],
            axis=1,
        )
        out_ref[pl.ds(start, step), :] = dot(picks, x_ref[...]).astype(BF16)
        return carry

    lax.fori_loop(0, out_ref.shape[0] // step, fill, 0, unroll=4)


def count_body(
    self_ref, near_ref, degree_ref, seed_ref, seed_near_ref,
    self_table, near_table, seed_table, seed_near_table, live_ref,
    capacity, per,
):
    slots, mids = near_table.shape
    fan = near_ref.shape[0]
    quarter = slots * per // capacity
    deep = capacity.bit_length() - 1
    low = per.bit_length() - 1

    def placed(slot):
        return (
            ((slot >> low) & (capacity // per - 1)) * quarter
            + (slot >> deep) * per
            + (slot & (per - 1))
        )

    step = 32
    live = lax.broadcasted_iota(I32, (fan, mids), 0) < degree_ref[...]
    live_ref[...] = jnp.where(live, placed(near_ref[...]), -1)
    own = placed(self_ref[...])

    def fill(at, carry):
        span = pl.ds(pl.multiple_of(at * step, step), step)
        line = lax.broadcasted_iota(I32, (step, mids), 0) + at * step
        total = jnp.zeros((step, mids), F32)
        for j in range(fan):
            total = total + jnp.where(live_ref[j : j + 1, :] == line, 1.0, 0.0)
        near_table[span, :] = total.astype(BF16)
        self_table[span, :] = jnp.where(own == line, 1.0, 0.0).astype(BF16)
        return carry

    lax.fori_loop(0, slots // step, fill, 0)
    seeds = seed_table.shape[1]
    line = lax.broadcasted_iota(I32, (mids, seeds), 0)
    seed_table[...] = jnp.where(seed_ref[...] == line, 1.0, 0.0).astype(BF16)
    total = jnp.zeros((mids, seeds), F32)
    for j in range(seed_near_ref.shape[0]):
        total = total + jnp.where(seed_near_ref[j : j + 1, :] == line, 1.0, 0.0)
    seed_near_table[...] = total.astype(BF16)


def slot_rows(x_ref, at):
    peers, _, per, cols = x_ref.shape
    return x_ref[:, at].astype(F32).reshape(peers * per, cols).astype(BF16)


def project_body(place_ref, x_ref, *refs):
    slices = (len(refs) - 1) // 2
    weight_refs, out_refs, held_ref = refs[:slices], refs[slices:-1], refs[-1]
    width = out_refs[0].shape[1]
    me = place_ref[0]
    total = None
    for shift, weight_ref in enumerate(weight_refs):
        part = dot(slot_rows(x_ref, lax.rem(me + slices - shift, slices)), weight_ref[...])
        total = part if total is None else total + part
    total = total.astype(BF16)
    for at in range(slices):
        held_ref[at] = total[:, at * width : (at + 1) * width]
    for shift, out_ref in enumerate(out_refs):
        out_ref[...] = held_ref[lax.rem(me + shift, slices)]


def turn_body(x_ref, out_ref):
    cols = x_ref.shape[3]
    for at in range(x_ref.shape[1]):
        out_ref[at * cols : (at + 1) * cols, :] = slot_rows(x_ref, at).T


def owner_body(
    place_ref, mask_ref, self_table, near_table, degree_ref, bias_ref, seed_table,
    seed_near_table, second_self_ref, second_near_ref, cotangent_ref, *refs, slices, fan_two
):
    slot_refs, grad_refs, seeds_ref = refs[:slices], refs[slices:-1], refs[-1]
    quarter, width = slot_refs[0].shape
    half = width // 2
    me = place_ref[0]
    mine = pl.ds(pl.multiple_of(me * half, half), half)
    degree = degree_ref[...].astype(F32)
    own, near = 0.0, 0.0
    for shift, slot_ref in enumerate(slot_refs):
        at = lax.rem(me + slices - shift, slices)
        span = pl.ds(pl.multiple_of(at * quarter, quarter), quarter)
        table = slot_ref[...] * mask_ref[span, :]
        own = own + dot(table, self_table[span, :], 0, 0)[:half]
        near = near + dot(table, near_table[span, :], 0, 0)[half:]
    pre = own + near / degree + bias_ref[mine, :]
    sigma = 1.0 / (1.0 + jnp.exp(-pre))
    active = (pre * sigma).astype(BF16)
    slope = (sigma * (1.0 + pre * (1.0 - sigma))).astype(BF16).astype(F32)
    seeds_ref[:half, :] = dot(active, seed_table[...]).astype(BF16)
    seeds_ref[half:, :] = (dot(active, seed_near_table[...]) / fan_two).astype(BF16)
    back_self = dot(second_self_ref[mine, :], cotangent_ref[...], 1, 1)
    back_near = dot(second_near_ref[mine, :], cotangent_ref[...], 1, 1) / fan_two

    def spread(back, picks):
        high = back.astype(BF16)
        low = (back - high.astype(F32)).astype(BF16)
        both = dot(jnp.concatenate([high, low], axis=0), picks, 1, 1)
        return both[:half] + both[half:]

    grad_active = spread(back_self, seed_table[...]) + spread(back_near, seed_near_table[...])
    grad_pre = grad_active * slope
    nothing = jnp.zeros(grad_pre.shape, BF16)
    for_self = jnp.concatenate([grad_pre.astype(BF16), nothing], axis=0)
    for_near = jnp.concatenate([nothing, (grad_pre / degree).astype(BF16)], axis=0)
    for shift, grad_ref in enumerate(grad_refs):
        at = lax.rem(me + shift, slices)
        span = pl.ds(pl.multiple_of(at * quarter, quarter), quarter)
        grad = dot(self_table[span, :], for_self, 1, 1) + dot(near_table[span, :], for_near, 1, 1)
        grad_ref[...] = grad.astype(BF16) * mask_ref[span, :]


def seeds_body(place_ref, second_self_ref, second_near_ref, cotangent_ref, *refs):
    seeds_refs, (out_ref, keep_ref, give_ref, held_ref) = refs[:-4], refs[-4:]
    slices = len(seeds_refs)
    half = seeds_refs[0].shape[0] // 2
    total = jnp.zeros(out_ref.shape, F32)
    cotangent = cotangent_ref[...]
    for shift, seeds_ref in enumerate(seeds_refs):
        at = lax.rem(place_ref[0] + slices - shift, slices)
        rows = pl.ds(pl.multiple_of(at * half, half), half)
        total = total + dot(seeds_ref[:half, :], second_self_ref[rows, :], 0, 0)
        total = total + dot(seeds_ref[half:, :], second_near_ref[rows, :], 0, 0)
        grad = dot(seeds_ref[...], cotangent)
        held_ref[0, rows, :] = grad[:half]
        held_ref[1, rows, :] = grad[half:]
    out_ref[...] = total.astype(BF16)
    keep_ref[...] = held_ref[place_ref[1]]
    give_ref[...] = held_ref[1 - place_ref[1]].astype(BF16)


def weight_body(place_ref, xt_ref, *refs):
    grads_refs, (keep_ref, give_ref, held_ref) = refs[:-3], refs[-3:]
    slices, step, _ = keep_ref.shape
    width = grads_refs[0].shape[1]
    for shift, grads_ref in enumerate(grads_refs):
        at = lax.rem(place_ref[0] + slices - shift, slices)
        held_ref[:, pl.ds(pl.multiple_of(at * width, width), width)] = grads_ref[...]
    grads = held_ref[...]
    for at in range(slices):
        mine = pl.multiple_of((2 * at + place_ref[1]) * step, step)
        other = pl.multiple_of((2 * at + 1 - place_ref[1]) * step, step)
        give_ref[at] = dot(xt_ref[pl.ds(other, step), :], grads).astype(BF16)
        keep_ref[at] = dot(xt_ref[pl.ds(mine, step), :], grads)


def halves_body(keep_ref, got_ref, out_ref):
    slices, step, cols = keep_ref.shape
    peers, deep, _ = out_ref.shape
    for at in range(slices):
        total = (keep_ref[at] + got_ref[at].astype(F32)).astype(BF16)
        for piece in range(peers // slices):
            out_ref[piece * slices + at] = total[piece * deep : (piece + 1) * deep]


def sum_body(parts_ref, out_ref):
    total = jnp.sum(parts_ref[...].astype(F32), axis=0).astype(BF16)
    for at in range(out_ref.shape[0]):
        out_ref[at] = total


def second_split_body(place_ref, keep_ref, got_ref, *out_refs):
    count = len(out_refs)
    step = out_refs[0].shape[0]
    for shift, out_ref in enumerate(out_refs):
        at = lax.rem(place_ref[2] + shift, count)
        span = pl.ds(pl.multiple_of(at * step, step), step)
        out_ref[...] = (keep_ref[span, :] + got_ref[span, :].astype(F32)).astype(BF16)


def add_body(*refs):
    total = refs[0][...].astype(F32)
    for ref in refs[1:-1]:
        total = total + ref[...].astype(F32)
    refs[-1][...] = total.astype(BF16)


def second_pair_body(place_ref, mine_ref, other_ref, out_ref):
    rows = mine_ref.shape[0]
    first = place_ref[1] == 0
    out_ref[:rows, :] = jnp.where(first, mine_ref[...], other_ref[...])
    out_ref[rows:, :] = jnp.where(first, other_ref[...], mine_ref[...])


def second_finish_body(place_ref, *refs):
    parts, (self_ref, near_ref) = refs[:-2], refs[-2:]
    count = len(parts)
    step = parts[0].shape[0] // 2
    for shift, part in enumerate(parts):
        at = lax.rem(place_ref[2] + count - shift, count)
        span = pl.ds(pl.multiple_of(at * step, step), step)
        self_ref[span, :] = part[:step, :].astype(F32)
        near_ref[span, :] = part[step:, :].astype(F32)


def first_finish_body(all_ref, self_ref, near_ref, cores, slices):
    peers, deep, cols = all_ref.shape
    width = cols // slices
    half = width // 2
    for at in range(peers):
        start = (at % cores) * (peers // cores) * deep + (at // cores) * deep
        value = all_ref[at].astype(F32)
        for side, ref in enumerate((self_ref, near_ref)):
            ref[start : start + deep, :] = jnp.concatenate(
                [
                    value[:, f * width + side * half : f * width + (side + 1) * half]
                    for f in range(slices)
                ],
                axis=1,
            )


def exchange(value, axis):
    return lax.all_to_all(value, axis, split_axis=0, concat_axis=0, tiled=True)


def shifted(pieces, axis, count):
    return [
        piece
        if shift == 0
        else lax.ppermute(piece, axis, [(at, (at + shift) % count) for at in range(count)])
        for shift, piece in enumerate(pieces)
    ]


def swapped(value, axis, count, step):
    return lax.ppermute(value, axis, [(at, at ^ step) for at in range(count)])


def per_device(
    features,
    first_self,
    first_neighbor,
    first_bias,
    second_self,
    second_neighbor,
    send_rows,
    arrive_count,
    self_slot,
    neighbor_slot,
    degree,
    seed_self,
    seed_neighbor,
    cotangent,
    sizes,
):
    count_x, count_z, cores, slices = (sizes[axis] for axis in AXES)
    peers = count_x * count_z * cores
    rows, slice_cols = features.shape
    hidden = first_self.shape[1]
    half = hidden // slices
    width = 2 * half
    slots = send_rows.shape[1]
    capacity = slots // peers
    per = capacity // slices
    quarter = slots // slices
    mids, fan = neighbor_slot.shape
    seeds, fan_two = seed_neighbor.shape
    out_cols = second_self.shape[1]
    place = jnp.stack([lax.axis_index(axis) for axis in ("feat", "core", "x")]).astype(I32)

    picked, weight = call(
        functools.partial(pick_body, slices=slices),
        [((slots, slice_cols), BF16), ((slice_cols, 2 * hidden), BF16)],
        (send_rows, features, first_self, first_neighbor), "pick",
        2 * slots * rows * slice_cols, 2 * slots * rows,
    )
    routed = exchange(picked.reshape(peers * slices, per, slice_cols), AXES)
    routed = routed.reshape(peers, slices, per, slice_cols)
    weights = shifted([weight] * slices, "feat", slices)

    self_table, near_table, seed_table, seed_near_table = call(
        functools.partial(count_body, capacity=capacity, per=per),
        [((slots, mids), BF16), ((slots, mids), BF16), ((mids, seeds), BF16), ((mids, seeds), BF16)],
        (
            self_slot.reshape(1, mids), neighbor_slot.T, degree.reshape(1, mids),
            seed_self.reshape(1, seeds), seed_neighbor.T,
        ),
        "count", 0, 16 * slots * mids, scratch=[pltpu.VMEM((fan, mids), I32)],
    )
    slot_at = lax.broadcasted_iota(I32, (slices, peers, per, width), 0) * per
    slot_at = slot_at + lax.broadcasted_iota(I32, (slices, peers, per, width), 2)
    mask = (slot_at < arrive_count.reshape(1, peers, 1, 1)).astype(BF16).reshape(slots, width)
    bias = first_bias.reshape(hidden, 1)
    routed, seed_table, mask, bias = lax.optimization_barrier((routed, seed_table, mask, bias))

    projected = call(
        project_body, [((quarter, width), BF16)] * slices, (place, routed, *weights), "project",
        2 * quarter * slices * slice_cols * 2 * hidden, 4 * quarter * slices * slice_cols,
        scratch=[pltpu.VMEM((slices, quarter, width), BF16)], scalars=1,
    )
    tables = shifted(projected, "feat", slices)
    (turned,) = call(
        turn_body, [((slices * slice_cols, quarter), BF16)], (routed,), "turn",
        0, 8 * quarter * slices * slice_cols,
    )

    *grad_tables, own_seeds = call(
        functools.partial(owner_body, slices=slices, fan_two=fan_two),
        [((quarter, width), BF16)] * slices + [((width, seeds), BF16)],
        (
            place, mask, self_table, near_table, degree.reshape(1, mids), bias, seed_table,
            seed_near_table, second_self, second_neighbor, cotangent, *tables,
        ),
        "owner", 8 * slots * mids * width, 4 * slots * mids, scalars=1,
    )
    grads = shifted(grad_tables, "feat", slices)
    all_seeds = shifted([own_seeds] * slices, "feat", slices)
    grads, all_seeds = lax.optimization_barrier((grads, all_seeds))

    step = slice_cols // cores
    keep, give = call(
        weight_body, [((slices, step, 2 * hidden), F32), ((slices, step, 2 * hidden), BF16)],
        (place, turned, *grads), "weight",
        2 * quarter * slices * slice_cols * 2 * hidden, 4 * quarter * slices * slice_cols,
        scratch=[pltpu.VMEM((quarter, 2 * hidden), BF16)], scalars=1,
    )
    got = swapped(give, "core", cores, 1)
    seed_embedding, second_keep, second_give = call(
        seeds_body,
        [((seeds, out_cols), BF16), ((hidden, out_cols), F32), ((hidden, out_cols), BF16)],
        (place, second_self, second_neighbor, cotangent, *all_seeds), "seeds",
        8 * seeds * hidden * out_cols, 2 * slots * width,
        scratch=[pltpu.VMEM((2, hidden, out_cols), F32)], scalars=1,
    )
    got, second_give = lax.optimization_barrier((got, second_give))
    deep = step // count_x
    (mixed,) = call(
        halves_body, [((count_x * slices, deep, 2 * hidden), BF16)], (keep, got), "halves",
        0, 8 * slices * step * hidden,
    )
    mixed = exchange(mixed, ("x", "feat"))

    second_got = swapped(second_give, "core", cores, 1)
    shard = [((hidden // count_x, out_cols), BF16)]
    second_parts = call(
        second_split_body, shard * count_x, (place, second_keep, second_got), "second_split",
        0, 8 * hidden * out_cols, scalars=1,
    )
    (second,) = call(
        add_body, shard, shifted(second_parts, "x", count_x), "second_add",
        0, 4 * hidden * out_cols,
    )

    def doubled(value, stride):
        (value,) = call(
            add_body, shard, (value, swapped(value, "z", count_z, stride)), "second_add",
            0, 2 * hidden * out_cols,
        )
        return value

    strides = [1 << at for at in range(count_z.bit_length() - 1)]
    second = doubled(second, strides[0])
    mixed, second = lax.optimization_barrier((mixed, second))
    (mixed,) = call(
        sum_body, [((count_z, deep, 2 * hidden), BF16)], (mixed,), "sum", 0, 64 * deep * hidden,
    )
    mixed = exchange(mixed, "z")
    for stride in strides[1:]:
        second = doubled(second, stride)
    mixed, second = lax.optimization_barrier((mixed, second))
    (mixed,) = call(
        sum_body, [((count_x * cores, deep, 2 * hidden), BF16)], (mixed,), "sum",
        0, 64 * deep * hidden,
    )
    mixed = exchange(mixed, ("x", "core"))
    (second,) = call(
        second_pair_body, [((2 * hidden // count_x, out_cols), BF16)],
        (place, second, swapped(second, "core", cores, 1)), "second_pair",
        0, 2 * hidden * out_cols, scalars=1,
    )
    grad_second_self, grad_second_neighbor = call(
        second_finish_body, [((hidden, out_cols), F32)] * 2,
        (place, *shifted([second] * count_x, "x", count_x)), "second_finish",
        0, 12 * hidden * out_cols, scalars=1,
    )

    grad_first_self, grad_first_neighbor = call(
        functools.partial(first_finish_body, cores=cores, slices=slices),
        [((slice_cols, hidden), F32)] * 2, (mixed,), "first_finish", 0, 12 * slice_cols * hidden,
    )
    return (
        seed_embedding,
        grad_first_self,
        grad_first_neighbor,
        grad_second_self,
        grad_second_neighbor,
    )


def solution(mesh):
    shape = (4, 8, 2, mesh.shape["feat"])
    sizes = dict(zip(AXES, shape))
    mesh = Mesh(mesh.devices.reshape(shape), AXES)
    dom = AXES[:3]
    in_specs = (
        P(dom, "feat"),
        P("feat", None),
        P("feat", None),
        P(),
        P(),
        P(),
        P(dom, None),
        P(dom, None),
        P(dom),
        P(dom, None),
        P(dom),
        P(dom),
        P(dom, None),
        P(dom, None),
    )
    out_specs = (P(dom, None), P("feat", None), P("feat", None), P(), P())
    return jax.shard_map(
        functools.partial(per_device, sizes=sizes),
        mesh=mesh,
        in_specs=in_specs,
        out_specs=out_specs,
        check_vma=False,
    )
```

time: 159 us -> 153 us (0.962); the launches traced: 158 us -> 150 us
  blocking collectives: 49.3 us -> 0 us
  starting transfers between devices: 36.2 us -> 64.6 us
  waiting for transfers between devices: 37.8 us -> 45.4 us
  Pallas kernels: 23.9 us -> 29.1 us
    all_to_all x2 -> x0, blocking collectives: 49.3 us -> none  [exchange(): return lax.all_to_all(value, axis, split_axis=0, concat_axis=0, tiled=True)]
    ppermute x6 -> x24, starting transfers between devices: 10 us -> 35 us  [the longest x18 23.1 us: shifted(): lax.ppermute(piece, axis, [(at, (at + shift) % count) for at in range(cou...]
    ppermute x6 -> x24, waiting for transfers between devices: 8.62 us -> 30.9 us  [the longest x18 20.6 us: shifted(): lax.ppermute(piece, axis, [(at, (at + shift) % count) for at in range(cou...]
    all_to_all x4, waiting for transfers between devices: 29.2 us -> 14.5 us  [exchange(): return lax.all_to_all(value, axis, split_axis=0, concat_axis=0, tiled=True)]
    pallas_call x10 -> x18, Pallas kernels: 23.9 us -> 29.1 us  [call(): pl.pallas_call(body, out_shape=[jax.ShapeDtypeStruct(shape, dtype) for sh...]
    all_to_all x4, starting transfers between devices: 26.1 us -> 29.6 us  [exchange(): return lax.all_to_all(value, axis, split_axis=0, concat_axis=0, tiled=True)]
  transfers between devices with their start and end apart: 10 -> 28, of which waited for: 5 -> 14; matrix products, arithmetic and copies ran while one was open for 0% -> 0% of each run, Pallas kernels for 8% -> 10%
where the time goes in v3:
time: 153 us; the launch traced here: 150 us
  starting transfers between devices  64.6 us (42%)
  waiting for transfers between devices  45.4 us (30%)
  Pallas kernels  29.1 us (19%)
  local copies, waits for them, and re-layouts  10.1 us (7%)
    all_to_all x4, starting transfers between devices, exchange(): return lax.all_to_all(value, axis, split_axis=0, concat_axis=0, tiled=True)  29.6 us
    pallas_call x18, Pallas kernels, call(): pl.pallas_call(body, out_shape=[jax.ShapeDtypeStruct(shape, dtype) for sh...  29.1 us
    ppermute x18, starting transfers between devices, shifted(): lax.ppermute(piece, axis, [(at, (at + shift) % count) for at in range(cou...  23.1 us
    ppermute x18, waiting for transfers between devices, shifted(): lax.ppermute(piece, axis, [(at, (at + shift) % count) for at in range(cou...  20.6 us
    all_to_all x4, waiting for transfers between devices, exchange(): return lax.all_to_all(value, axis, split_axis=0, concat_axis=0, tiled=True)  14.5 us
    ppermute x6, starting transfers between devices, swapped(): return lax.ppermute(value, axis, [(at, at ^ step) for at in range(count)])  11.9 us
    ppermute x6, waiting for transfers between devices, swapped(): return lax.ppermute(value, axis, [(at, at ^ step) for at in range(count)])  10.2 us
    unnamed x36, local copies, waits for them, and re-layouts  9.55 us
  transfers between devices with their start and end apart: 28, of which 14 were waited for; matrix products, arithmetic and copies ran while one was open for 0% of the time, Pallas kernels for 10%

profile of v3, /device:TPU:1, one launch (start us, length us, event | category | flops | bytes accessed | tf_op | source)
XLA Modules:
  0.0 150.3 jit_solution(5937745007109769274)
XLA Ops:
  0.6 1.1 copy-done.12
  1.8 0.9 copy-done.13
  2.7 0.9 copy-done.14
  4.3 3.7 %pick.1 = (bf16[2048,256]{1,0:T(8,128)(2,1)}, bf16[256,512]{1,0:T(8,128)(2,1)S(1)}) custom-call(s32[1,2048]{1,0:T(1,128)S(1)} %copy-done.15, bf16[1536,256]{1,0:T(8,128)(2,1)S(1)} %copy-done.12, bf16[256,256]{1,0:T(8,128)(2,1)S(1)} %copy-done.13, bf16[256,256]{1,0:T(8,128)(2,1)S(1)} %copy-done.14), custom_call_target="tpu_custom_call" | custom-call | flops 1610612736 | bytes 6291456 | tf_op jit(solution)/shard_map/pick/pallas_call | solution.py:29
  8.1 15.7 %all-to-all-start = ((bf16[256,8,256]{2,1,0:T(8,128)(2,1)}), bf16[256,8,256]{2,1,0:T(8,128)(2,1)S(1)}, u32[]{:S(2)}, u32[]{:S(2)}) async-start(bf16[256,8,256]{2,1,0:T(8,128)(2,1)} %bitcast.3), calls=%async_computation | async-start | bytes 2097152 | tf_op jit(solution)/shard_map/all_to_all | solution.py:283
  23.7 2.7 %collective-permute-start.2 = (bf16[256,512]{1,0:T(8,128)(2,1)S(1)}, bf16[256,512]{1,0:T(8,128)(2,1)S(1)}, u32[]{:S(2)}, u32[]{:S(2)}) collective-permute-start(bf16[256,512]{1,0:T(8,128)(2,1)S(1)} %get-tuple-element.60.refs_0_), channel_id=1, source_target_pairs={{0,3},{1,0},{2,1},{3,2},{4,7},{5,4},{6,5},{7,6},{8,11},{9,8},{10,9... | collective-permute-start | bytes 786440 | tf_op jit(solution)/shard_map/ppermute | solution.py:290
  27.8 11.1 %count.1 = (bf16[2048,512]{1,0:T(8,128)(2,1)S(1)}, bf16[2048,512]{1,0:T(8,128)(2,1)S(1)}, bf16[512,128]{1,0:T(8,128)(2,1)S(1)}, bf16[512,128]{1,0:T(8,128)(2,1)S(1)}) custom-call(s32[1,512]{1,0:T(1,128)S(1)} %bitcast.18, s32[25,512]{1,0:T(8,128)S(1)} %bitcast.14, s32[1,512]{1,0:T(1,128)S(1)} %bitcast.15, s32[1,128]{1,0:T(1,128)S(1)} %bitcast.19, ...), custom_call_target="tpu_custom_call" | custom-call | bytes 16777216 | tf_op jit(solution)/shard_map/count/pallas_call | solution.py:29
  38.9 1.3 copy-done
  40.2 1.4 copy-done.2
  41.7 14.5 %all-to-all-done = bf16[256,8,256]{2,1,0:T(8,128)(2,1)S(1)} async-done(((bf16[256,8,256]{2,1,0:T(8,128)(2,1)}), bf16[256,8,256]{2,1,0:T(8,128)(2,1)S(1)}, u32[]{:S(2)}, u32[]{:S(2)}) %all-to-all-start) | async-done | bytes 1048608 | tf_op jit(solution)/shard_map/all_to_all | solution.py:283
  56.5 2.1 %project.1 = (bf16[512,128]{1,0:T(8,128)(2,1)S(1)}, bf16[512,128]{1,0:T(8,128)(2,1)}, bf16[512,128]{1,0:T(8,128)(2,1)}, bf16[512,128]{1,0:T(8,128)(2,1)}) custom-call(s32[3]{0:T(128)S(1)} %pad_add_fusion.place_ref, bf16[64,4,8,256]{3,2,1,0:T(8,128)(2,1)S(1)} %bitcast.12, bf16[256,512]{1,0:T(8,128)(2,1)S(1)} %get-tuple-element.60.refs_0_, ...), custom_call_target="tpu_custom_call" | custom-call | flops 536870912 | bytes 2097152 | tf_op jit(solution)/shard_map/project/pallas_call | solution.py:29
  58.9 1.0 collective-permute-start.4
  59.9 1.5 collective-permute-start.5
  61.5 6.0 %collective-permute-done.3.refs_1_ = bf16[512,128]{1,0:T(8,128)(2,1)S(1)} collective-permute-done((bf16[512,128]{1,0:T(8,128)(2,1)}, bf16[512,128]{1,0:T(8,128)(2,1)S(1)}, u32[]{:S(2)}, u32[]{:S(2)}) %collective-permute-start.3) | collective-permute-done | bytes 131104 | tf_op jit(solution)/shard_map/ppermute | solution.py:290
  67.6 1.6 %copy-done.1 = bf16[2048,512]{1,0:T(8,128)(2,1)S(1)} copy-done((bf16[2048,512]{1,0:T(8,128)(2,1)S(1)}, bf16[2048,512]{1,0:T(8,128)(2,1)}, u32[]{:S(2)}) %copy-start.1) | copy-done | bytes 2097176
  69.2 1.6 %copy-done.3 = bf16[2048,512]{1,0:T(8,128)(2,1)S(1)} copy-done((bf16[2048,512]{1,0:T(8,128)(2,1)S(1)}, bf16[2048,512]{1,0:T(8,128)(2,1)}, u32[]{:S(2)}) %copy-start.3) | copy-done | bytes 2097176
  70.7 3.0 %owner.1 = (bf16[512,128]{1,0:T(8,128)(2,1)S(1)}, bf16[512,128]{1,0:T(8,128)(2,1)S(1)}, bf16[512,128]{1,0:T(8,128)(2,1)S(1)}, bf16[512,128]{1,0:T(8,128)(2,1)S(1)}, bf16[128,128]{1,0:T(8,128)(2,1)S(1)}) custom-call(s32[3]{0:T(128)S(1)} %pad_add_fusion.place_ref, bf16[2048,128]{1,0:T(8,128)(2,1)S(1)} %lt.18.mask_ref, bf16[2048,512]{1,0:T(8,128)(2,1)S(1)} %copy-done.1, ...), custom_call_target="tpu_custom_call" | custom-call | flops 1073741824 | bytes 4194304 | tf_op jit(solution)/shard_map/owner/pallas_call | solution.py:29
  74.3 3.8 %collective-permute-start.7 = (bf16[512,128]{1,0:T(8,128)(2,1)S(1)}, bf16[512,128]{1,0:T(8,128)(2,1)S(1)}, u32[]{:S(2)}, u32[]{:S(2)}) collective-permute-start(bf16[512,128]{1,0:T(8,128)(2,1)S(1)} %get-tuple-element.67), channel_id=1, source_target_pairs={{0,2},{1,3},{2,0},{3,1},{4,6},{5,7},{6,4},{7,5},{8,10},{9,11},{10,... | collective-permute-start | bytes 393224 | tf_op jit(solution)/shard_map/ppermute | solution.py:290
  78.4 3.0 %collective-permute-start.10 = (bf16[128,128]{1,0:T(8,128)(2,1)S(1)}, bf16[128,128]{1,0:T(8,128)(2,1)S(1)}, u32[]{:S(2)}, u32[]{:S(2)}) collective-permute-start(bf16[128,128]{1,0:T(8,128)(2,1)S(1)} %get-tuple-element.70.refs_0_), channel_id=1, source_target_pairs={{0,2},{1,3},{2,0},{3,1},{4,6},{5,7},{6,4},{7,5},{8,10},{9,11},{10,... | collective-permute-start | bytes 98312 | tf_op jit(solution)/shard_map/ppermute | solution.py:290
  81.3 2.8 %collective-permute-done.11.refs_3_ = bf16[128,128]{1,0:T(8,128)(2,1)S(1)} collective-permute-done((bf16[128,128]{1,0:T(8,128)(2,1)S(1)}, bf16[128,128]{1,0:T(8,128)(2,1)S(1)}, u32[]{:S(2)}, u32[]{:S(2)}) %collective-permute-start.11) | collective-permute-done | bytes 32800 | tf_op jit(solution)/shard_map/ppermute | solution.py:290
  84.5 3.6 %collective-permute-done.9.refs_1_ = bf16[128,128]{1,0:T(8,128)(2,1)S(1)} collective-permute-done((bf16[128,128]{1,0:T(8,128)(2,1)S(1)}, bf16[128,128]{1,0:T(8,128)(2,1)S(1)}, u32[]{:S(2)}, u32[]{:S(2)}) %collective-permute-start.9) | collective-permute-done | bytes 32800 | tf_op jit(solution)/shard_map/ppermute | solution.py:290
  88.2 1.4 weight.1
  89.6 3.5 %collective-permute-start.12 = (bf16[4,128,512]{2,1,0:T(8,128)(2,1)S(1)}, bf16[4,128,512]{2,1,0:T(8,128)(2,1)S(1)}, u32[]{:S(2)}, u32[]{:S(2)}) collective-permute-start(bf16[4,128,512]{2,1,0:T(8,128)(2,1)S(1)} %get-tuple-element.80), channel_id=1, source_target_pairs={{0,4},{4,0},{1,5},{5,1},{2,6},{6,2},{3,7},{7,3},{8,12},{12,8},{9,1... | collective-permute-start | bytes 1572872 | tf_op jit(solution)/shard_map/ppermute | solution.py:296
  93.1 1.6 %seeds.1 = (bf16[128,256]{1,0:T(8,128)(2,1)}, f32[256,256]{1,0:T(8,128)S(1)}, bf16[256,256]{1,0:T(8,128)(2,1)S(1)}) custom-call(s32[3]{0:T(128)S(1)} %pad_add_fusion.place_ref, bf16[256,256]{1,0:T(8,128)(2,1)S(1)} %copy-done.4, bf16[256,256]{1,0:T(8,128)(2,1)S(1)} %copy-done.5, bf16[128,256]{1,0:T(8,128)(2,1)S(1)} %copy-done.6, ...), custom_call_target="tpu_custom_call" | custom-call | flops 67108864 | bytes 524288 | tf_op jit(solution)/shard_map/seeds/pallas_call | solution.py:29
  94.7 0.9 halves.1
  95.6 3.6 %all-to-all-start.1 = ((bf16[16,32,512]{2,1,0:T(8,128)(2,1)}), bf16[16,32,512]{2,1,0:T(8,128)(2,1)S(1)}, u32[]{:S(2)}, u32[]{:S(2)}) async-start(bf16[16,32,512]{2,1,0:T(8,128)(2,1)} %halves.1), calls=%async_computation.1 | async-start | bytes 1048576 | tf_op jit(solution)/shard_map/all_to_all | solution.py:283
  99.6 1.0 collective-permute-done.13.got_ref
  101.2 1.5 %collective-permute-start.14 = (bf16[64,256]{1,0:T(8,128)(2,1)S(1)}, bf16[64,256]{1,0:T(8,128)(2,1)S(1)}, u32[]{:S(2)}, u32[]{:S(2)}) collective-permute-start(bf16[64,256]{1,0:T(8,128)(2,1)S(1)} %get-tuple-element.86), channel_id=1, source_target_pairs={{0,64},{64,128},{128,192},{192,0},{1,65},{65,129},{129,193},{193,1... | collective-permute-start | bytes 98312 | tf_op jit(solution)/shard_map/ppermute | solution.py:290
  102.7 2.4 %collective-permute-start.15 = (bf16[64,256]{1,0:T(8,128)(2,1)S(1)}, bf16[64,256]{1,0:T(8,128)(2,1)S(1)}, u32[]{:S(2)}, u32[]{:S(2)}) collective-permute-start(bf16[64,256]{1,0:T(8,128)(2,1)S(1)} %get-tuple-element.87), channel_id=1, source_target_pairs={{0,128},{64,192},{128,0},{192,64},{1,129},{65,193},{129,1},{193,65... | collective-permute-start | bytes 98312 | tf_op jit(solution)/shard_map/ppermute | solution.py:290
  105.1 1.2 collective-permute-start.16
  106.3 1.4 collective-permute-done.14.refs_1_
  107.7 1.9 %collective-permute-done.15.refs_2_ = bf16[64,256]{1,0:T(8,128)(2,1)S(1)} collective-permute-done((bf16[64,256]{1,0:T(8,128)(2,1)S(1)}, bf16[64,256]{1,0:T(8,128)(2,1)S(1)}, u32[]{:S(2)}, u32[]{:S(2)}) %collective-permute-start.15) | collective-permute-done | bytes 32800 | tf_op jit(solution)/shard_map/ppermute | solution.py:290
  110.4 2.1 %collective-permute-done.17.refs_1_ = bf16[64,256]{1,0:T(8,128)(2,1)S(1)} collective-permute-done((bf16[64,256]{1,0:T(8,128)(2,1)S(1)}, bf16[64,256]{1,0:T(8,128)(2,1)S(1)}, u32[]{:S(2)}, u32[]{:S(2)}) %collective-permute-start.17) | collective-permute-done | bytes 32800 | tf_op jit(solution)/shard_map/ppermute | solution.py:296
  112.6 0.8 sum.2
  113.3 3.4 %all-to-all-start.2 = ((bf16[8,32,512]{2,1,0:T(8,128)(2,1)}), bf16[8,32,512]{2,1,0:T(8,128)(2,1)S(1)}, u32[]{:S(2)}, u32[]{:S(2)}) async-start(bf16[8,32,512]{2,1,0:T(8,128)(2,1)} %sum.2), calls=%async_computation.2 | async-start | bytes 524288 | tf_op jit(solution)/shard_map/all_to_all | solution.py:283
  116.8 2.3 %collective-permute-start.18 = (bf16[64,256]{1,0:T(8,128)(2,1)S(1)}, bf16[64,256]{1,0:T(8,128)(2,1)S(1)}, u32[]{:S(2)}, u32[]{:S(2)}) collective-permute-start(bf16[64,256]{1,0:T(8,128)(2,1)S(1)} %second_add.5.refs_0_), channel_id=1, source_target_pairs={{0,16},{8,24},{16,0},{24,8},{32,48},{40,56},{48,32},{56,40},{1,17}... | collective-permute-start | bytes 98312 | tf_op jit(solution)/shard_map/ppermute | solution.py:296
  119.0 4.0 %collective-permute-done.18.refs_1_ = bf16[64,256]{1,0:T(8,128)(2,1)S(1)} collective-permute-done((bf16[64,256]{1,0:T(8,128)(2,1)S(1)}, bf16[64,256]{1,0:T(8,128)(2,1)S(1)}, u32[]{:S(2)}, u32[]{:S(2)}) %collective-permute-start.18) | collective-permute-done | bytes 32800 | tf_op jit(solution)/shard_map/ppermute | solution.py:296
  123.0 4.8 %collective-permute-start.19 = (bf16[64,256]{1,0:T(8,128)(2,1)S(1)}, bf16[64,256]{1,0:T(8,128)(2,1)S(1)}, u32[]{:S(2)}, u32[]{:S(2)}) collective-permute-start(bf16[64,256]{1,0:T(8,128)(2,1)S(1)} %second_add.6.refs_0_), channel_id=1, source_target_pairs={{0,32},{8,40},{16,48},{24,56},{32,0},{40,8},{48,16},{56,24},{1,33}... | collective-permute-start | bytes 98312 | tf_op jit(solution)/shard_map/ppermute | solution.py:296
  127.8 2.1 %collective-permute-done.19.refs_1_ = bf16[64,256]{1,0:T(8,128)(2,1)S(1)} collective-permute-done((bf16[64,256]{1,0:T(8,128)(2,1)S(1)}, bf16[64,256]{1,0:T(8,128)(2,1)S(1)}, u32[]{:S(2)}, u32[]{:S(2)}) %collective-permute-start.19) | collective-permute-done | bytes 32800 | tf_op jit(solution)/shard_map/ppermute | solution.py:296
  129.9 0.7 sum.3
  130.6 7.0 %all-to-all-start.3 = ((bf16[8,32,512]{2,1,0:T(8,128)(2,1)}), bf16[8,32,512]{2,1,0:T(8,128)(2,1)S(1)}, u32[]{:S(2)}, u32[]{:S(2)}) async-start(bf16[8,32,512]{2,1,0:T(8,128)(2,1)} %sum.3), calls=%async_computation.3 | async-start | bytes 524288 | tf_op jit(solution)/shard_map/all_to_all | solution.py:283
  137.8 1.0 collective-permute-done.20.other_ref
  139.4 2.7 %collective-permute-start.23 = (bf16[128,256]{1,0:T(8,128)(2,1)S(1)}, bf16[128,256]{1,0:T(8,128)(2,1)S(1)}, u32[]{:S(2)}, u32[]{:S(2)}) collective-permute-start(bf16[128,256]{1,0:T(8,128)(2,1)S(1)} %second_pair.1.refs_0_), channel_id=1, source_target_pairs={{0,192},{64,0},{128,64},{192,128},{1,193},{65,1},{129,65},{193,129... | collective-permute-start | bytes 196616 | tf_op jit(solution)/shard_map/ppermute | solution.py:290
  143.2 0.9 collective-permute-done.23.refs_3_
  144.2 2.6 %collective-permute-done.22.refs_2_ = bf16[128,256]{1,0:T(8,128)(2,1)S(1)} collective-permute-done((bf16[128,256]{1,0:T(8,128)(2,1)S(1)}, bf16[128,256]{1,0:T(8,128)(2,1)S(1)}, u32[]{:S(2)}, u32[]{:S(2)}) %collective-permute-start.22) | collective-permute-done | bytes 65568 | tf_op jit(solution)/shard_map/ppermute | solution.py:290
  146.8 1.3 collective-permute-done.21.refs_1_
  148.0 1.4 second_finish.1
  149.4 0.9 first_finish.1
  (68 shorter events, 7.7 us)
Async XLA Ops:
  0.6 1.1 copy-start.12
  1.8 0.9 copy-start.13
  2.7 0.9 copy-start.14
  3.6 0.7 copy-start.15
  8.0 19.6 %copy-start.17 = (s32[1,64]{1,0:T(1,128)S(1)}, s32[1,64]{1,0:T(1,128)}, u32[]{:S(2)}) copy-start(s32[1,64]{1,0:T(1,128)} %param.21) | copy-start | bytes 772
  8.0 19.8 %copy-start.7 = (s32[512,25]{0,1:T(8,128)S(1)}, s32[512,25]{0,1:T(8,128)}, u32[]{:S(2)}) copy-start(s32[512,25]{0,1:T(8,128)} %param.23) | copy-start | bytes 153604
  8.0 19.8 %copy-start.8 = (s32[512]{0:T(512)S(1)}, s32[512]{0:T(512)}, u32[]{:S(2)}) copy-start(s32[512]{0:T(512)} %param.24) | copy-start | bytes 6148
  8.0 19.8 %copy-start.9 = (s32[128,10]{0,1:T(8,128)S(1)}, s32[128,10]{0,1:T(8,128)}, u32[]{:S(2)}) copy-start(s32[128,10]{0,1:T(8,128)} %param.26) | copy-start | bytes 15364
  8.0 19.8 %copy-start.10 = (s32[512]{0:T(512)S(1)}, s32[512]{0:T(512)}, u32[]{:S(2)}) copy-start(s32[512]{0:T(512)} %param.22) | copy-start | bytes 6148
  8.0 19.8 %copy-start.11 = (s32[128]{0:T(128)S(1)}, s32[128]{0:T(128)}, u32[]{:S(2)}) copy-start(s32[128]{0:T(128)} %param.25) | copy-start | bytes 1540
  8.0 53.4 %copy-start.16 = (f32[256]{0:T(256)S(1)}, f32[256]{0:T(256)}, u32[]{:S(2)}) copy-start(f32[256]{0:T(256)} %param.17) | copy-start | bytes 3076
  8.0 59.5 %copy-start.4 = (bf16[256,256]{1,0:T(8,128)(2,1)S(1)}, bf16[256,256]{1,0:T(8,128)(2,1)}, u32[]{:S(2)}) copy-start(bf16[256,256]{1,0:T(8,128)(2,1)} %second_self_ref.3) | copy-start | bytes 393220
  8.0 59.5 %copy-start.5 = (bf16[256,256]{1,0:T(8,128)(2,1)S(1)}, bf16[256,256]{1,0:T(8,128)(2,1)}, u32[]{:S(2)}) copy-start(bf16[256,256]{1,0:T(8,128)(2,1)} %second_near_ref.3) | copy-start | bytes 393220
  8.0 59.5 %copy-start.6 = (bf16[128,256]{1,0:T(8,128)(2,1)S(1)}, bf16[128,256]{1,0:T(8,128)(2,1)}, u32[]{:S(2)}) copy-start(bf16[128,256]{1,0:T(8,128)(2,1)} %cotangent_ref.3) | copy-start | bytes 196612
  8.1 48.1 %all-to-all-start = ((bf16[256,8,256]{2,1,0:T(8,128)(2,1)}), bf16[256,8,256]{2,1,0:T(8,128)(2,1)S(1)}, u32[]{:S(2)}, u32[]{:S(2)}) async-start(bf16[256,8,256]{2,1,0:T(8,128)(2,1)} %bitcast.3), calls=%async_computation | async-start | bytes 2097152 | tf_op jit(solution)/shard_map/all_to_all | solution.py:283
  23.7 32.8 %collective-permute-start.2 = (bf16[256,512]{1,0:T(8,128)(2,1)S(1)}, bf16[256,512]{1,0:T(8,128)(2,1)S(1)}, u32[]{:S(2)}, u32[]{:S(2)}) collective-permute-start(bf16[256,512]{1,0:T(8,128)(2,1)S(1)} %get-tuple-element.60.refs_0_), channel_id=1, source_target_pairs={{0,3},{1,0},{2,1},{3,2},{4,7},{5,4},{6,5},{7,6},{8,11},{9,8},{10,9... | collective-permute-start | bytes 786440 | tf_op jit(solution)/shard_map/ppermute | solution.py:290
  26.4 30.1 %collective-permute-start.1 = (bf16[256,512]{1,0:T(8,128)(2,1)S(1)}, bf16[256,512]{1,0:T(8,128)(2,1)S(1)}, u32[]{:S(2)}, u32[]{:S(2)}) collective-permute-start(bf16[256,512]{1,0:T(8,128)(2,1)S(1)} %get-tuple-element.60.refs_0_), channel_id=1, source_target_pairs={{0,2},{1,3},{2,0},{3,1},{4,6},{5,7},{6,4},{7,5},{8,10},{9,11},{10,... | collective-permute-start | bytes 786440 | tf_op jit(solution)/shard_map/ppermute | solution.py:290
  27.0 29.6 %collective-permute-start = (bf16[256,512]{1,0:T(8,128)(2,1)S(1)}, bf16[256,512]{1,0:T(8,128)(2,1)S(1)}, u32[]{:S(2)}, u32[]{:S(2)}) collective-permute-start(bf16[256,512]{1,0:T(8,128)(2,1)S(1)} %get-tuple-element.60.refs_0_), channel_id=1, source_target_pairs={{0,1},{1,2},{2,3},{3,0},{4,5},{5,6},{6,7},{7,4},{8,9},{9,10},{10,1... | collective-permute-start | bytes 786440 | tf_op jit(solution)/shard_map/ppermute | solution.py:290
  38.9 1.3 copy-start
  40.2 1.4 copy-start.2
  58.7 8.8 %collective-permute-start.3 = (bf16[512,128]{1,0:T(8,128)(2,1)}, bf16[512,128]{1,0:T(8,128)(2,1)S(1)}, u32[]{:S(2)}, u32[]{:S(2)}) collective-permute-start(bf16[512,128]{1,0:T(8,128)(2,1)} %get-tuple-element.62), channel_id=1, source_target_pairs={{0,1},{1,2},{2,3},{3,0},{4,5},{5,6},{6,7},{7,4},{8,9},{9,10},{10,1... | collective-permute-start | bytes 393224 | tf_op jit(solution)/shard_map/ppermute | solution.py:290
  58.9 8.6 %collective-permute-start.4 = (bf16[512,128]{1,0:T(8,128)(2,1)}, bf16[512,128]{1,0:T(8,128)(2,1)S(1)}, u32[]{:S(2)}, u32[]{:S(2)}) collective-permute-start(bf16[512,128]{1,0:T(8,128)(2,1)} %get-tuple-element.63), channel_id=1, source_target_pairs={{0,2},{1,3},{2,0},{3,1},{4,6},{5,7},{6,4},{7,5},{8,10},{9,11},{10,... | collective-permute-start | bytes 393224 | tf_op jit(solution)/shard_map/ppermute | solution.py:290
  59.9 7.6 %collective-permute-start.5 = (bf16[512,128]{1,0:T(8,128)(2,1)}, bf16[512,128]{1,0:T(8,128)(2,1)S(1)}, u32[]{:S(2)}, u32[]{:S(2)}) collective-permute-start(bf16[512,128]{1,0:T(8,128)(2,1)} %get-tuple-element.64), channel_id=1, source_target_pairs={{0,3},{1,0},{2,1},{3,2},{4,7},{5,4},{6,5},{7,6},{8,11},{9,8},{10,9... | collective-permute-start | bytes 393224 | tf_op jit(solution)/shard_map/ppermute | solution.py:290
  67.6 1.6 %copy-start.1 = (bf16[2048,512]{1,0:T(8,128)(2,1)S(1)}, bf16[2048,512]{1,0:T(8,128)(2,1)}, u32[]{:S(2)}) copy-start(bf16[2048,512]{1,0:T(8,128)(2,1)} %copy-done) | copy-start | bytes 6291460
  69.2 1.6 %copy-start.3 = (bf16[2048,512]{1,0:T(8,128)(2,1)S(1)}, bf16[2048,512]{1,0:T(8,128)(2,1)}, u32[]{:S(2)}) copy-start(bf16[2048,512]{1,0:T(8,128)(2,1)} %copy-done.2) | copy-start | bytes 6291460
  73.7 14.4 %collective-permute-start.6 = (bf16[512,128]{1,0:T(8,128)(2,1)S(1)}, bf16[512,128]{1,0:T(8,128)(2,1)S(1)}, u32[]{:S(2)}, u32[]{:S(2)}) collective-permute-start(bf16[512,128]{1,0:T(8,128)(2,1)S(1)} %get-tuple-element.66), channel_id=1, source_target_pairs={{0,1},{1,2},{2,3},{3,0},{4,5},{5,6},{6,7},{7,4},{8,9},{9,10},{10,1... | collective-permute-start | bytes 393224 | tf_op jit(solution)/shard_map/ppermute | solution.py:290
  74.3 13.8 %collective-permute-start.7 = (bf16[512,128]{1,0:T(8,128)(2,1)S(1)}, bf16[512,128]{1,0:T(8,128)(2,1)S(1)}, u32[]{:S(2)}, u32[]{:S(2)}) collective-permute-start(bf16[512,128]{1,0:T(8,128)(2,1)S(1)} %get-tuple-element.67), channel_id=1, source_target_pairs={{0,2},{1,3},{2,0},{3,1},{4,6},{5,7},{6,4},{7,5},{8,10},{9,11},{10,... | collective-permute-start | bytes 393224 | tf_op jit(solution)/shard_map/ppermute | solution.py:290
  78.1 10.1 %collective-permute-start.8 = (bf16[512,128]{1,0:T(8,128)(2,1)S(1)}, bf16[512,128]{1,0:T(8,128)(2,1)S(1)}, u32[]{:S(2)}, u32[]{:S(2)}) collective-permute-start(bf16[512,128]{1,0:T(8,128)(2,1)S(1)} %get-tuple-element.68), channel_id=1, source_target_pairs={{0,3},{1,0},{2,1},{3,2},{4,7},{5,4},{6,5},{7,6},{8,11},{9,8},{10,9... | collective-permute-start | bytes 393224 | tf_op jit(solution)/shard_map/ppermute | solution.py:290
  78.1 6.1 %collective-permute-start.11 = (bf16[128,128]{1,0:T(8,128)(2,1)S(1)}, bf16[128,128]{1,0:T(8,128)(2,1)S(1)}, u32[]{:S(2)}, u32[]{:S(2)}) collective-permute-start(bf16[128,128]{1,0:T(8,128)(2,1)S(1)} %get-tuple-element.70.refs_0_), channel_id=1, source_target_pairs={{0,3},{1,0},{2,1},{3,2},{4,7},{5,4},{6,5},{7,6},{8,11},{9,8},{10,9... | collective-permute-start | bytes 98312 | tf_op jit(solution)/shard_map/ppermute | solution.py:290
  78.4 6.1 %collective-permute-start.10 = (bf16[128,128]{1,0:T(8,128)(2,1)S(1)}, bf16[128,128]{1,0:T(8,128)(2,1)S(1)}, u32[]{:S(2)}, u32[]{:S(2)}) collective-permute-start(bf16[128,128]{1,0:T(8,128)(2,1)S(1)} %get-tuple-element.70.refs_0_), channel_id=1, source_target_pairs={{0,2},{1,3},{2,0},{3,1},{4,6},{5,7},{6,4},{7,5},{8,10},{9,11},{10,... | collective-permute-start | bytes 98312 | tf_op jit(solution)/shard_map/ppermute | solution.py:290
  84.2 4.0 %collective-permute-start.9 = (bf16[128,128]{1,0:T(8,128)(2,1)S(1)}, bf16[128,128]{1,0:T(8,128)(2,1)S(1)}, u32[]{:S(2)}, u32[]{:S(2)}) collective-permute-start(bf16[128,128]{1,0:T(8,128)(2,1)S(1)} %get-tuple-element.70.refs_0_), channel_id=1, source_target_pairs={{0,1},{1,2},{2,3},{3,0},{4,5},{5,6},{6,7},{7,4},{8,9},{9,10},{10,1... | collective-permute-start | bytes 98312 | tf_op jit(solution)/shard_map/ppermute | solution.py:290
  89.6 5.1 %collective-permute-start.12 = (bf16[4,128,512]{2,1,0:T(8,128)(2,1)S(1)}, bf16[4,128,512]{2,1,0:T(8,128)(2,1)S(1)}, u32[]{:S(2)}, u32[]{:S(2)}) collective-permute-start(bf16[4,128,512]{2,1,0:T(8,128)(2,1)S(1)} %get-tuple-element.80), channel_id=1, source_target_pairs={{0,4},{4,0},{1,5},{5,1},{2,6},{6,2},{3,7},{7,3},{8,12},{12,8},{9,1... | collective-permute-start | bytes 1572872 | tf_op jit(solution)/shard_map/ppermute | solution.py:296
  95.6 17.0 %all-to-all-start.1 = ((bf16[16,32,512]{2,1,0:T(8,128)(2,1)}), bf16[16,32,512]{2,1,0:T(8,128)(2,1)S(1)}, u32[]{:S(2)}, u32[]{:S(2)}) async-start(bf16[16,32,512]{2,1,0:T(8,128)(2,1)} %halves.1), calls=%async_computation.1 | async-start | bytes 1048576 | tf_op jit(solution)/shard_map/all_to_all | solution.py:283
  99.2 1.4 collective-permute-start.13
  101.2 6.5 %collective-permute-start.14 = (bf16[64,256]{1,0:T(8,128)(2,1)S(1)}, bf16[64,256]{1,0:T(8,128)(2,1)S(1)}, u32[]{:S(2)}, u32[]{:S(2)}) collective-permute-start(bf16[64,256]{1,0:T(8,128)(2,1)S(1)} %get-tuple-element.86), channel_id=1, source_target_pairs={{0,64},{64,128},{128,192},{192,0},{1,65},{65,129},{129,193},{193,1... | collective-permute-start | bytes 98312 | tf_op jit(solution)/shard_map/ppermute | solution.py:290
  102.7 6.9 %collective-permute-start.15 = (bf16[64,256]{1,0:T(8,128)(2,1)S(1)}, bf16[64,256]{1,0:T(8,128)(2,1)S(1)}, u32[]{:S(2)}, u32[]{:S(2)}) collective-permute-start(bf16[64,256]{1,0:T(8,128)(2,1)S(1)} %get-tuple-element.87), channel_id=1, source_target_pairs={{0,128},{64,192},{128,0},{192,64},{1,129},{65,193},{129,1},{193,65... | collective-permute-start | bytes 98312 | tf_op jit(solution)/shard_map/ppermute | solution.py:290
  105.1 4.5 %collective-permute-start.16 = (bf16[64,256]{1,0:T(8,128)(2,1)S(1)}, bf16[64,256]{1,0:T(8,128)(2,1)S(1)}, u32[]{:S(2)}, u32[]{:S(2)}) collective-permute-start(bf16[64,256]{1,0:T(8,128)(2,1)S(1)} %get-tuple-element.88), channel_id=1, source_target_pairs={{0,192},{64,0},{128,64},{192,128},{1,193},{65,1},{129,65},{193,129... | collective-permute-start | bytes 98312 | tf_op jit(solution)/shard_map/ppermute | solution.py:290
  109.7 2.9 %collective-permute-start.17 = (bf16[64,256]{1,0:T(8,128)(2,1)S(1)}, bf16[64,256]{1,0:T(8,128)(2,1)S(1)}, u32[]{:S(2)}, u32[]{:S(2)}) collective-permute-start(bf16[64,256]{1,0:T(8,128)(2,1)S(1)} %second_add.4.refs_0_), channel_id=1, source_target_pairs={{0,8},{8,0},{16,24},{24,16},{32,40},{40,32},{48,56},{56,48},{1,9},... | collective-permute-start | bytes 98312 | tf_op jit(solution)/shard_map/ppermute | solution.py:296
  113.3 16.5 %all-to-all-start.2 = ((bf16[8,32,512]{2,1,0:T(8,128)(2,1)}), bf16[8,32,512]{2,1,0:T(8,128)(2,1)S(1)}, u32[]{:S(2)}, u32[]{:S(2)}) async-start(bf16[8,32,512]{2,1,0:T(8,128)(2,1)} %sum.2), calls=%async_computation.2 | async-start | bytes 524288 | tf_op jit(solution)/shard_map/all_to_all | solution.py:283
  116.8 6.2 %collective-permute-start.18 = (bf16[64,256]{1,0:T(8,128)(2,1)S(1)}, bf16[64,256]{1,0:T(8,128)(2,1)S(1)}, u32[]{:S(2)}, u32[]{:S(2)}) collective-permute-start(bf16[64,256]{1,0:T(8,128)(2,1)S(1)} %second_add.5.refs_0_), channel_id=1, source_target_pairs={{0,16},{8,24},{16,0},{24,8},{32,48},{40,56},{48,32},{56,40},{1,17}... | collective-permute-start | bytes 98312 | tf_op jit(solution)/shard_map/ppermute | solution.py:296
  123.0 6.9 %collective-permute-start.19 = (bf16[64,256]{1,0:T(8,128)(2,1)S(1)}, bf16[64,256]{1,0:T(8,128)(2,1)S(1)}, u32[]{:S(2)}, u32[]{:S(2)}) collective-permute-start(bf16[64,256]{1,0:T(8,128)(2,1)S(1)} %second_add.6.refs_0_), channel_id=1, source_target_pairs={{0,32},{8,40},{16,48},{24,56},{32,0},{40,8},{48,16},{56,24},{1,33}... | collective-permute-start | bytes 98312 | tf_op jit(solution)/shard_map/ppermute | solution.py:296
  130.6 18.7 %all-to-all-start.3 = ((bf16[8,32,512]{2,1,0:T(8,128)(2,1)}), bf16[8,32,512]{2,1,0:T(8,128)(2,1)S(1)}, u32[]{:S(2)}, u32[]{:S(2)}) async-start(bf16[8,32,512]{2,1,0:T(8,128)(2,1)} %sum.3), calls=%async_computation.3 | async-start | bytes 524288 | tf_op jit(solution)/shard_map/all_to_all | solution.py:283
  137.6 1.2 collective-permute-start.20
  139.4 4.8 %collective-permute-start.23 = (bf16[128,256]{1,0:T(8,128)(2,1)S(1)}, bf16[128,256]{1,0:T(8,128)(2,1)S(1)}, u32[]{:S(2)}, u32[]{:S(2)}) collective-permute-start(bf16[128,256]{1,0:T(8,128)(2,1)S(1)} %second_pair.1.refs_0_), channel_id=1, source_target_pairs={{0,192},{64,0},{128,64},{192,128},{1,193},{65,1},{129,65},{193,129... | collective-permute-start | bytes 196616 | tf_op jit(solution)/shard_map/ppermute | solution.py:290
  142.1 4.7 %collective-permute-start.22 = (bf16[128,256]{1,0:T(8,128)(2,1)S(1)}, bf16[128,256]{1,0:T(8,128)(2,1)S(1)}, u32[]{:S(2)}, u32[]{:S(2)}) collective-permute-start(bf16[128,256]{1,0:T(8,128)(2,1)S(1)} %second_pair.1.refs_0_), channel_id=1, source_target_pairs={{0,128},{64,192},{128,0},{192,64},{1,129},{65,193},{129,1},{193,65... | collective-permute-start | bytes 196616 | tf_op jit(solution)/shard_map/ppermute | solution.py:290
  142.6 5.4 %collective-permute-start.21 = (bf16[128,256]{1,0:T(8,128)(2,1)S(1)}, bf16[128,256]{1,0:T(8,128)(2,1)S(1)}, u32[]{:S(2)}, u32[]{:S(2)}) collective-permute-start(bf16[128,256]{1,0:T(8,128)(2,1)S(1)} %second_pair.1.refs_0_), channel_id=1, source_target_pairs={{0,64},{64,128},{128,192},{192,0},{1,65},{65,129},{129,193},{193,1... | collective-permute-start | bytes 196616 | tf_op jit(solution)/shard_map/ppermute | solution.py:290

commit v4 on v3

--- a/solution.py
+++ b/solution.py
@@ -20,9 +20,11 @@
     )
 
 
-def call(body, outs, args, name, flops=0, moved=0, vmem=16, scratch=(), scalars=0):
+def call(body, outs, args, name, flops=0, moved=0, vmem=16, scratch=(), scalars=0, far=()):
     specs = [
-        pl.BlockSpec(memory_space=pltpu.SMEM if at < scalars else pltpu.VMEM)
+        pl.BlockSpec(
+            memory_space=pltpu.SMEM if at < scalars else pltpu.HBM if at in far else pltpu.VMEM
+        )
         for at in range(len(args))
     ]
     out_specs = [pl.BlockSpec(memory_space=pltpu.VMEM) for _ in outs]
@@ -35,17 +37,28 @@
         name=name,
         compiler_params=pltpu.CompilerParams(vmem_limit_bytes=vmem << 20),
         cost_estimate=pl.CostEstimate(flops=flops, bytes_accessed=moved, transcendentals=0),
-    )(*args)
-
-
-def pick_body(row_ref, x_ref, self_ref, near_ref, out_ref, weight_ref, slices):
+    )(*[
+        pltpu.with_memory_space_constraint(arg, pltpu.HBM) if at in far else arg
+        for at, arg in enumerate(args)
+    ])
+
+
+def pick_body(
+    row_far, x_far, self_far, near_far, out_ref, weight_ref, row_ref, x_ref, self_ref, near_ref, sems,
+    slices,
+):
+    copies = [
+        pltpu.make_async_copy(far, ref, sems.at[at])
+        for at, (far, ref) in enumerate(
+            ((row_far, row_ref), (x_far, x_ref), (self_far, self_ref), (near_far, near_ref))
+        )
+    ]
+    for copy in copies:
+        copy.start()
     rows = x_ref.shape[0]
     half = self_ref.shape[1] // slices
-    for at in range(slices):
-        span = slice(at * half, (at + 1) * half)
-        weight_ref[:, 2 * at * half : 2 * (at + 1) * half] = jnp.concatenate(
-            [self_ref[:, span], near_ref[:, span]], axis=1
-        )
+    copies[0].wait()
+    copies[1].wait()
     step = 128
     lane = lax.broadcasted_iota(I32, (step, step), 1)
 
@@ -63,6 +76,13 @@
         return carry
 
     lax.fori_loop(0, out_ref.shape[0] // step, fill, 0, unroll=4)
+    copies[2].wait()
+    copies[3].wait()
+    for at in range(slices):
+        span = slice(at * half, (at + 1) * half)
+        weight_ref[:, 2 * at * half : 2 * (at + 1) * half] = jnp.concatenate(
+            [self_ref[:, span], near_ref[:, span]], axis=1
+        )
 
 
 def count_body(
@@ -136,28 +156,22 @@
 
 
 def owner_body(
-    place_ref, mask_ref, self_table, near_table, degree_ref, bias_ref, seed_table,
+    place_ref, self_far, near_far, mask_ref, degree_ref, bias_ref, seed_table,
     seed_near_table, second_self_ref, second_near_ref, cotangent_ref, *refs, slices, fan_two
 ):
-    slot_refs, grad_refs, seeds_ref = refs[:slices], refs[slices:-1], refs[-1]
-    quarter, width = slot_refs[0].shape
+    slot_refs, out_refs = refs[:slices], refs[slices : 2 * slices]
+    self_table, near_table, sems = refs[2 * slices :]
+    _, quarter, width = mask_ref.shape
     half = width // 2
     me = place_ref[0]
+    copies = []
+    for shift in range(slices):
+        at = lax.rem(me + slices - shift, slices)
+        for side, (far, ref) in enumerate(((self_far, self_table), (near_far, near_table))):
+            copies.append(pltpu.make_async_copy(far.at[at], ref.at[shift], sems.at[side, shift]))
+            copies[-1].start()
     mine = pl.ds(pl.multiple_of(me * half, half), half)
     degree = degree_ref[...].astype(F32)
-    own, near = 0.0, 0.0
-    for shift, slot_ref in enumerate(slot_refs):
-        at = lax.rem(me + slices - shift, slices)
-        span = pl.ds(pl.multiple_of(at * quarter, quarter), quarter)
-        table = slot_ref[...] * mask_ref[span, :]
-        own = own + dot(table, self_table[span, :], 0, 0)[:half]
-        near = near + dot(table, near_table[span, :], 0, 0)[half:]
-    pre = own + near / degree + bias_ref[mine, :]
-    sigma = 1.0 / (1.0 + jnp.exp(-pre))
-    active = (pre * sigma).astype(BF16)
-    slope = (sigma * (1.0 + pre * (1.0 - sigma))).astype(BF16).astype(F32)
-    seeds_ref[:half, :] = dot(active, seed_table[...]).astype(BF16)
-    seeds_ref[half:, :] = (dot(active, seed_near_table[...]) / fan_two).astype(BF16)
     back_self = dot(second_self_ref[mine, :], cotangent_ref[...], 1, 1)
     back_near = dot(second_near_ref[mine, :], cotangent_ref[...], 1, 1) / fan_two
 
@@ -168,29 +182,46 @@
         return both[:half] + both[half:]
 
     grad_active = spread(back_self, seed_table[...]) + spread(back_near, seed_near_table[...])
+    own, near = 0.0, 0.0
+    for shift, slot_ref in enumerate(slot_refs):
+        at = lax.rem(me + slices - shift, slices)
+        table = slot_ref[...] * mask_ref[at]
+        copies[2 * shift].wait()
+        own = own + dot(table, self_table[shift], 0, 0)[:half]
+        copies[2 * shift + 1].wait()
+        near = near + dot(table, near_table[shift], 0, 0)[half:]
+    pre = own + near / degree + bias_ref[mine, :]
+    sigma = 1.0 / (1.0 + jnp.exp(-pre))
+    active = (pre * sigma).astype(BF16)
+    slope = (sigma * (1.0 + pre * (1.0 - sigma))).astype(BF16).astype(F32)
+    own_seeds = dot(active, seed_table[...]).astype(BF16)
+    mean_seeds = (dot(active, seed_near_table[...]) / fan_two).astype(BF16)
+    for out_ref in out_refs:
+        out_ref[quarter : quarter + half, :] = own_seeds
+        out_ref[quarter + half :, :] = mean_seeds
     grad_pre = grad_active * slope
     nothing = jnp.zeros(grad_pre.shape, BF16)
     for_self = jnp.concatenate([grad_pre.astype(BF16), nothing], axis=0)
     for_near = jnp.concatenate([nothing, (grad_pre / degree).astype(BF16)], axis=0)
-    for shift, grad_ref in enumerate(grad_refs):
-        at = lax.rem(me + shift, slices)
-        span = pl.ds(pl.multiple_of(at * quarter, quarter), quarter)
-        grad = dot(self_table[span, :], for_self, 1, 1) + dot(near_table[span, :], for_near, 1, 1)
-        grad_ref[...] = grad.astype(BF16) * mask_ref[span, :]
+    for shift, out_ref in enumerate(out_refs):
+        held = (slices - shift) % slices
+        grad = dot(self_table[held], for_self, 1, 1) + dot(near_table[held], for_near, 1, 1)
+        out_ref[:quarter, :] = grad.astype(BF16) * mask_ref[lax.rem(me + shift, slices)]
 
 
 def seeds_body(place_ref, second_self_ref, second_near_ref, cotangent_ref, *refs):
     seeds_refs, (out_ref, keep_ref, give_ref, held_ref) = refs[:-4], refs[-4:]
     slices = len(seeds_refs)
-    half = seeds_refs[0].shape[0] // 2
+    half = held_ref.shape[1] // slices
+    low = seeds_refs[0].shape[0] - 2 * half
     total = jnp.zeros(out_ref.shape, F32)
     cotangent = cotangent_ref[...]
     for shift, seeds_ref in enumerate(seeds_refs):
         at = lax.rem(place_ref[0] + slices - shift, slices)
         rows = pl.ds(pl.multiple_of(at * half, half), half)
-        total = total + dot(seeds_ref[:half, :], second_self_ref[rows, :], 0, 0)
-        total = total + dot(seeds_ref[half:, :], second_near_ref[rows, :], 0, 0)
-        grad = dot(seeds_ref[...], cotangent)
+        total = total + dot(seeds_ref[low : low + half, :], second_self_ref[rows, :], 0, 0)
+        total = total + dot(seeds_ref[low + half :, :], second_near_ref[rows, :], 0, 0)
+        grad = dot(seeds_ref[low:, :], cotangent)
         held_ref[0, rows, :] = grad[:half]
         held_ref[1, rows, :] = grad[half:]
     out_ref[...] = total.astype(BF16)
@@ -204,7 +235,7 @@
     width = grads_refs[0].shape[1]
     for shift, grads_ref in enumerate(grads_refs):
         at = lax.rem(place_ref[0] + slices - shift, slices)
-        held_ref[:, pl.ds(pl.multiple_of(at * width, width), width)] = grads_ref[...]
+        held_ref[:, pl.ds(pl.multiple_of(at * width, width), width)] = grads_ref[: held_ref.shape[0], :]
     grads = held_ref[...]
     for at in range(slices):
         mine = pl.multiple_of((2 * at + place_ref[1]) * step, step)
@@ -244,39 +275,35 @@
     refs[-1][...] = total.astype(BF16)
 
 
-def second_pair_body(place_ref, mine_ref, other_ref, out_ref):
-    rows = mine_ref.shape[0]
-    first = place_ref[1] == 0
-    out_ref[:rows, :] = jnp.where(first, mine_ref[...], other_ref[...])
-    out_ref[rows:, :] = jnp.where(first, other_ref[...], mine_ref[...])
-
-
-def second_finish_body(place_ref, *refs):
-    parts, (self_ref, near_ref) = refs[:-2], refs[-2:]
-    count = len(parts)
-    step = parts[0].shape[0] // 2
-    for shift, part in enumerate(parts):
-        at = lax.rem(place_ref[2] + count - shift, count)
-        span = pl.ds(pl.multiple_of(at * step, step), step)
-        self_ref[span, :] = part[:step, :].astype(F32)
-        near_ref[span, :] = part[step:, :].astype(F32)
-
-
-def first_finish_body(all_ref, self_ref, near_ref, cores, slices):
+def join_body(parts_ref, second_ref, out_ref):
+    _, deep, cols = parts_ref.shape
+    total = jnp.sum(parts_ref[...].astype(F32), axis=0).astype(BF16)
+    for at in range(out_ref.shape[0]):
+        out_ref[at, :deep] = total
+        out_ref[at, deep:, : cols // 2] = second_ref[:deep, :]
+        out_ref[at, deep:, cols // 2 :] = second_ref[deep:, :]
+
+
+def finish_body(all_ref, self_ref, near_ref, second_self_ref, second_near_ref, cores, slices):
     peers, deep, cols = all_ref.shape
+    deep = deep // 2
     width = cols // slices
     half = width // 2
     for at in range(peers):
-        start = (at % cores) * (peers // cores) * deep + (at // cores) * deep
+        core, x = at % cores, at // cores
+        start = core * (peers // cores) * deep + x * deep
         value = all_ref[at].astype(F32)
         for side, ref in enumerate((self_ref, near_ref)):
             ref[start : start + deep, :] = jnp.concatenate(
                 [
-                    value[:, f * width + side * half : f * width + (side + 1) * half]
+                    value[:deep, f * width + side * half : f * width + (side + 1) * half]
                     for f in range(slices)
                 ],
                 axis=1,
             )
+        ref = (second_self_ref, second_near_ref)[core]
+        ref[2 * x * deep : (2 * x + 1) * deep, :] = value[deep:, : cols // 2]
+        ref[(2 * x + 1) * deep : (2 * x + 2) * deep, :] = value[deep:, cols // 2 :]
 
 
 def exchange(value, axis):
@@ -332,7 +359,12 @@
         functools.partial(pick_body, slices=slices),
         [((slots, slice_cols), BF16), ((slice_cols, 2 * hidden), BF16)],
         (send_rows, features, first_self, first_neighbor), "pick",
-        2 * slots * rows * slice_cols, 2 * slots * rows,
+        2 * slots * rows * slice_cols, 2 * slots * rows, far=(0, 1, 2, 3),
+        scratch=[
+            pltpu.VMEM(send_rows.shape, I32), pltpu.VMEM(features.shape, BF16),
+            pltpu.VMEM(first_self.shape, BF16), pltpu.VMEM(first_neighbor.shape, BF16),
+            pltpu.SemaphoreType.DMA((4,)),
+        ],
     )
     routed = exchange(picked.reshape(peers * slices, per, slice_cols), AXES)
     routed = routed.reshape(peers, slices, per, slice_cols)
@@ -349,7 +381,8 @@
     )
     slot_at = lax.broadcasted_iota(I32, (slices, peers, per, width), 0) * per
     slot_at = slot_at + lax.broadcasted_iota(I32, (slices, peers, per, width), 2)
-    mask = (slot_at < arrive_count.reshape(1, peers, 1, 1)).astype(BF16).reshape(slots, width)
+    mask = (slot_at < arrive_count.reshape(1, peers, 1, 1)).astype(BF16)
+    mask = mask.reshape(slices, quarter, width)
     bias = first_bias.reshape(hidden, 1)
     routed, seed_table, mask, bias = lax.optimization_barrier((routed, seed_table, mask, bias))
 
@@ -364,18 +397,21 @@
         0, 8 * quarter * slices * slice_cols,
     )
 
-    *grad_tables, own_seeds = call(
+    grads = call(
         functools.partial(owner_body, slices=slices, fan_two=fan_two),
-        [((quarter, width), BF16)] * slices + [((width, seeds), BF16)],
+        [((quarter + width, seeds), BF16)] * slices,
         (
-            place, mask, self_table, near_table, degree.reshape(1, mids), bias, seed_table,
+            place, self_table.reshape(slices, quarter, mids), near_table.reshape(slices, quarter, mids),
+            mask, degree.reshape(1, mids), bias, seed_table,
             seed_near_table, second_self, second_neighbor, cotangent, *tables,
         ),
-        "owner", 8 * slots * mids * width, 4 * slots * mids, scalars=1,
-    )
-    grads = shifted(grad_tables, "feat", slices)
-    all_seeds = shifted([own_seeds] * slices, "feat", slices)
-    grads, all_seeds = lax.optimization_barrier((grads, all_seeds))
+        "owner", 8 * slots * mids * width, 4 * slots * mids, scalars=1, far=(1, 2),
+        scratch=[
+            pltpu.VMEM((slices, quarter, mids), BF16), pltpu.VMEM((slices, quarter, mids), BF16),
+            pltpu.SemaphoreType.DMA((2, slices)),
+        ],
+    )
+    grads = shifted(grads, "feat", slices)
 
     step = slice_cols // cores
     keep, give = call(
@@ -388,7 +424,7 @@
     seed_embedding, second_keep, second_give = call(
         seeds_body,
         [((seeds, out_cols), BF16), ((hidden, out_cols), F32), ((hidden, out_cols), BF16)],
-        (place, second_self, second_neighbor, cotangent, *all_seeds), "seeds",
+        (place, second_self, second_neighbor, cotangent, *grads), "seeds",
         8 * seeds * hidden * out_cols, 2 * slots * width,
         scratch=[pltpu.VMEM((2, hidden, out_cols), F32)], scalars=1,
     )
@@ -427,26 +463,15 @@
     mixed = exchange(mixed, "z")
     for stride in strides[1:]:
         second = doubled(second, stride)
-    mixed, second = lax.optimization_barrier((mixed, second))
     (mixed,) = call(
-        sum_body, [((count_x * cores, deep, 2 * hidden), BF16)], (mixed,), "sum",
+        join_body, [((count_x * cores, 2 * deep, 2 * hidden), BF16)], (mixed, second), "join",
         0, 64 * deep * hidden,
     )
     mixed = exchange(mixed, ("x", "core"))
-    (second,) = call(
-        second_pair_body, [((2 * hidden // count_x, out_cols), BF16)],
-        (place, second, swapped(second, "core", cores, 1)), "second_pair",
-        0, 2 * hidden * out_cols, scalars=1,
-    )
-    grad_second_self, grad_second_neighbor = call(
-        second_finish_body, [((hidden, out_cols), F32)] * 2,
-        (place, *shifted([second] * count_x, "x", count_x)), "second_finish",
-        0, 12 * hidden * out_cols, scalars=1,
-    )
-
-    grad_first_self, grad_first_neighbor = call(
-        functools.partial(first_finish_body, cores=cores, slices=slices),
-        [((slice_cols, hidden), F32)] * 2, (mixed,), "first_finish", 0, 12 * slice_cols * hidden,
+    grad_first_self, grad_first_neighbor, grad_second_self, grad_second_neighbor = call(
+        functools.partial(finish_body, cores=cores, slices=slices),
+        [((slice_cols, hidden), F32)] * 2 + [((hidden, out_cols), F32)] * 2, (mixed,), "finish",
+        0, 24 * slice_cols * hidden,
     )
     return (
         seed_embedding,

time: 153 us -> 141 us (0.922)
  blocking collectives: 0 us -> 16.1 us
  starting transfers between devices: 64.6 us -> 49.7 us
  local copies, waits for them, and re-layouts: 10.1 us -> 3.14 us
  waiting for transfers between devices: 45.4 us -> 39.1 us
    all_to_all x0 -> x1, blocking collectives: none -> 16.1 us  [exchange(): return lax.all_to_all(value, axis, split_axis=0, concat_axis=0, tiled=True)]
    ppermute x18 -> x12, starting transfers between devices: 23.1 us -> 16.1 us  [shifted(): lax.ppermute(piece, axis, [(at, (at + shift) % count) for at in range(cou...]
    unnamed x36 -> x24, local copies, waits for them, and re-layouts: 9.55 us -> 2.75 us
    all_to_all x4 -> x3, starting transfers between devices: 29.6 us -> 23.5 us  [exchange(): return lax.all_to_all(value, axis, split_axis=0, concat_axis=0, tiled=True)]
    ppermute x18 -> x12, waiting for transfers between devices: 20.6 us -> 15.4 us  [shifted(): lax.ppermute(piece, axis, [(at, (at + shift) % count) for at in range(cou...]
    ppermute x6 -> x5, starting transfers between devices: 11.9 us -> 10.1 us  [swapped(): return lax.ppermute(value, axis, [(at, at ^ step) for at in range(count)])]
    ppermute x6 -> x5, waiting for transfers between devices: 10.2 us -> 9.49 us  [swapped(): return lax.ppermute(value, axis, [(at, at ^ step) for at in range(count)])]
    pallas_call x18 -> x16, Pallas kernels: 29.1 us -> 29.7 us  [call(): pl.pallas_call(body, out_shape=[jax.ShapeDtypeStruct(shape, dtype) for sh...]
  transfers between devices with their start and end apart: 28 -> 20, of which waited for: 14 -> 10; matrix products, arithmetic and copies ran while one was open for 0% -> 0% of each run, Pallas kernels for 10% -> 10%
where the time goes in v4:
time: 141 us; the launch traced here: 139 us
  starting transfers between devices  49.7 us (35%)
  waiting for transfers between devices  39.1 us (28%)
  Pallas kernels  29.7 us (21%)
  blocking collectives  16.1 us (11%)
  local copies, waits for them, and re-layouts  3.14 us (2%)
    pallas_call x16, Pallas kernels, call(): pl.pallas_call(body, out_shape=[jax.ShapeDtypeStruct(shape, dtype) for sh...  29.7 us
    all_to_all x3, starting transfers between devices, exchange(): return lax.all_to_all(value, axis, split_axis=0, concat_axis=0, tiled=True)  23.5 us
    all_to_all x1, blocking collectives, exchange(): return lax.all_to_all(value, axis, split_axis=0, concat_axis=0, tiled=True)  16.1 us
    ppermute x12, starting transfers between devices, shifted(): lax.ppermute(piece, axis, [(at, (at + shift) % count) for at in range(cou...  16.1 us
    ppermute x12, waiting for transfers between devices, shifted(): lax.ppermute(piece, axis, [(at, (at + shift) % count) for at in range(cou...  15.4 us
    all_to_all x3, waiting for transfers between devices, exchange(): return lax.all_to_all(value, axis, split_axis=0, concat_axis=0, tiled=True)  14.2 us
    ppermute x5, starting transfers between devices, swapped(): return lax.ppermute(value, axis, [(at, at ^ step) for at in range(count)])  10.1 us
    ppermute x5, waiting for transfers between devices, swapped(): return lax.ppermute(value, axis, [(at, at ^ step) for at in range(count)])  9.49 us
  transfers between devices with their start and end apart: 20, of which 10 were waited for; matrix products, arithmetic and copies ran while one was open for 0% of the time, Pallas kernels for 10%

profile of v4, /device:TPU:1, one launch (start us, length us, event | category | flops | bytes accessed | tf_op | source)
XLA Modules:
  0.0 139.0 jit_solution(1664718967379374223)
XLA Ops:
  0.6 4.8 %pick.1 = (bf16[2048,256]{1,0:T(8,128)(2,1)}, bf16[256,512]{1,0:T(8,128)(2,1)S(1)}) custom-call(s32[1,2048]{1,0:T(1,128)} %row_far.1, bf16[1536,256]{1,0:T(8,128)(2,1)} %x_far.1, bf16[256,256]{1,0:T(8,128)(2,1)} %self_far.1, bf16[256,256]{1,0:T(8,128)(2,1)} %near_far.1), custom_call_target="tpu_custom_call" | custom-call | flops 1610612736 | bytes 6291456 | tf_op jit(solution)/shard_map/pick/pallas_call | solution.py:31
  5.5 15.7 %all-to-all-start = ((bf16[256,8,256]{2,1,0:T(8,128)(2,1)}), bf16[256,8,256]{2,1,0:T(8,128)(2,1)S(1)}, u32[]{:S(2)}, u32[]{:S(2)}) async-start(bf16[256,8,256]{2,1,0:T(8,128)(2,1)} %bitcast.10), calls=%async_computation | async-start | bytes 2097152 | tf_op jit(solution)/shard_map/all_to_all | solution.py:310
  21.2 2.7 %collective-permute-start.2 = (bf16[256,512]{1,0:T(8,128)(2,1)S(1)}, bf16[256,512]{1,0:T(8,128)(2,1)S(1)}, u32[]{:S(2)}, u32[]{:S(2)}) collective-permute-start(bf16[256,512]{1,0:T(8,128)(2,1)S(1)} %get-tuple-element.49.refs_0_), channel_id=1, source_target_pairs={{0,3},{1,0},{2,1},{3,2},{4,7},{5,4},{6,5},{7,6},{8,11},{9,8},{10,9... | collective-permute-start | bytes 786440 | tf_op jit(solution)/shard_map/ppermute | solution.py:317
  23.9 0.5 collective-permute-start.1
  24.4 0.6 collective-permute-start
  25.0 0.1 pad_add_fusion.place_ref
  25.2 0.1 lt.17
  25.3 0.1 iota.20
  25.4 11.1 %count.1 = (bf16[2048,512]{1,0:T(8,128)(2,1)S(1)}, bf16[2048,512]{1,0:T(8,128)(2,1)S(1)}, bf16[512,128]{1,0:T(8,128)(2,1)S(1)}, bf16[512,128]{1,0:T(8,128)(2,1)S(1)}) custom-call(s32[1,512]{1,0:T(1,128)S(1)} %bitcast.22, s32[25,512]{1,0:T(8,128)S(1)} %bitcast.18, s32[1,512]{1,0:T(1,128)S(1)} %bitcast.19, s32[1,128]{1,0:T(1,128)S(1)} %bitcast.23, ...), custom_call_target="tpu_custom_call" | custom-call | bytes 16777216 | tf_op jit(solution)/shard_map/count/pallas_call | solution.py:31
  36.5 1.4 copy-done
  37.9 1.3 copy-done.1
  39.2 0.2 fusion.mask_ref
  39.4 14.2 %all-to-all-done = bf16[256,8,256]{2,1,0:T(8,128)(2,1)S(1)} async-done(((bf16[256,8,256]{2,1,0:T(8,128)(2,1)}), bf16[256,8,256]{2,1,0:T(8,128)(2,1)S(1)}, u32[]{:S(2)}, u32[]{:S(2)}) %all-to-all-start) | async-done | bytes 1048608 | tf_op jit(solution)/shard_map/all_to_all | solution.py:310
  53.7 2.1 %project.1 = (bf16[512,128]{1,0:T(8,128)(2,1)S(1)}, bf16[512,128]{1,0:T(8,128)(2,1)}, bf16[512,128]{1,0:T(8,128)(2,1)}, bf16[512,128]{1,0:T(8,128)(2,1)}) custom-call(s32[3]{0:T(128)S(1)} %pad_add_fusion.place_ref, bf16[64,4,8,256]{3,2,1,0:T(8,128)(2,1)S(1)} %bitcast.14, bf16[256,512]{1,0:T(8,128)(2,1)S(1)} %get-tuple-element.49.refs_0_, ...), custom_call_target="tpu_custom_call" | custom-call | flops 536870912 | bytes 2097152 | tf_op jit(solution)/shard_map/project/pallas_call | solution.py:31
  55.8 0.2 collective-permute-start.3
  56.0 1.0 collective-permute-start.4
  57.0 1.5 %collective-permute-start.5 = (bf16[512,128]{1,0:T(8,128)(2,1)}, bf16[512,128]{1,0:T(8,128)(2,1)S(1)}, u32[]{:S(2)}, u32[]{:S(2)}) collective-permute-start(bf16[512,128]{1,0:T(8,128)(2,1)} %get-tuple-element.53), channel_id=1, source_target_pairs={{0,3},{1,0},{2,1},{3,2},{4,7},{5,4},{6,5},{7,6},{8,11},{9,8},{10,9... | collective-permute-start | bytes 393224 | tf_op jit(solution)/shard_map/ppermute | solution.py:317
  58.5 0.1 copy.19.bias_ref
  58.6 6.0 %collective-permute-done.3.refs_1_ = bf16[512,128]{1,0:T(8,128)(2,1)S(1)} collective-permute-done((bf16[512,128]{1,0:T(8,128)(2,1)}, bf16[512,128]{1,0:T(8,128)(2,1)S(1)}, u32[]{:S(2)}, u32[]{:S(2)}) %collective-permute-start.3) | collective-permute-done | bytes 131104 | tf_op jit(solution)/shard_map/ppermute | solution.py:317
  64.7 5.0 %owner.1 = (bf16[640,128]{1,0:T(8,128)(2,1)S(1)}, bf16[640,128]{1,0:T(8,128)(2,1)S(1)}, bf16[640,128]{1,0:T(8,128)(2,1)S(1)}, bf16[640,128]{1,0:T(8,128)(2,1)S(1)}) custom-call(s32[3]{0:T(128)S(1)} %pad_add_fusion.place_ref, bf16[4,512,512]{2,1,0:T(8,128)(2,1)} %bitcast.16, bf16[4,512,512]{2,1,0:T(8,128)(2,1)} %bitcast.17, ...), custom_call_target="tpu_custom_call" | custom-call | flops 1073741824 | bytes 4194304 | tf_op jit(solution)/shard_map/owner/pallas_call | solution.py:31
  69.7 0.6 collective-permute-start.6
  70.3 3.8 %collective-permute-start.7 = (bf16[640,128]{1,0:T(8,128)(2,1)S(1)}, bf16[640,128]{1,0:T(8,128)(2,1)S(1)}, u32[]{:S(2)}, u32[]{:S(2)}) collective-permute-start(bf16[640,128]{1,0:T(8,128)(2,1)S(1)} %get-tuple-element.56), channel_id=1, source_target_pairs={{0,2},{1,3},{2,0},{3,1},{4,6},{5,7},{6,4},{7,5},{8,10},{9,11},{10,... | collective-permute-start | bytes 491528 | tf_op jit(solution)/shard_map/ppermute | solution.py:317
  74.1 0.3 turn.1.xt_ref
  74.4 1.2 collective-permute-done.6.refs_1_
  75.6 5.4 %collective-permute-done.7.refs_2_ = bf16[640,128]{1,0:T(8,128)(2,1)S(1)} collective-permute-done((bf16[640,128]{1,0:T(8,128)(2,1)S(1)}, bf16[640,128]{1,0:T(8,128)(2,1)S(1)}, u32[]{:S(2)}, u32[]{:S(2)}) %collective-permute-start.7) | collective-permute-done | bytes 163872 | tf_op jit(solution)/shard_map/ppermute | solution.py:317
  81.0 1.4 %weight.1 = (f32[4,128,512]{2,1,0:T(8,128)S(1)}, bf16[4,128,512]{2,1,0:T(8,128)(2,1)S(1)}) custom-call(s32[3]{0:T(128)S(1)} %pad_add_fusion.place_ref, bf16[1024,512]{1,0:T(8,128)(2,1)S(1)} %turn.1.xt_ref, bf16[640,128]{1,0:T(8,128)(2,1)S(1)} %get-tuple-element.54.refs_0_, bf16[640,128]{1,0:T(8,128)(2,1)S(1)} %collective-permute-done.6.refs_1_, ...), custom_call_target="tpu_custom_call" | custom-call | flops 536870912 | bytes 2097152 | tf_op jit(solution)/shard_map/weight/pallas_call | solution.py:31
  82.4 1.8 %collective-permute-start.9 = (bf16[4,128,512]{2,1,0:T(8,128)(2,1)S(1)}, bf16[4,128,512]{2,1,0:T(8,128)(2,1)S(1)}, u32[]{:S(2)}, u32[]{:S(2)}) collective-permute-start(bf16[4,128,512]{2,1,0:T(8,128)(2,1)S(1)} %get-tuple-element.60), channel_id=1, source_target_pairs={{0,4},{4,0},{1,5},{5,1},{2,6},{6,2},{3,7},{7,3},{8,12},{12,8},{9,1... | collective-permute-start | bytes 1572872 | tf_op jit(solution)/shard_map/ppermute | solution.py:323
  84.2 1.6 %seeds.1 = (bf16[128,256]{1,0:T(8,128)(2,1)}, f32[256,256]{1,0:T(8,128)S(1)}, bf16[256,256]{1,0:T(8,128)(2,1)S(1)}) custom-call(s32[3]{0:T(128)S(1)} %pad_add_fusion.place_ref, bf16[256,256]{1,0:T(8,128)(2,1)S(1)} %copy-done.2, bf16[256,256]{1,0:T(8,128)(2,1)S(1)} %copy-done.3, bf16[128,256]{1,0:T(8,128)(2,1)S(1)} %copy-done.4, ...), custom_call_target="tpu_custom_call" | custom-call | flops 67108864 | bytes 524288 | tf_op jit(solution)/shard_map/seeds/pallas_call | solution.py:31
  85.8 0.9 halves.1
  86.7 4.5 %all-to-all-start.1 = ((bf16[16,32,512]{2,1,0:T(8,128)(2,1)}), bf16[16,32,512]{2,1,0:T(8,128)(2,1)S(1)}, u32[]{:S(2)}, u32[]{:S(2)}) async-start(bf16[16,32,512]{2,1,0:T(8,128)(2,1)} %halves.1), calls=%async_computation.1 | async-start | bytes 1048576 | tf_op jit(solution)/shard_map/all_to_all | solution.py:310
  91.2 0.7 collective-permute-start.10
  91.9 1.0 collective-permute-done.10.got_ref
  92.9 0.6 second_split.1
  93.4 1.6 %collective-permute-start.11 = (bf16[64,256]{1,0:T(8,128)(2,1)S(1)}, bf16[64,256]{1,0:T(8,128)(2,1)S(1)}, u32[]{:S(2)}, u32[]{:S(2)}) collective-permute-start(bf16[64,256]{1,0:T(8,128)(2,1)S(1)} %get-tuple-element.66), channel_id=1, source_target_pairs={{0,64},{64,128},{128,192},{192,0},{1,65},{65,129},{129,193},{193,1... | collective-permute-start | bytes 98312 | tf_op jit(solution)/shard_map/ppermute | solution.py:317
  95.1 2.4 %collective-permute-start.12 = (bf16[64,256]{1,0:T(8,128)(2,1)S(1)}, bf16[64,256]{1,0:T(8,128)(2,1)S(1)}, u32[]{:S(2)}, u32[]{:S(2)}) collective-permute-start(bf16[64,256]{1,0:T(8,128)(2,1)S(1)} %get-tuple-element.67), channel_id=1, source_target_pairs={{0,128},{64,192},{128,0},{192,64},{1,129},{65,193},{129,1},{193,65... | collective-permute-start | bytes 98312 | tf_op jit(solution)/shard_map/ppermute | solution.py:317
  97.5 1.2 collective-permute-start.13
  98.7 0.8 collective-permute-done.11.refs_1_
  99.4 2.0 %collective-permute-done.12.refs_2_ = bf16[64,256]{1,0:T(8,128)(2,1)S(1)} collective-permute-done((bf16[64,256]{1,0:T(8,128)(2,1)S(1)}, bf16[64,256]{1,0:T(8,128)(2,1)S(1)}, u32[]{:S(2)}, u32[]{:S(2)}) %collective-permute-start.12) | collective-permute-done | bytes 32800 | tf_op jit(solution)/shard_map/ppermute | solution.py:317
  101.4 0.4 collective-permute-start.14
  101.9 2.4 %collective-permute-done.14.refs_1_ = bf16[64,256]{1,0:T(8,128)(2,1)S(1)} collective-permute-done((bf16[64,256]{1,0:T(8,128)(2,1)S(1)}, bf16[64,256]{1,0:T(8,128)(2,1)S(1)}, u32[]{:S(2)}, u32[]{:S(2)}) %collective-permute-start.14) | collective-permute-done | bytes 32800 | tf_op jit(solution)/shard_map/ppermute | solution.py:323
  104.3 0.8 sum.1
  105.1 3.4 %all-to-all-start.2 = ((bf16[8,32,512]{2,1,0:T(8,128)(2,1)}), bf16[8,32,512]{2,1,0:T(8,128)(2,1)S(1)}, u32[]{:S(2)}, u32[]{:S(2)}) async-start(bf16[8,32,512]{2,1,0:T(8,128)(2,1)} %sum.1), calls=%async_computation.2 | async-start | bytes 524288 | tf_op jit(solution)/shard_map/all_to_all | solution.py:310
  108.5 2.3 %collective-permute-start.15 = (bf16[64,256]{1,0:T(8,128)(2,1)S(1)}, bf16[64,256]{1,0:T(8,128)(2,1)S(1)}, u32[]{:S(2)}, u32[]{:S(2)}) collective-permute-start(bf16[64,256]{1,0:T(8,128)(2,1)S(1)} %second_add.5.refs_0_), channel_id=1, source_target_pairs={{0,16},{8,24},{16,0},{24,8},{32,48},{40,56},{48,32},{56,40},{1,17}... | collective-permute-start | bytes 98312 | tf_op jit(solution)/shard_map/ppermute | solution.py:323
  110.8 4.0 %collective-permute-done.15.refs_1_ = bf16[64,256]{1,0:T(8,128)(2,1)S(1)} collective-permute-done((bf16[64,256]{1,0:T(8,128)(2,1)S(1)}, bf16[64,256]{1,0:T(8,128)(2,1)S(1)}, u32[]{:S(2)}, u32[]{:S(2)}) %collective-permute-start.15) | collective-permute-done | bytes 32800 | tf_op jit(solution)/shard_map/ppermute | solution.py:323
  114.8 4.9 %collective-permute-start.16 = (bf16[64,256]{1,0:T(8,128)(2,1)S(1)}, bf16[64,256]{1,0:T(8,128)(2,1)S(1)}, u32[]{:S(2)}, u32[]{:S(2)}) collective-permute-start(bf16[64,256]{1,0:T(8,128)(2,1)S(1)} %second_add.6.refs_0_), channel_id=1, source_target_pairs={{0,32},{8,40},{16,48},{24,56},{32,0},{40,8},{48,16},{56,24},{1,33}... | collective-permute-start | bytes 98312 | tf_op jit(solution)/shard_map/ppermute | solution.py:323
  119.6 2.1 %collective-permute-done.16.refs_1_ = bf16[64,256]{1,0:T(8,128)(2,1)S(1)} collective-permute-done((bf16[64,256]{1,0:T(8,128)(2,1)S(1)}, bf16[64,256]{1,0:T(8,128)(2,1)S(1)}, u32[]{:S(2)}, u32[]{:S(2)}) %collective-permute-start.16) | collective-permute-done | bytes 32800 | tf_op jit(solution)/shard_map/ppermute | solution.py:323
  121.8 16.1 %all_to_all.20.all_ref = bf16[8,64,512]{2,1,0:T(8,128)(2,1)S(1)} all-to-all(bf16[8,64,512]{2,1,0:T(8,128)(2,1)S(1)} %join.1), channel_id=1, replica_groups=mesh['x'=4,'z'=8,'core'=2,'feat'=4] {'x','core'}, dimensions={0} | all-to-all | bytes 1048576 | tf_op jit(solution)/shard_map/all_to_all | solution.py:310
  137.9 1.1 finish.1
  (41 shorter events, 0.3 us)
Async XLA Ops:
  5.4 19.7 %copy-start.11 = (s32[1,64]{1,0:T(1,128)S(1)}, s32[1,64]{1,0:T(1,128)}, u32[]{:S(2)}) copy-start(s32[1,64]{1,0:T(1,128)} %param.21) | copy-start | bytes 772
  5.4 20.0 %copy-start.5 = (s32[512,25]{0,1:T(8,128)S(1)}, s32[512,25]{0,1:T(8,128)}, u32[]{:S(2)}) copy-start(s32[512,25]{0,1:T(8,128)} %param.23) | copy-start | bytes 153604
  5.4 20.0 %copy-start.6 = (s32[512]{0:T(512)S(1)}, s32[512]{0:T(512)}, u32[]{:S(2)}) copy-start(s32[512]{0:T(512)} %param.24) | copy-start | bytes 6148
  5.4 20.0 %copy-start.7 = (s32[128,10]{0,1:T(8,128)S(1)}, s32[128,10]{0,1:T(8,128)}, u32[]{:S(2)}) copy-start(s32[128,10]{0,1:T(8,128)} %param.26) | copy-start | bytes 15364
  5.5 20.0 %copy-start.8 = (s32[512]{0:T(512)S(1)}, s32[512]{0:T(512)}, u32[]{:S(2)}) copy-start(s32[512]{0:T(512)} %param.22) | copy-start | bytes 6148
  5.5 19.9 %copy-start.9 = (s32[128]{0:T(128)S(1)}, s32[128]{0:T(128)}, u32[]{:S(2)}) copy-start(s32[128]{0:T(128)} %param.25) | copy-start | bytes 1540
  5.5 53.0 %copy-start.10 = (f32[256]{0:T(256)S(1)}, f32[256]{0:T(256)}, u32[]{:S(2)}) copy-start(f32[256]{0:T(256)} %param.17) | copy-start | bytes 3076
  5.5 59.2 %copy-start.2 = (bf16[256,256]{1,0:T(8,128)(2,1)S(1)}, bf16[256,256]{1,0:T(8,128)(2,1)}, u32[]{:S(2)}) copy-start(bf16[256,256]{1,0:T(8,128)(2,1)} %second_self_ref.3) | copy-start | bytes 393220
  5.5 59.1 %copy-start.3 = (bf16[256,256]{1,0:T(8,128)(2,1)S(1)}, bf16[256,256]{1,0:T(8,128)(2,1)}, u32[]{:S(2)}) copy-start(bf16[256,256]{1,0:T(8,128)(2,1)} %second_near_ref.3) | copy-start | bytes 393220
  5.5 59.1 %copy-start.4 = (bf16[128,256]{1,0:T(8,128)(2,1)S(1)}, bf16[128,256]{1,0:T(8,128)(2,1)}, u32[]{:S(2)}) copy-start(bf16[128,256]{1,0:T(8,128)(2,1)} %cotangent_ref.3) | copy-start | bytes 196612
  5.5 48.1 %all-to-all-start = ((bf16[256,8,256]{2,1,0:T(8,128)(2,1)}), bf16[256,8,256]{2,1,0:T(8,128)(2,1)S(1)}, u32[]{:S(2)}, u32[]{:S(2)}) async-start(bf16[256,8,256]{2,1,0:T(8,128)(2,1)} %bitcast.10), calls=%async_computation | async-start | bytes 2097152 | tf_op jit(solution)/shard_map/all_to_all | solution.py:310
  21.2 32.5 %collective-permute-start.2 = (bf16[256,512]{1,0:T(8,128)(2,1)S(1)}, bf16[256,512]{1,0:T(8,128)(2,1)S(1)}, u32[]{:S(2)}, u32[]{:S(2)}) collective-permute-start(bf16[256,512]{1,0:T(8,128)(2,1)S(1)} %get-tuple-element.49.refs_0_), channel_id=1, source_target_pairs={{0,3},{1,0},{2,1},{3,2},{4,7},{5,4},{6,5},{7,6},{8,11},{9,8},{10,9... | collective-permute-start | bytes 786440 | tf_op jit(solution)/shard_map/ppermute | solution.py:317
  23.9 29.7 %collective-permute-start.1 = (bf16[256,512]{1,0:T(8,128)(2,1)S(1)}, bf16[256,512]{1,0:T(8,128)(2,1)S(1)}, u32[]{:S(2)}, u32[]{:S(2)}) collective-permute-start(bf16[256,512]{1,0:T(8,128)(2,1)S(1)} %get-tuple-element.49.refs_0_), channel_id=1, source_target_pairs={{0,2},{1,3},{2,0},{3,1},{4,6},{5,7},{6,4},{7,5},{8,10},{9,11},{10,... | collective-permute-start | bytes 786440 | tf_op jit(solution)/shard_map/ppermute | solution.py:317
  24.4 29.2 %collective-permute-start = (bf16[256,512]{1,0:T(8,128)(2,1)S(1)}, bf16[256,512]{1,0:T(8,128)(2,1)S(1)}, u32[]{:S(2)}, u32[]{:S(2)}) collective-permute-start(bf16[256,512]{1,0:T(8,128)(2,1)S(1)} %get-tuple-element.49.refs_0_), channel_id=1, source_target_pairs={{0,1},{1,2},{2,3},{3,0},{4,5},{5,6},{6,7},{7,4},{8,9},{9,10},{10,1... | collective-permute-start | bytes 786440 | tf_op jit(solution)/shard_map/ppermute | solution.py:317
  36.5 1.4 copy-start
  37.9 1.3 copy-start.1
  55.8 8.8 %collective-permute-start.3 = (bf16[512,128]{1,0:T(8,128)(2,1)}, bf16[512,128]{1,0:T(8,128)(2,1)S(1)}, u32[]{:S(2)}, u32[]{:S(2)}) collective-permute-start(bf16[512,128]{1,0:T(8,128)(2,1)} %get-tuple-element.51), channel_id=1, source_target_pairs={{0,1},{1,2},{2,3},{3,0},{4,5},{5,6},{6,7},{7,4},{8,9},{9,10},{10,1... | collective-permute-start | bytes 393224 | tf_op jit(solution)/shard_map/ppermute | solution.py:317
  56.0 8.6 %collective-permute-start.4 = (bf16[512,128]{1,0:T(8,128)(2,1)}, bf16[512,128]{1,0:T(8,128)(2,1)S(1)}, u32[]{:S(2)}, u32[]{:S(2)}) collective-permute-start(bf16[512,128]{1,0:T(8,128)(2,1)} %get-tuple-element.52), channel_id=1, source_target_pairs={{0,2},{1,3},{2,0},{3,1},{4,6},{5,7},{6,4},{7,5},{8,10},{9,11},{10,... | collective-permute-start | bytes 393224 | tf_op jit(solution)/shard_map/ppermute | solution.py:317
  57.0 7.6 %collective-permute-start.5 = (bf16[512,128]{1,0:T(8,128)(2,1)}, bf16[512,128]{1,0:T(8,128)(2,1)S(1)}, u32[]{:S(2)}, u32[]{:S(2)}) collective-permute-start(bf16[512,128]{1,0:T(8,128)(2,1)} %get-tuple-element.53), channel_id=1, source_target_pairs={{0,3},{1,0},{2,1},{3,2},{4,7},{5,4},{6,5},{7,6},{8,11},{9,8},{10,9... | collective-permute-start | bytes 393224 | tf_op jit(solution)/shard_map/ppermute | solution.py:317
  69.7 5.9 %collective-permute-start.6 = (bf16[640,128]{1,0:T(8,128)(2,1)S(1)}, bf16[640,128]{1,0:T(8,128)(2,1)S(1)}, u32[]{:S(2)}, u32[]{:S(2)}) collective-permute-start(bf16[640,128]{1,0:T(8,128)(2,1)S(1)} %get-tuple-element.55), channel_id=1, source_target_pairs={{0,1},{1,2},{2,3},{3,0},{4,5},{5,6},{6,7},{7,4},{8,9},{9,10},{10,1... | collective-permute-start | bytes 491528 | tf_op jit(solution)/shard_map/ppermute | solution.py:317
  70.3 10.7 %collective-permute-start.7 = (bf16[640,128]{1,0:T(8,128)(2,1)S(1)}, bf16[640,128]{1,0:T(8,128)(2,1)S(1)}, u32[]{:S(2)}, u32[]{:S(2)}) collective-permute-start(bf16[640,128]{1,0:T(8,128)(2,1)S(1)} %get-tuple-element.56), channel_id=1, source_target_pairs={{0,2},{1,3},{2,0},{3,1},{4,6},{5,7},{6,4},{7,5},{8,10},{9,11},{10,... | collective-permute-start | bytes 491528 | tf_op jit(solution)/shard_map/ppermute | solution.py:317
  74.0 6.9 %collective-permute-start.8 = (bf16[640,128]{1,0:T(8,128)(2,1)S(1)}, bf16[640,128]{1,0:T(8,128)(2,1)S(1)}, u32[]{:S(2)}, u32[]{:S(2)}) collective-permute-start(bf16[640,128]{1,0:T(8,128)(2,1)S(1)} %get-tuple-element.57), channel_id=1, source_target_pairs={{0,3},{1,0},{2,1},{3,2},{4,7},{5,4},{6,5},{7,6},{8,11},{9,8},{10,9... | collective-permute-start | bytes 491528 | tf_op jit(solution)/shard_map/ppermute | solution.py:317
  82.4 3.4 %collective-permute-start.9 = (bf16[4,128,512]{2,1,0:T(8,128)(2,1)S(1)}, bf16[4,128,512]{2,1,0:T(8,128)(2,1)S(1)}, u32[]{:S(2)}, u32[]{:S(2)}) collective-permute-start(bf16[4,128,512]{2,1,0:T(8,128)(2,1)S(1)} %get-tuple-element.60), channel_id=1, source_target_pairs={{0,4},{4,0},{1,5},{5,1},{2,6},{6,2},{3,7},{7,3},{8,12},{12,8},{9,1... | collective-permute-start | bytes 1572872 | tf_op jit(solution)/shard_map/ppermute | solution.py:323
  86.7 17.6 %all-to-all-start.1 = ((bf16[16,32,512]{2,1,0:T(8,128)(2,1)}), bf16[16,32,512]{2,1,0:T(8,128)(2,1)S(1)}, u32[]{:S(2)}, u32[]{:S(2)}) async-start(bf16[16,32,512]{2,1,0:T(8,128)(2,1)} %halves.1), calls=%async_computation.1 | async-start | bytes 1048576 | tf_op jit(solution)/shard_map/all_to_all | solution.py:310
  91.2 1.7 %collective-permute-start.10 = (bf16[256,256]{1,0:T(8,128)(2,1)S(1)}, bf16[256,256]{1,0:T(8,128)(2,1)S(1)}, u32[]{:S(2)}, u32[]{:S(2)}) collective-permute-start(bf16[256,256]{1,0:T(8,128)(2,1)S(1)} %get-tuple-element.64), channel_id=1, source_target_pairs={{0,4},{4,0},{1,5},{5,1},{2,6},{6,2},{3,7},{7,3},{8,12},{12,8},{9,1... | collective-permute-start | bytes 393224 | tf_op jit(solution)/shard_map/ppermute | solution.py:323
  93.4 6.0 %collective-permute-start.11 = (bf16[64,256]{1,0:T(8,128)(2,1)S(1)}, bf16[64,256]{1,0:T(8,128)(2,1)S(1)}, u32[]{:S(2)}, u32[]{:S(2)}) collective-permute-start(bf16[64,256]{1,0:T(8,128)(2,1)S(1)} %get-tuple-element.66), channel_id=1, source_target_pairs={{0,64},{64,128},{128,192},{192,0},{1,65},{65,129},{129,193},{193,1... | collective-permute-start | bytes 98312 | tf_op jit(solution)/shard_map/ppermute | solution.py:317
  95.1 6.3 %collective-permute-start.12 = (bf16[64,256]{1,0:T(8,128)(2,1)S(1)}, bf16[64,256]{1,0:T(8,128)(2,1)S(1)}, u32[]{:S(2)}, u32[]{:S(2)}) collective-permute-start(bf16[64,256]{1,0:T(8,128)(2,1)S(1)} %get-tuple-element.67), channel_id=1, source_target_pairs={{0,128},{64,192},{128,0},{192,64},{1,129},{65,193},{129,1},{193,65... | collective-permute-start | bytes 98312 | tf_op jit(solution)/shard_map/ppermute | solution.py:317
  97.5 3.9 %collective-permute-start.13 = (bf16[64,256]{1,0:T(8,128)(2,1)S(1)}, bf16[64,256]{1,0:T(8,128)(2,1)S(1)}, u32[]{:S(2)}, u32[]{:S(2)}) collective-permute-start(bf16[64,256]{1,0:T(8,128)(2,1)S(1)} %get-tuple-element.68), channel_id=1, source_target_pairs={{0,192},{64,0},{128,64},{192,128},{1,193},{65,1},{129,65},{193,129... | collective-permute-start | bytes 98312 | tf_op jit(solution)/shard_map/ppermute | solution.py:317
  101.4 2.9 %collective-permute-start.14 = (bf16[64,256]{1,0:T(8,128)(2,1)S(1)}, bf16[64,256]{1,0:T(8,128)(2,1)S(1)}, u32[]{:S(2)}, u32[]{:S(2)}) collective-permute-start(bf16[64,256]{1,0:T(8,128)(2,1)S(1)} %second_add.4.refs_0_), channel_id=1, source_target_pairs={{0,8},{8,0},{16,24},{24,16},{32,40},{40,32},{48,56},{56,48},{1,9},... | collective-permute-start | bytes 98312 | tf_op jit(solution)/shard_map/ppermute | solution.py:323
  105.1 16.6 %all-to-all-start.2 = ((bf16[8,32,512]{2,1,0:T(8,128)(2,1)}), bf16[8,32,512]{2,1,0:T(8,128)(2,1)S(1)}, u32[]{:S(2)}, u32[]{:S(2)}) async-start(bf16[8,32,512]{2,1,0:T(8,128)(2,1)} %sum.1), calls=%async_computation.2 | async-start | bytes 524288 | tf_op jit(solution)/shard_map/all_to_all | solution.py:310
  108.5 6.2 %collective-permute-start.15 = (bf16[64,256]{1,0:T(8,128)(2,1)S(1)}, bf16[64,256]{1,0:T(8,128)(2,1)S(1)}, u32[]{:S(2)}, u32[]{:S(2)}) collective-permute-start(bf16[64,256]{1,0:T(8,128)(2,1)S(1)} %second_add.5.refs_0_), channel_id=1, source_target_pairs={{0,16},{8,24},{16,0},{24,8},{32,48},{40,56},{48,32},{56,40},{1,17}... | collective-permute-start | bytes 98312 | tf_op jit(solution)/shard_map/ppermute | solution.py:323
  114.8 7.0 %collective-permute-start.16 = (bf16[64,256]{1,0:T(8,128)(2,1)S(1)}, bf16[64,256]{1,0:T(8,128)(2,1)S(1)}, u32[]{:S(2)}, u32[]{:S(2)}) collective-permute-start(bf16[64,256]{1,0:T(8,128)(2,1)S(1)} %second_add.6.refs_0_), channel_id=1, source_target_pairs={{0,32},{8,40},{16,48},{24,56},{32,0},{40,8},{48,16},{56,24},{1,33}... | collective-permute-start | bytes 98312 | tf_op jit(solution)/shard_map/ppermute | solution.py:323

commit v5 on v4

--- a/solution.py
+++ b/solution.py
@@ -44,8 +44,8 @@
 
 
 def pick_body(
-    row_far, x_far, self_far, near_far, out_ref, weight_ref, row_ref, x_ref, self_ref, near_ref, sems,
-    slices,
+    row_far, x_far, self_far, near_far, out_ref, weight_ref, row_ref, x_ref, self_ref, near_ref,
+    picks_ref, sems, slices,
 ):
     copies = [
         pltpu.make_async_copy(far, ref, sems.at[at])
@@ -60,22 +60,22 @@
     copies[0].wait()
     copies[1].wait()
     step = 128
+    tall = 4 * step
     lane = lax.broadcasted_iota(I32, (step, step), 1)
 
     def fill(at, carry):
-        start = pl.multiple_of(at * step, step)
-        wanted = jnp.broadcast_to(row_ref[:, pl.ds(start, step)], (step, step)).T
-        picks = jnp.concatenate(
-            [
-                jnp.where(wanted == lane + low, 1.0, 0.0).astype(BF16)
-                for low in range(0, rows, step)
-            ],
-            axis=1,
-        )
-        out_ref[pl.ds(start, step), :] = dot(picks, x_ref[...]).astype(BF16)
+        for piece in range(tall // step):
+            start = pl.multiple_of(at * tall + piece * step, step)
+            wanted = jnp.broadcast_to(row_ref[:, pl.ds(start, step)], (step, step)).T
+            for low in range(0, rows, step):
+                picks_ref[pl.ds(start, step), low : low + step] = jnp.where(
+                    wanted == lane + low, 1.0, 0.0
+                ).astype(BF16)
+        span = pl.ds(pl.multiple_of(at * tall, tall), tall)
+        out_ref[span, :] = dot(picks_ref[span, :], x_ref[...]).astype(BF16)
         return carry
 
-    lax.fori_loop(0, out_ref.shape[0] // step, fill, 0, unroll=4)
+    lax.fori_loop(0, out_ref.shape[0] // tall, fill, 0, unroll=2)
     copies[2].wait()
     copies[3].wait()
     for at in range(slices):
@@ -130,7 +130,7 @@
 
 def slot_rows(x_ref, at):
     peers, _, per, cols = x_ref.shape
-    return x_ref[:, at].astype(F32).reshape(peers * per, cols).astype(BF16)
+    return x_ref[:, at].reshape(peers * per, cols)
 
 
 def project_body(place_ref, x_ref, *refs):
@@ -277,33 +277,44 @@
 
 def join_body(parts_ref, second_ref, out_ref):
     _, deep, cols = parts_ref.shape
-    total = jnp.sum(parts_ref[...].astype(F32), axis=0).astype(BF16)
-    for at in range(out_ref.shape[0]):
-        out_ref[at, :deep] = total
-        out_ref[at, deep:, : cols // 2] = second_ref[:deep, :]
-        out_ref[at, deep:, cols // 2 :] = second_ref[deep:, :]
-
-
-def finish_body(all_ref, self_ref, near_ref, second_self_ref, second_near_ref, cores, slices):
-    peers, deep, cols = all_ref.shape
-    deep = deep // 2
+    out_ref[:deep] = jnp.sum(parts_ref[...].astype(F32), axis=0).astype(BF16)
+    out_ref[deep:, : cols // 2] = second_ref[:deep, :]
+    out_ref[deep:, cols // 2 :] = second_ref[deep:, :]
+
+
+def pair_body(place_ref, mine_ref, other_ref, out_ref):
+    rows = mine_ref.shape[0]
+    first = place_ref[1] == 0
+    out_ref[:rows, :] = jnp.where(first, mine_ref[...], other_ref[...])
+    out_ref[rows:, :] = jnp.where(first, other_ref[...], mine_ref[...])
+
+
+def finish_body(place_ref, *refs, cores, slices):
+    parts, (self_ref, near_ref, second_self_ref, second_near_ref) = refs[:-4], refs[-4:]
+    count = len(parts)
+    cols = parts[0].shape[1]
+    deep = parts[0].shape[0] // (2 * cores)
     width = cols // slices
     half = width // 2
-    for at in range(peers):
-        core, x = at % cores, at // cores
-        start = core * (peers // cores) * deep + x * deep
-        value = all_ref[at].astype(F32)
-        for side, ref in enumerate((self_ref, near_ref)):
-            ref[start : start + deep, :] = jnp.concatenate(
-                [
-                    value[:deep, f * width + side * half : f * width + (side + 1) * half]
-                    for f in range(slices)
-                ],
-                axis=1,
-            )
-        ref = (second_self_ref, second_near_ref)[core]
-        ref[2 * x * deep : (2 * x + 1) * deep, :] = value[deep:, : cols // 2]
-        ref[(2 * x + 1) * deep : (2 * x + 2) * deep, :] = value[deep:, cols // 2 :]
+    for shift, part in enumerate(parts):
+        x = lax.rem(place_ref[2] + count - shift, count)
+        for core in range(cores):
+            low = 2 * core * deep
+            value = part[low : low + deep, :].astype(F32)
+            span = pl.ds(pl.multiple_of((core * count + x) * deep, deep), deep)
+            for side, ref in enumerate((self_ref, near_ref)):
+                ref[span, :] = jnp.concatenate(
+                    [
+                        value[:, f * width + side * half : f * width + (side + 1) * half]
+                        for f in range(slices)
+                    ],
+                    axis=1,
+                )
+            value = part[low + deep : low + 2 * deep, :].astype(F32)
+            ref = (second_self_ref, second_near_ref)[core]
+            for side in range(2):
+                span = pl.ds(pl.multiple_of((2 * x + side) * deep, deep), deep)
+                ref[span, :] = value[:, side * cols // 2 : (side + 1) * cols // 2]
 
 
 def exchange(value, axis):
@@ -363,7 +374,7 @@
         scratch=[
             pltpu.VMEM(send_rows.shape, I32), pltpu.VMEM(features.shape, BF16),
             pltpu.VMEM(first_self.shape, BF16), pltpu.VMEM(first_neighbor.shape, BF16),
-            pltpu.SemaphoreType.DMA((4,)),
+            pltpu.VMEM((slots, rows), BF16), pltpu.SemaphoreType.DMA((4,)),
         ],
     )
     routed = exchange(picked.reshape(peers * slices, per, slice_cols), AXES)
@@ -464,14 +475,18 @@
     for stride in strides[1:]:
         second = doubled(second, stride)
     (mixed,) = call(
-        join_body, [((count_x * cores, 2 * deep, 2 * hidden), BF16)], (mixed, second), "join",
+        join_body, [((2 * deep, 2 * hidden), BF16)], (mixed, second), "join",
         0, 64 * deep * hidden,
     )
-    mixed = exchange(mixed, ("x", "core"))
+    (mixed,) = call(
+        pair_body, [((4 * deep, 2 * hidden), BF16)],
+        (place, mixed, swapped(mixed, "core", cores, 1)), "pair", 0, 32 * deep * hidden, scalars=1,
+    )
     grad_first_self, grad_first_neighbor, grad_second_self, grad_second_neighbor = call(
         functools.partial(finish_body, cores=cores, slices=slices),
-        [((slice_cols, hidden), F32)] * 2 + [((hidden, out_cols), F32)] * 2, (mixed,), "finish",
-        0, 24 * slice_cols * hidden,
+        [((slice_cols, hidden), F32)] * 2 + [((hidden, out_cols), F32)] * 2,
+        (place, *shifted([mixed] * count_x, "x", count_x)), "finish",
+        0, 24 * slice_cols * hidden, scalars=1,
     )
     return (
         seed_embedding,

time: 141 us -> 142 us (level)
  blocking collectives: 16.1 us -> 0 us
  waiting for transfers between devices: 39.1 us -> 48.4 us
  starting transfers between devices: 49.7 us -> 56 us
  Pallas kernels: 29.7 us -> 32.1 us
    all_to_all x1 -> x0, blocking collectives: 16.1 us -> none  [exchange(): return lax.all_to_all(value, axis, split_axis=0, concat_axis=0, tiled=True)]
    ppermute x12 -> x15, waiting for transfers between devices: 15.4 us -> 23.8 us  [shifted(): lax.ppermute(piece, axis, [(at, (at + shift) % count) for at in range(cou...]
    ppermute x5 -> x6, starting transfers between devices: 10.1 us -> 13.8 us  [swapped(): return lax.ppermute(value, axis, [(at, at ^ step) for at in range(count)])]
    ppermute x12 -> x15, starting transfers between devices: 16.1 us -> 18.6 us  [shifted(): lax.ppermute(piece, axis, [(at, (at + shift) % count) for at in range(cou...]
    pallas_call x16 -> x17, Pallas kernels: 29.7 us -> 32.1 us  [call(): pl.pallas_call(body, out_shape=[jax.ShapeDtypeStruct(shape, dtype) for sh...]
    ppermute x5 -> x6, waiting for transfers between devices: 9.49 us -> 10.4 us  [swapped(): return lax.ppermute(value, axis, [(at, at ^ step) for at in range(count)])]
  transfers between devices with their start and end apart: 20 -> 24, of which waited for: 10 -> 14; matrix products, arithmetic and copies ran while one was open for 0% -> 0% of each run, Pallas kernels for 10% -> 10%
where the time goes in v5:
time: 142 us; the launch traced here: 141 us
  starting transfers between devices  56 us (39%)
  waiting for transfers between devices  48.4 us (34%)
  Pallas kernels  32.1 us (23%)
  local copies, waits for them, and re-layouts  3.12 us (2%)
    pallas_call x17, Pallas kernels, call(): pl.pallas_call(body, out_shape=[jax.ShapeDtypeStruct(shape, dtype) for sh...  32.1 us
    ppermute x15, waiting for transfers between devices, shifted(): lax.ppermute(piece, axis, [(at, (at + shift) % count) for at in range(cou...  23.8 us
    all_to_all x3, starting transfers between devices, exchange(): return lax.all_to_all(value, axis, split_axis=0, concat_axis=0, tiled=True)  23.6 us
    ppermute x15, starting transfers between devices, shifted(): lax.ppermute(piece, axis, [(at, (at + shift) % count) for at in range(cou...  18.6 us
    all_to_all x3, waiting for transfers between devices, exchange(): return lax.all_to_all(value, axis, split_axis=0, concat_axis=0, tiled=True)  14.2 us
    ppermute x6, starting transfers between devices, swapped(): return lax.ppermute(value, axis, [(at, at ^ step) for at in range(count)])  13.8 us
    ppermute x6, waiting for transfers between devices, swapped(): return lax.ppermute(value, axis, [(at, at ^ step) for at in range(count)])  10.4 us
  transfers between devices with their start and end apart: 24, of which 14 were waited for; matrix products, arithmetic and copies ran while one was open for 0% of the time, Pallas kernels for 10%

profile of v5, /device:TPU:1, one launch (start us, length us, event | category | flops | bytes accessed | tf_op | source)
XLA Modules:
  0.0 140.9 jit_solution(18180294014977916506)
XLA Ops:
  0.6 6.1 %pick.1 = (bf16[2048,256]{1,0:T(8,128)(2,1)}, bf16[256,512]{1,0:T(8,128)(2,1)S(1)}) custom-call(s32[1,2048]{1,0:T(1,128)} %row_far.1, bf16[1536,256]{1,0:T(8,128)(2,1)} %x_far.1, bf16[256,256]{1,0:T(8,128)(2,1)} %self_far.1, bf16[256,256]{1,0:T(8,128)(2,1)} %near_far.1), custom_call_target="tpu_custom_call" | custom-call | flops 1610612736 | bytes 6291456 | tf_op jit(solution)/shard_map/pick/pallas_call | solution.py:31
  6.8 15.7 %all-to-all-start = ((bf16[256,8,256]{2,1,0:T(8,128)(2,1)}), bf16[256,8,256]{2,1,0:T(8,128)(2,1)S(1)}, u32[]{:S(2)}, u32[]{:S(2)}) async-start(bf16[256,8,256]{2,1,0:T(8,128)(2,1)} %bitcast.10), calls=%async_computation | async-start | bytes 2097152 | tf_op jit(solution)/shard_map/all_to_all | solution.py:321
  22.5 2.7 %collective-permute-start.2 = (bf16[256,512]{1,0:T(8,128)(2,1)S(1)}, bf16[256,512]{1,0:T(8,128)(2,1)S(1)}, u32[]{:S(2)}, u32[]{:S(2)}) collective-permute-start(bf16[256,512]{1,0:T(8,128)(2,1)S(1)} %get-tuple-element.49.refs_0_), channel_id=1, source_target_pairs={{0,3},{1,0},{2,1},{3,2},{4,7},{5,4},{6,5},{7,6},{8,11},{9,8},{10,9... | collective-permute-start | bytes 786440 | tf_op jit(solution)/shard_map/ppermute | solution.py:328
  25.2 0.5 collective-permute-start.1
  25.8 0.6 collective-permute-start
  26.7 11.1 %count.1 = (bf16[2048,512]{1,0:T(8,128)(2,1)S(1)}, bf16[2048,512]{1,0:T(8,128)(2,1)S(1)}, bf16[512,128]{1,0:T(8,128)(2,1)S(1)}, bf16[512,128]{1,0:T(8,128)(2,1)S(1)}) custom-call(s32[1,512]{1,0:T(1,128)S(1)} %bitcast.22, s32[25,512]{1,0:T(8,128)S(1)} %bitcast.18, s32[1,512]{1,0:T(1,128)S(1)} %bitcast.19, s32[1,128]{1,0:T(1,128)S(1)} %bitcast.23, ...), custom_call_target="tpu_custom_call" | custom-call | bytes 16777216 | tf_op jit(solution)/shard_map/count/pallas_call | solution.py:31
  37.8 1.3 copy-done
  39.2 1.3 copy-done.1
  40.7 14.2 %all-to-all-done = bf16[256,8,256]{2,1,0:T(8,128)(2,1)S(1)} async-done(((bf16[256,8,256]{2,1,0:T(8,128)(2,1)}), bf16[256,8,256]{2,1,0:T(8,128)(2,1)S(1)}, u32[]{:S(2)}, u32[]{:S(2)}) %all-to-all-start) | async-done | bytes 1048608 | tf_op jit(solution)/shard_map/all_to_all | solution.py:321
  55.0 2.1 %project.1 = (bf16[512,128]{1,0:T(8,128)(2,1)S(1)}, bf16[512,128]{1,0:T(8,128)(2,1)}, bf16[512,128]{1,0:T(8,128)(2,1)}, bf16[512,128]{1,0:T(8,128)(2,1)}) custom-call(s32[3]{0:T(128)S(1)} %pad_add_fusion.place_ref, bf16[64,4,8,256]{3,2,1,0:T(8,128)(2,1)S(1)} %bitcast.14, bf16[256,512]{1,0:T(8,128)(2,1)S(1)} %get-tuple-element.49.refs_0_, ...), custom_call_target="tpu_custom_call" | custom-call | flops 536870912 | bytes 2097152 | tf_op jit(solution)/shard_map/project/pallas_call | solution.py:31
  57.3 1.0 collective-permute-start.4
  58.3 1.5 %collective-permute-start.5 = (bf16[512,128]{1,0:T(8,128)(2,1)}, bf16[512,128]{1,0:T(8,128)(2,1)S(1)}, u32[]{:S(2)}, u32[]{:S(2)}) collective-permute-start(bf16[512,128]{1,0:T(8,128)(2,1)} %get-tuple-element.53), channel_id=1, source_target_pairs={{0,3},{1,0},{2,1},{3,2},{4,7},{5,4},{6,5},{7,6},{8,11},{9,8},{10,9... | collective-permute-start | bytes 393224 | tf_op jit(solution)/shard_map/ppermute | solution.py:328
  59.9 6.0 %collective-permute-done.3.refs_1_ = bf16[512,128]{1,0:T(8,128)(2,1)S(1)} collective-permute-done((bf16[512,128]{1,0:T(8,128)(2,1)}, bf16[512,128]{1,0:T(8,128)(2,1)S(1)}, u32[]{:S(2)}, u32[]{:S(2)}) %collective-permute-start.3) | collective-permute-done | bytes 131104 | tf_op jit(solution)/shard_map/ppermute | solution.py:328
  66.0 5.0 %owner.1 = (bf16[640,128]{1,0:T(8,128)(2,1)S(1)}, bf16[640,128]{1,0:T(8,128)(2,1)S(1)}, bf16[640,128]{1,0:T(8,128)(2,1)S(1)}, bf16[640,128]{1,0:T(8,128)(2,1)S(1)}) custom-call(s32[3]{0:T(128)S(1)} %pad_add_fusion.place_ref, bf16[4,512,512]{2,1,0:T(8,128)(2,1)} %bitcast.16, bf16[4,512,512]{2,1,0:T(8,128)(2,1)} %bitcast.17, ...), custom_call_target="tpu_custom_call" | custom-call | flops 1073741824 | bytes 4194304 | tf_op jit(solution)/shard_map/owner/pallas_call | solution.py:31
  71.0 0.6 collective-permute-start.6
  71.6 3.8 %collective-permute-start.7 = (bf16[640,128]{1,0:T(8,128)(2,1)S(1)}, bf16[640,128]{1,0:T(8,128)(2,1)S(1)}, u32[]{:S(2)}, u32[]{:S(2)}) collective-permute-start(bf16[640,128]{1,0:T(8,128)(2,1)S(1)} %get-tuple-element.56), channel_id=1, source_target_pairs={{0,2},{1,3},{2,0},{3,1},{4,6},{5,7},{6,4},{7,5},{8,10},{9,11},{10,... | collective-permute-start | bytes 491528 | tf_op jit(solution)/shard_map/ppermute | solution.py:328
  75.7 1.2 collective-permute-done.6.refs_1_
  76.9 5.4 %collective-permute-done.7.refs_2_ = bf16[640,128]{1,0:T(8,128)(2,1)S(1)} collective-permute-done((bf16[640,128]{1,0:T(8,128)(2,1)S(1)}, bf16[640,128]{1,0:T(8,128)(2,1)S(1)}, u32[]{:S(2)}, u32[]{:S(2)}) %collective-permute-start.7) | collective-permute-done | bytes 163872 | tf_op jit(solution)/shard_map/ppermute | solution.py:328
  82.3 1.4 %weight.1 = (f32[4,128,512]{2,1,0:T(8,128)S(1)}, bf16[4,128,512]{2,1,0:T(8,128)(2,1)S(1)}) custom-call(s32[3]{0:T(128)S(1)} %pad_add_fusion.place_ref, bf16[1024,512]{1,0:T(8,128)(2,1)S(1)} %turn.1.xt_ref, bf16[640,128]{1,0:T(8,128)(2,1)S(1)} %get-tuple-element.54.refs_0_, bf16[640,128]{1,0:T(8,128)(2,1)S(1)} %collective-permute-done.6.refs_1_, ...), custom_call_target="tpu_custom_call" | custom-call | flops 536870912 | bytes 2097152 | tf_op jit(solution)/shard_map/weight/pallas_call | solution.py:31
  83.7 1.8 %collective-permute-start.9 = (bf16[4,128,512]{2,1,0:T(8,128)(2,1)S(1)}, bf16[4,128,512]{2,1,0:T(8,128)(2,1)S(1)}, u32[]{:S(2)}, u32[]{:S(2)}) collective-permute-start(bf16[4,128,512]{2,1,0:T(8,128)(2,1)S(1)} %get-tuple-element.60), channel_id=1, source_target_pairs={{0,4},{4,0},{1,5},{5,1},{2,6},{6,2},{3,7},{7,3},{8,12},{12,8},{9,1... | collective-permute-start | bytes 1572872 | tf_op jit(solution)/shard_map/ppermute | solution.py:334
  85.5 1.6 %seeds.1 = (bf16[128,256]{1,0:T(8,128)(2,1)}, f32[256,256]{1,0:T(8,128)S(1)}, bf16[256,256]{1,0:T(8,128)(2,1)S(1)}) custom-call(s32[3]{0:T(128)S(1)} %pad_add_fusion.place_ref, bf16[256,256]{1,0:T(8,128)(2,1)S(1)} %copy-done.2, bf16[256,256]{1,0:T(8,128)(2,1)S(1)} %copy-done.3, bf16[128,256]{1,0:T(8,128)(2,1)S(1)} %copy-done.4, ...), custom_call_target="tpu_custom_call" | custom-call | flops 67108864 | bytes 524288 | tf_op jit(solution)/shard_map/seeds/pallas_call | solution.py:31
  87.1 0.9 halves.1
  88.0 4.5 %all-to-all-start.1 = ((bf16[16,32,512]{2,1,0:T(8,128)(2,1)}), bf16[16,32,512]{2,1,0:T(8,128)(2,1)S(1)}, u32[]{:S(2)}, u32[]{:S(2)}) async-start(bf16[16,32,512]{2,1,0:T(8,128)(2,1)} %halves.1), calls=%async_computation.1 | async-start | bytes 1048576 | tf_op jit(solution)/shard_map/all_to_all | solution.py:321
  92.5 0.7 collective-permute-start.10
  93.2 1.0 collective-permute-done.10.got_ref
  94.2 0.6 second_split.1
  94.8 1.6 %collective-permute-start.11 = (bf16[64,256]{1,0:T(8,128)(2,1)S(1)}, bf16[64,256]{1,0:T(8,128)(2,1)S(1)}, u32[]{:S(2)}, u32[]{:S(2)}) collective-permute-start(bf16[64,256]{1,0:T(8,128)(2,1)S(1)} %get-tuple-element.66), channel_id=1, source_target_pairs={{0,64},{64,128},{128,192},{192,0},{1,65},{65,129},{129,193},{193,1... | collective-permute-start | bytes 98312 | tf_op jit(solution)/shard_map/ppermute | solution.py:328
  96.4 2.4 %collective-permute-start.12 = (bf16[64,256]{1,0:T(8,128)(2,1)S(1)}, bf16[64,256]{1,0:T(8,128)(2,1)S(1)}, u32[]{:S(2)}, u32[]{:S(2)}) collective-permute-start(bf16[64,256]{1,0:T(8,128)(2,1)S(1)} %get-tuple-element.67), channel_id=1, source_target_pairs={{0,128},{64,192},{128,0},{192,64},{1,129},{65,193},{129,1},{193,65... | collective-permute-start | bytes 98312 | tf_op jit(solution)/shard_map/ppermute | solution.py:328
  98.8 1.2 collective-permute-start.13
  100.0 0.8 collective-permute-done.11.refs_1_
  100.8 2.0 %collective-permute-done.12.refs_2_ = bf16[64,256]{1,0:T(8,128)(2,1)S(1)} collective-permute-done((bf16[64,256]{1,0:T(8,128)(2,1)S(1)}, bf16[64,256]{1,0:T(8,128)(2,1)S(1)}, u32[]{:S(2)}, u32[]{:S(2)}) %collective-permute-start.12) | collective-permute-done | bytes 32800 | tf_op jit(solution)/shard_map/ppermute | solution.py:328
  102.8 0.4 collective-permute-start.14
  103.2 2.4 %collective-permute-done.14.refs_1_ = bf16[64,256]{1,0:T(8,128)(2,1)S(1)} collective-permute-done((bf16[64,256]{1,0:T(8,128)(2,1)S(1)}, bf16[64,256]{1,0:T(8,128)(2,1)S(1)}, u32[]{:S(2)}, u32[]{:S(2)}) %collective-permute-start.14) | collective-permute-done | bytes 32800 | tf_op jit(solution)/shard_map/ppermute | solution.py:334
  105.7 0.8 sum.1
  106.4 3.4 %all-to-all-start.2 = ((bf16[8,32,512]{2,1,0:T(8,128)(2,1)}), bf16[8,32,512]{2,1,0:T(8,128)(2,1)S(1)}, u32[]{:S(2)}, u32[]{:S(2)}) async-start(bf16[8,32,512]{2,1,0:T(8,128)(2,1)} %sum.1), calls=%async_computation.2 | async-start | bytes 524288 | tf_op jit(solution)/shard_map/all_to_all | solution.py:321
  109.9 2.3 %collective-permute-start.15 = (bf16[64,256]{1,0:T(8,128)(2,1)S(1)}, bf16[64,256]{1,0:T(8,128)(2,1)S(1)}, u32[]{:S(2)}, u32[]{:S(2)}) collective-permute-start(bf16[64,256]{1,0:T(8,128)(2,1)S(1)} %second_add.5.refs_0_), channel_id=1, source_target_pairs={{0,16},{8,24},{16,0},{24,8},{32,48},{40,56},{48,32},{56,40},{1,17}... | collective-permute-start | bytes 98312 | tf_op jit(solution)/shard_map/ppermute | solution.py:334
  112.1 4.0 %collective-permute-done.15.refs_1_ = bf16[64,256]{1,0:T(8,128)(2,1)S(1)} collective-permute-done((bf16[64,256]{1,0:T(8,128)(2,1)S(1)}, bf16[64,256]{1,0:T(8,128)(2,1)S(1)}, u32[]{:S(2)}, u32[]{:S(2)}) %collective-permute-start.15) | collective-permute-done | bytes 32800 | tf_op jit(solution)/shard_map/ppermute | solution.py:334
  116.1 4.9 %collective-permute-start.16 = (bf16[64,256]{1,0:T(8,128)(2,1)S(1)}, bf16[64,256]{1,0:T(8,128)(2,1)S(1)}, u32[]{:S(2)}, u32[]{:S(2)}) collective-permute-start(bf16[64,256]{1,0:T(8,128)(2,1)S(1)} %second_add.6.refs_0_), channel_id=1, source_target_pairs={{0,32},{8,40},{16,48},{24,56},{32,0},{40,8},{48,16},{56,24},{1,33}... | collective-permute-start | bytes 98312 | tf_op jit(solution)/shard_map/ppermute | solution.py:334
  121.0 2.1 %collective-permute-done.16.refs_1_ = bf16[64,256]{1,0:T(8,128)(2,1)S(1)} collective-permute-done((bf16[64,256]{1,0:T(8,128)(2,1)S(1)}, bf16[64,256]{1,0:T(8,128)(2,1)S(1)}, u32[]{:S(2)}, u32[]{:S(2)}) %collective-permute-start.16) | collective-permute-done | bytes 32800 | tf_op jit(solution)/shard_map/ppermute | solution.py:334
  123.1 3.8 %collective-permute-start.17 = (bf16[64,512]{1,0:T(8,128)(2,1)S(1)}, bf16[64,512]{1,0:T(8,128)(2,1)S(1)}, u32[]{:S(2)}, u32[]{:S(2)}) collective-permute-start(bf16[64,512]{1,0:T(8,128)(2,1)S(1)} %join.1.mine_ref), channel_id=1, source_target_pairs={{0,4},{4,0},{1,5},{5,1},{2,6},{6,2},{3,7},{7,3},{8,12},{12,8},{9,1... | collective-permute-start | bytes 196616 | tf_op jit(solution)/shard_map/ppermute | solution.py:334
  126.9 0.9 collective-permute-done.17.other_ref
  127.8 0.6 pair.1.refs_0_
  128.4 1.8 %collective-permute-start.20 = (bf16[128,512]{1,0:T(8,128)(2,1)S(1)}, bf16[128,512]{1,0:T(8,128)(2,1)S(1)}, u32[]{:S(2)}, u32[]{:S(2)}) collective-permute-start(bf16[128,512]{1,0:T(8,128)(2,1)S(1)} %pair.1.refs_0_), channel_id=1, source_target_pairs={{0,192},{64,0},{128,64},{192,128},{1,193},{65,1},{129,65},{193,129... | collective-permute-start | bytes 393224 | tf_op jit(solution)/shard_map/ppermute | solution.py:328
  130.2 0.7 collective-permute-start.18
  130.9 2.3 %collective-permute-done.20.refs_3_ = bf16[128,512]{1,0:T(8,128)(2,1)S(1)} collective-permute-done((bf16[128,512]{1,0:T(8,128)(2,1)S(1)}, bf16[128,512]{1,0:T(8,128)(2,1)S(1)}, u32[]{:S(2)}, u32[]{:S(2)}) %collective-permute-start.20) | collective-permute-done | bytes 131104 | tf_op jit(solution)/shard_map/ppermute | solution.py:328
  133.2 3.0 %collective-permute-done.19.refs_2_ = bf16[128,512]{1,0:T(8,128)(2,1)S(1)} collective-permute-done((bf16[128,512]{1,0:T(8,128)(2,1)S(1)}, bf16[128,512]{1,0:T(8,128)(2,1)S(1)}, u32[]{:S(2)}, u32[]{:S(2)}) %collective-permute-start.19) | collective-permute-done | bytes 131104 | tf_op jit(solution)/shard_map/ppermute | solution.py:328
  136.2 3.1 %collective-permute-done.18.refs_1_ = bf16[128,512]{1,0:T(8,128)(2,1)S(1)} collective-permute-done((bf16[128,512]{1,0:T(8,128)(2,1)S(1)}, bf16[128,512]{1,0:T(8,128)(2,1)S(1)}, u32[]{:S(2)}, u32[]{:S(2)}) %collective-permute-start.18) | collective-permute-done | bytes 131104 | tf_op jit(solution)/shard_map/ppermute | solution.py:328
  139.3 1.6 %finish.1 = (f32[256,256]{1,0:T(8,128)}, f32[256,256]{1,0:T(8,128)}, f32[256,256]{1,0:T(8,128)}, f32[256,256]{1,0:T(8,128)}) custom-call(s32[3]{0:T(128)S(1)} %pad_add_fusion.place_ref, bf16[128,512]{1,0:T(8,128)(2,1)S(1)} %pair.1.refs_0_, bf16[128,512]{1,0:T(8,128)(2,1)S(1)} %collective-permute-done.18.refs_1_, ...), custom_call_target="tpu_custom_call" | custom-call | bytes 1572864 | tf_op jit(solution)/shard_map/finish/pallas_call | solution.py:31
  (49 shorter events, 1.4 us)
Async XLA Ops:
  6.7 19.7 %copy-start.11 = (s32[1,64]{1,0:T(1,128)S(1)}, s32[1,64]{1,0:T(1,128)}, u32[]{:S(2)}) copy-start(s32[1,64]{1,0:T(1,128)} %param.21) | copy-start | bytes 772
  6.7 20.0 %copy-start.5 = (s32[512,25]{0,1:T(8,128)S(1)}, s32[512,25]{0,1:T(8,128)}, u32[]{:S(2)}) copy-start(s32[512,25]{0,1:T(8,128)} %param.23) | copy-start | bytes 153604
  6.7 20.0 %copy-start.6 = (s32[512]{0:T(512)S(1)}, s32[512]{0:T(512)}, u32[]{:S(2)}) copy-start(s32[512]{0:T(512)} %param.24) | copy-start | bytes 6148
  6.7 20.0 %copy-start.7 = (s32[128,10]{0,1:T(8,128)S(1)}, s32[128,10]{0,1:T(8,128)}, u32[]{:S(2)}) copy-start(s32[128,10]{0,1:T(8,128)} %param.26) | copy-start | bytes 15364
  6.8 20.0 %copy-start.8 = (s32[512]{0:T(512)S(1)}, s32[512]{0:T(512)}, u32[]{:S(2)}) copy-start(s32[512]{0:T(512)} %param.22) | copy-start | bytes 6148
  6.8 20.0 %copy-start.9 = (s32[128]{0:T(128)S(1)}, s32[128]{0:T(128)}, u32[]{:S(2)}) copy-start(s32[128]{0:T(128)} %param.25) | copy-start | bytes 1540
  6.8 53.0 %copy-start.10 = (f32[256]{0:T(256)S(1)}, f32[256]{0:T(256)}, u32[]{:S(2)}) copy-start(f32[256]{0:T(256)} %param.17) | copy-start | bytes 3076
  6.8 59.2 %copy-start.2 = (bf16[256,256]{1,0:T(8,128)(2,1)S(1)}, bf16[256,256]{1,0:T(8,128)(2,1)}, u32[]{:S(2)}) copy-start(bf16[256,256]{1,0:T(8,128)(2,1)} %second_self_ref.3) | copy-start | bytes 393220
  6.8 59.2 %copy-start.3 = (bf16[256,256]{1,0:T(8,128)(2,1)S(1)}, bf16[256,256]{1,0:T(8,128)(2,1)}, u32[]{:S(2)}) copy-start(bf16[256,256]{1,0:T(8,128)(2,1)} %second_near_ref.3) | copy-start | bytes 393220
  6.8 59.2 %copy-start.4 = (bf16[128,256]{1,0:T(8,128)(2,1)S(1)}, bf16[128,256]{1,0:T(8,128)(2,1)}, u32[]{:S(2)}) copy-start(bf16[128,256]{1,0:T(8,128)(2,1)} %cotangent_ref.3) | copy-start | bytes 196612
  6.8 48.1 %all-to-all-start = ((bf16[256,8,256]{2,1,0:T(8,128)(2,1)}), bf16[256,8,256]{2,1,0:T(8,128)(2,1)S(1)}, u32[]{:S(2)}, u32[]{:S(2)}) async-start(bf16[256,8,256]{2,1,0:T(8,128)(2,1)} %bitcast.10), calls=%async_computation | async-start | bytes 2097152 | tf_op jit(solution)/shard_map/all_to_all | solution.py:321
  22.5 32.5 %collective-permute-start.2 = (bf16[256,512]{1,0:T(8,128)(2,1)S(1)}, bf16[256,512]{1,0:T(8,128)(2,1)S(1)}, u32[]{:S(2)}, u32[]{:S(2)}) collective-permute-start(bf16[256,512]{1,0:T(8,128)(2,1)S(1)} %get-tuple-element.49.refs_0_), channel_id=1, source_target_pairs={{0,3},{1,0},{2,1},{3,2},{4,7},{5,4},{6,5},{7,6},{8,11},{9,8},{10,9... | collective-permute-start | bytes 786440 | tf_op jit(solution)/shard_map/ppermute | solution.py:328
  25.2 29.7 %collective-permute-start.1 = (bf16[256,512]{1,0:T(8,128)(2,1)S(1)}, bf16[256,512]{1,0:T(8,128)(2,1)S(1)}, u32[]{:S(2)}, u32[]{:S(2)}) collective-permute-start(bf16[256,512]{1,0:T(8,128)(2,1)S(1)} %get-tuple-element.49.refs_0_), channel_id=1, source_target_pairs={{0,2},{1,3},{2,0},{3,1},{4,6},{5,7},{6,4},{7,5},{8,10},{9,11},{10,... | collective-permute-start | bytes 786440 | tf_op jit(solution)/shard_map/ppermute | solution.py:328
  25.8 29.2 %collective-permute-start = (bf16[256,512]{1,0:T(8,128)(2,1)S(1)}, bf16[256,512]{1,0:T(8,128)(2,1)S(1)}, u32[]{:S(2)}, u32[]{:S(2)}) collective-permute-start(bf16[256,512]{1,0:T(8,128)(2,1)S(1)} %get-tuple-element.49.refs_0_), channel_id=1, source_target_pairs={{0,1},{1,2},{2,3},{3,0},{4,5},{5,6},{6,7},{7,4},{8,9},{9,10},{10,1... | collective-permute-start | bytes 786440 | tf_op jit(solution)/shard_map/ppermute | solution.py:328
  37.8 1.3 copy-start
  39.2 1.3 copy-start.1
  57.1 8.8 %collective-permute-start.3 = (bf16[512,128]{1,0:T(8,128)(2,1)}, bf16[512,128]{1,0:T(8,128)(2,1)S(1)}, u32[]{:S(2)}, u32[]{:S(2)}) collective-permute-start(bf16[512,128]{1,0:T(8,128)(2,1)} %get-tuple-element.51), channel_id=1, source_target_pairs={{0,1},{1,2},{2,3},{3,0},{4,5},{5,6},{6,7},{7,4},{8,9},{9,10},{10,1... | collective-permute-start | bytes 393224 | tf_op jit(solution)/shard_map/ppermute | solution.py:328
  57.3 8.6 %collective-permute-start.4 = (bf16[512,128]{1,0:T(8,128)(2,1)}, bf16[512,128]{1,0:T(8,128)(2,1)S(1)}, u32[]{:S(2)}, u32[]{:S(2)}) collective-permute-start(bf16[512,128]{1,0:T(8,128)(2,1)} %get-tuple-element.52), channel_id=1, source_target_pairs={{0,2},{1,3},{2,0},{3,1},{4,6},{5,7},{6,4},{7,5},{8,10},{9,11},{10,... | collective-permute-start | bytes 393224 | tf_op jit(solution)/shard_map/ppermute | solution.py:328
  58.3 7.6 %collective-permute-start.5 = (bf16[512,128]{1,0:T(8,128)(2,1)}, bf16[512,128]{1,0:T(8,128)(2,1)S(1)}, u32[]{:S(2)}, u32[]{:S(2)}) collective-permute-start(bf16[512,128]{1,0:T(8,128)(2,1)} %get-tuple-element.53), channel_id=1, source_target_pairs={{0,3},{1,0},{2,1},{3,2},{4,7},{5,4},{6,5},{7,6},{8,11},{9,8},{10,9... | collective-permute-start | bytes 393224 | tf_op jit(solution)/shard_map/ppermute | solution.py:328
  71.0 5.9 %collective-permute-start.6 = (bf16[640,128]{1,0:T(8,128)(2,1)S(1)}, bf16[640,128]{1,0:T(8,128)(2,1)S(1)}, u32[]{:S(2)}, u32[]{:S(2)}) collective-permute-start(bf16[640,128]{1,0:T(8,128)(2,1)S(1)} %get-tuple-element.55), channel_id=1, source_target_pairs={{0,1},{1,2},{2,3},{3,0},{4,5},{5,6},{6,7},{7,4},{8,9},{9,10},{10,1... | collective-permute-start | bytes 491528 | tf_op jit(solution)/shard_map/ppermute | solution.py:328
  71.6 10.7 %collective-permute-start.7 = (bf16[640,128]{1,0:T(8,128)(2,1)S(1)}, bf16[640,128]{1,0:T(8,128)(2,1)S(1)}, u32[]{:S(2)}, u32[]{:S(2)}) collective-permute-start(bf16[640,128]{1,0:T(8,128)(2,1)S(1)} %get-tuple-element.56), channel_id=1, source_target_pairs={{0,2},{1,3},{2,0},{3,1},{4,6},{5,7},{6,4},{7,5},{8,10},{9,11},{10,... | collective-permute-start | bytes 491528 | tf_op jit(solution)/shard_map/ppermute | solution.py:328
  75.4 6.9 %collective-permute-start.8 = (bf16[640,128]{1,0:T(8,128)(2,1)S(1)}, bf16[640,128]{1,0:T(8,128)(2,1)S(1)}, u32[]{:S(2)}, u32[]{:S(2)}) collective-permute-start(bf16[640,128]{1,0:T(8,128)(2,1)S(1)} %get-tuple-element.57), channel_id=1, source_target_pairs={{0,3},{1,0},{2,1},{3,2},{4,7},{5,4},{6,5},{7,6},{8,11},{9,8},{10,9... | collective-permute-start | bytes 491528 | tf_op jit(solution)/shard_map/ppermute | solution.py:328
  83.7 3.4 %collective-permute-start.9 = (bf16[4,128,512]{2,1,0:T(8,128)(2,1)S(1)}, bf16[4,128,512]{2,1,0:T(8,128)(2,1)S(1)}, u32[]{:S(2)}, u32[]{:S(2)}) collective-permute-start(bf16[4,128,512]{2,1,0:T(8,128)(2,1)S(1)} %get-tuple-element.60), channel_id=1, source_target_pairs={{0,4},{4,0},{1,5},{5,1},{2,6},{6,2},{3,7},{7,3},{8,12},{12,8},{9,1... | collective-permute-start | bytes 1572872 | tf_op jit(solution)/shard_map/ppermute | solution.py:334
  88.0 17.6 %all-to-all-start.1 = ((bf16[16,32,512]{2,1,0:T(8,128)(2,1)}), bf16[16,32,512]{2,1,0:T(8,128)(2,1)S(1)}, u32[]{:S(2)}, u32[]{:S(2)}) async-start(bf16[16,32,512]{2,1,0:T(8,128)(2,1)} %halves.1), calls=%async_computation.1 | async-start | bytes 1048576 | tf_op jit(solution)/shard_map/all_to_all | solution.py:321
  92.5 1.7 %collective-permute-start.10 = (bf16[256,256]{1,0:T(8,128)(2,1)S(1)}, bf16[256,256]{1,0:T(8,128)(2,1)S(1)}, u32[]{:S(2)}, u32[]{:S(2)}) collective-permute-start(bf16[256,256]{1,0:T(8,128)(2,1)S(1)} %get-tuple-element.64), channel_id=1, source_target_pairs={{0,4},{4,0},{1,5},{5,1},{2,6},{6,2},{3,7},{7,3},{8,12},{12,8},{9,1... | collective-permute-start | bytes 393224 | tf_op jit(solution)/shard_map/ppermute | solution.py:334
  94.8 6.0 %collective-permute-start.11 = (bf16[64,256]{1,0:T(8,128)(2,1)S(1)}, bf16[64,256]{1,0:T(8,128)(2,1)S(1)}, u32[]{:S(2)}, u32[]{:S(2)}) collective-permute-start(bf16[64,256]{1,0:T(8,128)(2,1)S(1)} %get-tuple-element.66), channel_id=1, source_target_pairs={{0,64},{64,128},{128,192},{192,0},{1,65},{65,129},{129,193},{193,1... | collective-permute-start | bytes 98312 | tf_op jit(solution)/shard_map/ppermute | solution.py:328
  96.4 6.3 %collective-permute-start.12 = (bf16[64,256]{1,0:T(8,128)(2,1)S(1)}, bf16[64,256]{1,0:T(8,128)(2,1)S(1)}, u32[]{:S(2)}, u32[]{:S(2)}) collective-permute-start(bf16[64,256]{1,0:T(8,128)(2,1)S(1)} %get-tuple-element.67), channel_id=1, source_target_pairs={{0,128},{64,192},{128,0},{192,64},{1,129},{65,193},{129,1},{193,65... | collective-permute-start | bytes 98312 | tf_op jit(solution)/shard_map/ppermute | solution.py:328
  98.8 3.9 %collective-permute-start.13 = (bf16[64,256]{1,0:T(8,128)(2,1)S(1)}, bf16[64,256]{1,0:T(8,128)(2,1)S(1)}, u32[]{:S(2)}, u32[]{:S(2)}) collective-permute-start(bf16[64,256]{1,0:T(8,128)(2,1)S(1)} %get-tuple-element.68), channel_id=1, source_target_pairs={{0,192},{64,0},{128,64},{192,128},{1,193},{65,1},{129,65},{193,129... | collective-permute-start | bytes 98312 | tf_op jit(solution)/shard_map/ppermute | solution.py:328
  102.8 2.9 %collective-permute-start.14 = (bf16[64,256]{1,0:T(8,128)(2,1)S(1)}, bf16[64,256]{1,0:T(8,128)(2,1)S(1)}, u32[]{:S(2)}, u32[]{:S(2)}) collective-permute-start(bf16[64,256]{1,0:T(8,128)(2,1)S(1)} %second_add.4.refs_0_), channel_id=1, source_target_pairs={{0,8},{8,0},{16,24},{24,16},{32,40},{40,32},{48,56},{56,48},{1,9},... | collective-permute-start | bytes 98312 | tf_op jit(solution)/shard_map/ppermute | solution.py:334
  106.4 16.6 %all-to-all-start.2 = ((bf16[8,32,512]{2,1,0:T(8,128)(2,1)}), bf16[8,32,512]{2,1,0:T(8,128)(2,1)S(1)}, u32[]{:S(2)}, u32[]{:S(2)}) async-start(bf16[8,32,512]{2,1,0:T(8,128)(2,1)} %sum.1), calls=%async_computation.2 | async-start | bytes 524288 | tf_op jit(solution)/shard_map/all_to_all | solution.py:321
  109.9 6.2 %collective-permute-start.15 = (bf16[64,256]{1,0:T(8,128)(2,1)S(1)}, bf16[64,256]{1,0:T(8,128)(2,1)S(1)}, u32[]{:S(2)}, u32[]{:S(2)}) collective-permute-start(bf16[64,256]{1,0:T(8,128)(2,1)S(1)} %second_add.5.refs_0_), channel_id=1, source_target_pairs={{0,16},{8,24},{16,0},{24,8},{32,48},{40,56},{48,32},{56,40},{1,17}... | collective-permute-start | bytes 98312 | tf_op jit(solution)/shard_map/ppermute | solution.py:334
  116.1 7.0 %collective-permute-start.16 = (bf16[64,256]{1,0:T(8,128)(2,1)S(1)}, bf16[64,256]{1,0:T(8,128)(2,1)S(1)}, u32[]{:S(2)}, u32[]{:S(2)}) collective-permute-start(bf16[64,256]{1,0:T(8,128)(2,1)S(1)} %second_add.6.refs_0_), channel_id=1, source_target_pairs={{0,32},{8,40},{16,48},{24,56},{32,0},{40,8},{48,16},{56,24},{1,33}... | collective-permute-start | bytes 98312 | tf_op jit(solution)/shard_map/ppermute | solution.py:334
  123.1 4.7 %collective-permute-start.17 = (bf16[64,512]{1,0:T(8,128)(2,1)S(1)}, bf16[64,512]{1,0:T(8,128)(2,1)S(1)}, u32[]{:S(2)}, u32[]{:S(2)}) collective-permute-start(bf16[64,512]{1,0:T(8,128)(2,1)S(1)} %join.1.mine_ref), channel_id=1, source_target_pairs={{0,4},{4,0},{1,5},{5,1},{2,6},{6,2},{3,7},{7,3},{8,12},{12,8},{9,1... | collective-permute-start | bytes 196616 | tf_op jit(solution)/shard_map/ppermute | solution.py:334
  128.4 4.8 %collective-permute-start.20 = (bf16[128,512]{1,0:T(8,128)(2,1)S(1)}, bf16[128,512]{1,0:T(8,128)(2,1)S(1)}, u32[]{:S(2)}, u32[]{:S(2)}) collective-permute-start(bf16[128,512]{1,0:T(8,128)(2,1)S(1)} %pair.1.refs_0_), channel_id=1, source_target_pairs={{0,192},{64,0},{128,64},{192,128},{1,193},{65,1},{129,65},{193,129... | collective-permute-start | bytes 393224 | tf_op jit(solution)/shard_map/ppermute | solution.py:328
  130.2 6.0 %collective-permute-start.19 = (bf16[128,512]{1,0:T(8,128)(2,1)S(1)}, bf16[128,512]{1,0:T(8,128)(2,1)S(1)}, u32[]{:S(2)}, u32[]{:S(2)}) collective-permute-start(bf16[128,512]{1,0:T(8,128)(2,1)S(1)} %pair.1.refs_0_), channel_id=1, source_target_pairs={{0,128},{64,192},{128,0},{192,64},{1,129},{65,193},{129,1},{193,65... | collective-permute-start | bytes 393224 | tf_op jit(solution)/shard_map/ppermute | solution.py:328
  130.2 9.1 %collective-permute-start.18 = (bf16[128,512]{1,0:T(8,128)(2,1)S(1)}, bf16[128,512]{1,0:T(8,128)(2,1)S(1)}, u32[]{:S(2)}, u32[]{:S(2)}) collective-permute-start(bf16[128,512]{1,0:T(8,128)(2,1)S(1)} %pair.1.refs_0_), channel_id=1, source_target_pairs={{0,64},{64,128},{128,192},{192,0},{1,65},{65,129},{129,193},{193,1... | collective-permute-start | bytes 393224 | tf_op jit(solution)/shard_map/ppermute | solution.py:328

commit v6 on v2

v6 whole, which is shorter than its diff:
```python
import functools

import jax
import jax.numpy as jnp
from jax import lax
from jax.experimental import pallas as pl
from jax.experimental.pallas import tpu as pltpu
from jax.sharding import PartitionSpec as P

BF16 = jnp.bfloat16
F32 = jnp.float32
I32 = jnp.int32


def dot(left, right, left_dim=1, right_dim=0):
    return lax.dot_general(
        left, right, (((left_dim,), (right_dim,)), ((), ())), preferred_element_type=F32
    )


def call(body, outs, args, name, flops=0, moved=0, vmem=16, scratch=(), scalars=0, far=()):
    specs = [
        pl.BlockSpec(
            memory_space=pltpu.SMEM if at < scalars else pltpu.HBM if at in far else pltpu.VMEM
        )
        for at in range(len(args))
    ]
    out_specs = [pl.BlockSpec(memory_space=pltpu.VMEM) for _ in outs]
    return pl.pallas_call(
        body,
        out_shape=[jax.ShapeDtypeStruct(shape, dtype) for shape, dtype in outs],
        in_specs=specs,
        out_specs=out_specs,
        scratch_shapes=scratch,
        name=name,
        compiler_params=pltpu.CompilerParams(vmem_limit_bytes=vmem << 20),
        cost_estimate=pl.CostEstimate(flops=flops, bytes_accessed=moved, transcendentals=0),
    )(*[
        pltpu.with_memory_space_constraint(arg, pltpu.HBM) if at in far else arg
        for at, arg in enumerate(args)
    ])


def pick_body(row_far, x_far, out_ref, row_ref, x_ref, sems):
    copies = [
        pltpu.make_async_copy(row_far, row_ref, sems.at[0]),
        pltpu.make_async_copy(x_far, x_ref, sems.at[1]),
    ]
    for copy in copies:
        copy.start()
    for copy in copies:
        copy.wait()
    rows = x_ref.shape[0]
    step = 128
    lane = lax.broadcasted_iota(I32, (step, step), 1)

    def fill(at, carry):
        start = pl.multiple_of(at * step, step)
        wanted = jnp.broadcast_to(row_ref[:, pl.ds(start, step)], (step, step)).T
        picks = jnp.concatenate(
            [
                jnp.where(wanted == lane + low, 1.0, 0.0).astype(BF16)
                for low in range(0, rows, step)
            ],
            axis=1,
        )
        out_ref[pl.ds(start, step), :] = dot(picks, x_ref[...]).astype(BF16)
        return carry

    lax.fori_loop(0, out_ref.shape[0] // step, fill, 0, unroll=4)


def count_body(
    self_ref, near_ref, degree_ref, mask_ref, seed_ref, seed_near_ref,
    self_table, near_table, seed_table, seed_near_table, live_ref,
):
    slots, mids = near_table.shape
    fan = near_ref.shape[0]
    step = 32
    live = lax.broadcasted_iota(I32, (fan, mids), 0) < degree_ref[...]
    live_ref[...] = jnp.where(live, near_ref[...], -1)
    own = self_ref[...]

    def fill(at, carry):
        span = pl.ds(pl.multiple_of(at * step, step), step)
        line = lax.broadcasted_iota(I32, (step, mids), 0) + at * step
        total = jnp.zeros((step, mids), F32)
        for j in range(fan):
            total = total + jnp.where(live_ref[j : j + 1, :] == line, 1.0, 0.0)
        filled = mask_ref[span, :].astype(F32)
        filled = jnp.concatenate([filled] * (mids // filled.shape[1]), axis=1)
        near_table[span, :] = (total * filled).astype(BF16)
        self_table[span, :] = jnp.where(own == line, filled, 0.0).astype(BF16)
        return carry

    lax.fori_loop(0, slots // step, fill, 0)
    seeds = seed_table.shape[1]
    line = lax.broadcasted_iota(I32, (mids, seeds), 0)
    seed_table[...] = jnp.where(seed_ref[...] == line, 1.0, 0.0).astype(BF16)
    total = jnp.zeros((mids, seeds), F32)
    for j in range(seed_near_ref.shape[0]):
        total = total + jnp.where(seed_near_ref[j : j + 1, :] == line, 1.0, 0.0)
    seed_near_table[...] = total.astype(BF16)


def gather_body(
    place_ref, x_ref, self_far, near_far, degree_ref, weight_self_ref, weight_near_ref, *refs, slices
):
    own_ref, near_ref = refs[:2]
    out_refs = refs[2 : 2 + slices]
    self_table, near_table, held_ref, sems = refs[2 + slices :]
    pieces, step, _ = self_table.shape
    copies = []
    for piece in range(pieces):
        for side, (far, ref) in enumerate(((self_far, self_table), (near_far, near_table))):
            copy = pltpu.make_async_copy(far.at[piece], ref.at[piece], sems.at[side, piece])
            copy.start()
            copies.append(copy)
    own, near = 0.0, 0.0
    for piece in range(pieces):
        turned = x_ref[pl.ds(piece * step, step), :].T
        copies[2 * piece].wait()
        own = own + dot(turned, self_table[piece])
        copies[2 * piece + 1].wait()
        near = near + dot(turned, near_table[piece])
    own = own.astype(BF16)
    near = (near / degree_ref[...].astype(F32)).astype(BF16)
    own_ref[...] = own
    near_ref[...] = near
    pre = dot(weight_self_ref[...], own, 0, 0) + dot(weight_near_ref[...], near, 0, 0)
    half = held_ref.shape[1]
    for at in range(slices):
        held_ref[at] = pre[at * half : (at + 1) * half].astype(BF16)
    for shift, out_ref in enumerate(out_refs):
        out_ref[...] = held_ref[lax.rem(place_ref[0] + shift, slices)]


def owner_body(
    place_ref, bias_ref, seed_table, seed_near_table, second_self_ref, second_near_ref,
    cotangent_ref, *refs, fan_two
):
    pre_refs, out_ref = refs[:-1], refs[-1]
    half = pre_refs[0].shape[0]
    mine = pl.ds(pl.multiple_of(place_ref[0] * half, half), half)
    back_self = dot(second_self_ref[mine, :], cotangent_ref[...], 1, 1)
    back_near = dot(second_near_ref[mine, :], cotangent_ref[...], 1, 1) / fan_two

    def spread(back, picks):
        high = back.astype(BF16)
        low = (back - high.astype(F32)).astype(BF16)
        both = dot(jnp.concatenate([high, low], axis=0), picks, 1, 1)
        return both[:half] + both[half:]

    grad_active = spread(back_self, seed_table[...]) + spread(back_near, seed_near_table[...])
    pre = bias_ref[mine, :]
    for pre_ref in pre_refs:
        pre = pre + pre_ref[...].astype(F32)
    sigma = 1.0 / (1.0 + jnp.exp(-pre))
    active = (pre * sigma).astype(BF16)
    slope = (sigma * (1.0 + pre * (1.0 - sigma))).astype(BF16).astype(F32)
    out_ref[:half, :] = (grad_active * slope).astype(BF16)
    own_seeds = dot(active, seed_table[...]).astype(BF16)
    mean_seeds = (dot(active, seed_near_table[...]) / fan_two).astype(BF16)
    seeds = jnp.concatenate([own_seeds, mean_seeds], axis=0)
    width = seeds.shape[1]
    tall = out_ref.shape[0] - half
    for at in range(seeds.shape[0] // tall):
        out_ref[half:, at * width : (at + 1) * width] = seeds[at * tall : (at + 1) * tall]


def unpacked_seeds(ref, half, width):
    return jnp.concatenate(
        [ref[half:, at : at + width] for at in range(0, ref.shape[1], width)], axis=0
    )


def weight_body(place_ref, own_ref, near_ref, cotangent_ref, *refs, half):
    grads_refs, (out_ref, held_ref) = refs[:-2], refs[-2:]
    slices = len(grads_refs)
    tiles = out_ref.shape[0] // 2
    lines = out_ref.shape[1] // 2
    per = half // lines
    cotangent = cotangent_ref[...]
    for shift, grads_ref in enumerate(grads_refs):
        at = lax.rem(place_ref[0] + slices - shift, slices)
        held_ref[pl.ds(pl.multiple_of(at * half, half), half), :] = grads_ref[:half, :]
        second = dot(unpacked_seeds(grads_ref, half, cotangent.shape[0]), cotangent)
        for side in range(2):
            part = second[side * half : (side + 1) * half].reshape(per, lines, second.shape[1])
            out_ref[pl.ds(side * tiles + at * per, per), lines:] = part.astype(BF16)
    grads = held_ref[...]
    for side, ref in enumerate((own_ref, near_ref)):
        part = dot(ref[...], grads, 1, 1)
        part = part.reshape(tiles, lines, part.shape[1])
        out_ref[pl.ds(side * tiles, tiles), :lines] = part.astype(BF16)


def embed_body(place_ref, second_self_ref, second_near_ref, *refs, half):
    grads_refs, out_ref = refs[:-1], refs[-1]
    slices = len(grads_refs)
    total = jnp.zeros(out_ref.shape, F32)
    for shift, grads_ref in enumerate(grads_refs):
        at = lax.rem(place_ref[0] + slices - shift, slices)
        rows = pl.ds(pl.multiple_of(at * half, half), half)
        seeds = unpacked_seeds(grads_ref, half, out_ref.shape[0])
        total = total + dot(seeds[:half], second_self_ref[rows, :], 0, 0)
        total = total + dot(seeds[half:], second_near_ref[rows, :], 0, 0)
    out_ref[...] = total.astype(BF16)


def sum_body(parts_ref, out_ref):
    total = jnp.sum(parts_ref[...].astype(F32), axis=0).astype(BF16)
    for at in range(out_ref.shape[0]):
        out_ref[at] = total


def finish_body(all_ref, first_self_ref, first_near_ref, second_self_ref, second_near_ref):
    peers, tall, width = all_ref.shape
    lines = tall // 2
    tiles = peers // 2
    value = all_ref[...].astype(F32)
    first_self_ref[...] = value[:tiles, :lines].reshape(tiles * lines, width)
    first_near_ref[...] = value[tiles:, :lines].reshape(tiles * lines, width)
    second_self_ref[...] = value[:tiles, lines:].reshape(tiles * lines, width)
    second_near_ref[...] = value[tiles:, lines:].reshape(tiles * lines, width)


def exchange(value, axis):
    return lax.all_to_all(value, axis, split_axis=0, concat_axis=0, tiled=True)


def shifted(pieces, axis, count):
    return [
        piece
        if shift == 0
        else lax.ppermute(piece, axis, [(at, (at + shift) % count) for at in range(count)])
        for shift, piece in enumerate(pieces)
    ]


def per_device(
    features,
    first_self,
    first_neighbor,
    first_bias,
    second_self,
    second_neighbor,
    send_rows,
    arrive_count,
    self_slot,
    neighbor_slot,
    degree,
    seed_self,
    seed_neighbor,
    cotangent,
):
    peers = lax.axis_size("dom")
    slices = lax.axis_size("feat")
    rows, slice_cols = features.shape
    hidden = first_self.shape[1]
    half = hidden // slices
    slots = send_rows.shape[1]
    capacity = slots // peers
    mids, fan = neighbor_slot.shape
    seeds, fan_two = seed_neighbor.shape
    out_cols = second_self.shape[1]
    lines = 2 * hidden // peers
    pieces = 4
    place = lax.axis_index("feat").astype(I32).reshape(1)

    (picked,) = call(
        pick_body, [((slots, slice_cols), BF16)], (send_rows, features), "pick",
        2 * slots * rows * slice_cols, 2 * slots * rows, far=(0, 1),
        scratch=[
            pltpu.VMEM(send_rows.shape, I32), pltpu.VMEM(features.shape, BF16),
            pltpu.SemaphoreType.DMA((2,)),
        ],
    )
    routed = exchange(picked.reshape(peers, capacity, slice_cols), "dom").reshape(slots, slice_cols)

    slot_at = lax.broadcasted_iota(I32, (peers, capacity, 128), 1)
    mask = (slot_at < arrive_count.reshape(peers, 1, 1)).astype(BF16).reshape(slots, 128)
    self_table, near_table, seed_table, seed_near_table = call(
        count_body,
        [((slots, mids), BF16), ((slots, mids), BF16), ((mids, seeds), BF16), ((mids, seeds), BF16)],
        (
            self_slot.reshape(1, mids), neighbor_slot.T, degree.reshape(1, mids), mask,
            seed_self.reshape(1, seeds), seed_neighbor.T,
        ),
        "count", 0, 16 * slots * mids, scratch=[pltpu.VMEM((fan, mids), I32)],
    )
    bias = first_bias.reshape(hidden, 1)
    routed, seed_table, bias = lax.optimization_barrier((routed, seed_table, bias))

    own_rows, near_rows, *pre = call(
        functools.partial(gather_body, slices=slices),
        [((slice_cols, mids), BF16)] * 2 + [((half, mids), BF16)] * slices,
        (
            place, routed, self_table.reshape(pieces, slots // pieces, mids),
            near_table.reshape(pieces, slots // pieces, mids), degree.reshape(1, mids),
            first_self, first_neighbor,
        ),
        "gather", 4 * slots * slice_cols * mids, 4 * slots * mids, scalars=1, far=(2, 3),
        scratch=[
            pltpu.VMEM((pieces, slots // pieces, mids), BF16),
            pltpu.VMEM((pieces, slots // pieces, mids), BF16),
            pltpu.VMEM((slices, half, mids), BF16), pltpu.SemaphoreType.DMA((2, pieces)),
        ],
    )
    pre = shifted(pre, "feat", slices)
    tall = 2 * half * seeds // mids
    (grads,) = call(
        functools.partial(owner_body, fan_two=fan_two), [((half + tall, mids), BF16)],
        (
            place, bias, seed_table, seed_near_table, second_self, second_neighbor, cotangent, *pre,
        ),
        "owner", 16 * half * seeds * mids, 8 * half * mids, scalars=1,
    )
    grads = shifted([grads] * slices, "feat", slices)
    (merged,) = call(
        functools.partial(weight_body, half=half), [((peers, 2 * lines, hidden), BF16)],
        (place, own_rows, near_rows, cotangent, *grads), "weight",
        4 * slice_cols * mids * hidden, 8 * slice_cols * mids,
        scratch=[pltpu.VMEM((hidden, mids), BF16)], scalars=1,
    )
    merged = exchange(merged, "dom")
    (seed_embedding,) = call(
        functools.partial(embed_body, half=half), [((seeds, out_cols), BF16)],
        (place, second_self, second_neighbor, *grads), "embed",
        4 * seeds * hidden * out_cols, 8 * seeds * hidden, scalars=1,
    )
    (summed,) = call(
        sum_body, [((peers, 2 * lines, hidden), BF16)], (merged,), "sum",
        0, 8 * peers * lines * hidden,
    )
    summed = exchange(summed, "dom")
    grad_first_self, grad_first_neighbor, grad_second_self, grad_second_neighbor = call(
        finish_body, [((slice_cols, hidden), F32)] * 2 + [((hidden, out_cols), F32)] * 2,
        (summed,), "finish", 0, 8 * peers * lines * hidden,
    )
    return (
        seed_embedding,
        grad_first_self,
        grad_first_neighbor,
        grad_second_self,
        grad_second_neighbor,
    )


def solution(mesh):
    in_specs = (
        P("dom", "feat"),
        P("feat", None),
        P("feat", None),
        P(),
        P(),
        P(),
        P("dom", None),
        P("dom", None),
        P("dom"),
        P("dom", None),
        P("dom"),
        P("dom"),
        P("dom", None),
        P("dom", None),
    )
    out_specs = (P("dom", None), P("feat", None), P("feat", None), P(), P())
    return jax.shard_map(
        per_device, mesh=mesh, in_specs=in_specs, out_specs=out_specs, check_vma=False
    )
```

time: 159 us -> 119 us (0.75)
  blocking collectives: 49.3 us -> 26.2 us
  starting transfers between devices: 36.2 us -> 27.4 us
  local copies, waits for them, and re-layouts: 10.1 us -> 3.25 us
    all_to_all x2 -> x1, blocking collectives: 49.3 us -> 26.2 us  [exchange(): return lax.all_to_all(value, axis, split_axis=0, concat_axis=0, tiled=True)]
    unnamed x36 -> x28, local copies, waits for them, and re-layouts: 9.51 us -> 2.69 us
    all_to_all x4 -> x2, starting transfers between devices: 26.1 us -> 19.4 us  [exchange(): return lax.all_to_all(value, axis, split_axis=0, concat_axis=0, tiled=True)]
    ppermute x6, starting transfers between devices: 10 us -> 7.94 us  [shifted(): lax.ppermute(piece, axis, [(at, (at + shift) % count) for at in range(cou...]
    all_to_all x4 -> x2, waiting for transfers between devices: 29.2 us -> 30.5 us  [exchange(): return lax.all_to_all(value, axis, split_axis=0, concat_axis=0, tiled=True)]
    pallas_call x10 -> x8, Pallas kernels: 23.9 us -> 23.1 us  [call(): pl.pallas_call(body, out_shape=[jax.ShapeDtypeStruct(shape, dtype) for sh...]
  transfers between devices with their start and end apart: 10 -> 8, of which waited for: 5 -> 6; matrix products, arithmetic and copies ran while one was open for 0% -> 1% of each run, Pallas kernels for 8% -> 10%
where the time goes in v6:
time: 119 us
  waiting for transfers between devices  37.8 us (32%)
  starting transfers between devices  27.4 us (23%)
  blocking collectives  26.2 us (22%)
  Pallas kernels  23.1 us (19%)
  local copies, waits for them, and re-layouts  3.25 us (3%)
    all_to_all x2, waiting for transfers between devices, exchange(): return lax.all_to_all(value, axis, split_axis=0, concat_axis=0, tiled=True)  30.5 us
    all_to_all x1, blocking collectives, exchange(): return lax.all_to_all(value, axis, split_axis=0, concat_axis=0, tiled=True)  26.2 us
    pallas_call x8, Pallas kernels, call(): pl.pallas_call(body, out_shape=[jax.ShapeDtypeStruct(shape, dtype) for sh...  23.1 us
    all_to_all x2, starting transfers between devices, exchange(): return lax.all_to_all(value, axis, split_axis=0, concat_axis=0, tiled=True)  19.4 us
    ppermute x6, starting transfers between devices, shifted(): lax.ppermute(piece, axis, [(at, (at + shift) % count) for at in range(cou...  7.94 us
    ppermute x6, waiting for transfers between devices, shifted(): lax.ppermute(piece, axis, [(at, (at + shift) % count) for at in range(cou...  7.34 us
    unnamed x28, local copies, waits for them, and re-layouts  2.69 us
  transfers between devices with their start and end apart: 8, of which 6 were waited for; matrix products, arithmetic and copies ran while one was open for 1% of the time, Pallas kernels for 10%

profile of v6, /device:TPU:1, one launch (start us, length us, event | category | flops | bytes accessed | tf_op | source)
XLA Modules:
  0.0 118.7 jit_solution(17849498113764467590)
XLA Ops:
  0.6 4.7 %pick.1 = bf16[2048,256]{1,0:T(8,128)(2,1)} custom-call(s32[1,2048]{1,0:T(1,128)} %row_far.1, bf16[1536,256]{1,0:T(8,128)(2,1)} %x_far.1), custom_call_target="tpu_custom_call" | custom-call | flops 1610612736 | bytes 6291456 | tf_op jit(solution)/shard_map/pick/pallas_call | solution.py:29
  5.4 0.0 copy-start.13
  5.4 0.0 copy-start.7
  5.4 0.0 copy-start.8
  5.4 0.0 copy-start.9
  5.4 0.0 copy-start.10
  5.4 0.0 copy-start.11
  5.4 0.0 copy-start.5
  5.4 0.0 copy-start.6
  5.5 13.1 %all-to-all-start = ((bf16[64,32,256]{2,1,0:T(8,128)(2,1)}), bf16[64,32,256]{2,1,0:T(8,128)(2,1)S(1)}, u32[]{:S(2)}, u32[]{:S(2)}) async-start(bf16[64,32,256]{2,1,0:T(8,128)(2,1)} %bitcast.1), calls=%async_computation | async-start | bytes 2097152 | tf_op jit(solution)/shard_map/all_to_all | solution.py:229
  18.6 0.0 copy-done.13
  18.6 0.1 fusion
  18.7 0.1 reshape.55
  18.8 0.3 iota.10.mask_ref
  19.1 0.0 copy-done.7
  19.1 0.0 copy-done.8
  19.2 0.0 copy-done.9
  19.2 0.0 copy-done.10
  19.2 11.2 %count.1 = (bf16[2048,512]{1,0:T(8,128)(2,1)S(1)}, bf16[2048,512]{1,0:T(8,128)(2,1)S(1)}, bf16[512,128]{1,0:T(8,128)(2,1)S(1)}, bf16[512,128]{1,0:T(8,128)(2,1)S(1)}) custom-call(s32[1,512]{1,0:T(1,128)S(1)} %bitcast.19, s32[25,512]{1,0:T(8,128)S(1)} %bitcast.15, s32[1,512]{1,0:T(1,128)S(1)} %bitcast.17, bf16[2048,128]{1,0:T(8,128)(2,1)S(1)} %iota.10.mask_ref, ...), custom_call_target="tpu_custom_call" | custom-call | bytes 16777216 | tf_op jit(solution)/shard_map/count/pallas_call | solution.py:29
  30.4 1.3 %copy-done = bf16[2048,512]{1,0:T(8,128)(2,1)} copy-done((bf16[2048,512]{1,0:T(8,128)(2,1)}, bf16[2048,512]{1,0:T(8,128)(2,1)S(1)}, u32[]{:S(2)}) %copy-start) | copy-done | bytes 2097176
  31.7 1.3 %copy-done.1 = bf16[2048,512]{1,0:T(8,128)(2,1)} copy-done((bf16[2048,512]{1,0:T(8,128)(2,1)}, bf16[2048,512]{1,0:T(8,128)(2,1)S(1)}, u32[]{:S(2)}) %copy-start.1) | copy-done | bytes 2097176
  33.0 14.1 %all-to-all-done = bf16[64,32,256]{2,1,0:T(8,128)(2,1)S(1)} async-done(((bf16[64,32,256]{2,1,0:T(8,128)(2,1)}), bf16[64,32,256]{2,1,0:T(8,128)(2,1)S(1)}, u32[]{:S(2)}, u32[]{:S(2)}) %all-to-all-start) | async-done | bytes 1048608 | tf_op jit(solution)/shard_map/all_to_all | solution.py:229
  47.2 0.0 copy-start.3
  47.2 0.0 copy-start.4
  47.2 3.5 %gather.1 = (bf16[256,512]{1,0:T(8,128)(2,1)S(1)}, bf16[256,512]{1,0:T(8,128)(2,1)S(1)}, bf16[64,512]{1,0:T(8,128)(2,1)S(1)}, bf16[64,512]{1,0:T(8,128)(2,1)S(1)...) custom-call(s32[1]{0:T(128)} %bitcast.place_ref, bf16[2048,256]{1,0:T(8,128)(2,1)S(1)} %bitcast.12, ...), custom_call_target="tpu_custom_call" | custom-call | flops 1073741824 | bytes 4194304 | tf_op jit(solution)/shard_map/gather/pallas_call | solution.py:29
  50.7 1.4 %collective-permute-start = (bf16[64,512]{1,0:T(8,128)(2,1)S(1)}, bf16[64,512]{1,0:T(8,128)(2,1)S(1)}, u32[]{:S(2)}, u32[]{:S(2)}) collective-permute-start(bf16[64,512]{1,0:T(8,128)(2,1)S(1)} %get-tuple-element.30), channel_id=1, source_target_pairs={{0,1},{1,2},{2,3},{3,0},{4,5},{5,6},{6,7},{7,4},{8,9},{9,10},{10,1... | collective-permute-start | bytes 196616 | tf_op jit(solution)/shard_map/ppermute | solution.py:236
  52.1 2.6 %collective-permute-start.1 = (bf16[64,512]{1,0:T(8,128)(2,1)S(1)}, bf16[64,512]{1,0:T(8,128)(2,1)S(1)}, u32[]{:S(2)}, u32[]{:S(2)}) collective-permute-start(bf16[64,512]{1,0:T(8,128)(2,1)S(1)} %get-tuple-element.31), channel_id=1, source_target_pairs={{0,2},{1,3},{2,0},{3,1},{4,6},{5,7},{6,4},{7,5},{8,10},{9,11},{10,... | collective-permute-start | bytes 196616 | tf_op jit(solution)/shard_map/ppermute | solution.py:236
  54.7 1.1 collective-permute-start.2
  55.7 0.0 copy-done.12
  55.7 0.1 copy.19.bias_ref
  55.9 0.0 collective-permute-done.refs_1_
  55.9 2.4 %collective-permute-done.1.refs_2_ = bf16[64,512]{1,0:T(8,128)(2,1)S(1)} collective-permute-done((bf16[64,512]{1,0:T(8,128)(2,1)S(1)}, bf16[64,512]{1,0:T(8,128)(2,1)S(1)}, u32[]{:S(2)}, u32[]{:S(2)}) %collective-permute-start.1) | collective-permute-done | bytes 65568 | tf_op jit(solution)/shard_map/ppermute | solution.py:236
  58.3 0.0 collective-permute-done.2.refs_3_
  58.3 0.0 copy-done.2
  58.3 0.4 owner.1.refs_0_
  58.7 1.9 %collective-permute-start.5 = (bf16[96,512]{1,0:T(8,128)(2,1)S(1)}, bf16[96,512]{1,0:T(8,128)(2,1)S(1)}, u32[]{:S(2)}, u32[]{:S(2)}) collective-permute-start(bf16[96,512]{1,0:T(8,128)(2,1)S(1)} %owner.1.refs_0_), channel_id=1, source_target_pairs={{0,3},{1,0},{2,1},{3,2},{4,7},{5,4},{6,5},{7,6},{8,11},{9,8},{10,9... | collective-permute-start | bytes 294920 | tf_op jit(solution)/shard_map/ppermute | solution.py:236
  60.6 0.2 collective-permute-start.4
  60.8 0.8 collective-permute-start.3
  61.5 1.1 collective-permute-done.5.refs_3_
  62.7 2.9 %collective-permute-done.4.refs_2_ = bf16[96,512]{1,0:T(8,128)(2,1)S(1)} collective-permute-done((bf16[96,512]{1,0:T(8,128)(2,1)S(1)}, bf16[96,512]{1,0:T(8,128)(2,1)S(1)}, u32[]{:S(2)}, u32[]{:S(2)}) %collective-permute-start.4) | collective-permute-done | bytes 98336 | tf_op jit(solution)/shard_map/ppermute | solution.py:236
  65.6 0.9 collective-permute-done.3.refs_1_
  66.5 0.4 weight.1
  66.9 26.2 %all_to_all.15.parts_ref = bf16[64,16,256]{2,1,0:T(8,128)(2,1)S(1)} all-to-all(bf16[64,16,256]{2,1,0:T(8,128)(2,1)S(1)} %weight.1), channel_id=1, replica_groups=mesh['dom'=64,'feat'=4] {'dom'}, dimensions={0} | all-to-all | bytes 1048576 | tf_op jit(solution)/shard_map/all_to_all | solution.py:229
  93.2 0.9 sum.1
  94.1 6.3 %all-to-all-start.2 = ((bf16[64,16,256]{2,1,0:T(8,128)(2,1)}), bf16[64,16,256]{2,1,0:T(8,128)(2,1)S(1)}, u32[]{:S(2)}, u32[]{:S(2)}) async-start(bf16[64,16,256]{2,1,0:T(8,128)(2,1)} %sum.1), calls=%async_computation.2 | async-start | bytes 1048576 | tf_op jit(solution)/shard_map/all_to_all | solution.py:229
  100.3 1.0 embed.1
  101.3 16.4 %all-to-all-done.2.all_ref = bf16[64,16,256]{2,1,0:T(8,128)(2,1)S(1)} async-done(((bf16[64,16,256]{2,1,0:T(8,128)(2,1)}), bf16[64,16,256]{2,1,0:T(8,128)(2,1)S(1)}, u32[]{:S(2)}, u32[]{:S(2)}) %all-to-all-start.2) | async-done | bytes 524320 | tf_op jit(solution)/shard_map/all_to_all | solution.py:229
  117.7 1.0 finish.1
  (9 shorter events, 0.0 us)
Async XLA Ops:
  5.4 13.3 %copy-start.13 = (s32[1,64]{1,0:T(1,128)S(1)}, s32[1,64]{1,0:T(1,128)}, u32[]{:S(2)}) copy-start(s32[1,64]{1,0:T(1,128)} %param.21) | copy-start | bytes 772
  5.4 13.8 %copy-start.7 = (s32[512,25]{0,1:T(8,128)S(1)}, s32[512,25]{0,1:T(8,128)}, u32[]{:S(2)}) copy-start(s32[512,25]{0,1:T(8,128)} %param.23) | copy-start | bytes 153604
  5.4 13.8 %copy-start.8 = (s32[128,10]{0,1:T(8,128)S(1)}, s32[128,10]{0,1:T(8,128)}, u32[]{:S(2)}) copy-start(s32[128,10]{0,1:T(8,128)} %param.26) | copy-start | bytes 15364
  5.4 13.8 %copy-start.9 = (s32[512]{0:T(512)S(1)}, s32[512]{0:T(512)}, u32[]{:S(2)}) copy-start(s32[512]{0:T(512)} %param.24) | copy-start | bytes 6148
  5.4 13.8 %copy-start.10 = (s32[512]{0:T(512)S(1)}, s32[512]{0:T(512)}, u32[]{:S(2)}) copy-start(s32[512]{0:T(512)} %param.22) | copy-start | bytes 6148
  5.4 13.8 %copy-start.11 = (s32[128]{0:T(128)S(1)}, s32[128]{0:T(128)}, u32[]{:S(2)}) copy-start(s32[128]{0:T(128)} %param.25) | copy-start | bytes 1540
  5.4 41.7 %copy-start.5 = (bf16[256,256]{1,0:T(8,128)(2,1)S(1)}, bf16[256,256]{1,0:T(8,128)(2,1)}, u32[]{:S(2)}) copy-start(bf16[256,256]{1,0:T(8,128)(2,1)} %weight_self_ref.1) | copy-start | bytes 393220
  5.4 41.7 %copy-start.6 = (bf16[256,256]{1,0:T(8,128)(2,1)S(1)}, bf16[256,256]{1,0:T(8,128)(2,1)}, u32[]{:S(2)}) copy-start(bf16[256,256]{1,0:T(8,128)(2,1)} %weight_near_ref.1) | copy-start | bytes 393220
  5.5 41.7 %all-to-all-start = ((bf16[64,32,256]{2,1,0:T(8,128)(2,1)}), bf16[64,32,256]{2,1,0:T(8,128)(2,1)S(1)}, u32[]{:S(2)}, u32[]{:S(2)}) async-start(bf16[64,32,256]{2,1,0:T(8,128)(2,1)} %bitcast.1), calls=%async_computation | async-start | bytes 2097152 | tf_op jit(solution)/shard_map/all_to_all | solution.py:229
  30.4 1.3 %copy-start = (bf16[2048,512]{1,0:T(8,128)(2,1)}, bf16[2048,512]{1,0:T(8,128)(2,1)S(1)}, u32[]{:S(2)}) copy-start(bf16[2048,512]{1,0:T(8,128)(2,1)S(1)} %get-tuple-element.27) | copy-start | bytes 6291460
  31.7 1.3 %copy-start.1 = (bf16[2048,512]{1,0:T(8,128)(2,1)}, bf16[2048,512]{1,0:T(8,128)(2,1)S(1)}, u32[]{:S(2)}) copy-start(bf16[2048,512]{1,0:T(8,128)(2,1)S(1)} %get-tuple-element.28) | copy-start | bytes 6291460
  47.2 8.6 %copy-start.12 = (f32[256]{0:T(256)S(1)}, f32[256]{0:T(256)}, u32[]{:S(2)}) copy-start(f32[256]{0:T(256)} %param.17) | copy-start | bytes 3076
  47.2 11.1 %copy-start.2 = (bf16[256,256]{1,0:T(8,128)(2,1)S(1)}, bf16[256,256]{1,0:T(8,128)(2,1)}, u32[]{:S(2)}) copy-start(bf16[256,256]{1,0:T(8,128)(2,1)} %second_self_ref.3) | copy-start | bytes 393220
  47.2 11.1 %copy-start.3 = (bf16[256,256]{1,0:T(8,128)(2,1)S(1)}, bf16[256,256]{1,0:T(8,128)(2,1)}, u32[]{:S(2)}) copy-start(bf16[256,256]{1,0:T(8,128)(2,1)} %second_near_ref.3) | copy-start | bytes 393220
  47.2 11.1 %copy-start.4 = (bf16[128,256]{1,0:T(8,128)(2,1)S(1)}, bf16[128,256]{1,0:T(8,128)(2,1)}, u32[]{:S(2)}) copy-start(bf16[128,256]{1,0:T(8,128)(2,1)} %cotangent_ref.3) | copy-start | bytes 196612
  50.7 5.2 %collective-permute-start = (bf16[64,512]{1,0:T(8,128)(2,1)S(1)}, bf16[64,512]{1,0:T(8,128)(2,1)S(1)}, u32[]{:S(2)}, u32[]{:S(2)}) collective-permute-start(bf16[64,512]{1,0:T(8,128)(2,1)S(1)} %get-tuple-element.30), channel_id=1, source_target_pairs={{0,1},{1,2},{2,3},{3,0},{4,5},{5,6},{6,7},{7,4},{8,9},{9,10},{10,1... | collective-permute-start | bytes 196616 | tf_op jit(solution)/shard_map/ppermute | solution.py:236
  52.1 6.2 %collective-permute-start.1 = (bf16[64,512]{1,0:T(8,128)(2,1)S(1)}, bf16[64,512]{1,0:T(8,128)(2,1)S(1)}, u32[]{:S(2)}, u32[]{:S(2)}) collective-permute-start(bf16[64,512]{1,0:T(8,128)(2,1)S(1)} %get-tuple-element.31), channel_id=1, source_target_pairs={{0,2},{1,3},{2,0},{3,1},{4,6},{5,7},{6,4},{7,5},{8,10},{9,11},{10,... | collective-permute-start | bytes 196616 | tf_op jit(solution)/shard_map/ppermute | solution.py:236
  54.7 3.6 %collective-permute-start.2 = (bf16[64,512]{1,0:T(8,128)(2,1)S(1)}, bf16[64,512]{1,0:T(8,128)(2,1)S(1)}, u32[]{:S(2)}, u32[]{:S(2)}) collective-permute-start(bf16[64,512]{1,0:T(8,128)(2,1)S(1)} %get-tuple-element.32), channel_id=1, source_target_pairs={{0,3},{1,0},{2,1},{3,2},{4,7},{5,4},{6,5},{7,6},{8,11},{9,8},{10,9... | collective-permute-start | bytes 196616 | tf_op jit(solution)/shard_map/ppermute | solution.py:236
  58.7 4.0 %collective-permute-start.5 = (bf16[96,512]{1,0:T(8,128)(2,1)S(1)}, bf16[96,512]{1,0:T(8,128)(2,1)S(1)}, u32[]{:S(2)}, u32[]{:S(2)}) collective-permute-start(bf16[96,512]{1,0:T(8,128)(2,1)S(1)} %owner.1.refs_0_), channel_id=1, source_target_pairs={{0,3},{1,0},{2,1},{3,2},{4,7},{5,4},{6,5},{7,6},{8,11},{9,8},{10,9... | collective-permute-start | bytes 294920 | tf_op jit(solution)/shard_map/ppermute | solution.py:236
  60.6 5.1 %collective-permute-start.4 = (bf16[96,512]{1,0:T(8,128)(2,1)S(1)}, bf16[96,512]{1,0:T(8,128)(2,1)S(1)}, u32[]{:S(2)}, u32[]{:S(2)}) collective-permute-start(bf16[96,512]{1,0:T(8,128)(2,1)S(1)} %owner.1.refs_0_), channel_id=1, source_target_pairs={{0,2},{1,3},{2,0},{3,1},{4,6},{5,7},{6,4},{7,5},{8,10},{9,11},{10,... | collective-permute-start | bytes 294920 | tf_op jit(solution)/shard_map/ppermute | solution.py:236
  60.8 5.7 %collective-permute-start.3 = (bf16[96,512]{1,0:T(8,128)(2,1)S(1)}, bf16[96,512]{1,0:T(8,128)(2,1)S(1)}, u32[]{:S(2)}, u32[]{:S(2)}) collective-permute-start(bf16[96,512]{1,0:T(8,128)(2,1)S(1)} %owner.1.refs_0_), channel_id=1, source_target_pairs={{0,1},{1,2},{2,3},{3,0},{4,5},{5,6},{6,7},{7,4},{8,9},{9,10},{10,1... | collective-permute-start | bytes 294920 | tf_op jit(solution)/shard_map/ppermute | solution.py:236
  94.1 23.6 %all-to-all-start.2 = ((bf16[64,16,256]{2,1,0:T(8,128)(2,1)}), bf16[64,16,256]{2,1,0:T(8,128)(2,1)S(1)}, u32[]{:S(2)}, u32[]{:S(2)}) async-start(bf16[64,16,256]{2,1,0:T(8,128)(2,1)} %sum.1), calls=%async_computation.2 | async-start | bytes 1048576 | tf_op jit(solution)/shard_map/all_to_all | solution.py:229

commit v7 on v6

--- a/solution.py
+++ b/solution.py
@@ -5,11 +5,13 @@
 from jax import lax
 from jax.experimental import pallas as pl
 from jax.experimental.pallas import tpu as pltpu
+from jax.sharding import Mesh
 from jax.sharding import PartitionSpec as P
 
 BF16 = jnp.bfloat16
 F32 = jnp.float32
 I32 = jnp.int32
+AXES = ("x", "z", "core", "feat")
 
 
 def dot(left, right, left_dim=1, right_dim=0):
@@ -174,25 +176,89 @@
     )
 
 
-def weight_body(place_ref, own_ref, near_ref, cotangent_ref, *refs, half):
-    grads_refs, (out_ref, held_ref) = refs[:-2], refs[-2:]
+def weight_body(place_ref, own_ref, near_ref, cotangent_ref, *refs, half, count):
+    grads_refs, (keep_ref, give_ref, grads_held, held_ref) = refs[:-4], refs[-4:]
     slices = len(grads_refs)
-    tiles = out_ref.shape[0] // 2
-    lines = out_ref.shape[1] // 2
-    per = half // lines
+    cores, tall, cols = held_ref.shape
+    hidden = cols // 2
+    deep = tall // (2 * count)
     cotangent = cotangent_ref[...]
     for shift, grads_ref in enumerate(grads_refs):
         at = lax.rem(place_ref[0] + slices - shift, slices)
-        held_ref[pl.ds(pl.multiple_of(at * half, half), half), :] = grads_ref[:half, :]
+        grads_held[pl.ds(pl.multiple_of(at * half, half), half), :] = grads_ref[:half, :]
         second = dot(unpacked_seeds(grads_ref, half, cotangent.shape[0]), cotangent)
-        for side in range(2):
-            part = second[side * half : (side + 1) * half].reshape(per, lines, second.shape[1])
-            out_ref[pl.ds(side * tiles + at * per, per), lines:] = part.astype(BF16)
-    grads = held_ref[...]
+        for piece in range(half // deep):
+            index = at * (half // deep) + piece
+            core = lax.div(index, count)
+            x = lax.rem(index, count)
+            span = pl.ds(pl.multiple_of((2 * x + 1) * deep, deep), deep)
+            for side in range(2):
+                held_ref[core, span, side * hidden : (side + 1) * hidden] = second[
+                    side * half + piece * deep : side * half + (piece + 1) * deep
+                ]
+    grads = grads_held[...]
     for side, ref in enumerate((own_ref, near_ref)):
         part = dot(ref[...], grads, 1, 1)
-        part = part.reshape(tiles, lines, part.shape[1])
-        out_ref[pl.ds(side * tiles, tiles), :lines] = part.astype(BF16)
+        for core in range(cores):
+            for x in range(count):
+                low = (core * count + x) * deep
+                held_ref[
+                    core, 2 * x * deep : (2 * x + 1) * deep, side * hidden : (side + 1) * hidden
+                ] = part[low : low + deep]
+    keep_ref[...] = held_ref[place_ref[1]]
+    give_ref[...] = held_ref[1 - place_ref[1]].astype(BF16)
+
+
+def split_body(place_ref, keep_ref, got_ref, *out_refs):
+    count = len(out_refs)
+    step = out_refs[0].shape[0]
+    for shift, out_ref in enumerate(out_refs):
+        at = lax.rem(place_ref[2] + shift, count)
+        span = pl.ds(pl.multiple_of(at * step, step), step)
+        out_ref[...] = (keep_ref[span, :] + got_ref[span, :].astype(F32)).astype(BF16)
+
+
+def spread_body(*refs):
+    parts, out_ref = refs[:-1], refs[-1]
+    total = parts[0][...].astype(F32)
+    for part in parts[1:]:
+        total = total + part[...].astype(F32)
+    total = total.astype(BF16)
+    for at in range(out_ref.shape[0]):
+        out_ref[at] = total
+
+
+def sum_body(parts_ref, out_ref):
+    out_ref[...] = jnp.sum(parts_ref[...].astype(F32), axis=0).astype(BF16)
+
+
+def stack_body(place_ref, *refs):
+    parts, out_ref = refs[:-1], refs[-1]
+    count = len(parts)
+    step = parts[0].shape[0]
+    for shift, part in enumerate(parts):
+        at = lax.rem(place_ref[2] + count - shift, count)
+        out_ref[pl.ds(pl.multiple_of(at * step, step), step), :] = part[...]
+
+
+def finish_body(
+    place_ref, mine_ref, other_ref, first_self_ref, first_near_ref, second_self_ref, second_near_ref,
+    count, cores,
+):
+    hidden = first_self_ref.shape[0]
+    deep = hidden // (count * cores)
+    mine, other = mine_ref[...].astype(F32), other_ref[...].astype(F32)
+    refs = ((first_self_ref, first_near_ref), (second_self_ref, second_near_ref))
+    for core in range(cores):
+        value = jnp.where(place_ref[1] == core, mine, other)
+        for x in range(count):
+            low = (core * count + x) * deep
+            for layer in range(2):
+                start = (2 * x + layer) * deep
+                for side in range(2):
+                    refs[layer][side][low : low + deep, :] = value[
+                        start : start + deep, side * hidden : (side + 1) * hidden
+                    ]
 
 
 def embed_body(place_ref, second_self_ref, second_near_ref, *refs, half):
@@ -208,23 +274,6 @@
     out_ref[...] = total.astype(BF16)
 
 
-def sum_body(parts_ref, out_ref):
-    total = jnp.sum(parts_ref[...].astype(F32), axis=0).astype(BF16)
-    for at in range(out_ref.shape[0]):
-        out_ref[at] = total
-
-
-def finish_body(all_ref, first_self_ref, first_near_ref, second_self_ref, second_near_ref):
-    peers, tall, width = all_ref.shape
-    lines = tall // 2
-    tiles = peers // 2
-    value = all_ref[...].astype(F32)
-    first_self_ref[...] = value[:tiles, :lines].reshape(tiles * lines, width)
-    first_near_ref[...] = value[tiles:, :lines].reshape(tiles * lines, width)
-    second_self_ref[...] = value[:tiles, lines:].reshape(tiles * lines, width)
-    second_near_ref[...] = value[tiles:, lines:].reshape(tiles * lines, width)
-
-
 def exchange(value, axis):
     return lax.all_to_all(value, axis, split_axis=0, concat_axis=0, tiled=True)
 
@@ -236,6 +285,10 @@
         else lax.ppermute(piece, axis, [(at, (at + shift) % count) for at in range(count)])
         for shift, piece in enumerate(pieces)
     ]
+
+
+def swapped(value, axis, count, step):
+    return lax.ppermute(value, axis, [(at, at ^ step) for at in range(count)])
 
 
 def per_device(
@@ -253,9 +306,10 @@
     seed_self,
     seed_neighbor,
     cotangent,
+    sizes,
 ):
-    peers = lax.axis_size("dom")
-    slices = lax.axis_size("feat")
+    count_x, count_z, cores, slices = (sizes[axis] for axis in AXES)
+    peers = count_x * count_z * cores
     rows, slice_cols = features.shape
     hidden = first_self.shape[1]
     half = hidden // slices
@@ -264,9 +318,8 @@
     mids, fan = neighbor_slot.shape
     seeds, fan_two = seed_neighbor.shape
     out_cols = second_self.shape[1]
-    lines = 2 * hidden // peers
     pieces = 4
-    place = lax.axis_index("feat").astype(I32).reshape(1)
+    place = jnp.stack([lax.axis_index(axis) for axis in ("feat", "core", "x")]).astype(I32)
 
     (picked,) = call(
         pick_body, [((slots, slice_cols), BF16)], (send_rows, features), "pick",
@@ -276,7 +329,7 @@
             pltpu.SemaphoreType.DMA((2,)),
         ],
     )
-    routed = exchange(picked.reshape(peers, capacity, slice_cols), "dom").reshape(slots, slice_cols)
+    routed = exchange(picked.reshape(peers, capacity, slice_cols), AXES[:3]).reshape(slots, slice_cols)
 
     slot_at = lax.broadcasted_iota(I32, (peers, capacity, 128), 1)
     mask = (slot_at < arrive_count.reshape(peers, 1, 1)).astype(BF16).reshape(slots, 128)
@@ -317,26 +370,41 @@
         "owner", 16 * half * seeds * mids, 8 * half * mids, scalars=1,
     )
     grads = shifted([grads] * slices, "feat", slices)
-    (merged,) = call(
-        functools.partial(weight_body, half=half), [((peers, 2 * lines, hidden), BF16)],
+    tall = 2 * hidden // cores
+    keep, give = call(
+        functools.partial(weight_body, half=half, count=count_x),
+        [((tall, 2 * hidden), F32), ((tall, 2 * hidden), BF16)],
         (place, own_rows, near_rows, cotangent, *grads), "weight",
         4 * slice_cols * mids * hidden, 8 * slice_cols * mids,
-        scratch=[pltpu.VMEM((hidden, mids), BF16)], scalars=1,
-    )
-    merged = exchange(merged, "dom")
+        scratch=[pltpu.VMEM((hidden, mids), BF16), pltpu.VMEM((cores, tall, 2 * hidden), F32)],
+        scalars=1,
+    )
+    got = swapped(give, "core", cores, 1)
+    shard = (tall // count_x, 2 * hidden)
+    parts = call(
+        split_body, [(shard, BF16)] * count_x, (place, keep, got), "split", 0, 16 * tall * hidden,
+        scalars=1,
+    )
+    (mixed,) = call(
+        spread_body, [((count_z,) + shard, BF16)], shifted(parts, "x", count_x), "spread",
+        0, 4 * tall * hidden,
+    )
+    mixed = exchange(mixed, "z")
     (seed_embedding,) = call(
         functools.partial(embed_body, half=half), [((seeds, out_cols), BF16)],
         (place, second_self, second_neighbor, *grads), "embed",
         4 * seeds * hidden * out_cols, 8 * seeds * hidden, scalars=1,
     )
-    (summed,) = call(
-        sum_body, [((peers, 2 * lines, hidden), BF16)], (merged,), "sum",
-        0, 8 * peers * lines * hidden,
-    )
-    summed = exchange(summed, "dom")
+    mixed, seed_embedding = lax.optimization_barrier((mixed, seed_embedding))
+    (mixed,) = call(sum_body, [(shard, BF16)], (mixed,), "sum", 0, 8 * tall * hidden)
+    (mixed,) = call(
+        stack_body, [((tall, 2 * hidden), BF16)],
+        (place, *shifted([mixed] * count_x, "x", count_x)), "stack", 0, 8 * tall * hidden, scalars=1,
+    )
     grad_first_self, grad_first_neighbor, grad_second_self, grad_second_neighbor = call(
-        finish_body, [((slice_cols, hidden), F32)] * 2 + [((hidden, out_cols), F32)] * 2,
-        (summed,), "finish", 0, 8 * peers * lines * hidden,
+        functools.partial(finish_body, count=count_x, cores=cores),
+        [((slice_cols, hidden), F32)] * 2 + [((hidden, out_cols), F32)] * 2,
+        (place, mixed, swapped(mixed, "core", cores, 1)), "finish", 0, 24 * tall * hidden, scalars=1,
     )
     return (
         seed_embedding,
@@ -348,23 +416,31 @@
 
 
 def solution(mesh):
+    shape = (4, 8, 2, mesh.shape["feat"])
+    sizes = dict(zip(AXES, shape))
+    mesh = Mesh(mesh.devices.reshape(shape), AXES)
+    dom = AXES[:3]
     in_specs = (
-        P("dom", "feat"),
+        P(dom, "feat"),
         P("feat", None),
         P("feat", None),
         P(),
         P(),
         P(),
-        P("dom", None),
-        P("dom", None),
-        P("dom"),
-        P("dom", None),
-        P("dom"),
-        P("dom"),
-        P("dom", None),
-        P("dom", None),
-    )
-    out_specs = (P("dom", None), P("feat", None), P("feat", None), P(), P())
+        P(dom, None),
+        P(dom, None),
+        P(dom),
+        P(dom, None),
+        P(dom),
+        P(dom),
+        P(dom, None),
+        P(dom, None),
+    )
+    out_specs = (P(dom, None), P("feat", None), P("feat", None), P(), P())
     return jax.shard_map(
-        per_device, mesh=mesh, in_specs=in_specs, out_specs=out_specs, check_vma=False
-    )
+        functools.partial(per_device, sizes=sizes),
+        mesh=mesh,
+        in_specs=in_specs,
+        out_specs=out_specs,
+        check_vma=False,
+    )

time: 119 us -> 116 us (0.975)
  blocking collectives: 26.2 us -> 0 us
  starting transfers between devices: 27.4 us -> 39.7 us
  waiting for transfers between devices: 37.8 us -> 44.9 us
  Pallas kernels: 23.1 us -> 26.9 us
    all_to_all x1 -> x0, blocking collectives: 26.2 us -> none  [exchange(): return lax.all_to_all(value, axis, split_axis=0, concat_axis=0, tiled=True)]
    ppermute x6 -> x12, starting transfers between devices: 7.94 us -> 15.6 us  [shifted(): lax.ppermute(piece, axis, [(at, (at + shift) % count) for at in range(cou...]
    ppermute x0 -> x2, starting transfers between devices: none -> 7.46 us  [swapped(): return lax.ppermute(value, axis, [(at, at ^ step) for at in range(count)])]
    ppermute x6 -> x12, waiting for transfers between devices: 7.34 us -> 14.2 us  [shifted(): lax.ppermute(piece, axis, [(at, (at + shift) % count) for at in range(cou...]
    pallas_call x8 -> x11, Pallas kernels: 23.1 us -> 26.9 us  [call(): pl.pallas_call(body, out_shape=[jax.ShapeDtypeStruct(shape, dtype) for sh...]
    all_to_all x2, starting transfers between devices: 19.4 us -> 16.6 us  [exchange(): return lax.all_to_all(value, axis, split_axis=0, concat_axis=0, tiled=True)]
    ppermute x0 -> x2, waiting for transfers between devices: none -> 2.32 us  [swapped(): return lax.ppermute(value, axis, [(at, at ^ step) for at in range(count)])]
    all_to_all x2, waiting for transfers between devices: 30.5 us -> 28.5 us  [exchange(): return lax.all_to_all(value, axis, split_axis=0, concat_axis=0, tiled=True)]
  transfers between devices with their start and end apart: 8 -> 16, of which waited for: 6 -> 12; matrix products, arithmetic and copies ran while one was open for 1% -> 1% of each run, Pallas kernels for 10% -> 11%
where the time goes in v7:
time: 116 us
  waiting for transfers between devices  44.9 us (39%)
  starting transfers between devices  39.7 us (34%)
  Pallas kernels  26.9 us (23%)
  local copies, waits for them, and re-layouts  3.29 us (3%)
    all_to_all x2, waiting for transfers between devices, exchange(): return lax.all_to_all(value, axis, split_axis=0, concat_axis=0, tiled=True)  28.5 us
    pallas_call x11, Pallas kernels, call(): pl.pallas_call(body, out_shape=[jax.ShapeDtypeStruct(shape, dtype) for sh...  26.9 us
    all_to_all x2, starting transfers between devices, exchange(): return lax.all_to_all(value, axis, split_axis=0, concat_axis=0, tiled=True)  16.6 us
    ppermute x12, starting transfers between devices, shifted(): lax.ppermute(piece, axis, [(at, (at + shift) % count) for at in range(cou...  15.6 us
    ppermute x12, waiting for transfers between devices, shifted(): lax.ppermute(piece, axis, [(at, (at + shift) % count) for at in range(cou...  14.2 us
    ppermute x2, starting transfers between devices, swapped(): return lax.ppermute(value, axis, [(at, at ^ step) for at in range(count)])  7.46 us
    unnamed x28, local copies, waits for them, and re-layouts  2.73 us
    ppermute x2, waiting for transfers between devices, swapped(): return lax.ppermute(value, axis, [(at, at ^ step) for at in range(count)])  2.32 us
  transfers between devices with their start and end apart: 16, of which 12 were waited for; matrix products, arithmetic and copies ran while one was open for 1% of the time, Pallas kernels for 11%

profile of v7, /device:TPU:1, one launch (start us, length us, event | category | flops | bytes accessed | tf_op | source)
XLA Modules:
  0.0 115.9 jit_solution(14782848733524405816)
XLA Ops:
  0.6 4.7 %pick.1 = bf16[2048,256]{1,0:T(8,128)(2,1)} custom-call(s32[1,2048]{1,0:T(1,128)} %row_far.1, bf16[1536,256]{1,0:T(8,128)(2,1)} %x_far.1), custom_call_target="tpu_custom_call" | custom-call | flops 1610612736 | bytes 6291456 | tf_op jit(solution)/shard_map/pick/pallas_call | solution.py:31
  5.4 0.0 copy-start.13
  5.4 0.0 copy-start.9
  5.4 0.0 copy-start.10
  5.5 13.2 %all-to-all-start = ((bf16[64,32,256]{2,1,0:T(8,128)(2,1)}), bf16[64,32,256]{2,1,0:T(8,128)(2,1)S(1)}, u32[]{:S(2)}, u32[]{:S(2)}) async-start(bf16[64,32,256]{2,1,0:T(8,128)(2,1)} %bitcast.3), calls=%async_computation | async-start | bytes 2097152 | tf_op jit(solution)/shard_map/all_to_all | solution.py:278
  18.6 0.1 fusion
  18.7 0.1 reshape.51
  18.8 0.3 iota.10.mask_ref
  19.2 11.2 %count.1 = (bf16[2048,512]{1,0:T(8,128)(2,1)S(1)}, bf16[2048,512]{1,0:T(8,128)(2,1)S(1)}, bf16[512,128]{1,0:T(8,128)(2,1)S(1)}, bf16[512,128]{1,0:T(8,128)(2,1)S(1)}) custom-call(s32[1,512]{1,0:T(1,128)S(1)} %bitcast.21, s32[25,512]{1,0:T(8,128)S(1)} %bitcast.17, s32[1,512]{1,0:T(1,128)S(1)} %bitcast.19, bf16[2048,128]{1,0:T(8,128)(2,1)S(1)} %iota.10.mask_ref, ...), custom_call_target="tpu_custom_call" | custom-call | bytes 16777216 | tf_op jit(solution)/shard_map/count/pallas_call | solution.py:31
  30.4 1.3 %copy-done = bf16[2048,512]{1,0:T(8,128)(2,1)} copy-done((bf16[2048,512]{1,0:T(8,128)(2,1)}, bf16[2048,512]{1,0:T(8,128)(2,1)S(1)}, u32[]{:S(2)}) %copy-start) | copy-done | bytes 2097176
  31.8 1.3 %copy-done.1 = bf16[2048,512]{1,0:T(8,128)(2,1)} copy-done((bf16[2048,512]{1,0:T(8,128)(2,1)}, bf16[2048,512]{1,0:T(8,128)(2,1)S(1)}, u32[]{:S(2)}) %copy-start.1) | copy-done | bytes 2097176
  33.1 0.1 pad_add_fusion.place_ref
  33.2 14.0 %all-to-all-done = bf16[64,32,256]{2,1,0:T(8,128)(2,1)S(1)} async-done(((bf16[64,32,256]{2,1,0:T(8,128)(2,1)}), bf16[64,32,256]{2,1,0:T(8,128)(2,1)S(1)}, u32[]{:S(2)}, u32[]{:S(2)}) %all-to-all-start) | async-done | bytes 1048608 | tf_op jit(solution)/shard_map/all_to_all | solution.py:278
  47.2 3.9 %gather.1 = (bf16[256,512]{1,0:T(8,128)(2,1)S(1)}, bf16[256,512]{1,0:T(8,128)(2,1)S(1)}, bf16[64,512]{1,0:T(8,128)(2,1)S(1)}, bf16[64,512]{1,0:T(8,128)(2,1)S(1)...) custom-call(s32[3]{0:T(128)S(1)} %pad_add_fusion.place_ref, bf16[2048,256]{1,0:T(8,128)(2,1)S(1)} %bitcast.14, ...), custom_call_target="tpu_custom_call" | custom-call | flops 1073741824 | bytes 4194304 | tf_op jit(solution)/shard_map/gather/pallas_call | solution.py:31
  51.2 1.4 %collective-permute-start = (bf16[64,512]{1,0:T(8,128)(2,1)S(1)}, bf16[64,512]{1,0:T(8,128)(2,1)S(1)}, u32[]{:S(2)}, u32[]{:S(2)}) collective-permute-start(bf16[64,512]{1,0:T(8,128)(2,1)S(1)} %get-tuple-element.40), channel_id=1, source_target_pairs={{0,1},{1,2},{2,3},{3,0},{4,5},{5,6},{6,7},{7,4},{8,9},{9,10},{10,1... | collective-permute-start | bytes 196616 | tf_op jit(solution)/shard_map/ppermute | solution.py:285
  52.6 2.6 %collective-permute-start.1 = (bf16[64,512]{1,0:T(8,128)(2,1)S(1)}, bf16[64,512]{1,0:T(8,128)(2,1)S(1)}, u32[]{:S(2)}, u32[]{:S(2)}) collective-permute-start(bf16[64,512]{1,0:T(8,128)(2,1)S(1)} %get-tuple-element.41), channel_id=1, source_target_pairs={{0,2},{1,3},{2,0},{3,1},{4,6},{5,7},{6,4},{7,5},{8,10},{9,11},{10,... | collective-permute-start | bytes 196616 | tf_op jit(solution)/shard_map/ppermute | solution.py:285
  55.1 1.1 collective-permute-start.2
  56.2 0.1 copy.19.bias_ref
  56.4 2.4 %collective-permute-done.1.refs_2_ = bf16[64,512]{1,0:T(8,128)(2,1)S(1)} collective-permute-done((bf16[64,512]{1,0:T(8,128)(2,1)S(1)}, bf16[64,512]{1,0:T(8,128)(2,1)S(1)}, u32[]{:S(2)}, u32[]{:S(2)}) %collective-permute-start.1) | collective-permute-done | bytes 65568 | tf_op jit(solution)/shard_map/ppermute | solution.py:285
  58.8 0.9 owner.1.refs_0_
  59.7 1.9 %collective-permute-start.5 = (bf16[96,512]{1,0:T(8,128)(2,1)S(1)}, bf16[96,512]{1,0:T(8,128)(2,1)S(1)}, u32[]{:S(2)}, u32[]{:S(2)}) collective-permute-start(bf16[96,512]{1,0:T(8,128)(2,1)S(1)} %owner.1.refs_0_), channel_id=1, source_target_pairs={{0,3},{1,0},{2,1},{3,2},{4,7},{5,4},{6,5},{7,6},{8,11},{9,8},{10,9... | collective-permute-start | bytes 294920 | tf_op jit(solution)/shard_map/ppermute | solution.py:285
  61.6 0.2 collective-permute-start.4
  61.8 0.8 collective-permute-start.3
  62.6 1.1 collective-permute-done.5.refs_3_
  63.7 2.9 %collective-permute-done.4.refs_2_ = bf16[96,512]{1,0:T(8,128)(2,1)S(1)} collective-permute-done((bf16[96,512]{1,0:T(8,128)(2,1)S(1)}, bf16[96,512]{1,0:T(8,128)(2,1)S(1)}, u32[]{:S(2)}, u32[]{:S(2)}) %collective-permute-start.4) | collective-permute-done | bytes 98336 | tf_op jit(solution)/shard_map/ppermute | solution.py:285
  66.6 0.9 collective-permute-done.3.refs_1_
  67.5 1.0 weight.1
  68.5 3.4 %collective-permute-start.6 = (bf16[256,512]{1,0:T(8,128)(2,1)S(1)}, bf16[256,512]{1,0:T(8,128)(2,1)S(1)}, u32[]{:S(2)}, u32[]{:S(2)}) collective-permute-start(bf16[256,512]{1,0:T(8,128)(2,1)S(1)} %get-tuple-element.44), channel_id=1, source_target_pairs={{0,4},{4,0},{1,5},{5,1},{2,6},{6,2},{3,7},{7,3},{8,12},{12,8},{9,1... | collective-permute-start | bytes 786440 | tf_op jit(solution)/shard_map/ppermute | solution.py:291
  71.9 1.2 %collective-permute-done.6.got_ref = bf16[256,512]{1,0:T(8,128)(2,1)S(1)} collective-permute-done((bf16[256,512]{1,0:T(8,128)(2,1)S(1)}, bf16[256,512]{1,0:T(8,128)(2,1)S(1)}, u32[]{:S(2)}, u32[]{:S(2)}) %collective-permute-start.6) | collective-permute-done | bytes 262176 | tf_op jit(solution)/shard_map/ppermute | solution.py:291
  73.1 0.6 split.1
  73.7 1.7 %collective-permute-start.7 = (bf16[64,512]{1,0:T(8,128)(2,1)S(1)}, bf16[64,512]{1,0:T(8,128)(2,1)S(1)}, u32[]{:S(2)}, u32[]{:S(2)}) collective-permute-start(bf16[64,512]{1,0:T(8,128)(2,1)S(1)} %get-tuple-element.46), channel_id=1, source_target_pairs={{0,64},{64,128},{128,192},{192,0},{1,65},{65,129},{129,193},{193,1... | collective-permute-start | bytes 196616 | tf_op jit(solution)/shard_map/ppermute | solution.py:285
  75.4 2.0 %collective-permute-start.8 = (bf16[64,512]{1,0:T(8,128)(2,1)S(1)}, bf16[64,512]{1,0:T(8,128)(2,1)S(1)}, u32[]{:S(2)}, u32[]{:S(2)}) collective-permute-start(bf16[64,512]{1,0:T(8,128)(2,1)S(1)} %get-tuple-element.47), channel_id=1, source_target_pairs={{0,128},{64,192},{128,0},{192,64},{1,129},{65,193},{129,1},{193,65... | collective-permute-start | bytes 196616 | tf_op jit(solution)/shard_map/ppermute | solution.py:285
  77.5 1.1 collective-permute-start.9
  78.5 2.5 %collective-permute-done.8.refs_2_ = bf16[64,512]{1,0:T(8,128)(2,1)S(1)} collective-permute-done((bf16[64,512]{1,0:T(8,128)(2,1)S(1)}, bf16[64,512]{1,0:T(8,128)(2,1)S(1)}, u32[]{:S(2)}, u32[]{:S(2)}) %collective-permute-start.8) | collective-permute-done | bytes 65568 | tf_op jit(solution)/shard_map/ppermute | solution.py:285
  81.0 0.8 spread.1
  81.9 3.5 %all-to-all-start.1 = ((bf16[8,64,512]{2,1,0:T(8,128)(2,1)}), bf16[8,64,512]{2,1,0:T(8,128)(2,1)S(1)}, u32[]{:S(2)}, u32[]{:S(2)}) async-start(bf16[8,64,512]{2,1,0:T(8,128)(2,1)} %spread.1), calls=%async_computation.1 | async-start | bytes 1048576 | tf_op jit(solution)/shard_map/all_to_all | solution.py:278
  85.4 1.5 %embed.1 = bf16[128,256]{1,0:T(8,128)(2,1)} custom-call(s32[3]{0:T(128)S(1)} %pad_add_fusion.place_ref, bf16[256,256]{1,0:T(8,128)(2,1)S(1)} %copy-done.2, bf16[256,256]{1,0:T(8,128)(2,1)S(1)} %copy-done.3, bf16[96,512]{1,0:T(8,128)(2,1)S(1)} %owner.1.refs_0_, bf16[96,512]{1,0:T(8,128)(2,1)S(1)} %collective-permute-done.3.refs_1_, ...), custom_call_target="tpu_custom_call" | custom-call | flops 33554432 | bytes 262144 | tf_op jit(solution)/shard_map/embed/pallas_call | solution.py:31
  86.9 14.4 %all-to-all-done.1.parts_ref = bf16[8,64,512]{2,1,0:T(8,128)(2,1)S(1)} async-done(((bf16[8,64,512]{2,1,0:T(8,128)(2,1)}), bf16[8,64,512]{2,1,0:T(8,128)(2,1)S(1)}, u32[]{:S(2)}, u32[]{:S(2)}) %all-to-all-start.1) | async-done | bytes 524320 | tf_op jit(solution)/shard_map/all_to_all | solution.py:278
  101.3 0.1 sum.1.refs_0_
  101.4 1.7 %collective-permute-start.12 = (bf16[64,512]{1,0:T(8,128)(2,1)S(1)}, bf16[64,512]{1,0:T(8,128)(2,1)S(1)}, u32[]{:S(2)}, u32[]{:S(2)}) collective-permute-start(bf16[64,512]{1,0:T(8,128)(2,1)S(1)} %sum.1.refs_0_), channel_id=1, source_target_pairs={{0,192},{64,0},{128,64},{192,128},{1,193},{65,1},{129,65},{193,129... | collective-permute-start | bytes 196616 | tf_op jit(solution)/shard_map/ppermute | solution.py:285
  103.1 1.1 collective-permute-start.11
  104.2 0.4 collective-permute-done.12.refs_3_
  104.6 3.1 %collective-permute-done.11.refs_2_ = bf16[64,512]{1,0:T(8,128)(2,1)S(1)} collective-permute-done((bf16[64,512]{1,0:T(8,128)(2,1)S(1)}, bf16[64,512]{1,0:T(8,128)(2,1)S(1)}, u32[]{:S(2)}, u32[]{:S(2)}) %collective-permute-start.11) | collective-permute-done | bytes 65568 | tf_op jit(solution)/shard_map/ppermute | solution.py:285
  107.7 0.8 collective-permute-done.10.refs_1_
  108.5 0.6 stack.17.mine_ref
  109.1 4.1 %collective-permute-start.13 = (bf16[256,512]{1,0:T(8,128)(2,1)S(1)}, bf16[256,512]{1,0:T(8,128)(2,1)S(1)}, u32[]{:S(2)}, u32[]{:S(2)}) collective-permute-start(bf16[256,512]{1,0:T(8,128)(2,1)S(1)} %stack.17.mine_ref), channel_id=1, source_target_pairs={{0,4},{4,0},{1,5},{5,1},{2,6},{6,2},{3,7},{7,3},{8,12},{12,8},{9,1... | collective-permute-start | bytes 786440 | tf_op jit(solution)/shard_map/ppermute | solution.py:291
  113.2 1.2 %collective-permute-done.13.other_ref = bf16[256,512]{1,0:T(8,128)(2,1)S(1)} collective-permute-done((bf16[256,512]{1,0:T(8,128)(2,1)S(1)}, bf16[256,512]{1,0:T(8,128)(2,1)S(1)}, u32[]{:S(2)}, u32[]{:S(2)}) %collective-permute-start.13) | collective-permute-done | bytes 262176 | tf_op jit(solution)/shard_map/ppermute | solution.py:291
  114.4 1.5 %finish.1 = (f32[256,256]{1,0:T(8,128)}, f32[256,256]{1,0:T(8,128)}, f32[256,256]{1,0:T(8,128)}, f32[256,256]{1,0:T(8,128)}) custom-call(s32[3]{0:T(128)S(1)} %pad_add_fusion.place_ref, bf16[256,512]{1,0:T(8,128)(2,1)S(1)} %stack.17.mine_ref, bf16[256,512]{1,0:T(8,128)(2,1)S(1)} %collective-permute-done.13.other_ref), custom_call_target="tpu_custom_call" | custom-call | bytes 1572864 | tf_op jit(solution)/shard_map/finish/pallas_call | solution.py:31
  (28 shorter events, 0.1 us)
Async XLA Ops:
  5.4 13.3 %copy-start.13 = (s32[1,64]{1,0:T(1,128)S(1)}, s32[1,64]{1,0:T(1,128)}, u32[]{:S(2)}) copy-start(s32[1,64]{1,0:T(1,128)} %param.21) | copy-start | bytes 772
  5.4 13.8 %copy-start.7 = (s32[512,25]{0,1:T(8,128)S(1)}, s32[512,25]{0,1:T(8,128)}, u32[]{:S(2)}) copy-start(s32[512,25]{0,1:T(8,128)} %param.23) | copy-start | bytes 153604
  5.4 13.8 %copy-start.8 = (s32[128,10]{0,1:T(8,128)S(1)}, s32[128,10]{0,1:T(8,128)}, u32[]{:S(2)}) copy-start(s32[128,10]{0,1:T(8,128)} %param.26) | copy-start | bytes 15364
  5.4 13.8 %copy-start.9 = (s32[512]{0:T(512)S(1)}, s32[512]{0:T(512)}, u32[]{:S(2)}) copy-start(s32[512]{0:T(512)} %param.24) | copy-start | bytes 6148
  5.4 13.8 %copy-start.10 = (s32[512]{0:T(512)S(1)}, s32[512]{0:T(512)}, u32[]{:S(2)}) copy-start(s32[512]{0:T(512)} %param.22) | copy-start | bytes 6148
  5.4 13.8 %copy-start.11 = (s32[128]{0:T(128)S(1)}, s32[128]{0:T(128)}, u32[]{:S(2)}) copy-start(s32[128]{0:T(128)} %param.25) | copy-start | bytes 1540
  5.4 41.7 %copy-start.5 = (bf16[256,256]{1,0:T(8,128)(2,1)S(1)}, bf16[256,256]{1,0:T(8,128)(2,1)}, u32[]{:S(2)}) copy-start(bf16[256,256]{1,0:T(8,128)(2,1)} %weight_self_ref.1) | copy-start | bytes 393220
  5.5 41.7 %copy-start.6 = (bf16[256,256]{1,0:T(8,128)(2,1)S(1)}, bf16[256,256]{1,0:T(8,128)(2,1)}, u32[]{:S(2)}) copy-start(bf16[256,256]{1,0:T(8,128)(2,1)} %weight_near_ref.1) | copy-start | bytes 393220
  5.5 41.7 %all-to-all-start = ((bf16[64,32,256]{2,1,0:T(8,128)(2,1)}), bf16[64,32,256]{2,1,0:T(8,128)(2,1)S(1)}, u32[]{:S(2)}, u32[]{:S(2)}) async-start(bf16[64,32,256]{2,1,0:T(8,128)(2,1)} %bitcast.3), calls=%async_computation | async-start | bytes 2097152 | tf_op jit(solution)/shard_map/all_to_all | solution.py:278
  30.4 1.3 %copy-start = (bf16[2048,512]{1,0:T(8,128)(2,1)}, bf16[2048,512]{1,0:T(8,128)(2,1)S(1)}, u32[]{:S(2)}) copy-start(bf16[2048,512]{1,0:T(8,128)(2,1)S(1)} %get-tuple-element.32) | copy-start | bytes 6291460
  31.8 1.3 %copy-start.1 = (bf16[2048,512]{1,0:T(8,128)(2,1)}, bf16[2048,512]{1,0:T(8,128)(2,1)S(1)}, u32[]{:S(2)}) copy-start(bf16[2048,512]{1,0:T(8,128)(2,1)S(1)} %get-tuple-element.33) | copy-start | bytes 6291460
  47.2 9.0 %copy-start.12 = (f32[256]{0:T(256)S(1)}, f32[256]{0:T(256)}, u32[]{:S(2)}) copy-start(f32[256]{0:T(256)} %param.17) | copy-start | bytes 3076
  47.2 11.5 %copy-start.2 = (bf16[256,256]{1,0:T(8,128)(2,1)S(1)}, bf16[256,256]{1,0:T(8,128)(2,1)}, u32[]{:S(2)}) copy-start(bf16[256,256]{1,0:T(8,128)(2,1)} %second_self_ref.3) | copy-start | bytes 393220
  47.2 11.5 %copy-start.3 = (bf16[256,256]{1,0:T(8,128)(2,1)S(1)}, bf16[256,256]{1,0:T(8,128)(2,1)}, u32[]{:S(2)}) copy-start(bf16[256,256]{1,0:T(8,128)(2,1)} %second_near_ref.3) | copy-start | bytes 393220
  47.2 11.5 %copy-start.4 = (bf16[128,256]{1,0:T(8,128)(2,1)S(1)}, bf16[128,256]{1,0:T(8,128)(2,1)}, u32[]{:S(2)}) copy-start(bf16[128,256]{1,0:T(8,128)(2,1)} %cotangent_ref.3) | copy-start | bytes 196612
  51.2 5.2 %collective-permute-start = (bf16[64,512]{1,0:T(8,128)(2,1)S(1)}, bf16[64,512]{1,0:T(8,128)(2,1)S(1)}, u32[]{:S(2)}, u32[]{:S(2)}) collective-permute-start(bf16[64,512]{1,0:T(8,128)(2,1)S(1)} %get-tuple-element.40), channel_id=1, source_target_pairs={{0,1},{1,2},{2,3},{3,0},{4,5},{5,6},{6,7},{7,4},{8,9},{9,10},{10,1... | collective-permute-start | bytes 196616 | tf_op jit(solution)/shard_map/ppermute | solution.py:285
  52.6 6.2 %collective-permute-start.1 = (bf16[64,512]{1,0:T(8,128)(2,1)S(1)}, bf16[64,512]{1,0:T(8,128)(2,1)S(1)}, u32[]{:S(2)}, u32[]{:S(2)}) collective-permute-start(bf16[64,512]{1,0:T(8,128)(2,1)S(1)} %get-tuple-element.41), channel_id=1, source_target_pairs={{0,2},{1,3},{2,0},{3,1},{4,6},{5,7},{6,4},{7,5},{8,10},{9,11},{10,... | collective-permute-start | bytes 196616 | tf_op jit(solution)/shard_map/ppermute | solution.py:285
  55.1 3.6 %collective-permute-start.2 = (bf16[64,512]{1,0:T(8,128)(2,1)S(1)}, bf16[64,512]{1,0:T(8,128)(2,1)S(1)}, u32[]{:S(2)}, u32[]{:S(2)}) collective-permute-start(bf16[64,512]{1,0:T(8,128)(2,1)S(1)} %get-tuple-element.42), channel_id=1, source_target_pairs={{0,3},{1,0},{2,1},{3,2},{4,7},{5,4},{6,5},{7,6},{8,11},{9,8},{10,9... | collective-permute-start | bytes 196616 | tf_op jit(solution)/shard_map/ppermute | solution.py:285
  59.7 4.0 %collective-permute-start.5 = (bf16[96,512]{1,0:T(8,128)(2,1)S(1)}, bf16[96,512]{1,0:T(8,128)(2,1)S(1)}, u32[]{:S(2)}, u32[]{:S(2)}) collective-permute-start(bf16[96,512]{1,0:T(8,128)(2,1)S(1)} %owner.1.refs_0_), channel_id=1, source_target_pairs={{0,3},{1,0},{2,1},{3,2},{4,7},{5,4},{6,5},{7,6},{8,11},{9,8},{10,9... | collective-permute-start | bytes 294920 | tf_op jit(solution)/shard_map/ppermute | solution.py:285
  61.6 5.1 %collective-permute-start.4 = (bf16[96,512]{1,0:T(8,128)(2,1)S(1)}, bf16[96,512]{1,0:T(8,128)(2,1)S(1)}, u32[]{:S(2)}, u32[]{:S(2)}) collective-permute-start(bf16[96,512]{1,0:T(8,128)(2,1)S(1)} %owner.1.refs_0_), channel_id=1, source_target_pairs={{0,2},{1,3},{2,0},{3,1},{4,6},{5,7},{6,4},{7,5},{8,10},{9,11},{10,... | collective-permute-start | bytes 294920 | tf_op jit(solution)/shard_map/ppermute | solution.py:285
  61.8 5.7 %collective-permute-start.3 = (bf16[96,512]{1,0:T(8,128)(2,1)S(1)}, bf16[96,512]{1,0:T(8,128)(2,1)S(1)}, u32[]{:S(2)}, u32[]{:S(2)}) collective-permute-start(bf16[96,512]{1,0:T(8,128)(2,1)S(1)} %owner.1.refs_0_), channel_id=1, source_target_pairs={{0,1},{1,2},{2,3},{3,0},{4,5},{5,6},{6,7},{7,4},{8,9},{9,10},{10,1... | collective-permute-start | bytes 294920 | tf_op jit(solution)/shard_map/ppermute | solution.py:285
  68.5 4.5 %collective-permute-start.6 = (bf16[256,512]{1,0:T(8,128)(2,1)S(1)}, bf16[256,512]{1,0:T(8,128)(2,1)S(1)}, u32[]{:S(2)}, u32[]{:S(2)}) collective-permute-start(bf16[256,512]{1,0:T(8,128)(2,1)S(1)} %get-tuple-element.44), channel_id=1, source_target_pairs={{0,4},{4,0},{1,5},{5,1},{2,6},{6,2},{3,7},{7,3},{8,12},{12,8},{9,1... | collective-permute-start | bytes 786440 | tf_op jit(solution)/shard_map/ppermute | solution.py:291
  73.7 4.9 %collective-permute-start.7 = (bf16[64,512]{1,0:T(8,128)(2,1)S(1)}, bf16[64,512]{1,0:T(8,128)(2,1)S(1)}, u32[]{:S(2)}, u32[]{:S(2)}) collective-permute-start(bf16[64,512]{1,0:T(8,128)(2,1)S(1)} %get-tuple-element.46), channel_id=1, source_target_pairs={{0,64},{64,128},{128,192},{192,0},{1,65},{65,129},{129,193},{193,1... | collective-permute-start | bytes 196616 | tf_op jit(solution)/shard_map/ppermute | solution.py:285
  75.4 5.6 %collective-permute-start.8 = (bf16[64,512]{1,0:T(8,128)(2,1)S(1)}, bf16[64,512]{1,0:T(8,128)(2,1)S(1)}, u32[]{:S(2)}, u32[]{:S(2)}) collective-permute-start(bf16[64,512]{1,0:T(8,128)(2,1)S(1)} %get-tuple-element.47), channel_id=1, source_target_pairs={{0,128},{64,192},{128,0},{192,64},{1,129},{65,193},{129,1},{193,65... | collective-permute-start | bytes 196616 | tf_op jit(solution)/shard_map/ppermute | solution.py:285
  77.5 3.6 %collective-permute-start.9 = (bf16[64,512]{1,0:T(8,128)(2,1)S(1)}, bf16[64,512]{1,0:T(8,128)(2,1)S(1)}, u32[]{:S(2)}, u32[]{:S(2)}) collective-permute-start(bf16[64,512]{1,0:T(8,128)(2,1)S(1)} %get-tuple-element.48), channel_id=1, source_target_pairs={{0,192},{64,0},{128,64},{192,128},{1,193},{65,1},{129,65},{193,129... | collective-permute-start | bytes 196616 | tf_op jit(solution)/shard_map/ppermute | solution.py:285
  81.9 19.4 %all-to-all-start.1 = ((bf16[8,64,512]{2,1,0:T(8,128)(2,1)}), bf16[8,64,512]{2,1,0:T(8,128)(2,1)S(1)}, u32[]{:S(2)}, u32[]{:S(2)}) async-start(bf16[8,64,512]{2,1,0:T(8,128)(2,1)} %spread.1), calls=%async_computation.1 | async-start | bytes 1048576 | tf_op jit(solution)/shard_map/all_to_all | solution.py:278
  101.4 3.2 %collective-permute-start.12 = (bf16[64,512]{1,0:T(8,128)(2,1)S(1)}, bf16[64,512]{1,0:T(8,128)(2,1)S(1)}, u32[]{:S(2)}, u32[]{:S(2)}) collective-permute-start(bf16[64,512]{1,0:T(8,128)(2,1)S(1)} %sum.1.refs_0_), channel_id=1, source_target_pairs={{0,192},{64,0},{128,64},{192,128},{1,193},{65,1},{129,65},{193,129... | collective-permute-start | bytes 196616 | tf_op jit(solution)/shard_map/ppermute | solution.py:285
  103.1 4.6 %collective-permute-start.11 = (bf16[64,512]{1,0:T(8,128)(2,1)S(1)}, bf16[64,512]{1,0:T(8,128)(2,1)S(1)}, u32[]{:S(2)}, u32[]{:S(2)}) collective-permute-start(bf16[64,512]{1,0:T(8,128)(2,1)S(1)} %sum.1.refs_0_), channel_id=1, source_target_pairs={{0,128},{64,192},{128,0},{192,64},{1,129},{65,193},{129,1},{193,65... | collective-permute-start | bytes 196616 | tf_op jit(solution)/shard_map/ppermute | solution.py:285
  104.2 4.3 %collective-permute-start.10 = (bf16[64,512]{1,0:T(8,128)(2,1)S(1)}, bf16[64,512]{1,0:T(8,128)(2,1)S(1)}, u32[]{:S(2)}, u32[]{:S(2)}) collective-permute-start(bf16[64,512]{1,0:T(8,128)(2,1)S(1)} %sum.1.refs_0_), channel_id=1, source_target_pairs={{0,64},{64,128},{128,192},{192,0},{1,65},{65,129},{129,193},{193,1... | collective-permute-start | bytes 196616 | tf_op jit(solution)/shard_map/ppermute | solution.py:285
  109.1 5.3 %collective-permute-start.13 = (bf16[256,512]{1,0:T(8,128)(2,1)S(1)}, bf16[256,512]{1,0:T(8,128)(2,1)S(1)}, u32[]{:S(2)}, u32[]{:S(2)}) collective-permute-start(bf16[256,512]{1,0:T(8,128)(2,1)S(1)} %stack.17.mine_ref), channel_id=1, source_target_pairs={{0,4},{4,0},{1,5},{5,1},{2,6},{6,2},{3,7},{7,3},{8,12},{12,8},{9,1... | collective-permute-start | bytes 786440 | tf_op jit(solution)/shard_map/ppermute | solution.py:291

commit v8 on v7

--- a/solution.py
+++ b/solution.py
@@ -59,43 +59,48 @@
     def fill(at, carry):
         start = pl.multiple_of(at * step, step)
         wanted = jnp.broadcast_to(row_ref[:, pl.ds(start, step)], (step, step)).T
+        within = jnp.where((wanted & (step - 1)) == lane, 1.0, 0.0).astype(BF16)
+        block = (wanted >> (step.bit_length() - 1)).astype(F32).astype(BF16)
+        nothing = jnp.zeros_like(within)
         picks = jnp.concatenate(
-            [
-                jnp.where(wanted == lane + low, 1.0, 0.0).astype(BF16)
-                for low in range(0, rows, step)
-            ],
-            axis=1,
+            [jnp.where(block == BF16(at), within, nothing) for at in range(rows // step)], axis=1
         )
         out_ref[pl.ds(start, step), :] = dot(picks, x_ref[...]).astype(BF16)
         return carry
 
-    lax.fori_loop(0, out_ref.shape[0] // step, fill, 0, unroll=4)
+    lax.fori_loop(0, out_ref.shape[0] // step, fill, 0, unroll=8)
 
 
 def count_body(
-    self_ref, near_ref, degree_ref, mask_ref, seed_ref, seed_near_ref,
-    self_table, near_table, seed_table, seed_near_table, live_ref,
+    self_ref, near_ref, degree_ref, mask_ref, seed_ref, seed_near_ref, seed_table, seed_near_table,
+    *refs,
 ):
-    slots, mids = near_table.shape
+    tables, live_ref = refs[:-1], refs[-1]
+    tall, mids = tables[0].shape
     fan = near_ref.shape[0]
     step = 32
     live = lax.broadcasted_iota(I32, (fan, mids), 0) < degree_ref[...]
     live_ref[...] = jnp.where(live, near_ref[...], -1)
     own = self_ref[...]
 
-    def fill(at, carry):
-        span = pl.ds(pl.multiple_of(at * step, step), step)
-        line = lax.broadcasted_iota(I32, (step, mids), 0) + at * step
-        total = jnp.zeros((step, mids), F32)
-        for j in range(fan):
-            total = total + jnp.where(live_ref[j : j + 1, :] == line, 1.0, 0.0)
-        filled = mask_ref[span, :].astype(F32)
-        filled = jnp.concatenate([filled] * (mids // filled.shape[1]), axis=1)
-        near_table[span, :] = (total * filled).astype(BF16)
-        self_table[span, :] = jnp.where(own == line, filled, 0.0).astype(BF16)
-        return carry
-
-    lax.fori_loop(0, slots // step, fill, 0)
+    for index in range(len(tables) // 2):
+        self_table, near_table = tables[2 * index], tables[2 * index + 1]
+        low = index * tall
+
+        def fill(at, carry, self_table=self_table, near_table=near_table, low=low):
+            start = pl.multiple_of(at * step, step)
+            span = pl.ds(start, step)
+            line = lax.broadcasted_iota(I32, (step, mids), 0) + (low + start)
+            total = jnp.zeros((step, mids), F32)
+            for j in range(fan):
+                total = total + jnp.where(live_ref[j : j + 1, :] == line, 1.0, 0.0)
+            filled = mask_ref[pl.ds(low + start, step), :].astype(F32)
+            filled = jnp.concatenate([filled] * (mids // filled.shape[1]), axis=1)
+            near_table[span, :] = (total * filled).astype(BF16)
+            self_table[span, :] = jnp.where(own == line, filled, 0.0).astype(BF16)
+            return carry
+
+        lax.fori_loop(0, tall // step, fill, 0)
     seeds = seed_table.shape[1]
     line = lax.broadcasted_iota(I32, (mids, seeds), 0)
     seed_table[...] = jnp.where(seed_ref[...] == line, 1.0, 0.0).astype(BF16)
@@ -106,25 +111,30 @@
 
 
 def gather_body(
-    place_ref, x_ref, self_far, near_far, degree_ref, weight_self_ref, weight_near_ref, *refs, slices
+    place_ref, x_ref, degree_ref, weight_self_ref, weight_near_ref, *refs, slices, pieces
 ):
-    own_ref, near_ref = refs[:2]
-    out_refs = refs[2 : 2 + slices]
-    self_table, near_table, held_ref, sems = refs[2 + slices :]
-    pieces, step, _ = self_table.shape
-    copies = []
-    for piece in range(pieces):
-        for side, (far, ref) in enumerate(((self_far, self_table), (near_far, near_table))):
-            copy = pltpu.make_async_copy(far.at[piece], ref.at[piece], sems.at[side, piece])
-            copy.start()
-            copies.append(copy)
+    tables, fars = refs[:pieces], refs[pieces : 2 * pieces]
+    own_ref, near_ref = refs[2 * pieces : 2 * pieces + 2]
+    out_refs = refs[2 * pieces + 2 : 2 * pieces + 2 + slices]
+    held_ref, table_ref, sems = refs[2 * pieces + 2 + slices :]
+    copies = [
+        pltpu.make_async_copy(far, table_ref.at[at], sems.at[at]) for at, far in enumerate(fars)
+    ]
+    for copy in copies:
+        copy.start()
+    step = tables[0].shape[0]
     own, near = 0.0, 0.0
     for piece in range(pieces):
         turned = x_ref[pl.ds(piece * step, step), :].T
-        copies[2 * piece].wait()
-        own = own + dot(turned, self_table[piece])
-        copies[2 * piece + 1].wait()
-        near = near + dot(turned, near_table[piece])
+        if 2 * piece < pieces:
+            own = own + dot(turned, tables[2 * piece][...])
+            near = near + dot(turned, tables[2 * piece + 1][...])
+        else:
+            at = 2 * piece - pieces
+            copies[at].wait()
+            own = own + dot(turned, table_ref[at])
+            copies[at + 1].wait()
+            near = near + dot(turned, table_ref[at + 1])
     own = own.astype(BF16)
     near = (near / degree_ref[...].astype(F32)).astype(BF16)
     own_ref[...] = own
@@ -176,7 +186,7 @@
     )
 
 
-def weight_body(place_ref, own_ref, near_ref, cotangent_ref, *refs, half, count):
+def weight_body(place_ref, core_ref, own_ref, near_ref, cotangent_ref, *refs, half, count):
     grads_refs, (keep_ref, give_ref, grads_held, held_ref) = refs[:-4], refs[-4:]
     slices = len(grads_refs)
     cores, tall, cols = held_ref.shape
@@ -205,15 +215,15 @@
                 held_ref[
                     core, 2 * x * deep : (2 * x + 1) * deep, side * hidden : (side + 1) * hidden
                 ] = part[low : low + deep]
-    keep_ref[...] = held_ref[place_ref[1]]
-    give_ref[...] = held_ref[1 - place_ref[1]].astype(BF16)
+    keep_ref[...] = held_ref[core_ref[0]]
+    give_ref[...] = held_ref[1 - core_ref[0]].astype(BF16)
 
 
 def split_body(place_ref, keep_ref, got_ref, *out_refs):
     count = len(out_refs)
     step = out_refs[0].shape[0]
     for shift, out_ref in enumerate(out_refs):
-        at = lax.rem(place_ref[2] + shift, count)
+        at = lax.rem(place_ref[0] + shift, count)
         span = pl.ds(pl.multiple_of(at * step, step), step)
         out_ref[...] = (keep_ref[span, :] + got_ref[span, :].astype(F32)).astype(BF16)
 
@@ -237,7 +247,7 @@
     count = len(parts)
     step = parts[0].shape[0]
     for shift, part in enumerate(parts):
-        at = lax.rem(place_ref[2] + count - shift, count)
+        at = lax.rem(place_ref[0] + count - shift, count)
         out_ref[pl.ds(pl.multiple_of(at * step, step), step), :] = part[...]
 
 
@@ -250,7 +260,7 @@
     mine, other = mine_ref[...].astype(F32), other_ref[...].astype(F32)
     refs = ((first_self_ref, first_near_ref), (second_self_ref, second_near_ref))
     for core in range(cores):
-        value = jnp.where(place_ref[1] == core, mine, other)
+        value = jnp.where(place_ref[0] == core, mine, other)
         for x in range(count):
             low = (core * count + x) * deep
             for layer in range(2):
@@ -319,7 +329,9 @@
     seeds, fan_two = seed_neighbor.shape
     out_cols = second_self.shape[1]
     pieces = 4
-    place = jnp.stack([lax.axis_index(axis) for axis in ("feat", "core", "x")]).astype(I32)
+    at_feat, at_core, at_x = (
+        lax.axis_index(axis).astype(I32).reshape(1) for axis in ("feat", "core", "x")
+    )
 
     (picked,) = call(
         pick_body, [((slots, slice_cols), BF16)], (send_rows, features), "pick",
@@ -333,9 +345,9 @@
 
     slot_at = lax.broadcasted_iota(I32, (peers, capacity, 128), 1)
     mask = (slot_at < arrive_count.reshape(peers, 1, 1)).astype(BF16).reshape(slots, 128)
-    self_table, near_table, seed_table, seed_near_table = call(
+    seed_table, seed_near_table, *tables = call(
         count_body,
-        [((slots, mids), BF16), ((slots, mids), BF16), ((mids, seeds), BF16), ((mids, seeds), BF16)],
+        [((mids, seeds), BF16)] * 2 + [((slots // pieces, mids), BF16)] * (2 * pieces),
         (
             self_slot.reshape(1, mids), neighbor_slot.T, degree.reshape(1, mids), mask,
             seed_self.reshape(1, seeds), seed_neighbor.T,
@@ -346,18 +358,14 @@
     routed, seed_table, bias = lax.optimization_barrier((routed, seed_table, bias))
 
     own_rows, near_rows, *pre = call(
-        functools.partial(gather_body, slices=slices),
+        functools.partial(gather_body, slices=slices, pieces=pieces),
         [((slice_cols, mids), BF16)] * 2 + [((half, mids), BF16)] * slices,
-        (
-            place, routed, self_table.reshape(pieces, slots // pieces, mids),
-            near_table.reshape(pieces, slots // pieces, mids), degree.reshape(1, mids),
-            first_self, first_neighbor,
-        ),
-        "gather", 4 * slots * slice_cols * mids, 4 * slots * mids, scalars=1, far=(2, 3),
+        (at_feat, routed, degree.reshape(1, mids), first_self, first_neighbor, *tables),
+        "gather", 4 * slots * slice_cols * mids, 4 * slots * mids, scalars=1,
+        far=range(5 + pieces, 5 + 2 * pieces),
         scratch=[
-            pltpu.VMEM((pieces, slots // pieces, mids), BF16),
-            pltpu.VMEM((pieces, slots // pieces, mids), BF16),
-            pltpu.VMEM((slices, half, mids), BF16), pltpu.SemaphoreType.DMA((2, pieces)),
+            pltpu.VMEM((slices, half, mids), BF16),
+            pltpu.VMEM((pieces, slots // pieces, mids), BF16), pltpu.SemaphoreType.DMA((pieces,)),
         ],
     )
     pre = shifted(pre, "feat", slices)
@@ -365,7 +373,7 @@
     (grads,) = call(
         functools.partial(owner_body, fan_two=fan_two), [((half + tall, mids), BF16)],
         (
-            place, bias, seed_table, seed_near_table, second_self, second_neighbor, cotangent, *pre,
+            at_feat, bias, seed_table, seed_near_table, second_self, second_neighbor, cotangent, *pre,
         ),
         "owner", 16 * half * seeds * mids, 8 * half * mids, scalars=1,
     )
@@ -374,15 +382,15 @@
     keep, give = call(
         functools.partial(weight_body, half=half, count=count_x),
         [((tall, 2 * hidden), F32), ((tall, 2 * hidden), BF16)],
-        (place, own_rows, near_rows, cotangent, *grads), "weight",
+        (at_feat, at_core, own_rows, near_rows, cotangent, *grads), "weight",
         4 * slice_cols * mids * hidden, 8 * slice_cols * mids,
         scratch=[pltpu.VMEM((hidden, mids), BF16), pltpu.VMEM((cores, tall, 2 * hidden), F32)],
-        scalars=1,
+        scalars=2,
     )
     got = swapped(give, "core", cores, 1)
     shard = (tall // count_x, 2 * hidden)
     parts = call(
-        split_body, [(shard, BF16)] * count_x, (place, keep, got), "split", 0, 16 * tall * hidden,
+        split_body, [(shard, BF16)] * count_x, (at_x, keep, got), "split", 0, 16 * tall * hidden,
         scalars=1,
     )
     (mixed,) = call(
@@ -392,19 +400,19 @@
     mixed = exchange(mixed, "z")
     (seed_embedding,) = call(
         functools.partial(embed_body, half=half), [((seeds, out_cols), BF16)],
-        (place, second_self, second_neighbor, *grads), "embed",
+        (at_feat, second_self, second_neighbor, *grads), "embed",
         4 * seeds * hidden * out_cols, 8 * seeds * hidden, scalars=1,
     )
     mixed, seed_embedding = lax.optimization_barrier((mixed, seed_embedding))
     (mixed,) = call(sum_body, [(shard, BF16)], (mixed,), "sum", 0, 8 * tall * hidden)
     (mixed,) = call(
         stack_body, [((tall, 2 * hidden), BF16)],
-        (place, *shifted([mixed] * count_x, "x", count_x)), "stack", 0, 8 * tall * hidden, scalars=1,
+        (at_x, *shifted([mixed] * count_x, "x", count_x)), "stack", 0, 8 * tall * hidden, scalars=1,
     )
     grad_first_self, grad_first_neighbor, grad_second_self, grad_second_neighbor = call(
         functools.partial(finish_body, count=count_x, cores=cores),
         [((slice_cols, hidden), F32)] * 2 + [((hidden, out_cols), F32)] * 2,
-        (place, mixed, swapped(mixed, "core", cores, 1)), "finish", 0, 24 * tall * hidden, scalars=1,
+        (at_core, mixed, swapped(mixed, "core", cores, 1)), "finish", 0, 24 * tall * hidden, scalars=1,
     )
     return (
         seed_embedding,

time: 116 us -> 119 us (1.026)
  local copies, waits for them, and re-layouts: 3.29 us -> 12.9 us
  Pallas kernels: 26.9 us -> 22.6 us
  waiting for transfers between devices: 44.9 us -> 43 us
    unnamed x28 -> x50, local copies, waits for them, and re-layouts: 2.73 us -> 12.3 us
    pallas_call x11, Pallas kernels: 26.9 us -> 22.6 us  [call(): pl.pallas_call(body, out_shape=[jax.ShapeDtypeStruct(shape, dtype) for sh...]
    all_to_all x2, waiting for transfers between devices: 28.5 us -> 26.1 us  [exchange(): return lax.all_to_all(value, axis, split_axis=0, concat_axis=0, tiled=True)]
  transfers between devices with their start and end apart: 16 -> 16, of which waited for: 12 -> 12; matrix products, arithmetic and copies ran while one was open for 1% -> 1% of each run, Pallas kernels for 11% -> 10%
where the time goes in v8:
time: 119 us
  waiting for transfers between devices  43 us (36%)
  starting transfers between devices  39.2 us (33%)
  Pallas kernels  22.6 us (19%)
  local copies, waits for them, and re-layouts  12.9 us (11%)
    all_to_all x2, waiting for transfers between devices, exchange(): return lax.all_to_all(value, axis, split_axis=0, concat_axis=0, tiled=True)  26.1 us
    pallas_call x11, Pallas kernels, call(): pl.pallas_call(body, out_shape=[jax.ShapeDtypeStruct(shape, dtype) for sh...  22.6 us
    all_to_all x2, starting transfers between devices, exchange(): return lax.all_to_all(value, axis, split_axis=0, concat_axis=0, tiled=True)  16.5 us
    ppermute x12, starting transfers between devices, shifted(): lax.ppermute(piece, axis, [(at, (at + shift) % count) for at in range(cou...  15.1 us
    ppermute x12, waiting for transfers between devices, shifted(): lax.ppermute(piece, axis, [(at, (at + shift) % count) for at in range(cou...  14.6 us
    unnamed x50, local copies, waits for them, and re-layouts  12.3 us
    ppermute x2, starting transfers between devices, swapped(): return lax.ppermute(value, axis, [(at, at ^ step) for at in range(count)])  7.58 us
  transfers between devices with their start and end apart: 16, of which 12 were waited for; matrix products, arithmetic and copies ran while one was open for 1% of the time, Pallas kernels for 10%

profile of v8, /device:TPU:1, one launch (start us, length us, event | category | flops | bytes accessed | tf_op | source)
XLA Modules:
  0.0 118.5 jit_solution(10247908673900594275)
XLA Ops:
  0.6 4.2 %pick.1 = bf16[2048,256]{1,0:T(8,128)(2,1)} custom-call(s32[1,2048]{1,0:T(1,128)} %row_far.1, bf16[1536,256]{1,0:T(8,128)(2,1)} %x_far.1), custom_call_target="tpu_custom_call" | custom-call | flops 1610612736 | bytes 6291456 | tf_op jit(solution)/shard_map/pick/pallas_call | solution.py:31
  4.9 13.0 %all-to-all-start = ((bf16[64,32,256]{2,1,0:T(8,128)(2,1)}), bf16[64,32,256]{2,1,0:T(8,128)(2,1)S(1)}, u32[]{:S(2)}, u32[]{:S(2)}) async-start(bf16[64,32,256]{2,1,0:T(8,128)(2,1)} %bitcast.3), calls=%async_computation | async-start | bytes 2097152 | tf_op jit(solution)/shard_map/all_to_all | solution.py:288
  17.9 0.6 copy-done.24
  19.6 11.3 %count.1 = (bf16[512,128]{1,0:T(8,128)(2,1)S(1)}, bf16[512,128]{1,0:T(8,128)(2,1)S(1)}, bf16[512,512]{1,0:T(8,128)(2,1)S(1)}, bf16[512,512]{1,0:T(8,128)(2,1)S(1...) custom-call(s32[1,512]{1,0:T(1,128)S(1)} %bitcast.17, ...), custom_call_target="tpu_custom_call" | custom-call | bytes 16777216 | tf_op jit(solution)/shard_map/count/pallas_call | solution.py:31
  30.8 0.8 copy-done.2
  31.7 0.8 copy-done.3
  32.5 0.8 copy-done.4
  33.3 0.8 copy-done.5
  34.1 0.7 copy-done.10
  34.7 0.7 copy-done.12
  35.4 11.1 %all-to-all-done = bf16[64,32,256]{2,1,0:T(8,128)(2,1)S(1)} async-done(((bf16[64,32,256]{2,1,0:T(8,128)(2,1)}), bf16[64,32,256]{2,1,0:T(8,128)(2,1)S(1)}, u32[]{:S(2)}, u32[]{:S(2)}) %all-to-all-start) | async-done | bytes 1048608 | tf_op jit(solution)/shard_map/all_to_all | solution.py:288
  46.5 0.9 copy-done.14
  47.4 0.9 copy-done.15
  48.3 3.3 %gather.1 = (bf16[256,512]{1,0:T(8,128)(2,1)S(1)}, bf16[256,512]{1,0:T(8,128)(2,1)S(1)}, bf16[64,512]{1,0:T(8,128)(2,1)S(1)}, bf16[64,512]{1,0:T(8,128)(2,1)}, b...) custom-call(s32[1]{0:T(128)} %bitcast.1.place_ref, bf16[2048,256]{1,0:T(8,128)(2,1)S(1)} %bitcast.12, ...), custom_call_target="tpu_custom_call" | custom-call | flops 1073741824 | bytes 4194304 | tf_op jit(solution)/shard_map/gather/pallas_call | solution.py:31
  51.5 0.7 copy-done.6
  52.2 0.6 copy-done.17
  52.9 1.3 %collective-permute-start = (bf16[64,512]{1,0:T(8,128)(2,1)}, bf16[64,512]{1,0:T(8,128)(2,1)S(1)}, u32[]{:S(2)}, u32[]{:S(2)}) collective-permute-start(bf16[64,512]{1,0:T(8,128)(2,1)} %get-tuple-element.52), channel_id=1, source_target_pairs={{0,1},{1,2},{2,3},{3,0},{4,5},{5,6},{6,7},{7,4},{8,9},{9,10},{10,1... | collective-permute-start | bytes 196616 | tf_op jit(solution)/shard_map/ppermute | solution.py:295
  54.2 2.6 %collective-permute-start.1 = (bf16[64,512]{1,0:T(8,128)(2,1)}, bf16[64,512]{1,0:T(8,128)(2,1)S(1)}, u32[]{:S(2)}, u32[]{:S(2)}) collective-permute-start(bf16[64,512]{1,0:T(8,128)(2,1)} %get-tuple-element.53), channel_id=1, source_target_pairs={{0,2},{1,3},{2,0},{3,1},{4,6},{5,7},{6,4},{7,5},{8,10},{9,11},{10,... | collective-permute-start | bytes 196616 | tf_op jit(solution)/shard_map/ppermute | solution.py:295
  56.8 1.1 collective-permute-start.2
  58.0 2.6 %collective-permute-done.1.refs_2_ = bf16[64,512]{1,0:T(8,128)(2,1)S(1)} collective-permute-done((bf16[64,512]{1,0:T(8,128)(2,1)}, bf16[64,512]{1,0:T(8,128)(2,1)S(1)}, u32[]{:S(2)}, u32[]{:S(2)}) %collective-permute-start.1) | collective-permute-done | bytes 65568 | tf_op jit(solution)/shard_map/ppermute | solution.py:295
  60.6 0.8 copy-done.8
  61.4 0.9 copy-done.11
  62.3 0.9 copy-done.13
  63.2 0.8 copy-done.18
  64.5 1.9 %collective-permute-start.5 = (bf16[96,512]{1,0:T(8,128)(2,1)S(1)}, bf16[96,512]{1,0:T(8,128)(2,1)S(1)}, u32[]{:S(2)}, u32[]{:S(2)}) collective-permute-start(bf16[96,512]{1,0:T(8,128)(2,1)S(1)} %owner.1.refs_0_), channel_id=1, source_target_pairs={{0,3},{1,0},{2,1},{3,2},{4,7},{5,4},{6,5},{7,6},{8,11},{9,8},{10,9... | collective-permute-start | bytes 294920 | tf_op jit(solution)/shard_map/ppermute | solution.py:295
  66.6 0.8 collective-permute-start.3
  67.3 1.1 collective-permute-done.5.refs_3_
  68.5 2.9 %collective-permute-done.4.refs_2_ = bf16[96,512]{1,0:T(8,128)(2,1)S(1)} collective-permute-done((bf16[96,512]{1,0:T(8,128)(2,1)S(1)}, bf16[96,512]{1,0:T(8,128)(2,1)S(1)}, u32[]{:S(2)}, u32[]{:S(2)}) %collective-permute-start.4) | collective-permute-done | bytes 98336 | tf_op jit(solution)/shard_map/ppermute | solution.py:295
  71.4 0.9 collective-permute-done.3.refs_1_
  72.3 0.5 weight.1
  72.8 3.4 %collective-permute-start.6 = (bf16[256,512]{1,0:T(8,128)(2,1)S(1)}, bf16[256,512]{1,0:T(8,128)(2,1)S(1)}, u32[]{:S(2)}, u32[]{:S(2)}) collective-permute-start(bf16[256,512]{1,0:T(8,128)(2,1)S(1)} %get-tuple-element.56), channel_id=1, source_target_pairs={{0,4},{4,0},{1,5},{5,1},{2,6},{6,2},{3,7},{7,3},{8,12},{12,8},{9,1... | collective-permute-start | bytes 786440 | tf_op jit(solution)/shard_map/ppermute | solution.py:301
  76.2 1.2 collective-permute-done.6.got_ref
  77.4 1.7 %collective-permute-start.7 = (bf16[64,512]{1,0:T(8,128)(2,1)S(1)}, bf16[64,512]{1,0:T(8,128)(2,1)S(1)}, u32[]{:S(2)}, u32[]{:S(2)}) collective-permute-start(bf16[64,512]{1,0:T(8,128)(2,1)S(1)} %get-tuple-element.58), channel_id=1, source_target_pairs={{0,64},{64,128},{128,192},{192,0},{1,65},{65,129},{129,193},{193,1... | collective-permute-start | bytes 196616 | tf_op jit(solution)/shard_map/ppermute | solution.py:295
  79.1 2.0 %collective-permute-start.8 = (bf16[64,512]{1,0:T(8,128)(2,1)S(1)}, bf16[64,512]{1,0:T(8,128)(2,1)S(1)}, u32[]{:S(2)}, u32[]{:S(2)}) collective-permute-start(bf16[64,512]{1,0:T(8,128)(2,1)S(1)} %get-tuple-element.59), channel_id=1, source_target_pairs={{0,128},{64,192},{128,0},{192,64},{1,129},{65,193},{129,1},{193,65... | collective-permute-start | bytes 196616 | tf_op jit(solution)/shard_map/ppermute | solution.py:295
  81.2 1.1 collective-permute-start.9
  82.2 2.5 %collective-permute-done.8.refs_2_ = bf16[64,512]{1,0:T(8,128)(2,1)S(1)} collective-permute-done((bf16[64,512]{1,0:T(8,128)(2,1)S(1)}, bf16[64,512]{1,0:T(8,128)(2,1)S(1)}, u32[]{:S(2)}, u32[]{:S(2)}) %collective-permute-start.8) | collective-permute-done | bytes 65568 | tf_op jit(solution)/shard_map/ppermute | solution.py:295
  84.7 0.8 spread.1
  85.6 3.5 %all-to-all-start.1 = ((bf16[8,64,512]{2,1,0:T(8,128)(2,1)}), bf16[8,64,512]{2,1,0:T(8,128)(2,1)S(1)}, u32[]{:S(2)}, u32[]{:S(2)}) async-start(bf16[8,64,512]{2,1,0:T(8,128)(2,1)} %spread.1), calls=%async_computation.1 | async-start | bytes 1048576 | tf_op jit(solution)/shard_map/all_to_all | solution.py:288
  89.1 1.0 embed.1
  90.0 15.0 %all-to-all-done.1.parts_ref = bf16[8,64,512]{2,1,0:T(8,128)(2,1)S(1)} async-done(((bf16[8,64,512]{2,1,0:T(8,128)(2,1)}), bf16[8,64,512]{2,1,0:T(8,128)(2,1)S(1)}, u32[]{:S(2)}, u32[]{:S(2)}) %all-to-all-start.1) | async-done | bytes 524320 | tf_op jit(solution)/shard_map/all_to_all | solution.py:288
  105.1 1.7 %collective-permute-start.12 = (bf16[64,512]{1,0:T(8,128)(2,1)S(1)}, bf16[64,512]{1,0:T(8,128)(2,1)S(1)}, u32[]{:S(2)}, u32[]{:S(2)}) collective-permute-start(bf16[64,512]{1,0:T(8,128)(2,1)S(1)} %sum.1.refs_0_), channel_id=1, source_target_pairs={{0,192},{64,0},{128,64},{192,128},{1,193},{65,1},{129,65},{193,129... | collective-permute-start | bytes 196616 | tf_op jit(solution)/shard_map/ppermute | solution.py:295
  106.8 0.8 collective-permute-start.11
  107.6 0.7 collective-permute-done.12.refs_3_
  108.3 3.1 %collective-permute-done.11.refs_2_ = bf16[64,512]{1,0:T(8,128)(2,1)S(1)} collective-permute-done((bf16[64,512]{1,0:T(8,128)(2,1)S(1)}, bf16[64,512]{1,0:T(8,128)(2,1)S(1)}, u32[]{:S(2)}, u32[]{:S(2)}) %collective-permute-start.11) | collective-permute-done | bytes 65568 | tf_op jit(solution)/shard_map/ppermute | solution.py:295
  111.4 0.7 collective-permute-done.10.refs_1_
  112.1 4.2 %collective-permute-start.13 = (bf16[256,512]{1,0:T(8,128)(2,1)S(1)}, bf16[256,512]{1,0:T(8,128)(2,1)S(1)}, u32[]{:S(2)}, u32[]{:S(2)}) collective-permute-start(bf16[256,512]{1,0:T(8,128)(2,1)S(1)} %stack.1.mine_ref), channel_id=1, source_target_pairs={{0,4},{4,0},{1,5},{5,1},{2,6},{6,2},{3,7},{7,3},{8,12},{12,8},{9,1... | collective-permute-start | bytes 786440 | tf_op jit(solution)/shard_map/ppermute | solution.py:301
  116.4 1.2 collective-permute-done.13.other_ref
  117.5 1.0 finish.1
  (49 shorter events, 2.0 us)
Async XLA Ops:
  4.9 41.6 %all-to-all-start = ((bf16[64,32,256]{2,1,0:T(8,128)(2,1)}), bf16[64,32,256]{2,1,0:T(8,128)(2,1)S(1)}, u32[]{:S(2)}, u32[]{:S(2)}) async-start(bf16[64,32,256]{2,1,0:T(8,128)(2,1)} %bitcast.3), calls=%async_computation | async-start | bytes 2097152 | tf_op jit(solution)/shard_map/all_to_all | solution.py:288
  17.9 0.7 copy-start.24
  18.7 0.8 copy-start.16
  18.7 0.8 copy-start.19
  18.7 0.8 copy-start.20
  18.7 0.8 copy-start.21
  18.7 0.8 copy-start.22
  30.8 0.8 copy-start.2
  31.7 0.8 copy-start.3
  32.5 0.8 copy-start.4
  33.3 0.8 copy-start.5
  34.1 0.7 copy-start.10
  34.7 0.7 copy-start.12
  46.4 0.9 copy-start.14
  47.4 0.9 copy-start.15
  48.3 9.6 %copy-start.23 = (f32[256]{0:T(256)S(1)}, f32[256]{0:T(256)}, u32[]{:S(2)}) copy-start(f32[256]{0:T(256)} %param.17) | copy-start | bytes 3076
  48.3 12.3 %copy-start.1 = (bf16[256,256]{1,0:T(8,128)(2,1)S(1)}, bf16[256,256]{1,0:T(8,128)(2,1)}, u32[]{:S(2)}) copy-start(bf16[256,256]{1,0:T(8,128)(2,1)} %second_near_ref.3) | copy-start | bytes 393220
  51.5 0.7 copy-start.6
  52.2 0.6 copy-start.17
  52.9 7.7 %copy-start = (bf16[256,256]{1,0:T(8,128)(2,1)S(1)}, bf16[256,256]{1,0:T(8,128)(2,1)}, u32[]{:S(2)}) copy-start(bf16[256,256]{1,0:T(8,128)(2,1)} %second_self_ref.3) | copy-start | bytes 393220
  52.9 5.2 %collective-permute-start = (bf16[64,512]{1,0:T(8,128)(2,1)}, bf16[64,512]{1,0:T(8,128)(2,1)S(1)}, u32[]{:S(2)}, u32[]{:S(2)}) collective-permute-start(bf16[64,512]{1,0:T(8,128)(2,1)} %get-tuple-element.52), channel_id=1, source_target_pairs={{0,1},{1,2},{2,3},{3,0},{4,5},{5,6},{6,7},{7,4},{8,9},{9,10},{10,1... | collective-permute-start | bytes 196616 | tf_op jit(solution)/shard_map/ppermute | solution.py:295
  54.2 6.4 %collective-permute-start.1 = (bf16[64,512]{1,0:T(8,128)(2,1)}, bf16[64,512]{1,0:T(8,128)(2,1)S(1)}, u32[]{:S(2)}, u32[]{:S(2)}) collective-permute-start(bf16[64,512]{1,0:T(8,128)(2,1)} %get-tuple-element.53), channel_id=1, source_target_pairs={{0,2},{1,3},{2,0},{3,1},{4,6},{5,7},{6,4},{7,5},{8,10},{9,11},{10,... | collective-permute-start | bytes 196616 | tf_op jit(solution)/shard_map/ppermute | solution.py:295
  56.8 3.8 %collective-permute-start.2 = (bf16[64,512]{1,0:T(8,128)(2,1)}, bf16[64,512]{1,0:T(8,128)(2,1)S(1)}, u32[]{:S(2)}, u32[]{:S(2)}) collective-permute-start(bf16[64,512]{1,0:T(8,128)(2,1)} %get-tuple-element.54), channel_id=1, source_target_pairs={{0,3},{1,0},{2,1},{3,2},{4,7},{5,4},{6,5},{7,6},{8,11},{9,8},{10,9... | collective-permute-start | bytes 196616 | tf_op jit(solution)/shard_map/ppermute | solution.py:295
  60.6 0.8 copy-start.8
  61.4 0.9 copy-start.11
  62.3 0.9 copy-start.13
  63.2 0.8 copy-start.18
  64.1 8.2 %copy-start.7 = (bf16[256,512]{1,0:T(8,128)(2,1)S(1)}, bf16[256,512]{1,0:T(8,128)(2,1)}, u32[]{:S(2)}) copy-start(bf16[256,512]{1,0:T(8,128)(2,1)} %copy-done.6) | copy-start | bytes 786436
  64.1 8.2 %copy-start.9 = (bf16[128,256]{1,0:T(8,128)(2,1)S(1)}, bf16[128,256]{1,0:T(8,128)(2,1)}, u32[]{:S(2)}) copy-start(bf16[128,256]{1,0:T(8,128)(2,1)} %cotangent_ref.3) | copy-start | bytes 196612
  64.5 4.0 %collective-permute-start.5 = (bf16[96,512]{1,0:T(8,128)(2,1)S(1)}, bf16[96,512]{1,0:T(8,128)(2,1)S(1)}, u32[]{:S(2)}, u32[]{:S(2)}) collective-permute-start(bf16[96,512]{1,0:T(8,128)(2,1)S(1)} %owner.1.refs_0_), channel_id=1, source_target_pairs={{0,3},{1,0},{2,1},{3,2},{4,7},{5,4},{6,5},{7,6},{8,11},{9,8},{10,9... | collective-permute-start | bytes 294920 | tf_op jit(solution)/shard_map/ppermute | solution.py:295
  66.4 5.1 %collective-permute-start.4 = (bf16[96,512]{1,0:T(8,128)(2,1)S(1)}, bf16[96,512]{1,0:T(8,128)(2,1)S(1)}, u32[]{:S(2)}, u32[]{:S(2)}) collective-permute-start(bf16[96,512]{1,0:T(8,128)(2,1)S(1)} %owner.1.refs_0_), channel_id=1, source_target_pairs={{0,2},{1,3},{2,0},{3,1},{4,6},{5,7},{6,4},{7,5},{8,10},{9,11},{10,... | collective-permute-start | bytes 294920 | tf_op jit(solution)/shard_map/ppermute | solution.py:295
  66.6 5.7 %collective-permute-start.3 = (bf16[96,512]{1,0:T(8,128)(2,1)S(1)}, bf16[96,512]{1,0:T(8,128)(2,1)S(1)}, u32[]{:S(2)}, u32[]{:S(2)}) collective-permute-start(bf16[96,512]{1,0:T(8,128)(2,1)S(1)} %owner.1.refs_0_), channel_id=1, source_target_pairs={{0,1},{1,2},{2,3},{3,0},{4,5},{5,6},{6,7},{7,4},{8,9},{9,10},{10,1... | collective-permute-start | bytes 294920 | tf_op jit(solution)/shard_map/ppermute | solution.py:295
  72.8 4.5 %collective-permute-start.6 = (bf16[256,512]{1,0:T(8,128)(2,1)S(1)}, bf16[256,512]{1,0:T(8,128)(2,1)S(1)}, u32[]{:S(2)}, u32[]{:S(2)}) collective-permute-start(bf16[256,512]{1,0:T(8,128)(2,1)S(1)} %get-tuple-element.56), channel_id=1, source_target_pairs={{0,4},{4,0},{1,5},{5,1},{2,6},{6,2},{3,7},{7,3},{8,12},{12,8},{9,1... | collective-permute-start | bytes 786440 | tf_op jit(solution)/shard_map/ppermute | solution.py:301
  77.4 4.9 %collective-permute-start.7 = (bf16[64,512]{1,0:T(8,128)(2,1)S(1)}, bf16[64,512]{1,0:T(8,128)(2,1)S(1)}, u32[]{:S(2)}, u32[]{:S(2)}) collective-permute-start(bf16[64,512]{1,0:T(8,128)(2,1)S(1)} %get-tuple-element.58), channel_id=1, source_target_pairs={{0,64},{64,128},{128,192},{192,0},{1,65},{65,129},{129,193},{193,1... | collective-permute-start | bytes 196616 | tf_op jit(solution)/shard_map/ppermute | solution.py:295
  79.1 5.6 %collective-permute-start.8 = (bf16[64,512]{1,0:T(8,128)(2,1)S(1)}, bf16[64,512]{1,0:T(8,128)(2,1)S(1)}, u32[]{:S(2)}, u32[]{:S(2)}) collective-permute-start(bf16[64,512]{1,0:T(8,128)(2,1)S(1)} %get-tuple-element.59), channel_id=1, source_target_pairs={{0,128},{64,192},{128,0},{192,64},{1,129},{65,193},{129,1},{193,65... | collective-permute-start | bytes 196616 | tf_op jit(solution)/shard_map/ppermute | solution.py:295
  81.2 3.6 %collective-permute-start.9 = (bf16[64,512]{1,0:T(8,128)(2,1)S(1)}, bf16[64,512]{1,0:T(8,128)(2,1)S(1)}, u32[]{:S(2)}, u32[]{:S(2)}) collective-permute-start(bf16[64,512]{1,0:T(8,128)(2,1)S(1)} %get-tuple-element.60), channel_id=1, source_target_pairs={{0,192},{64,0},{128,64},{192,128},{1,193},{65,1},{129,65},{193,129... | collective-permute-start | bytes 196616 | tf_op jit(solution)/shard_map/ppermute | solution.py:295
  85.6 19.4 %all-to-all-start.1 = ((bf16[8,64,512]{2,1,0:T(8,128)(2,1)}), bf16[8,64,512]{2,1,0:T(8,128)(2,1)S(1)}, u32[]{:S(2)}, u32[]{:S(2)}) async-start(bf16[8,64,512]{2,1,0:T(8,128)(2,1)} %spread.1), calls=%async_computation.1 | async-start | bytes 1048576 | tf_op jit(solution)/shard_map/all_to_all | solution.py:288
  105.1 3.2 %collective-permute-start.12 = (bf16[64,512]{1,0:T(8,128)(2,1)S(1)}, bf16[64,512]{1,0:T(8,128)(2,1)S(1)}, u32[]{:S(2)}, u32[]{:S(2)}) collective-permute-start(bf16[64,512]{1,0:T(8,128)(2,1)S(1)} %sum.1.refs_0_), channel_id=1, source_target_pairs={{0,192},{64,0},{128,64},{192,128},{1,193},{65,1},{129,65},{193,129... | collective-permute-start | bytes 196616 | tf_op jit(solution)/shard_map/ppermute | solution.py:295
  106.8 4.6 %collective-permute-start.11 = (bf16[64,512]{1,0:T(8,128)(2,1)S(1)}, bf16[64,512]{1,0:T(8,128)(2,1)S(1)}, u32[]{:S(2)}, u32[]{:S(2)}) collective-permute-start(bf16[64,512]{1,0:T(8,128)(2,1)S(1)} %sum.1.refs_0_), channel_id=1, source_target_pairs={{0,128},{64,192},{128,0},{192,64},{1,129},{65,193},{129,1},{193,65... | collective-permute-start | bytes 196616 | tf_op jit(solution)/shard_map/ppermute | solution.py:295
  107.5 4.6 %collective-permute-start.10 = (bf16[64,512]{1,0:T(8,128)(2,1)S(1)}, bf16[64,512]{1,0:T(8,128)(2,1)S(1)}, u32[]{:S(2)}, u32[]{:S(2)}) collective-permute-start(bf16[64,512]{1,0:T(8,128)(2,1)S(1)} %sum.1.refs_0_), channel_id=1, source_target_pairs={{0,64},{64,128},{128,192},{192,0},{1,65},{65,129},{129,193},{193,1... | collective-permute-start | bytes 196616 | tf_op jit(solution)/shard_map/ppermute | solution.py:295
  112.1 5.4 %collective-permute-start.13 = (bf16[256,512]{1,0:T(8,128)(2,1)S(1)}, bf16[256,512]{1,0:T(8,128)(2,1)S(1)}, u32[]{:S(2)}, u32[]{:S(2)}) collective-permute-start(bf16[256,512]{1,0:T(8,128)(2,1)S(1)} %stack.1.mine_ref), channel_id=1, source_target_pairs={{0,4},{4,0},{1,5},{5,1},{2,6},{6,2},{3,7},{7,3},{8,12},{12,8},{9,1... | collective-permute-start | bytes 786440 | tf_op jit(solution)/shard_map/ppermute | solution.py:301

commit v9 on v7

--- a/solution.py
+++ b/solution.py
@@ -59,17 +59,16 @@
     def fill(at, carry):
         start = pl.multiple_of(at * step, step)
         wanted = jnp.broadcast_to(row_ref[:, pl.ds(start, step)], (step, step)).T
+        within = jnp.where((wanted & (step - 1)) == lane, 1.0, 0.0).astype(BF16)
+        block = (wanted >> (step.bit_length() - 1)).astype(F32).astype(BF16)
+        nothing = jnp.zeros_like(within)
         picks = jnp.concatenate(
-            [
-                jnp.where(wanted == lane + low, 1.0, 0.0).astype(BF16)
-                for low in range(0, rows, step)
-            ],
-            axis=1,
+            [jnp.where(block == BF16(at), within, nothing) for at in range(rows // step)], axis=1
         )
         out_ref[pl.ds(start, step), :] = dot(picks, x_ref[...]).astype(BF16)
         return carry
 
-    lax.fori_loop(0, out_ref.shape[0] // step, fill, 0, unroll=4)
+    lax.fori_loop(0, out_ref.shape[0] // step, fill, 0, unroll=8)
 
 
 def count_body(
@@ -176,7 +175,7 @@
     )
 
 
-def weight_body(place_ref, own_ref, near_ref, cotangent_ref, *refs, half, count):
+def weight_body(place_ref, core_ref, own_ref, near_ref, cotangent_ref, *refs, half, count):
     grads_refs, (keep_ref, give_ref, grads_held, held_ref) = refs[:-4], refs[-4:]
     slices = len(grads_refs)
     cores, tall, cols = held_ref.shape
@@ -205,15 +204,15 @@
                 held_ref[
                     core, 2 * x * deep : (2 * x + 1) * deep, side * hidden : (side + 1) * hidden
                 ] = part[low : low + deep]
-    keep_ref[...] = held_ref[place_ref[1]]
-    give_ref[...] = held_ref[1 - place_ref[1]].astype(BF16)
+    keep_ref[...] = held_ref[core_ref[0]]
+    give_ref[...] = held_ref[1 - core_ref[0]].astype(BF16)
 
 
 def split_body(place_ref, keep_ref, got_ref, *out_refs):
     count = len(out_refs)
     step = out_refs[0].shape[0]
     for shift, out_ref in enumerate(out_refs):
-        at = lax.rem(place_ref[2] + shift, count)
+        at = lax.rem(place_ref[0] + shift, count)
         span = pl.ds(pl.multiple_of(at * step, step), step)
         out_ref[...] = (keep_ref[span, :] + got_ref[span, :].astype(F32)).astype(BF16)
 
@@ -237,7 +236,7 @@
     count = len(parts)
     step = parts[0].shape[0]
     for shift, part in enumerate(parts):
-        at = lax.rem(place_ref[2] + count - shift, count)
+        at = lax.rem(place_ref[0] + count - shift, count)
         out_ref[pl.ds(pl.multiple_of(at * step, step), step), :] = part[...]
 
 
@@ -250,7 +249,7 @@
     mine, other = mine_ref[...].astype(F32), other_ref[...].astype(F32)
     refs = ((first_self_ref, first_near_ref), (second_self_ref, second_near_ref))
     for core in range(cores):
-        value = jnp.where(place_ref[1] == core, mine, other)
+        value = jnp.where(place_ref[0] == core, mine, other)
         for x in range(count):
             low = (core * count + x) * deep
             for layer in range(2):
@@ -319,7 +318,9 @@
     seeds, fan_two = seed_neighbor.shape
     out_cols = second_self.shape[1]
     pieces = 4
-    place = jnp.stack([lax.axis_index(axis) for axis in ("feat", "core", "x")]).astype(I32)
+    at_feat, at_core, at_x = (
+        lax.axis_index(axis).astype(I32).reshape(1) for axis in ("feat", "core", "x")
+    )
 
     (picked,) = call(
         pick_body, [((slots, slice_cols), BF16)], (send_rows, features), "pick",
@@ -349,7 +350,7 @@
         functools.partial(gather_body, slices=slices),
         [((slice_cols, mids), BF16)] * 2 + [((half, mids), BF16)] * slices,
         (
-            place, routed, self_table.reshape(pieces, slots // pieces, mids),
+            at_feat, routed, self_table.reshape(pieces, slots // pieces, mids),
             near_table.reshape(pieces, slots // pieces, mids), degree.reshape(1, mids),
             first_self, first_neighbor,
         ),
@@ -365,7 +366,7 @@
     (grads,) = call(
         functools.partial(owner_body, fan_two=fan_two), [((half + tall, mids), BF16)],
         (
-            place, bias, seed_table, seed_near_table, second_self, second_neighbor, cotangent, *pre,
+            at_feat, bias, seed_table, seed_near_table, second_self, second_neighbor, cotangent, *pre,
         ),
         "owner", 16 * half * seeds * mids, 8 * half * mids, scalars=1,
     )
@@ -374,15 +375,15 @@
     keep, give = call(
         functools.partial(weight_body, half=half, count=count_x),
         [((tall, 2 * hidden), F32), ((tall, 2 * hidden), BF16)],
-        (place, own_rows, near_rows, cotangent, *grads), "weight",
+        (at_feat, at_core, own_rows, near_rows, cotangent, *grads), "weight",
         4 * slice_cols * mids * hidden, 8 * slice_cols * mids,
         scratch=[pltpu.VMEM((hidden, mids), BF16), pltpu.VMEM((cores, tall, 2 * hidden), F32)],
-        scalars=1,
+        scalars=2,
     )
     got = swapped(give, "core", cores, 1)
     shard = (tall // count_x, 2 * hidden)
     parts = call(
-        split_body, [(shard, BF16)] * count_x, (place, keep, got), "split", 0, 16 * tall * hidden,
+        split_body, [(shard, BF16)] * count_x, (at_x, keep, got), "split", 0, 16 * tall * hidden,
         scalars=1,
     )
     (mixed,) = call(
@@ -392,19 +393,19 @@
     mixed = exchange(mixed, "z")
     (seed_embedding,) = call(
         functools.partial(embed_body, half=half), [((seeds, out_cols), BF16)],
-        (place, second_self, second_neighbor, *grads), "embed",
+        (at_feat, second_self, second_neighbor, *grads), "embed",
         4 * seeds * hidden * out_cols, 8 * seeds * hidden, scalars=1,
     )
     mixed, seed_embedding = lax.optimization_barrier((mixed, seed_embedding))
     (mixed,) = call(sum_body, [(shard, BF16)], (mixed,), "sum", 0, 8 * tall * hidden)
     (mixed,) = call(
         stack_body, [((tall, 2 * hidden), BF16)],
-        (place, *shifted([mixed] * count_x, "x", count_x)), "stack", 0, 8 * tall * hidden, scalars=1,
+        (at_x, *shifted([mixed] * count_x, "x", count_x)), "stack", 0, 8 * tall * hidden, scalars=1,
     )
     grad_first_self, grad_first_neighbor, grad_second_self, grad_second_neighbor = call(
         functools.partial(finish_body, count=count_x, cores=cores),
         [((slice_cols, hidden), F32)] * 2 + [((hidden, out_cols), F32)] * 2,
-        (place, mixed, swapped(mixed, "core", cores, 1)), "finish", 0, 24 * tall * hidden, scalars=1,
+        (at_core, mixed, swapped(mixed, "core", cores, 1)), "finish", 0, 24 * tall * hidden, scalars=1,
     )
     return (
         seed_embedding,

time: 116 us -> 113 us (0.974)
  Pallas kernels: 26.9 us -> 22.8 us
    pallas_call x11, Pallas kernels: 26.9 us -> 22.8 us  [call(): pl.pallas_call(body, out_shape=[jax.ShapeDtypeStruct(shape, dtype) for sh...]
where the time goes in v9:
time: 113 us; the launch traced here: 112 us
  waiting for transfers between devices  45.9 us (41%)
  starting transfers between devices  39.3 us (35%)
  Pallas kernels  22.8 us (20%)
  local copies, waits for them, and re-layouts  3.29 us (3%)
    all_to_all x2, waiting for transfers between devices, exchange(): return lax.all_to_all(value, axis, split_axis=0, concat_axis=0, tiled=True)  29.1 us
    pallas_call x11, Pallas kernels, call(): pl.pallas_call(body, out_shape=[jax.ShapeDtypeStruct(shape, dtype) for sh...  22.8 us
    all_to_all x2, starting transfers between devices, exchange(): return lax.all_to_all(value, axis, split_axis=0, concat_axis=0, tiled=True)  16.6 us
    ppermute x12, starting transfers between devices, shifted(): lax.ppermute(piece, axis, [(at, (at + shift) % count) for at in range(cou...  15.1 us
    ppermute x12, waiting for transfers between devices, shifted(): lax.ppermute(piece, axis, [(at, (at + shift) % count) for at in range(cou...  14.5 us
    ppermute x2, starting transfers between devices, swapped(): return lax.ppermute(value, axis, [(at, at ^ step) for at in range(count)])  7.58 us
    unnamed x28, local copies, waits for them, and re-layouts  2.73 us
    ppermute x2, waiting for transfers between devices, swapped(): return lax.ppermute(value, axis, [(at, at ^ step) for at in range(count)])  2.32 us
  transfers between devices with their start and end apart: 16, of which 12 were waited for; matrix products, arithmetic and copies ran while one was open for 1% of the time, Pallas kernels for 11%

profile of v9, /device:TPU:1, one launch (start us, length us, event | category | flops | bytes accessed | tf_op | source)
XLA Modules:
  0.0 112.3 jit_solution(1877320428980788428)
XLA Ops:
  0.6 4.3 %pick.1 = bf16[2048,256]{1,0:T(8,128)(2,1)} custom-call(s32[1,2048]{1,0:T(1,128)} %row_far.1, bf16[1536,256]{1,0:T(8,128)(2,1)} %x_far.1), custom_call_target="tpu_custom_call" | custom-call | flops 1610612736 | bytes 6291456 | tf_op jit(solution)/shard_map/pick/pallas_call | solution.py:31
  4.9 0.0 copy-start.13
  4.9 0.0 copy-start.7
  4.9 0.0 copy-start.8
  5.0 0.0 copy-start.11
  5.0 0.0 copy-start.5
  5.0 13.1 %all-to-all-start = ((bf16[64,32,256]{2,1,0:T(8,128)(2,1)}), bf16[64,32,256]{2,1,0:T(8,128)(2,1)S(1)}, u32[]{:S(2)}, u32[]{:S(2)}) async-start(bf16[64,32,256]{2,1,0:T(8,128)(2,1)} %bitcast.3), calls=%async_computation | async-start | bytes 2097152 | tf_op jit(solution)/shard_map/all_to_all | solution.py:277
  18.1 0.1 fusion
  18.2 0.1 reshape.63
  18.3 0.3 iota.10.mask_ref
  18.7 11.2 %count.1 = (bf16[2048,512]{1,0:T(8,128)(2,1)S(1)}, bf16[2048,512]{1,0:T(8,128)(2,1)S(1)}, bf16[512,128]{1,0:T(8,128)(2,1)S(1)}, bf16[512,128]{1,0:T(8,128)(2,1)S(1)}) custom-call(s32[1,512]{1,0:T(1,128)S(1)} %bitcast.21, s32[25,512]{1,0:T(8,128)S(1)} %bitcast.17, s32[1,512]{1,0:T(1,128)S(1)} %bitcast.19, bf16[2048,128]{1,0:T(8,128)(2,1)S(1)} %iota.10.mask_ref, ...), custom_call_target="tpu_custom_call" | custom-call | bytes 16777216 | tf_op jit(solution)/shard_map/count/pallas_call | solution.py:31
  29.9 1.3 %copy-done = bf16[2048,512]{1,0:T(8,128)(2,1)} copy-done((bf16[2048,512]{1,0:T(8,128)(2,1)}, bf16[2048,512]{1,0:T(8,128)(2,1)S(1)}, u32[]{:S(2)}) %copy-start) | copy-done | bytes 2097176
  31.3 1.3 %copy-done.1 = bf16[2048,512]{1,0:T(8,128)(2,1)} copy-done((bf16[2048,512]{1,0:T(8,128)(2,1)}, bf16[2048,512]{1,0:T(8,128)(2,1)S(1)}, u32[]{:S(2)}) %copy-start.1) | copy-done | bytes 2097176
  32.6 14.1 %all-to-all-done = bf16[64,32,256]{2,1,0:T(8,128)(2,1)S(1)} async-done(((bf16[64,32,256]{2,1,0:T(8,128)(2,1)}), bf16[64,32,256]{2,1,0:T(8,128)(2,1)S(1)}, u32[]{:S(2)}, u32[]{:S(2)}) %all-to-all-start) | async-done | bytes 1048608 | tf_op jit(solution)/shard_map/all_to_all | solution.py:277
  46.7 0.0 copy-start.3
  46.7 3.5 %gather.1 = (bf16[256,512]{1,0:T(8,128)(2,1)S(1)}, bf16[256,512]{1,0:T(8,128)(2,1)S(1)}, bf16[64,512]{1,0:T(8,128)(2,1)S(1)}, bf16[64,512]{1,0:T(8,128)(2,1)S(1)...) custom-call(s32[1]{0:T(128)} %bitcast.1.place_ref, bf16[2048,256]{1,0:T(8,128)(2,1)S(1)} %bitcast.14, ...), custom_call_target="tpu_custom_call" | custom-call | flops 1073741824 | bytes 4194304 | tf_op jit(solution)/shard_map/gather/pallas_call | solution.py:31
  50.2 1.4 %collective-permute-start = (bf16[64,512]{1,0:T(8,128)(2,1)S(1)}, bf16[64,512]{1,0:T(8,128)(2,1)S(1)}, u32[]{:S(2)}, u32[]{:S(2)}) collective-permute-start(bf16[64,512]{1,0:T(8,128)(2,1)S(1)} %get-tuple-element.40), channel_id=1, source_target_pairs={{0,1},{1,2},{2,3},{3,0},{4,5},{5,6},{6,7},{7,4},{8,9},{9,10},{10,1... | collective-permute-start | bytes 196616 | tf_op jit(solution)/shard_map/ppermute | solution.py:284
  51.6 2.6 %collective-permute-start.1 = (bf16[64,512]{1,0:T(8,128)(2,1)S(1)}, bf16[64,512]{1,0:T(8,128)(2,1)S(1)}, u32[]{:S(2)}, u32[]{:S(2)}) collective-permute-start(bf16[64,512]{1,0:T(8,128)(2,1)S(1)} %get-tuple-element.41), channel_id=1, source_target_pairs={{0,2},{1,3},{2,0},{3,1},{4,6},{5,7},{6,4},{7,5},{8,10},{9,11},{10,... | collective-permute-start | bytes 196616 | tf_op jit(solution)/shard_map/ppermute | solution.py:284
  54.2 1.1 collective-permute-start.2
  55.3 0.1 copy.19.bias_ref
  55.4 2.4 %collective-permute-done.1.refs_2_ = bf16[64,512]{1,0:T(8,128)(2,1)S(1)} collective-permute-done((bf16[64,512]{1,0:T(8,128)(2,1)S(1)}, bf16[64,512]{1,0:T(8,128)(2,1)S(1)}, u32[]{:S(2)}, u32[]{:S(2)}) %collective-permute-start.1) | collective-permute-done | bytes 65568 | tf_op jit(solution)/shard_map/ppermute | solution.py:284
  57.8 0.4 owner.1.refs_0_
  58.2 1.9 %collective-permute-start.5 = (bf16[96,512]{1,0:T(8,128)(2,1)S(1)}, bf16[96,512]{1,0:T(8,128)(2,1)S(1)}, u32[]{:S(2)}, u32[]{:S(2)}) collective-permute-start(bf16[96,512]{1,0:T(8,128)(2,1)S(1)} %owner.1.refs_0_), channel_id=1, source_target_pairs={{0,3},{1,0},{2,1},{3,2},{4,7},{5,4},{6,5},{7,6},{8,11},{9,8},{10,9... | collective-permute-start | bytes 294920 | tf_op jit(solution)/shard_map/ppermute | solution.py:284
  60.1 0.2 collective-permute-start.4
  60.3 0.8 collective-permute-start.3
  61.1 1.1 %collective-permute-done.5.refs_3_ = bf16[96,512]{1,0:T(8,128)(2,1)S(1)} collective-permute-done((bf16[96,512]{1,0:T(8,128)(2,1)S(1)}, bf16[96,512]{1,0:T(8,128)(2,1)S(1)}, u32[]{:S(2)}, u32[]{:S(2)}) %collective-permute-start.5) | collective-permute-done | bytes 98336 | tf_op jit(solution)/shard_map/ppermute | solution.py:284
  62.2 2.9 %collective-permute-done.4.refs_2_ = bf16[96,512]{1,0:T(8,128)(2,1)S(1)} collective-permute-done((bf16[96,512]{1,0:T(8,128)(2,1)S(1)}, bf16[96,512]{1,0:T(8,128)(2,1)S(1)}, u32[]{:S(2)}, u32[]{:S(2)}) %collective-permute-start.4) | collective-permute-done | bytes 98336 | tf_op jit(solution)/shard_map/ppermute | solution.py:284
  65.2 0.9 collective-permute-done.3.refs_1_
  66.1 0.5 weight.1
  66.5 3.4 %collective-permute-start.6 = (bf16[256,512]{1,0:T(8,128)(2,1)S(1)}, bf16[256,512]{1,0:T(8,128)(2,1)S(1)}, u32[]{:S(2)}, u32[]{:S(2)}) collective-permute-start(bf16[256,512]{1,0:T(8,128)(2,1)S(1)} %get-tuple-element.44), channel_id=1, source_target_pairs={{0,4},{4,0},{1,5},{5,1},{2,6},{6,2},{3,7},{7,3},{8,12},{12,8},{9,1... | collective-permute-start | bytes 786440 | tf_op jit(solution)/shard_map/ppermute | solution.py:290
  69.9 1.2 %collective-permute-done.6.got_ref = bf16[256,512]{1,0:T(8,128)(2,1)S(1)} collective-permute-done((bf16[256,512]{1,0:T(8,128)(2,1)S(1)}, bf16[256,512]{1,0:T(8,128)(2,1)S(1)}, u32[]{:S(2)}, u32[]{:S(2)}) %collective-permute-start.6) | collective-permute-done | bytes 262176 | tf_op jit(solution)/shard_map/ppermute | solution.py:290
  71.1 1.8 %collective-permute-start.7 = (bf16[64,512]{1,0:T(8,128)(2,1)S(1)}, bf16[64,512]{1,0:T(8,128)(2,1)S(1)}, u32[]{:S(2)}, u32[]{:S(2)}) collective-permute-start(bf16[64,512]{1,0:T(8,128)(2,1)S(1)} %get-tuple-element.46), channel_id=1, source_target_pairs={{0,64},{64,128},{128,192},{192,0},{1,65},{65,129},{129,193},{193,1... | collective-permute-start | bytes 196616 | tf_op jit(solution)/shard_map/ppermute | solution.py:284
  72.9 2.0 %collective-permute-start.8 = (bf16[64,512]{1,0:T(8,128)(2,1)S(1)}, bf16[64,512]{1,0:T(8,128)(2,1)S(1)}, u32[]{:S(2)}, u32[]{:S(2)}) collective-permute-start(bf16[64,512]{1,0:T(8,128)(2,1)S(1)} %get-tuple-element.47), channel_id=1, source_target_pairs={{0,128},{64,192},{128,0},{192,64},{1,129},{65,193},{129,1},{193,65... | collective-permute-start | bytes 196616 | tf_op jit(solution)/shard_map/ppermute | solution.py:284
  74.9 1.1 collective-permute-start.9
  76.0 2.5 %collective-permute-done.8.refs_2_ = bf16[64,512]{1,0:T(8,128)(2,1)S(1)} collective-permute-done((bf16[64,512]{1,0:T(8,128)(2,1)S(1)}, bf16[64,512]{1,0:T(8,128)(2,1)S(1)}, u32[]{:S(2)}, u32[]{:S(2)}) %collective-permute-start.8) | collective-permute-done | bytes 65568 | tf_op jit(solution)/shard_map/ppermute | solution.py:284
  78.5 0.8 spread.1
  79.3 3.5 %all-to-all-start.1 = ((bf16[8,64,512]{2,1,0:T(8,128)(2,1)}), bf16[8,64,512]{2,1,0:T(8,128)(2,1)S(1)}, u32[]{:S(2)}, u32[]{:S(2)}) async-start(bf16[8,64,512]{2,1,0:T(8,128)(2,1)} %spread.1), calls=%async_computation.1 | async-start | bytes 1048576 | tf_op jit(solution)/shard_map/all_to_all | solution.py:277
  82.8 1.0 embed.1
  83.8 15.0 %all-to-all-done.1.parts_ref = bf16[8,64,512]{2,1,0:T(8,128)(2,1)S(1)} async-done(((bf16[8,64,512]{2,1,0:T(8,128)(2,1)}), bf16[8,64,512]{2,1,0:T(8,128)(2,1)S(1)}, u32[]{:S(2)}, u32[]{:S(2)}) %all-to-all-start.1) | async-done | bytes 524320 | tf_op jit(solution)/shard_map/all_to_all | solution.py:277
  98.8 0.1 sum.1.refs_0_
  98.9 1.7 %collective-permute-start.12 = (bf16[64,512]{1,0:T(8,128)(2,1)S(1)}, bf16[64,512]{1,0:T(8,128)(2,1)S(1)}, u32[]{:S(2)}, u32[]{:S(2)}) collective-permute-start(bf16[64,512]{1,0:T(8,128)(2,1)S(1)} %sum.1.refs_0_), channel_id=1, source_target_pairs={{0,192},{64,0},{128,64},{192,128},{1,193},{65,1},{129,65},{193,129... | collective-permute-start | bytes 196616 | tf_op jit(solution)/shard_map/ppermute | solution.py:284
  100.5 0.7 collective-permute-start.11
  101.2 0.8 collective-permute-done.12.refs_3_
  102.1 3.1 %collective-permute-done.11.refs_2_ = bf16[64,512]{1,0:T(8,128)(2,1)S(1)} collective-permute-done((bf16[64,512]{1,0:T(8,128)(2,1)S(1)}, bf16[64,512]{1,0:T(8,128)(2,1)S(1)}, u32[]{:S(2)}, u32[]{:S(2)}) %collective-permute-start.11) | collective-permute-done | bytes 65568 | tf_op jit(solution)/shard_map/ppermute | solution.py:284
  105.2 0.7 collective-permute-done.10.refs_1_
  105.9 4.2 %collective-permute-start.13 = (bf16[256,512]{1,0:T(8,128)(2,1)S(1)}, bf16[256,512]{1,0:T(8,128)(2,1)S(1)}, u32[]{:S(2)}, u32[]{:S(2)}) collective-permute-start(bf16[256,512]{1,0:T(8,128)(2,1)S(1)} %stack.1.mine_ref), channel_id=1, source_target_pairs={{0,4},{4,0},{1,5},{5,1},{2,6},{6,2},{3,7},{7,3},{8,12},{12,8},{9,1... | collective-permute-start | bytes 786440 | tf_op jit(solution)/shard_map/ppermute | solution.py:290
  110.1 1.2 %collective-permute-done.13.other_ref = bf16[256,512]{1,0:T(8,128)(2,1)S(1)} collective-permute-done((bf16[256,512]{1,0:T(8,128)(2,1)S(1)}, bf16[256,512]{1,0:T(8,128)(2,1)S(1)}, u32[]{:S(2)}, u32[]{:S(2)}) %collective-permute-start.13) | collective-permute-done | bytes 262176 | tf_op jit(solution)/shard_map/ppermute | solution.py:290
  111.3 1.0 finish.1
  (27 shorter events, 0.1 us)
Async XLA Ops:
  4.9 13.2 %copy-start.13 = (s32[1,64]{1,0:T(1,128)S(1)}, s32[1,64]{1,0:T(1,128)}, u32[]{:S(2)}) copy-start(s32[1,64]{1,0:T(1,128)} %param.21) | copy-start | bytes 772
  4.9 13.7 %copy-start.7 = (s32[512,25]{0,1:T(8,128)S(1)}, s32[512,25]{0,1:T(8,128)}, u32[]{:S(2)}) copy-start(s32[512,25]{0,1:T(8,128)} %param.23) | copy-start | bytes 153604
  4.9 13.7 %copy-start.8 = (s32[128,10]{0,1:T(8,128)S(1)}, s32[128,10]{0,1:T(8,128)}, u32[]{:S(2)}) copy-start(s32[128,10]{0,1:T(8,128)} %param.26) | copy-start | bytes 15364
  4.9 13.7 %copy-start.9 = (s32[512]{0:T(512)S(1)}, s32[512]{0:T(512)}, u32[]{:S(2)}) copy-start(s32[512]{0:T(512)} %param.24) | copy-start | bytes 6148
  5.0 13.7 %copy-start.10 = (s32[512]{0:T(512)S(1)}, s32[512]{0:T(512)}, u32[]{:S(2)}) copy-start(s32[512]{0:T(512)} %param.22) | copy-start | bytes 6148
  5.0 13.7 %copy-start.11 = (s32[128]{0:T(128)S(1)}, s32[128]{0:T(128)}, u32[]{:S(2)}) copy-start(s32[128]{0:T(128)} %param.25) | copy-start | bytes 1540
  5.0 41.7 %copy-start.5 = (bf16[256,256]{1,0:T(8,128)(2,1)S(1)}, bf16[256,256]{1,0:T(8,128)(2,1)}, u32[]{:S(2)}) copy-start(bf16[256,256]{1,0:T(8,128)(2,1)} %weight_self_ref.1) | copy-start | bytes 393220
  5.0 41.7 %copy-start.6 = (bf16[256,256]{1,0:T(8,128)(2,1)S(1)}, bf16[256,256]{1,0:T(8,128)(2,1)}, u32[]{:S(2)}) copy-start(bf16[256,256]{1,0:T(8,128)(2,1)} %weight_near_ref.1) | copy-start | bytes 393220
  5.0 41.7 %all-to-all-start = ((bf16[64,32,256]{2,1,0:T(8,128)(2,1)}), bf16[64,32,256]{2,1,0:T(8,128)(2,1)S(1)}, u32[]{:S(2)}, u32[]{:S(2)}) async-start(bf16[64,32,256]{2,1,0:T(8,128)(2,1)} %bitcast.3), calls=%async_computation | async-start | bytes 2097152 | tf_op jit(solution)/shard_map/all_to_all | solution.py:277
  29.9 1.3 %copy-start = (bf16[2048,512]{1,0:T(8,128)(2,1)}, bf16[2048,512]{1,0:T(8,128)(2,1)S(1)}, u32[]{:S(2)}) copy-start(bf16[2048,512]{1,0:T(8,128)(2,1)S(1)} %get-tuple-element.32) | copy-start | bytes 6291460
  31.3 1.3 %copy-start.1 = (bf16[2048,512]{1,0:T(8,128)(2,1)}, bf16[2048,512]{1,0:T(8,128)(2,1)S(1)}, u32[]{:S(2)}) copy-start(bf16[2048,512]{1,0:T(8,128)(2,1)S(1)} %get-tuple-element.33) | copy-start | bytes 6291460
  46.7 8.6 %copy-start.12 = (f32[256]{0:T(256)S(1)}, f32[256]{0:T(256)}, u32[]{:S(2)}) copy-start(f32[256]{0:T(256)} %param.17) | copy-start | bytes 3076
  46.7 11.1 %copy-start.2 = (bf16[256,256]{1,0:T(8,128)(2,1)S(1)}, bf16[256,256]{1,0:T(8,128)(2,1)}, u32[]{:S(2)}) copy-start(bf16[256,256]{1,0:T(8,128)(2,1)} %second_self_ref.3) | copy-start | bytes 393220
  46.7 11.1 %copy-start.3 = (bf16[256,256]{1,0:T(8,128)(2,1)S(1)}, bf16[256,256]{1,0:T(8,128)(2,1)}, u32[]{:S(2)}) copy-start(bf16[256,256]{1,0:T(8,128)(2,1)} %second_near_ref.3) | copy-start | bytes 393220
  46.7 11.1 %copy-start.4 = (bf16[128,256]{1,0:T(8,128)(2,1)S(1)}, bf16[128,256]{1,0:T(8,128)(2,1)}, u32[]{:S(2)}) copy-start(bf16[128,256]{1,0:T(8,128)(2,1)} %cotangent_ref.3) | copy-start | bytes 196612
  50.2 5.2 %collective-permute-start = (bf16[64,512]{1,0:T(8,128)(2,1)S(1)}, bf16[64,512]{1,0:T(8,128)(2,1)S(1)}, u32[]{:S(2)}, u32[]{:S(2)}) collective-permute-start(bf16[64,512]{1,0:T(8,128)(2,1)S(1)} %get-tuple-element.40), channel_id=1, source_target_pairs={{0,1},{1,2},{2,3},{3,0},{4,5},{5,6},{6,7},{7,4},{8,9},{9,10},{10,1... | collective-permute-start | bytes 196616 | tf_op jit(solution)/shard_map/ppermute | solution.py:284
  51.6 6.2 %collective-permute-start.1 = (bf16[64,512]{1,0:T(8,128)(2,1)S(1)}, bf16[64,512]{1,0:T(8,128)(2,1)S(1)}, u32[]{:S(2)}, u32[]{:S(2)}) collective-permute-start(bf16[64,512]{1,0:T(8,128)(2,1)S(1)} %get-tuple-element.41), channel_id=1, source_target_pairs={{0,2},{1,3},{2,0},{3,1},{4,6},{5,7},{6,4},{7,5},{8,10},{9,11},{10,... | collective-permute-start | bytes 196616 | tf_op jit(solution)/shard_map/ppermute | solution.py:284
  54.2 3.6 %collective-permute-start.2 = (bf16[64,512]{1,0:T(8,128)(2,1)S(1)}, bf16[64,512]{1,0:T(8,128)(2,1)S(1)}, u32[]{:S(2)}, u32[]{:S(2)}) collective-permute-start(bf16[64,512]{1,0:T(8,128)(2,1)S(1)} %get-tuple-element.42), channel_id=1, source_target_pairs={{0,3},{1,0},{2,1},{3,2},{4,7},{5,4},{6,5},{7,6},{8,11},{9,8},{10,9... | collective-permute-start | bytes 196616 | tf_op jit(solution)/shard_map/ppermute | solution.py:284
  58.2 4.0 %collective-permute-start.5 = (bf16[96,512]{1,0:T(8,128)(2,1)S(1)}, bf16[96,512]{1,0:T(8,128)(2,1)S(1)}, u32[]{:S(2)}, u32[]{:S(2)}) collective-permute-start(bf16[96,512]{1,0:T(8,128)(2,1)S(1)} %owner.1.refs_0_), channel_id=1, source_target_pairs={{0,3},{1,0},{2,1},{3,2},{4,7},{5,4},{6,5},{7,6},{8,11},{9,8},{10,9... | collective-permute-start | bytes 294920 | tf_op jit(solution)/shard_map/ppermute | solution.py:284
  60.1 5.1 %collective-permute-start.4 = (bf16[96,512]{1,0:T(8,128)(2,1)S(1)}, bf16[96,512]{1,0:T(8,128)(2,1)S(1)}, u32[]{:S(2)}, u32[]{:S(2)}) collective-permute-start(bf16[96,512]{1,0:T(8,128)(2,1)S(1)} %owner.1.refs_0_), channel_id=1, source_target_pairs={{0,2},{1,3},{2,0},{3,1},{4,6},{5,7},{6,4},{7,5},{8,10},{9,11},{10,... | collective-permute-start | bytes 294920 | tf_op jit(solution)/shard_map/ppermute | solution.py:284
  60.3 5.7 %collective-permute-start.3 = (bf16[96,512]{1,0:T(8,128)(2,1)S(1)}, bf16[96,512]{1,0:T(8,128)(2,1)S(1)}, u32[]{:S(2)}, u32[]{:S(2)}) collective-permute-start(bf16[96,512]{1,0:T(8,128)(2,1)S(1)} %owner.1.refs_0_), channel_id=1, source_target_pairs={{0,1},{1,2},{2,3},{3,0},{4,5},{5,6},{6,7},{7,4},{8,9},{9,10},{10,1... | collective-permute-start | bytes 294920 | tf_op jit(solution)/shard_map/ppermute | solution.py:284
  66.5 4.5 %collective-permute-start.6 = (bf16[256,512]{1,0:T(8,128)(2,1)S(1)}, bf16[256,512]{1,0:T(8,128)(2,1)S(1)}, u32[]{:S(2)}, u32[]{:S(2)}) collective-permute-start(bf16[256,512]{1,0:T(8,128)(2,1)S(1)} %get-tuple-element.44), channel_id=1, source_target_pairs={{0,4},{4,0},{1,5},{5,1},{2,6},{6,2},{3,7},{7,3},{8,12},{12,8},{9,1... | collective-permute-start | bytes 786440 | tf_op jit(solution)/shard_map/ppermute | solution.py:290
  71.1 4.8 %collective-permute-start.7 = (bf16[64,512]{1,0:T(8,128)(2,1)S(1)}, bf16[64,512]{1,0:T(8,128)(2,1)S(1)}, u32[]{:S(2)}, u32[]{:S(2)}) collective-permute-start(bf16[64,512]{1,0:T(8,128)(2,1)S(1)} %get-tuple-element.46), channel_id=1, source_target_pairs={{0,64},{64,128},{128,192},{192,0},{1,65},{65,129},{129,193},{193,1... | collective-permute-start | bytes 196616 | tf_op jit(solution)/shard_map/ppermute | solution.py:284
  72.9 5.6 %collective-permute-start.8 = (bf16[64,512]{1,0:T(8,128)(2,1)S(1)}, bf16[64,512]{1,0:T(8,128)(2,1)S(1)}, u32[]{:S(2)}, u32[]{:S(2)}) collective-permute-start(bf16[64,512]{1,0:T(8,128)(2,1)S(1)} %get-tuple-element.47), channel_id=1, source_target_pairs={{0,128},{64,192},{128,0},{192,64},{1,129},{65,193},{129,1},{193,65... | collective-permute-start | bytes 196616 | tf_op jit(solution)/shard_map/ppermute | solution.py:284
  74.9 3.6 %collective-permute-start.9 = (bf16[64,512]{1,0:T(8,128)(2,1)S(1)}, bf16[64,512]{1,0:T(8,128)(2,1)S(1)}, u32[]{:S(2)}, u32[]{:S(2)}) collective-permute-start(bf16[64,512]{1,0:T(8,128)(2,1)S(1)} %get-tuple-element.48), channel_id=1, source_target_pairs={{0,192},{64,0},{128,64},{192,128},{1,193},{65,1},{129,65},{193,129... | collective-permute-start | bytes 196616 | tf_op jit(solution)/shard_map/ppermute | solution.py:284
  79.3 19.5 %all-to-all-start.1 = ((bf16[8,64,512]{2,1,0:T(8,128)(2,1)}), bf16[8,64,512]{2,1,0:T(8,128)(2,1)S(1)}, u32[]{:S(2)}, u32[]{:S(2)}) async-start(bf16[8,64,512]{2,1,0:T(8,128)(2,1)} %spread.1), calls=%async_computation.1 | async-start | bytes 1048576 | tf_op jit(solution)/shard_map/all_to_all | solution.py:277
  98.9 3.2 %collective-permute-start.12 = (bf16[64,512]{1,0:T(8,128)(2,1)S(1)}, bf16[64,512]{1,0:T(8,128)(2,1)S(1)}, u32[]{:S(2)}, u32[]{:S(2)}) collective-permute-start(bf16[64,512]{1,0:T(8,128)(2,1)S(1)} %sum.1.refs_0_), channel_id=1, source_target_pairs={{0,192},{64,0},{128,64},{192,128},{1,193},{65,1},{129,65},{193,129... | collective-permute-start | bytes 196616 | tf_op jit(solution)/shard_map/ppermute | solution.py:284
  100.5 4.6 %collective-permute-start.11 = (bf16[64,512]{1,0:T(8,128)(2,1)S(1)}, bf16[64,512]{1,0:T(8,128)(2,1)S(1)}, u32[]{:S(2)}, u32[]{:S(2)}) collective-permute-start(bf16[64,512]{1,0:T(8,128)(2,1)S(1)} %sum.1.refs_0_), channel_id=1, source_target_pairs={{0,128},{64,192},{128,0},{192,64},{1,129},{65,193},{129,1},{193,65... | collective-permute-start | bytes 196616 | tf_op jit(solution)/shard_map/ppermute | solution.py:284
  101.2 4.6 %collective-permute-start.10 = (bf16[64,512]{1,0:T(8,128)(2,1)S(1)}, bf16[64,512]{1,0:T(8,128)(2,1)S(1)}, u32[]{:S(2)}, u32[]{:S(2)}) collective-permute-start(bf16[64,512]{1,0:T(8,128)(2,1)S(1)} %sum.1.refs_0_), channel_id=1, source_target_pairs={{0,64},{64,128},{128,192},{192,0},{1,65},{65,129},{129,193},{193,1... | collective-permute-start | bytes 196616 | tf_op jit(solution)/shard_map/ppermute | solution.py:284
  105.9 5.4 %collective-permute-start.13 = (bf16[256,512]{1,0:T(8,128)(2,1)S(1)}, bf16[256,512]{1,0:T(8,128)(2,1)S(1)}, u32[]{:S(2)}, u32[]{:S(2)}) collective-permute-start(bf16[256,512]{1,0:T(8,128)(2,1)S(1)} %stack.1.mine_ref), channel_id=1, source_target_pairs={{0,4},{4,0},{1,5},{5,1},{2,6},{6,2},{3,7},{7,3},{8,12},{12,8},{9,1... | collective-permute-start | bytes 786440 | tf_op jit(solution)/shard_map/ppermute | solution.py:290

commit v10 on v9

--- a/solution.py
+++ b/solution.py
@@ -72,15 +72,14 @@
 
 
 def count_body(
-    self_ref, near_ref, degree_ref, mask_ref, seed_ref, seed_near_ref,
-    self_table, near_table, seed_table, seed_near_table, live_ref,
+    near_ref, degree_ref, mask_ref, seed_ref, seed_near_ref, near_table,
+    seed_table, seed_near_table, live_ref,
 ):
     slots, mids = near_table.shape
     fan = near_ref.shape[0]
     step = 32
     live = lax.broadcasted_iota(I32, (fan, mids), 0) < degree_ref[...]
     live_ref[...] = jnp.where(live, near_ref[...], -1)
-    own = self_ref[...]
 
     def fill(at, carry):
         span = pl.ds(pl.multiple_of(at * step, step), step)
@@ -91,7 +90,6 @@
         filled = mask_ref[span, :].astype(F32)
         filled = jnp.concatenate([filled] * (mids // filled.shape[1]), axis=1)
         near_table[span, :] = (total * filled).astype(BF16)
-        self_table[span, :] = jnp.where(own == line, filled, 0.0).astype(BF16)
         return carry
 
     lax.fori_loop(0, slots // step, fill, 0)
@@ -105,24 +103,28 @@
 
 
 def gather_body(
-    place_ref, x_ref, self_far, near_far, degree_ref, weight_self_ref, weight_near_ref, *refs, slices
+    place_ref, x_ref, slot_ref, mask_ref, near_far, degree_ref, weight_self_ref, weight_near_ref,
+    *refs, slices
 ):
     own_ref, near_ref = refs[:2]
     out_refs = refs[2 : 2 + slices]
-    self_table, near_table, held_ref, sems = refs[2 + slices :]
-    pieces, step, _ = self_table.shape
-    copies = []
-    for piece in range(pieces):
-        for side, (far, ref) in enumerate(((self_far, self_table), (near_far, near_table))):
-            copy = pltpu.make_async_copy(far.at[piece], ref.at[piece], sems.at[side, piece])
-            copy.start()
-            copies.append(copy)
+    near_table, held_ref, sems = refs[2 + slices :]
+    pieces, step, mids = near_table.shape
+    copies = [
+        pltpu.make_async_copy(near_far.at[at], near_table.at[at], sems.at[at])
+        for at in range(pieces)
+    ]
+    for copy in copies:
+        copy.start()
     own, near = 0.0, 0.0
     for piece in range(pieces):
-        turned = x_ref[pl.ds(piece * step, step), :].T
-        copies[2 * piece].wait()
-        own = own + dot(turned, self_table[piece])
-        copies[2 * piece + 1].wait()
+        span = pl.ds(piece * step, step)
+        turned = x_ref[span, :].T
+        line = lax.broadcasted_iota(I32, (step, mids), 0) + piece * step
+        filled = mask_ref[span, :].astype(F32)
+        filled = jnp.concatenate([filled] * (mids // filled.shape[1]), axis=1)
+        own = own + dot(turned, jnp.where(slot_ref[...] == line, filled, 0.0).astype(BF16))
+        copies[piece].wait()
         near = near + dot(turned, near_table[piece])
     own = own.astype(BF16)
     near = (near / degree_ref[...].astype(F32)).astype(BF16)
@@ -231,33 +233,21 @@
     out_ref[...] = jnp.sum(parts_ref[...].astype(F32), axis=0).astype(BF16)
 
 
-def stack_body(place_ref, *refs):
-    parts, out_ref = refs[:-1], refs[-1]
-    count = len(parts)
-    step = parts[0].shape[0]
-    for shift, part in enumerate(parts):
-        at = lax.rem(place_ref[0] + count - shift, count)
-        out_ref[pl.ds(pl.multiple_of(at * step, step), step), :] = part[...]
-
-
-def finish_body(
-    place_ref, mine_ref, other_ref, first_self_ref, first_near_ref, second_self_ref, second_near_ref,
-    count, cores,
-):
-    hidden = first_self_ref.shape[0]
-    deep = hidden // (count * cores)
-    mine, other = mine_ref[...].astype(F32), other_ref[...].astype(F32)
-    refs = ((first_self_ref, first_near_ref), (second_self_ref, second_near_ref))
-    for core in range(cores):
-        value = jnp.where(place_ref[0] == core, mine, other)
-        for x in range(count):
-            low = (core * count + x) * deep
-            for layer in range(2):
-                start = (2 * x + layer) * deep
-                for side in range(2):
-                    refs[layer][side][low : low + deep, :] = value[
-                        start : start + deep, side * hidden : (side + 1) * hidden
-                    ]
+def finish_body(core_ref, x_ref, *refs, count, cores):
+    mine, other, outs = refs[:count], refs[count : 2 * count], refs[2 * count :]
+    deep = mine[0].shape[0] // 2
+    hidden = outs[0].shape[1]
+    for shift in range(count):
+        x = lax.rem(x_ref[0] + count - shift, count)
+        own, got = mine[shift][...].astype(F32), other[shift][...].astype(F32)
+        for core in range(cores):
+            value = jnp.where(core_ref[0] == core, own, got)
+            span = pl.ds(pl.multiple_of((core * count + x) * deep, deep), deep)
+            for at, out_ref in enumerate(outs):
+                layer, side = at // 2, at % 2
+                out_ref[span, :] = value[
+                    layer * deep : (layer + 1) * deep, side * hidden : (side + 1) * hidden
+                ]
 
 
 def embed_body(place_ref, second_self_ref, second_near_ref, *refs, half):
@@ -334,11 +324,11 @@
 
     slot_at = lax.broadcasted_iota(I32, (peers, capacity, 128), 1)
     mask = (slot_at < arrive_count.reshape(peers, 1, 1)).astype(BF16).reshape(slots, 128)
-    self_table, near_table, seed_table, seed_near_table = call(
+    near_table, seed_table, seed_near_table = call(
         count_body,
-        [((slots, mids), BF16), ((slots, mids), BF16), ((mids, seeds), BF16), ((mids, seeds), BF16)],
+        [((slots, mids), BF16), ((mids, seeds), BF16), ((mids, seeds), BF16)],
         (
-            self_slot.reshape(1, mids), neighbor_slot.T, degree.reshape(1, mids), mask,
+            neighbor_slot.T, degree.reshape(1, mids), mask,
             seed_self.reshape(1, seeds), seed_neighbor.T,
         ),
         "count", 0, 16 * slots * mids, scratch=[pltpu.VMEM((fan, mids), I32)],
@@ -350,15 +340,14 @@
         functools.partial(gather_body, slices=slices),
         [((slice_cols, mids), BF16)] * 2 + [((half, mids), BF16)] * slices,
         (
-            at_feat, routed, self_table.reshape(pieces, slots // pieces, mids),
+            at_feat, routed, self_slot.reshape(1, mids), mask,
             near_table.reshape(pieces, slots // pieces, mids), degree.reshape(1, mids),
             first_self, first_neighbor,
         ),
-        "gather", 4 * slots * slice_cols * mids, 4 * slots * mids, scalars=1, far=(2, 3),
+        "gather", 4 * slots * slice_cols * mids, 4 * slots * mids, scalars=1, far=(4,),
         scratch=[
             pltpu.VMEM((pieces, slots // pieces, mids), BF16),
-            pltpu.VMEM((pieces, slots // pieces, mids), BF16),
-            pltpu.VMEM((slices, half, mids), BF16), pltpu.SemaphoreType.DMA((2, pieces)),
+            pltpu.VMEM((slices, half, mids), BF16), pltpu.SemaphoreType.DMA((pieces,)),
         ],
     )
     pre = shifted(pre, "feat", slices)
@@ -398,14 +387,12 @@
     )
     mixed, seed_embedding = lax.optimization_barrier((mixed, seed_embedding))
     (mixed,) = call(sum_body, [(shard, BF16)], (mixed,), "sum", 0, 8 * tall * hidden)
-    (mixed,) = call(
-        stack_body, [((tall, 2 * hidden), BF16)],
-        (at_x, *shifted([mixed] * count_x, "x", count_x)), "stack", 0, 8 * tall * hidden, scalars=1,
-    )
+    mine = shifted([mixed] * count_x, "x", count_x)
+    other = [swapped(piece, "core", cores, 1) for piece in mine]
     grad_first_self, grad_first_neighbor, grad_second_self, grad_second_neighbor = call(
         functools.partial(finish_body, count=count_x, cores=cores),
         [((slice_cols, hidden), F32)] * 2 + [((hidden, out_cols), F32)] * 2,
-        (at_core, mixed, swapped(mixed, "core", cores, 1)), "finish", 0, 24 * tall * hidden, scalars=1,
+        (at_core, at_x, *mine, *other), "finish", 0, 24 * tall * hidden, scalars=2,
     )
     return (
         seed_embedding,

time: 113 us -> 112 us (level)
  starting transfers between devices: 39.3 us -> 43.7 us
  waiting for transfers between devices: 45.9 us -> 42.5 us
  local copies, waits for them, and re-layouts: 3.29 us -> 1.99 us
    ppermute x12, waiting for transfers between devices: 14.5 us -> 9.89 us  [shifted(): lax.ppermute(piece, axis, [(at, (at + shift) % count) for at in range(cou...]
    ppermute x2 -> x5, starting transfers between devices: 7.58 us -> 11.6 us  [swapped(): return lax.ppermute(value, axis, [(at, at ^ step) for at in range(count)])]
    all_to_all x2, waiting for transfers between devices: 29.1 us -> 30.6 us  [exchange(): return lax.all_to_all(value, axis, split_axis=0, concat_axis=0, tiled=True)]
    unnamed x28 -> x26, local copies, waits for them, and re-layouts: 2.73 us -> 1.43 us
    pallas_call x11 -> x10, Pallas kernels: 22.8 us -> 22.3 us  [call(): pl.pallas_call(body, out_shape=[jax.ShapeDtypeStruct(shape, dtype) for sh...]
    ppermute x2 -> x5, waiting for transfers between devices: 2.32 us -> 2.06 us  [swapped(): return lax.ppermute(value, axis, [(at, at ^ step) for at in range(count)])]
  transfers between devices with their start and end apart: 16 -> 19, of which waited for: 12 -> 10; matrix products, arithmetic and copies ran while one was open for 1% -> 1% of each run, Pallas kernels for 11% -> 11%
where the time goes in v10:
time: 112 us; the launch traced here: 111 us
  starting transfers between devices  43.7 us (39%)
  waiting for transfers between devices  42.5 us (38%)
  Pallas kernels  22.3 us (20%)
  local copies, waits for them, and re-layouts  1.99 us (2%)
    all_to_all x2, waiting for transfers between devices, exchange(): return lax.all_to_all(value, axis, split_axis=0, concat_axis=0, tiled=True)  30.6 us
    pallas_call x10, Pallas kernels, call(): pl.pallas_call(body, out_shape=[jax.ShapeDtypeStruct(shape, dtype) for sh...  22.3 us
    all_to_all x2, starting transfers between devices, exchange(): return lax.all_to_all(value, axis, split_axis=0, concat_axis=0, tiled=True)  16.8 us
    ppermute x12, starting transfers between devices, shifted(): lax.ppermute(piece, axis, [(at, (at + shift) % count) for at in range(cou...  15.3 us
    ppermute x5, starting transfers between devices, swapped(): return lax.ppermute(value, axis, [(at, at ^ step) for at in range(count)])  11.6 us
    ppermute x12, waiting for transfers between devices, shifted(): lax.ppermute(piece, axis, [(at, (at + shift) % count) for at in range(cou...  9.89 us
  transfers between devices with their start and end apart: 19, of which 10 were waited for; matrix products, arithmetic and copies ran while one was open for 1% of the time, Pallas kernels for 11%

profile of v10, /device:TPU:1, one launch (start us, length us, event | category | flops | bytes accessed | tf_op | source)
XLA Modules:
  0.0 111.4 jit_solution(18441304417328638060)
XLA Ops:
  0.6 4.2 %pick.1 = bf16[2048,256]{1,0:T(8,128)(2,1)} custom-call(s32[1,2048]{1,0:T(1,128)} %row_far.1, bf16[1536,256]{1,0:T(8,128)(2,1)} %x_far.1), custom_call_target="tpu_custom_call" | custom-call | flops 1610612736 | bytes 6291456 | tf_op jit(solution)/shard_map/pick/pallas_call | solution.py:31
  4.9 0.0 copy-start.12
  4.9 0.0 copy-start.3
  4.9 0.0 copy-start.4
  4.9 0.0 copy-start.5
  4.9 0.0 copy-start.6
  4.9 0.0 copy-start.8
  5.0 13.1 %all-to-all-start = ((bf16[64,32,256]{2,1,0:T(8,128)(2,1)}), bf16[64,32,256]{2,1,0:T(8,128)(2,1)S(1)}, u32[]{:S(2)}, u32[]{:S(2)}) async-start(bf16[64,32,256]{2,1,0:T(8,128)(2,1)} %bitcast.3), calls=%async_computation | async-start | bytes 2097152 | tf_op jit(solution)/shard_map/all_to_all | solution.py:267
  18.1 0.1 fusion
  18.2 0.1 reshape.59
  18.3 0.3 iota.10.mask_ref
  18.7 11.2 %count.1 = (bf16[2048,512]{1,0:T(8,128)(2,1)S(1)}, bf16[512,128]{1,0:T(8,128)(2,1)S(1)}, bf16[512,128]{1,0:T(8,128)(2,1)S(1)}) custom-call(s32[25,512]{1,0:T(8,128)S(1)} %bitcast.14, s32[1,512]{1,0:T(1,128)S(1)} %bitcast.16, bf16[2048,128]{1,0:T(8,128)(2,1)S(1)} %iota.10.mask_ref, s32[1,128]{1,0:T(1,128)S(1)} %bitcast.18, s32[10,128]{1,0:T(8,128)S(1)} %bitcast.15), custom_call_target="tpu_custom_call" | custom-call | bytes 16777216 | tf_op jit(solution)/shard_map/count/pallas_call | solution.py:31
  29.9 1.4 %copy-done.7 = bf16[2048,512]{1,0:T(8,128)(2,1)} copy-done((bf16[2048,512]{1,0:T(8,128)(2,1)}, bf16[2048,512]{1,0:T(8,128)(2,1)S(1)}, u32[]{:S(2)}) %copy-start.7) | copy-done | bytes 2097176
  31.3 15.4 %all-to-all-done = bf16[64,32,256]{2,1,0:T(8,128)(2,1)S(1)} async-done(((bf16[64,32,256]{2,1,0:T(8,128)(2,1)}), bf16[64,32,256]{2,1,0:T(8,128)(2,1)S(1)}, u32[]{:S(2)}, u32[]{:S(2)}) %all-to-all-start) | async-done | bytes 1048608 | tf_op jit(solution)/shard_map/all_to_all | solution.py:267
  46.7 3.0 %gather.1 = (bf16[256,512]{1,0:T(8,128)(2,1)S(1)}, bf16[256,512]{1,0:T(8,128)(2,1)S(1)}, bf16[64,512]{1,0:T(8,128)(2,1)S(1)}, bf16[64,512]{1,0:T(8,128)(2,1)S(1)...) custom-call(s32[1]{0:T(128)} %bitcast.1.place_ref, bf16[2048,256]{1,0:T(8,128)(2,1)S(1)} %bitcast.13, ...), custom_call_target="tpu_custom_call" | custom-call | flops 1073741824 | bytes 4194304 | tf_op jit(solution)/shard_map/gather/pallas_call | solution.py:31
  49.7 1.4 %collective-permute-start = (bf16[64,512]{1,0:T(8,128)(2,1)S(1)}, bf16[64,512]{1,0:T(8,128)(2,1)S(1)}, u32[]{:S(2)}, u32[]{:S(2)}) collective-permute-start(bf16[64,512]{1,0:T(8,128)(2,1)S(1)} %get-tuple-element.38), channel_id=1, source_target_pairs={{0,1},{1,2},{2,3},{3,0},{4,5},{5,6},{6,7},{7,4},{8,9},{9,10},{10,1... | collective-permute-start | bytes 196616 | tf_op jit(solution)/shard_map/ppermute | solution.py:274
  51.1 2.6 %collective-permute-start.1 = (bf16[64,512]{1,0:T(8,128)(2,1)S(1)}, bf16[64,512]{1,0:T(8,128)(2,1)S(1)}, u32[]{:S(2)}, u32[]{:S(2)}) collective-permute-start(bf16[64,512]{1,0:T(8,128)(2,1)S(1)} %get-tuple-element.39), channel_id=1, source_target_pairs={{0,2},{1,3},{2,0},{3,1},{4,6},{5,7},{6,4},{7,5},{8,10},{9,11},{10,... | collective-permute-start | bytes 196616 | tf_op jit(solution)/shard_map/ppermute | solution.py:274
  53.7 1.1 collective-permute-start.2
  54.8 0.1 copy.19.bias_ref
  54.9 2.4 %collective-permute-done.1.refs_2_ = bf16[64,512]{1,0:T(8,128)(2,1)S(1)} collective-permute-done((bf16[64,512]{1,0:T(8,128)(2,1)S(1)}, bf16[64,512]{1,0:T(8,128)(2,1)S(1)}, u32[]{:S(2)}, u32[]{:S(2)}) %collective-permute-start.1) | collective-permute-done | bytes 65568 | tf_op jit(solution)/shard_map/ppermute | solution.py:274
  57.3 0.4 owner.1.refs_0_
  57.7 1.9 %collective-permute-start.5 = (bf16[96,512]{1,0:T(8,128)(2,1)S(1)}, bf16[96,512]{1,0:T(8,128)(2,1)S(1)}, u32[]{:S(2)}, u32[]{:S(2)}) collective-permute-start(bf16[96,512]{1,0:T(8,128)(2,1)S(1)} %owner.1.refs_0_), channel_id=1, source_target_pairs={{0,3},{1,0},{2,1},{3,2},{4,7},{5,4},{6,5},{7,6},{8,11},{9,8},{10,9... | collective-permute-start | bytes 294920 | tf_op jit(solution)/shard_map/ppermute | solution.py:274
  59.6 0.2 collective-permute-start.4
  59.8 0.8 collective-permute-start.3
  60.6 1.1 %collective-permute-done.5.refs_3_ = bf16[96,512]{1,0:T(8,128)(2,1)S(1)} collective-permute-done((bf16[96,512]{1,0:T(8,128)(2,1)S(1)}, bf16[96,512]{1,0:T(8,128)(2,1)S(1)}, u32[]{:S(2)}, u32[]{:S(2)}) %collective-permute-start.5) | collective-permute-done | bytes 98336 | tf_op jit(solution)/shard_map/ppermute | solution.py:274
  61.7 3.0 %collective-permute-done.4.refs_2_ = bf16[96,512]{1,0:T(8,128)(2,1)S(1)} collective-permute-done((bf16[96,512]{1,0:T(8,128)(2,1)S(1)}, bf16[96,512]{1,0:T(8,128)(2,1)S(1)}, u32[]{:S(2)}, u32[]{:S(2)}) %collective-permute-start.4) | collective-permute-done | bytes 98336 | tf_op jit(solution)/shard_map/ppermute | solution.py:274
  64.7 0.9 collective-permute-done.3.refs_1_
  65.5 0.5 weight.1
  66.0 3.4 %collective-permute-start.6 = (bf16[256,512]{1,0:T(8,128)(2,1)S(1)}, bf16[256,512]{1,0:T(8,128)(2,1)S(1)}, u32[]{:S(2)}, u32[]{:S(2)}) collective-permute-start(bf16[256,512]{1,0:T(8,128)(2,1)S(1)} %get-tuple-element.42), channel_id=1, source_target_pairs={{0,4},{4,0},{1,5},{5,1},{2,6},{6,2},{3,7},{7,3},{8,12},{12,8},{9,1... | collective-permute-start | bytes 786440 | tf_op jit(solution)/shard_map/ppermute | solution.py:280
  69.4 1.2 %collective-permute-done.6.got_ref = bf16[256,512]{1,0:T(8,128)(2,1)S(1)} collective-permute-done((bf16[256,512]{1,0:T(8,128)(2,1)S(1)}, bf16[256,512]{1,0:T(8,128)(2,1)S(1)}, u32[]{:S(2)}, u32[]{:S(2)}) %collective-permute-start.6) | collective-permute-done | bytes 262176 | tf_op jit(solution)/shard_map/ppermute | solution.py:280
  70.6 1.8 %collective-permute-start.7 = (bf16[64,512]{1,0:T(8,128)(2,1)S(1)}, bf16[64,512]{1,0:T(8,128)(2,1)S(1)}, u32[]{:S(2)}, u32[]{:S(2)}) collective-permute-start(bf16[64,512]{1,0:T(8,128)(2,1)S(1)} %get-tuple-element.44), channel_id=1, source_target_pairs={{0,64},{64,128},{128,192},{192,0},{1,65},{65,129},{129,193},{193,1... | collective-permute-start | bytes 196616 | tf_op jit(solution)/shard_map/ppermute | solution.py:274
  72.3 2.0 %collective-permute-start.8 = (bf16[64,512]{1,0:T(8,128)(2,1)S(1)}, bf16[64,512]{1,0:T(8,128)(2,1)S(1)}, u32[]{:S(2)}, u32[]{:S(2)}) collective-permute-start(bf16[64,512]{1,0:T(8,128)(2,1)S(1)} %get-tuple-element.45), channel_id=1, source_target_pairs={{0,128},{64,192},{128,0},{192,64},{1,129},{65,193},{129,1},{193,65... | collective-permute-start | bytes 196616 | tf_op jit(solution)/shard_map/ppermute | solution.py:274
  74.3 1.1 collective-permute-start.9
  75.4 2.5 %collective-permute-done.8.refs_2_ = bf16[64,512]{1,0:T(8,128)(2,1)S(1)} collective-permute-done((bf16[64,512]{1,0:T(8,128)(2,1)S(1)}, bf16[64,512]{1,0:T(8,128)(2,1)S(1)}, u32[]{:S(2)}, u32[]{:S(2)}) %collective-permute-start.8) | collective-permute-done | bytes 65568 | tf_op jit(solution)/shard_map/ppermute | solution.py:274
  78.0 0.8 spread.1
  78.8 3.7 %all-to-all-start.1 = ((bf16[8,64,512]{2,1,0:T(8,128)(2,1)}), bf16[8,64,512]{2,1,0:T(8,128)(2,1)S(1)}, u32[]{:S(2)}, u32[]{:S(2)}) async-start(bf16[8,64,512]{2,1,0:T(8,128)(2,1)} %spread.1), calls=%async_computation.1 | async-start | bytes 1048576 | tf_op jit(solution)/shard_map/all_to_all | solution.py:267
  82.5 1.0 embed.1
  83.4 15.2 %all-to-all-done.1.parts_ref = bf16[8,64,512]{2,1,0:T(8,128)(2,1)S(1)} async-done(((bf16[8,64,512]{2,1,0:T(8,128)(2,1)}), bf16[8,64,512]{2,1,0:T(8,128)(2,1)S(1)}, u32[]{:S(2)}, u32[]{:S(2)}) %all-to-all-start.1) | async-done | bytes 524320 | tf_op jit(solution)/shard_map/all_to_all | solution.py:267
  98.6 0.1 sum.1.refs_0_
  98.7 1.4 %collective-permute-start.12 = (bf16[64,512]{1,0:T(8,128)(2,1)S(1)}, bf16[64,512]{1,0:T(8,128)(2,1)S(1)}, u32[]{:S(2)}, u32[]{:S(2)}) collective-permute-start(bf16[64,512]{1,0:T(8,128)(2,1)S(1)} %sum.1.refs_0_), channel_id=1, source_target_pairs={{0,192},{64,0},{128,64},{192,128},{1,193},{65,1},{129,65},{193,129... | collective-permute-start | bytes 196616 | tf_op jit(solution)/shard_map/ppermute | solution.py:274
  100.1 1.2 %collective-permute-start.11 = (bf16[64,512]{1,0:T(8,128)(2,1)S(1)}, bf16[64,512]{1,0:T(8,128)(2,1)S(1)}, u32[]{:S(2)}, u32[]{:S(2)}) collective-permute-start(bf16[64,512]{1,0:T(8,128)(2,1)S(1)} %sum.1.refs_0_), channel_id=1, source_target_pairs={{0,128},{64,192},{128,0},{192,64},{1,129},{65,193},{129,1},{193,65... | collective-permute-start | bytes 196616 | tf_op jit(solution)/shard_map/ppermute | solution.py:274
  101.2 2.7 %collective-permute-start.13 = (bf16[64,512]{1,0:T(8,128)(2,1)S(1)}, bf16[64,512]{1,0:T(8,128)(2,1)S(1)}, u32[]{:S(2)}, u32[]{:S(2)}) collective-permute-start(bf16[64,512]{1,0:T(8,128)(2,1)S(1)} %sum.1.refs_0_), channel_id=1, source_target_pairs={{0,4},{4,0},{1,5},{5,1},{2,6},{6,2},{3,7},{7,3},{8,12},{12,8},{9,1... | collective-permute-start | bytes 196616 | tf_op jit(solution)/shard_map/ppermute | solution.py:280
  103.9 1.6 %collective-permute-start.16 = (bf16[64,512]{1,0:T(8,128)(2,1)S(1)}, bf16[64,512]{1,0:T(8,128)(2,1)S(1)}, u32[]{:S(2)}, u32[]{:S(2)}) collective-permute-start(bf16[64,512]{1,0:T(8,128)(2,1)S(1)} %collective-permute-done.12.refs_3_), channel_id=1, source_target_pairs={{0,4},{4,0},{1,5},{5,1},{2,6},{6,2},{3,7},{7,3},{8,12},{12,8},{9,1... | collective-permute-start | bytes 196616 | tf_op jit(solution)/shard_map/ppermute | solution.py:280
  105.5 3.3 %collective-permute-start.15 = (bf16[64,512]{1,0:T(8,128)(2,1)S(1)}, bf16[64,512]{1,0:T(8,128)(2,1)S(1)}, u32[]{:S(2)}, u32[]{:S(2)}) collective-permute-start(bf16[64,512]{1,0:T(8,128)(2,1)S(1)} %collective-permute-done.11.refs_2_), channel_id=1, source_target_pairs={{0,4},{4,0},{1,5},{5,1},{2,6},{6,2},{3,7},{7,3},{8,12},{12,8},{9,1... | collective-permute-start | bytes 196616 | tf_op jit(solution)/shard_map/ppermute | solution.py:280
  108.8 0.7 collective-permute-start.14
  109.5 0.2 collective-permute-done.15.refs_6_
  109.7 0.7 collective-permute-done.14.refs_5_
  110.4 1.0 finish.1
  (30 shorter events, 0.1 us)
Async XLA Ops:
  4.9 13.2 %copy-start.12 = (s32[1,64]{1,0:T(1,128)S(1)}, s32[1,64]{1,0:T(1,128)}, u32[]{:S(2)}) copy-start(s32[1,64]{1,0:T(1,128)} %param.21) | copy-start | bytes 772
  4.9 13.8 %copy-start.3 = (s32[512,25]{0,1:T(8,128)S(1)}, s32[512,25]{0,1:T(8,128)}, u32[]{:S(2)}) copy-start(s32[512,25]{0,1:T(8,128)} %param.23) | copy-start | bytes 153604
  4.9 13.8 %copy-start.4 = (s32[128,10]{0,1:T(8,128)S(1)}, s32[128,10]{0,1:T(8,128)}, u32[]{:S(2)}) copy-start(s32[128,10]{0,1:T(8,128)} %param.26) | copy-start | bytes 15364
  4.9 13.7 %copy-start.5 = (s32[512]{0:T(512)S(1)}, s32[512]{0:T(512)}, u32[]{:S(2)}) copy-start(s32[512]{0:T(512)} %param.24) | copy-start | bytes 6148
  4.9 13.7 %copy-start.6 = (s32[128]{0:T(128)S(1)}, s32[128]{0:T(128)}, u32[]{:S(2)}) copy-start(s32[128]{0:T(128)} %param.25) | copy-start | bytes 1540
  4.9 41.7 %copy-start.8 = (bf16[256,256]{1,0:T(8,128)(2,1)S(1)}, bf16[256,256]{1,0:T(8,128)(2,1)}, u32[]{:S(2)}) copy-start(bf16[256,256]{1,0:T(8,128)(2,1)} %weight_self_ref.1) | copy-start | bytes 393220
  4.9 41.7 %copy-start.9 = (bf16[256,256]{1,0:T(8,128)(2,1)S(1)}, bf16[256,256]{1,0:T(8,128)(2,1)}, u32[]{:S(2)}) copy-start(bf16[256,256]{1,0:T(8,128)(2,1)} %weight_near_ref.1) | copy-start | bytes 393220
  4.9 41.7 %copy-start.10 = (s32[512]{0:T(512)S(1)}, s32[512]{0:T(512)}, u32[]{:S(2)}) copy-start(s32[512]{0:T(512)} %param.22) | copy-start | bytes 6148
  5.0 41.7 %all-to-all-start = ((bf16[64,32,256]{2,1,0:T(8,128)(2,1)}), bf16[64,32,256]{2,1,0:T(8,128)(2,1)S(1)}, u32[]{:S(2)}, u32[]{:S(2)}) async-start(bf16[64,32,256]{2,1,0:T(8,128)(2,1)} %bitcast.3), calls=%async_computation | async-start | bytes 2097152 | tf_op jit(solution)/shard_map/all_to_all | solution.py:267
  29.9 1.4 %copy-start.7 = (bf16[2048,512]{1,0:T(8,128)(2,1)}, bf16[2048,512]{1,0:T(8,128)(2,1)S(1)}, u32[]{:S(2)}) copy-start(bf16[2048,512]{1,0:T(8,128)(2,1)S(1)} %get-tuple-element.31) | copy-start | bytes 6291460
  31.3 23.5 %copy-start.11 = (f32[256]{0:T(256)S(1)}, f32[256]{0:T(256)}, u32[]{:S(2)}) copy-start(f32[256]{0:T(256)} %param.17) | copy-start | bytes 3076
  31.3 26.0 %copy-start = (bf16[256,256]{1,0:T(8,128)(2,1)S(1)}, bf16[256,256]{1,0:T(8,128)(2,1)}, u32[]{:S(2)}) copy-start(bf16[256,256]{1,0:T(8,128)(2,1)} %second_self_ref.3) | copy-start | bytes 393220
  31.3 26.0 %copy-start.1 = (bf16[256,256]{1,0:T(8,128)(2,1)S(1)}, bf16[256,256]{1,0:T(8,128)(2,1)}, u32[]{:S(2)}) copy-start(bf16[256,256]{1,0:T(8,128)(2,1)} %second_near_ref.3) | copy-start | bytes 393220
  31.3 26.0 %copy-start.2 = (bf16[128,256]{1,0:T(8,128)(2,1)S(1)}, bf16[128,256]{1,0:T(8,128)(2,1)}, u32[]{:S(2)}) copy-start(bf16[128,256]{1,0:T(8,128)(2,1)} %cotangent_ref.3) | copy-start | bytes 196612
  49.7 5.2 %collective-permute-start = (bf16[64,512]{1,0:T(8,128)(2,1)S(1)}, bf16[64,512]{1,0:T(8,128)(2,1)S(1)}, u32[]{:S(2)}, u32[]{:S(2)}) collective-permute-start(bf16[64,512]{1,0:T(8,128)(2,1)S(1)} %get-tuple-element.38), channel_id=1, source_target_pairs={{0,1},{1,2},{2,3},{3,0},{4,5},{5,6},{6,7},{7,4},{8,9},{9,10},{10,1... | collective-permute-start | bytes 196616 | tf_op jit(solution)/shard_map/ppermute | solution.py:274
  51.1 6.2 %collective-permute-start.1 = (bf16[64,512]{1,0:T(8,128)(2,1)S(1)}, bf16[64,512]{1,0:T(8,128)(2,1)S(1)}, u32[]{:S(2)}, u32[]{:S(2)}) collective-permute-start(bf16[64,512]{1,0:T(8,128)(2,1)S(1)} %get-tuple-element.39), channel_id=1, source_target_pairs={{0,2},{1,3},{2,0},{3,1},{4,6},{5,7},{6,4},{7,5},{8,10},{9,11},{10,... | collective-permute-start | bytes 196616 | tf_op jit(solution)/shard_map/ppermute | solution.py:274
  53.7 3.6 %collective-permute-start.2 = (bf16[64,512]{1,0:T(8,128)(2,1)S(1)}, bf16[64,512]{1,0:T(8,128)(2,1)S(1)}, u32[]{:S(2)}, u32[]{:S(2)}) collective-permute-start(bf16[64,512]{1,0:T(8,128)(2,1)S(1)} %get-tuple-element.40), channel_id=1, source_target_pairs={{0,3},{1,0},{2,1},{3,2},{4,7},{5,4},{6,5},{7,6},{8,11},{9,8},{10,9... | collective-permute-start | bytes 196616 | tf_op jit(solution)/shard_map/ppermute | solution.py:274
  57.7 4.0 %collective-permute-start.5 = (bf16[96,512]{1,0:T(8,128)(2,1)S(1)}, bf16[96,512]{1,0:T(8,128)(2,1)S(1)}, u32[]{:S(2)}, u32[]{:S(2)}) collective-permute-start(bf16[96,512]{1,0:T(8,128)(2,1)S(1)} %owner.1.refs_0_), channel_id=1, source_target_pairs={{0,3},{1,0},{2,1},{3,2},{4,7},{5,4},{6,5},{7,6},{8,11},{9,8},{10,9... | collective-permute-start | bytes 294920 | tf_op jit(solution)/shard_map/ppermute | solution.py:274
  59.6 5.1 %collective-permute-start.4 = (bf16[96,512]{1,0:T(8,128)(2,1)S(1)}, bf16[96,512]{1,0:T(8,128)(2,1)S(1)}, u32[]{:S(2)}, u32[]{:S(2)}) collective-permute-start(bf16[96,512]{1,0:T(8,128)(2,1)S(1)} %owner.1.refs_0_), channel_id=1, source_target_pairs={{0,2},{1,3},{2,0},{3,1},{4,6},{5,7},{6,4},{7,5},{8,10},{9,11},{10,... | collective-permute-start | bytes 294920 | tf_op jit(solution)/shard_map/ppermute | solution.py:274
  59.8 5.7 %collective-permute-start.3 = (bf16[96,512]{1,0:T(8,128)(2,1)S(1)}, bf16[96,512]{1,0:T(8,128)(2,1)S(1)}, u32[]{:S(2)}, u32[]{:S(2)}) collective-permute-start(bf16[96,512]{1,0:T(8,128)(2,1)S(1)} %owner.1.refs_0_), channel_id=1, source_target_pairs={{0,1},{1,2},{2,3},{3,0},{4,5},{5,6},{6,7},{7,4},{8,9},{9,10},{10,1... | collective-permute-start | bytes 294920 | tf_op jit(solution)/shard_map/ppermute | solution.py:274
  66.0 4.5 %collective-permute-start.6 = (bf16[256,512]{1,0:T(8,128)(2,1)S(1)}, bf16[256,512]{1,0:T(8,128)(2,1)S(1)}, u32[]{:S(2)}, u32[]{:S(2)}) collective-permute-start(bf16[256,512]{1,0:T(8,128)(2,1)S(1)} %get-tuple-element.42), channel_id=1, source_target_pairs={{0,4},{4,0},{1,5},{5,1},{2,6},{6,2},{3,7},{7,3},{8,12},{12,8},{9,1... | collective-permute-start | bytes 786440 | tf_op jit(solution)/shard_map/ppermute | solution.py:280
  70.6 4.8 %collective-permute-start.7 = (bf16[64,512]{1,0:T(8,128)(2,1)S(1)}, bf16[64,512]{1,0:T(8,128)(2,1)S(1)}, u32[]{:S(2)}, u32[]{:S(2)}) collective-permute-start(bf16[64,512]{1,0:T(8,128)(2,1)S(1)} %get-tuple-element.44), channel_id=1, source_target_pairs={{0,64},{64,128},{128,192},{192,0},{1,65},{65,129},{129,193},{193,1... | collective-permute-start | bytes 196616 | tf_op jit(solution)/shard_map/ppermute | solution.py:274
  72.3 5.6 %collective-permute-start.8 = (bf16[64,512]{1,0:T(8,128)(2,1)S(1)}, bf16[64,512]{1,0:T(8,128)(2,1)S(1)}, u32[]{:S(2)}, u32[]{:S(2)}) collective-permute-start(bf16[64,512]{1,0:T(8,128)(2,1)S(1)} %get-tuple-element.45), channel_id=1, source_target_pairs={{0,128},{64,192},{128,0},{192,64},{1,129},{65,193},{129,1},{193,65... | collective-permute-start | bytes 196616 | tf_op jit(solution)/shard_map/ppermute | solution.py:274
  74.3 3.6 %collective-permute-start.9 = (bf16[64,512]{1,0:T(8,128)(2,1)S(1)}, bf16[64,512]{1,0:T(8,128)(2,1)S(1)}, u32[]{:S(2)}, u32[]{:S(2)}) collective-permute-start(bf16[64,512]{1,0:T(8,128)(2,1)S(1)} %get-tuple-element.46), channel_id=1, source_target_pairs={{0,192},{64,0},{128,64},{192,128},{1,193},{65,1},{129,65},{193,129... | collective-permute-start | bytes 196616 | tf_op jit(solution)/shard_map/ppermute | solution.py:274
  78.8 19.8 %all-to-all-start.1 = ((bf16[8,64,512]{2,1,0:T(8,128)(2,1)}), bf16[8,64,512]{2,1,0:T(8,128)(2,1)S(1)}, u32[]{:S(2)}, u32[]{:S(2)}) async-start(bf16[8,64,512]{2,1,0:T(8,128)(2,1)} %spread.1), calls=%async_computation.1 | async-start | bytes 1048576 | tf_op jit(solution)/shard_map/all_to_all | solution.py:267
  98.7 5.2 %collective-permute-start.12 = (bf16[64,512]{1,0:T(8,128)(2,1)S(1)}, bf16[64,512]{1,0:T(8,128)(2,1)S(1)}, u32[]{:S(2)}, u32[]{:S(2)}) collective-permute-start(bf16[64,512]{1,0:T(8,128)(2,1)S(1)} %sum.1.refs_0_), channel_id=1, source_target_pairs={{0,192},{64,0},{128,64},{192,128},{1,193},{65,1},{129,65},{193,129... | collective-permute-start | bytes 196616 | tf_op jit(solution)/shard_map/ppermute | solution.py:274
  100.1 5.4 %collective-permute-start.11 = (bf16[64,512]{1,0:T(8,128)(2,1)S(1)}, bf16[64,512]{1,0:T(8,128)(2,1)S(1)}, u32[]{:S(2)}, u32[]{:S(2)}) collective-permute-start(bf16[64,512]{1,0:T(8,128)(2,1)S(1)} %sum.1.refs_0_), channel_id=1, source_target_pairs={{0,128},{64,192},{128,0},{192,64},{1,129},{65,193},{129,1},{193,65... | collective-permute-start | bytes 196616 | tf_op jit(solution)/shard_map/ppermute | solution.py:274
  101.2 7.5 %collective-permute-start.10 = (bf16[64,512]{1,0:T(8,128)(2,1)S(1)}, bf16[64,512]{1,0:T(8,128)(2,1)S(1)}, u32[]{:S(2)}, u32[]{:S(2)}) collective-permute-start(bf16[64,512]{1,0:T(8,128)(2,1)S(1)} %sum.1.refs_0_), channel_id=1, source_target_pairs={{0,64},{64,128},{128,192},{192,0},{1,65},{65,129},{129,193},{193,1... | collective-permute-start | bytes 196616 | tf_op jit(solution)/shard_map/ppermute | solution.py:274
  101.2 8.2 %collective-permute-start.13 = (bf16[64,512]{1,0:T(8,128)(2,1)S(1)}, bf16[64,512]{1,0:T(8,128)(2,1)S(1)}, u32[]{:S(2)}, u32[]{:S(2)}) collective-permute-start(bf16[64,512]{1,0:T(8,128)(2,1)S(1)} %sum.1.refs_0_), channel_id=1, source_target_pairs={{0,4},{4,0},{1,5},{5,1},{2,6},{6,2},{3,7},{7,3},{8,12},{12,8},{9,1... | collective-permute-start | bytes 196616 | tf_op jit(solution)/shard_map/ppermute | solution.py:280
  103.9 5.5 %collective-permute-start.16 = (bf16[64,512]{1,0:T(8,128)(2,1)S(1)}, bf16[64,512]{1,0:T(8,128)(2,1)S(1)}, u32[]{:S(2)}, u32[]{:S(2)}) collective-permute-start(bf16[64,512]{1,0:T(8,128)(2,1)S(1)} %collective-permute-done.12.refs_3_), channel_id=1, source_target_pairs={{0,4},{4,0},{1,5},{5,1},{2,6},{6,2},{3,7},{7,3},{8,12},{12,8},{9,1... | collective-permute-start | bytes 196616 | tf_op jit(solution)/shard_map/ppermute | solution.py:280
  105.5 4.2 %collective-permute-start.15 = (bf16[64,512]{1,0:T(8,128)(2,1)S(1)}, bf16[64,512]{1,0:T(8,128)(2,1)S(1)}, u32[]{:S(2)}, u32[]{:S(2)}) collective-permute-start(bf16[64,512]{1,0:T(8,128)(2,1)S(1)} %collective-permute-done.11.refs_2_), channel_id=1, source_target_pairs={{0,4},{4,0},{1,5},{5,1},{2,6},{6,2},{3,7},{7,3},{8,12},{12,8},{9,1... | collective-permute-start | bytes 196616 | tf_op jit(solution)/shard_map/ppermute | solution.py:280
  108.8 1.6 %collective-permute-start.14 = (bf16[64,512]{1,0:T(8,128)(2,1)S(1)}, bf16[64,512]{1,0:T(8,128)(2,1)S(1)}, u32[]{:S(2)}, u32[]{:S(2)}) collective-permute-start(bf16[64,512]{1,0:T(8,128)(2,1)S(1)} %collective-permute-done.10.refs_1_), channel_id=1, source_target_pairs={{0,4},{4,0},{1,5},{5,1},{2,6},{6,2},{3,7},{7,3},{8,12},{12,8},{9,1... | collective-permute-start | bytes 196616 | tf_op jit(solution)/shard_map/ppermute | solution.py:280

commit v11 on v10

--- a/solution.py
+++ b/solution.py
@@ -68,7 +68,7 @@
         out_ref[pl.ds(start, step), :] = dot(picks, x_ref[...]).astype(BF16)
         return carry
 
-    lax.fori_loop(0, out_ref.shape[0] // step, fill, 0, unroll=8)
+    lax.fori_loop(0, out_ref.shape[0] // step, fill, 0, unroll=True)
 
 
 def count_body(
@@ -219,18 +219,11 @@
         out_ref[...] = (keep_ref[span, :] + got_ref[span, :].astype(F32)).astype(BF16)
 
 
-def spread_body(*refs):
-    parts, out_ref = refs[:-1], refs[-1]
-    total = parts[0][...].astype(F32)
-    for part in parts[1:]:
-        total = total + part[...].astype(F32)
-    total = total.astype(BF16)
-    for at in range(out_ref.shape[0]):
-        out_ref[at] = total
-
-
-def sum_body(parts_ref, out_ref):
-    out_ref[...] = jnp.sum(parts_ref[...].astype(F32), axis=0).astype(BF16)
+def add_body(*refs):
+    total = refs[0][...].astype(F32)
+    for ref in refs[1:-1]:
+        total = total + ref[...].astype(F32)
+    refs[-1][...] = total.astype(BF16)
 
 
 def finish_body(core_ref, x_ref, *refs, count, cores):
@@ -376,17 +369,20 @@
         scalars=1,
     )
     (mixed,) = call(
-        spread_body, [((count_z,) + shard, BF16)], shifted(parts, "x", count_x), "spread",
-        0, 4 * tall * hidden,
-    )
-    mixed = exchange(mixed, "z")
+        add_body, [(shard, BF16)], shifted(parts, "x", count_x), "add", 0, 4 * tall * hidden
+    )
+    stride = 1
+    while stride < count_z:
+        (mixed,) = call(
+            add_body, [(shard, BF16)], (mixed, swapped(mixed, "z", count_z, stride)), "add",
+            0, 2 * tall * hidden,
+        )
+        stride *= 2
     (seed_embedding,) = call(
         functools.partial(embed_body, half=half), [((seeds, out_cols), BF16)],
         (at_feat, second_self, second_neighbor, *grads), "embed",
         4 * seeds * hidden * out_cols, 8 * seeds * hidden, scalars=1,
     )
-    mixed, seed_embedding = lax.optimization_barrier((mixed, seed_embedding))
-    (mixed,) = call(sum_body, [(shard, BF16)], (mixed,), "sum", 0, 8 * tall * hidden)
     mine = shifted([mixed] * count_x, "x", count_x)
     other = [swapped(piece, "core", cores, 1) for piece in mine]
     grad_first_self, grad_first_neighbor, grad_second_self, grad_second_neighbor = call(

time: 112 us -> 110 us (0.982)
  waiting for transfers between devices: 42.5 us -> 39.3 us
  starting transfers between devices: 43.7 us -> 46.1 us
    all_to_all x2 -> x1, waiting for transfers between devices: 30.6 us -> 15.4 us  [exchange(): return lax.all_to_all(value, axis, split_axis=0, concat_axis=0, tiled=True)]
    ppermute x5 -> x8, waiting for transfers between devices: 2.06 us -> 14 us  [swapped(): return lax.ppermute(value, axis, [(at, at ^ step) for at in range(count)])]
    ppermute x5 -> x8, starting transfers between devices: 11.6 us -> 18 us  [swapped(): return lax.ppermute(value, axis, [(at, at ^ step) for at in range(count)])]
    all_to_all x2 -> x1, starting transfers between devices: 16.8 us -> 13.1 us  [exchange(): return lax.all_to_all(value, axis, split_axis=0, concat_axis=0, tiled=True)]
    pallas_call x10 -> x12, Pallas kernels: 22.3 us -> 21.2 us  [call(): pl.pallas_call(body, out_shape=[jax.ShapeDtypeStruct(shape, dtype) for sh...]
  transfers between devices with their start and end apart: 19 -> 21, of which waited for: 10 -> 10; matrix products, arithmetic and copies ran while one was open for 1% -> 1% of each run, Pallas kernels for 11% -> 11%
where the time goes in v11:
time: 110 us
  starting transfers between devices  46.1 us (42%)
  waiting for transfers between devices  39.3 us (36%)
  Pallas kernels  21.2 us (19%)
  local copies, waits for them, and re-layouts  1.99 us (2%)
    pallas_call x12, Pallas kernels, call(): pl.pallas_call(body, out_shape=[jax.ShapeDtypeStruct(shape, dtype) for sh...  21.2 us
    ppermute x8, starting transfers between devices, swapped(): return lax.ppermute(value, axis, [(at, at ^ step) for at in range(count)])  18 us
    all_to_all x1, waiting for transfers between devices, exchange(): return lax.all_to_all(value, axis, split_axis=0, concat_axis=0, tiled=True)  15.4 us
    ppermute x12, starting transfers between devices, shifted(): lax.ppermute(piece, axis, [(at, (at + shift) % count) for at in range(cou...  15 us
    ppermute x8, waiting for transfers between devices, swapped(): return lax.ppermute(value, axis, [(at, at ^ step) for at in range(count)])  14 us
    all_to_all x1, starting transfers between devices, exchange(): return lax.all_to_all(value, axis, split_axis=0, concat_axis=0, tiled=True)  13.1 us
    ppermute x12, waiting for transfers between devices, shifted(): lax.ppermute(piece, axis, [(at, (at + shift) % count) for at in range(cou...  9.88 us
  transfers between devices with their start and end apart: 21, of which 10 were waited for; matrix products, arithmetic and copies ran while one was open for 1% of the time, Pallas kernels for 11%

profile of v11, /device:TPU:1, one launch (start us, length us, event | category | flops | bytes accessed | tf_op | source)
XLA Modules:
  0.0 109.5 jit_solution(7839079892129347771)
XLA Ops:
  0.6 4.0 %pick.1 = bf16[2048,256]{1,0:T(8,128)(2,1)} custom-call(s32[1,2048]{1,0:T(1,128)} %row_far.1, bf16[1536,256]{1,0:T(8,128)(2,1)} %x_far.1), custom_call_target="tpu_custom_call" | custom-call | flops 1610612736 | bytes 6291456 | tf_op jit(solution)/shard_map/pick/pallas_call | solution.py:31
  4.6 0.0 copy-start.12
  4.6 0.0 copy-start.3
  4.7 0.0 copy-start.4
  4.7 0.0 copy-start.6
  4.7 0.0 copy-start.8
  4.7 13.1 %all-to-all-start = ((bf16[64,32,256]{2,1,0:T(8,128)(2,1)}), bf16[64,32,256]{2,1,0:T(8,128)(2,1)S(1)}, u32[]{:S(2)}, u32[]{:S(2)}) async-start(bf16[64,32,256]{2,1,0:T(8,128)(2,1)} %bitcast.1), calls=%async_computation | async-start | bytes 2097152 | tf_op jit(solution)/shard_map/all_to_all | solution.py:260
  17.9 0.1 fusion
  18.0 0.1 reshape.59
  18.1 0.3 iota.10.mask_ref
  18.4 11.2 %count.1 = (bf16[2048,512]{1,0:T(8,128)(2,1)S(1)}, bf16[512,128]{1,0:T(8,128)(2,1)S(1)}, bf16[512,128]{1,0:T(8,128)(2,1)S(1)}) custom-call(s32[25,512]{1,0:T(8,128)S(1)} %bitcast.14, s32[1,512]{1,0:T(1,128)S(1)} %bitcast.16, bf16[2048,128]{1,0:T(8,128)(2,1)S(1)} %iota.10.mask_ref, s32[1,128]{1,0:T(1,128)S(1)} %bitcast.18, s32[10,128]{1,0:T(8,128)S(1)} %bitcast.15), custom_call_target="tpu_custom_call" | custom-call | bytes 16777216 | tf_op jit(solution)/shard_map/count/pallas_call | solution.py:31
  29.7 1.4 %copy-done.7 = bf16[2048,512]{1,0:T(8,128)(2,1)} copy-done((bf16[2048,512]{1,0:T(8,128)(2,1)}, bf16[2048,512]{1,0:T(8,128)(2,1)S(1)}, u32[]{:S(2)}) %copy-start.7) | copy-done | bytes 2097176
  31.0 15.4 %all-to-all-done = bf16[64,32,256]{2,1,0:T(8,128)(2,1)S(1)} async-done(((bf16[64,32,256]{2,1,0:T(8,128)(2,1)}), bf16[64,32,256]{2,1,0:T(8,128)(2,1)S(1)}, u32[]{:S(2)}, u32[]{:S(2)}) %all-to-all-start) | async-done | bytes 1048608 | tf_op jit(solution)/shard_map/all_to_all | solution.py:260
  46.4 3.0 %gather.1 = (bf16[256,512]{1,0:T(8,128)(2,1)S(1)}, bf16[256,512]{1,0:T(8,128)(2,1)S(1)}, bf16[64,512]{1,0:T(8,128)(2,1)S(1)}, bf16[64,512]{1,0:T(8,128)(2,1)S(1)...) custom-call(s32[1]{0:T(128)} %bitcast.place_ref, bf16[2048,256]{1,0:T(8,128)(2,1)S(1)} %bitcast.13, ...), custom_call_target="tpu_custom_call" | custom-call | flops 1073741824 | bytes 4194304 | tf_op jit(solution)/shard_map/gather/pallas_call | solution.py:31
  49.4 1.4 %collective-permute-start = (bf16[64,512]{1,0:T(8,128)(2,1)S(1)}, bf16[64,512]{1,0:T(8,128)(2,1)S(1)}, u32[]{:S(2)}, u32[]{:S(2)}) collective-permute-start(bf16[64,512]{1,0:T(8,128)(2,1)S(1)} %get-tuple-element.34), channel_id=1, source_target_pairs={{0,1},{1,2},{2,3},{3,0},{4,5},{5,6},{6,7},{7,4},{8,9},{9,10},{10,1... | collective-permute-start | bytes 196616 | tf_op jit(solution)/shard_map/ppermute | solution.py:267
  50.8 2.6 %collective-permute-start.1 = (bf16[64,512]{1,0:T(8,128)(2,1)S(1)}, bf16[64,512]{1,0:T(8,128)(2,1)S(1)}, u32[]{:S(2)}, u32[]{:S(2)}) collective-permute-start(bf16[64,512]{1,0:T(8,128)(2,1)S(1)} %get-tuple-element.35), channel_id=1, source_target_pairs={{0,2},{1,3},{2,0},{3,1},{4,6},{5,7},{6,4},{7,5},{8,10},{9,11},{10,... | collective-permute-start | bytes 196616 | tf_op jit(solution)/shard_map/ppermute | solution.py:267
  53.5 1.1 collective-permute-start.2
  54.5 0.1 copy.19.bias_ref
  54.7 2.4 %collective-permute-done.1.refs_2_ = bf16[64,512]{1,0:T(8,128)(2,1)S(1)} collective-permute-done((bf16[64,512]{1,0:T(8,128)(2,1)S(1)}, bf16[64,512]{1,0:T(8,128)(2,1)S(1)}, u32[]{:S(2)}, u32[]{:S(2)}) %collective-permute-start.1) | collective-permute-done | bytes 65568 | tf_op jit(solution)/shard_map/ppermute | solution.py:267
  57.1 0.4 owner.1.refs_0_
  57.5 1.9 %collective-permute-start.5 = (bf16[96,512]{1,0:T(8,128)(2,1)S(1)}, bf16[96,512]{1,0:T(8,128)(2,1)S(1)}, u32[]{:S(2)}, u32[]{:S(2)}) collective-permute-start(bf16[96,512]{1,0:T(8,128)(2,1)S(1)} %owner.1.refs_0_), channel_id=1, source_target_pairs={{0,3},{1,0},{2,1},{3,2},{4,7},{5,4},{6,5},{7,6},{8,11},{9,8},{10,9... | collective-permute-start | bytes 294920 | tf_op jit(solution)/shard_map/ppermute | solution.py:267
  59.3 0.2 collective-permute-start.4
  59.6 0.8 collective-permute-start.3
  60.3 1.1 %collective-permute-done.5.refs_3_ = bf16[96,512]{1,0:T(8,128)(2,1)S(1)} collective-permute-done((bf16[96,512]{1,0:T(8,128)(2,1)S(1)}, bf16[96,512]{1,0:T(8,128)(2,1)S(1)}, u32[]{:S(2)}, u32[]{:S(2)}) %collective-permute-start.5) | collective-permute-done | bytes 98336 | tf_op jit(solution)/shard_map/ppermute | solution.py:267
  61.5 3.0 %collective-permute-done.4.refs_2_ = bf16[96,512]{1,0:T(8,128)(2,1)S(1)} collective-permute-done((bf16[96,512]{1,0:T(8,128)(2,1)S(1)}, bf16[96,512]{1,0:T(8,128)(2,1)S(1)}, u32[]{:S(2)}, u32[]{:S(2)}) %collective-permute-start.4) | collective-permute-done | bytes 98336 | tf_op jit(solution)/shard_map/ppermute | solution.py:267
  64.4 0.9 collective-permute-done.3.refs_1_
  65.3 0.5 weight.1
  65.8 3.4 %collective-permute-start.6 = (bf16[256,512]{1,0:T(8,128)(2,1)S(1)}, bf16[256,512]{1,0:T(8,128)(2,1)S(1)}, u32[]{:S(2)}, u32[]{:S(2)}) collective-permute-start(bf16[256,512]{1,0:T(8,128)(2,1)S(1)} %get-tuple-element.40), channel_id=1, source_target_pairs={{0,4},{4,0},{1,5},{5,1},{2,6},{6,2},{3,7},{7,3},{8,12},{12,8},{9,1... | collective-permute-start | bytes 786440 | tf_op jit(solution)/shard_map/ppermute | solution.py:273
  69.1 1.2 %collective-permute-done.6.got_ref = bf16[256,512]{1,0:T(8,128)(2,1)S(1)} collective-permute-done((bf16[256,512]{1,0:T(8,128)(2,1)S(1)}, bf16[256,512]{1,0:T(8,128)(2,1)S(1)}, u32[]{:S(2)}, u32[]{:S(2)}) %collective-permute-start.6) | collective-permute-done | bytes 262176 | tf_op jit(solution)/shard_map/ppermute | solution.py:273
  70.3 1.8 %collective-permute-start.7 = (bf16[64,512]{1,0:T(8,128)(2,1)S(1)}, bf16[64,512]{1,0:T(8,128)(2,1)S(1)}, u32[]{:S(2)}, u32[]{:S(2)}) collective-permute-start(bf16[64,512]{1,0:T(8,128)(2,1)S(1)} %get-tuple-element.42), channel_id=1, source_target_pairs={{0,64},{64,128},{128,192},{192,0},{1,65},{65,129},{129,193},{193,1... | collective-permute-start | bytes 196616 | tf_op jit(solution)/shard_map/ppermute | solution.py:267
  72.1 2.0 %collective-permute-start.8 = (bf16[64,512]{1,0:T(8,128)(2,1)S(1)}, bf16[64,512]{1,0:T(8,128)(2,1)S(1)}, u32[]{:S(2)}, u32[]{:S(2)}) collective-permute-start(bf16[64,512]{1,0:T(8,128)(2,1)S(1)} %get-tuple-element.43), channel_id=1, source_target_pairs={{0,128},{64,192},{128,0},{192,64},{1,129},{65,193},{129,1},{193,65... | collective-permute-start | bytes 196616 | tf_op jit(solution)/shard_map/ppermute | solution.py:267
  74.1 1.1 collective-permute-start.9
  75.2 2.5 %collective-permute-done.8.refs_2_ = bf16[64,512]{1,0:T(8,128)(2,1)S(1)} collective-permute-done((bf16[64,512]{1,0:T(8,128)(2,1)S(1)}, bf16[64,512]{1,0:T(8,128)(2,1)S(1)}, u32[]{:S(2)}, u32[]{:S(2)}) %collective-permute-start.8) | collective-permute-done | bytes 65568 | tf_op jit(solution)/shard_map/ppermute | solution.py:267
  77.8 0.5 collective-permute-start.10
  78.3 2.7 %collective-permute-done.10.refs_1_ = bf16[64,512]{1,0:T(8,128)(2,1)S(1)} collective-permute-done((bf16[64,512]{1,0:T(8,128)(2,1)S(1)}, bf16[64,512]{1,0:T(8,128)(2,1)S(1)}, u32[]{:S(2)}, u32[]{:S(2)}) %collective-permute-start.10) | collective-permute-done | bytes 65568 | tf_op jit(solution)/shard_map/ppermute | solution.py:273
  81.0 0.7 collective-permute-start.11
  81.7 4.1 %collective-permute-done.11.refs_1_ = bf16[64,512]{1,0:T(8,128)(2,1)S(1)} collective-permute-done((bf16[64,512]{1,0:T(8,128)(2,1)S(1)}, bf16[64,512]{1,0:T(8,128)(2,1)S(1)}, u32[]{:S(2)}, u32[]{:S(2)}) %collective-permute-start.11) | collective-permute-done | bytes 65568 | tf_op jit(solution)/shard_map/ppermute | solution.py:273
  85.8 1.8 %collective-permute-start.12 = (bf16[64,512]{1,0:T(8,128)(2,1)S(1)}, bf16[64,512]{1,0:T(8,128)(2,1)S(1)}, u32[]{:S(2)}, u32[]{:S(2)}) collective-permute-start(bf16[64,512]{1,0:T(8,128)(2,1)S(1)} %add.6.refs_0_), channel_id=1, source_target_pairs={{0,32},{8,40},{16,48},{24,56},{32,0},{40,8},{48,16},{56,24},{1,33}... | collective-permute-start | bytes 196616 | tf_op jit(solution)/shard_map/ppermute | solution.py:273
  87.6 6.0 %collective-permute-done.12.refs_1_ = bf16[64,512]{1,0:T(8,128)(2,1)S(1)} collective-permute-done((bf16[64,512]{1,0:T(8,128)(2,1)S(1)}, bf16[64,512]{1,0:T(8,128)(2,1)S(1)}, u32[]{:S(2)}, u32[]{:S(2)}) %collective-permute-start.12) | collective-permute-done | bytes 65568 | tf_op jit(solution)/shard_map/ppermute | solution.py:273
  93.7 1.2 %collective-permute-start.15 = (bf16[64,512]{1,0:T(8,128)(2,1)S(1)}, bf16[64,512]{1,0:T(8,128)(2,1)S(1)}, u32[]{:S(2)}, u32[]{:S(2)}) collective-permute-start(bf16[64,512]{1,0:T(8,128)(2,1)S(1)} %add.7.refs_0_), channel_id=1, source_target_pairs={{0,192},{64,0},{128,64},{192,128},{1,193},{65,1},{129,65},{193,129... | collective-permute-start | bytes 196616 | tf_op jit(solution)/shard_map/ppermute | solution.py:267
  94.8 0.2 collective-permute-start.14
  95.1 0.8 collective-permute-start.13
  95.8 6.5 %collective-permute-start.16 = (bf16[64,512]{1,0:T(8,128)(2,1)S(1)}, bf16[64,512]{1,0:T(8,128)(2,1)S(1)}, u32[]{:S(2)}, u32[]{:S(2)}) collective-permute-start(bf16[64,512]{1,0:T(8,128)(2,1)S(1)} %add.7.refs_0_), channel_id=1, source_target_pairs={{0,4},{4,0},{1,5},{5,1},{2,6},{6,2},{3,7},{7,3},{8,12},{12,8},{9,1... | collective-permute-start | bytes 196616 | tf_op jit(solution)/shard_map/ppermute | solution.py:273
  102.3 1.6 %collective-permute-start.19 = (bf16[64,512]{1,0:T(8,128)(2,1)S(1)}, bf16[64,512]{1,0:T(8,128)(2,1)S(1)}, u32[]{:S(2)}, u32[]{:S(2)}) collective-permute-start(bf16[64,512]{1,0:T(8,128)(2,1)S(1)} %collective-permute-done.15.refs_3_), channel_id=1, source_target_pairs={{0,4},{4,0},{1,5},{5,1},{2,6},{6,2},{3,7},{7,3},{8,12},{12,8},{9,1... | collective-permute-start | bytes 196616 | tf_op jit(solution)/shard_map/ppermute | solution.py:273
  103.8 3.4 %collective-permute-start.18 = (bf16[64,512]{1,0:T(8,128)(2,1)S(1)}, bf16[64,512]{1,0:T(8,128)(2,1)S(1)}, u32[]{:S(2)}, u32[]{:S(2)}) collective-permute-start(bf16[64,512]{1,0:T(8,128)(2,1)S(1)} %collective-permute-done.14.refs_2_), channel_id=1, source_target_pairs={{0,4},{4,0},{1,5},{5,1},{2,6},{6,2},{3,7},{7,3},{8,12},{12,8},{9,1... | collective-permute-start | bytes 196616 | tf_op jit(solution)/shard_map/ppermute | solution.py:273
  107.2 0.3 collective-permute-start.17
  107.5 1.0 embed.1
  108.5 1.1 finish.1
  (36 shorter events, 0.2 us)
Async XLA Ops:
  4.6 13.2 %copy-start.12 = (s32[1,64]{1,0:T(1,128)S(1)}, s32[1,64]{1,0:T(1,128)}, u32[]{:S(2)}) copy-start(s32[1,64]{1,0:T(1,128)} %param.21) | copy-start | bytes 772
  4.6 13.8 %copy-start.3 = (s32[512,25]{0,1:T(8,128)S(1)}, s32[512,25]{0,1:T(8,128)}, u32[]{:S(2)}) copy-start(s32[512,25]{0,1:T(8,128)} %param.23) | copy-start | bytes 153604
  4.7 13.8 %copy-start.4 = (s32[128,10]{0,1:T(8,128)S(1)}, s32[128,10]{0,1:T(8,128)}, u32[]{:S(2)}) copy-start(s32[128,10]{0,1:T(8,128)} %param.26) | copy-start | bytes 15364
  4.7 13.8 %copy-start.5 = (s32[512]{0:T(512)S(1)}, s32[512]{0:T(512)}, u32[]{:S(2)}) copy-start(s32[512]{0:T(512)} %param.24) | copy-start | bytes 6148
  4.7 13.7 %copy-start.6 = (s32[128]{0:T(128)S(1)}, s32[128]{0:T(128)}, u32[]{:S(2)}) copy-start(s32[128]{0:T(128)} %param.25) | copy-start | bytes 1540
  4.7 41.7 %copy-start.8 = (bf16[256,256]{1,0:T(8,128)(2,1)S(1)}, bf16[256,256]{1,0:T(8,128)(2,1)}, u32[]{:S(2)}) copy-start(bf16[256,256]{1,0:T(8,128)(2,1)} %weight_self_ref.1) | copy-start | bytes 393220
  4.7 41.7 %copy-start.9 = (bf16[256,256]{1,0:T(8,128)(2,1)S(1)}, bf16[256,256]{1,0:T(8,128)(2,1)}, u32[]{:S(2)}) copy-start(bf16[256,256]{1,0:T(8,128)(2,1)} %weight_near_ref.1) | copy-start | bytes 393220
  4.7 41.7 %copy-start.10 = (s32[512]{0:T(512)S(1)}, s32[512]{0:T(512)}, u32[]{:S(2)}) copy-start(s32[512]{0:T(512)} %param.22) | copy-start | bytes 6148
  4.7 41.7 %all-to-all-start = ((bf16[64,32,256]{2,1,0:T(8,128)(2,1)}), bf16[64,32,256]{2,1,0:T(8,128)(2,1)S(1)}, u32[]{:S(2)}, u32[]{:S(2)}) async-start(bf16[64,32,256]{2,1,0:T(8,128)(2,1)} %bitcast.1), calls=%async_computation | async-start | bytes 2097152 | tf_op jit(solution)/shard_map/all_to_all | solution.py:260
  29.7 1.4 %copy-start.7 = (bf16[2048,512]{1,0:T(8,128)(2,1)}, bf16[2048,512]{1,0:T(8,128)(2,1)S(1)}, u32[]{:S(2)}) copy-start(bf16[2048,512]{1,0:T(8,128)(2,1)S(1)} %get-tuple-element.32) | copy-start | bytes 6291460
  31.0 23.5 %copy-start.11 = (f32[256]{0:T(256)S(1)}, f32[256]{0:T(256)}, u32[]{:S(2)}) copy-start(f32[256]{0:T(256)} %param.17) | copy-start | bytes 3076
  31.0 26.0 %copy-start = (bf16[256,256]{1,0:T(8,128)(2,1)S(1)}, bf16[256,256]{1,0:T(8,128)(2,1)}, u32[]{:S(2)}) copy-start(bf16[256,256]{1,0:T(8,128)(2,1)} %second_self_ref.3) | copy-start | bytes 393220
  31.0 26.0 %copy-start.1 = (bf16[256,256]{1,0:T(8,128)(2,1)S(1)}, bf16[256,256]{1,0:T(8,128)(2,1)}, u32[]{:S(2)}) copy-start(bf16[256,256]{1,0:T(8,128)(2,1)} %second_near_ref.3) | copy-start | bytes 393220
  31.0 26.0 %copy-start.2 = (bf16[128,256]{1,0:T(8,128)(2,1)S(1)}, bf16[128,256]{1,0:T(8,128)(2,1)}, u32[]{:S(2)}) copy-start(bf16[128,256]{1,0:T(8,128)(2,1)} %cotangent_ref.3) | copy-start | bytes 196612
  49.4 5.2 %collective-permute-start = (bf16[64,512]{1,0:T(8,128)(2,1)S(1)}, bf16[64,512]{1,0:T(8,128)(2,1)S(1)}, u32[]{:S(2)}, u32[]{:S(2)}) collective-permute-start(bf16[64,512]{1,0:T(8,128)(2,1)S(1)} %get-tuple-element.34), channel_id=1, source_target_pairs={{0,1},{1,2},{2,3},{3,0},{4,5},{5,6},{6,7},{7,4},{8,9},{9,10},{10,1... | collective-permute-start | bytes 196616 | tf_op jit(solution)/shard_map/ppermute | solution.py:267
  50.8 6.2 %collective-permute-start.1 = (bf16[64,512]{1,0:T(8,128)(2,1)S(1)}, bf16[64,512]{1,0:T(8,128)(2,1)S(1)}, u32[]{:S(2)}, u32[]{:S(2)}) collective-permute-start(bf16[64,512]{1,0:T(8,128)(2,1)S(1)} %get-tuple-element.35), channel_id=1, source_target_pairs={{0,2},{1,3},{2,0},{3,1},{4,6},{5,7},{6,4},{7,5},{8,10},{9,11},{10,... | collective-permute-start | bytes 196616 | tf_op jit(solution)/shard_map/ppermute | solution.py:267
  53.5 3.6 %collective-permute-start.2 = (bf16[64,512]{1,0:T(8,128)(2,1)S(1)}, bf16[64,512]{1,0:T(8,128)(2,1)S(1)}, u32[]{:S(2)}, u32[]{:S(2)}) collective-permute-start(bf16[64,512]{1,0:T(8,128)(2,1)S(1)} %get-tuple-element.36), channel_id=1, source_target_pairs={{0,3},{1,0},{2,1},{3,2},{4,7},{5,4},{6,5},{7,6},{8,11},{9,8},{10,9... | collective-permute-start | bytes 196616 | tf_op jit(solution)/shard_map/ppermute | solution.py:267
  57.5 4.0 %collective-permute-start.5 = (bf16[96,512]{1,0:T(8,128)(2,1)S(1)}, bf16[96,512]{1,0:T(8,128)(2,1)S(1)}, u32[]{:S(2)}, u32[]{:S(2)}) collective-permute-start(bf16[96,512]{1,0:T(8,128)(2,1)S(1)} %owner.1.refs_0_), channel_id=1, source_target_pairs={{0,3},{1,0},{2,1},{3,2},{4,7},{5,4},{6,5},{7,6},{8,11},{9,8},{10,9... | collective-permute-start | bytes 294920 | tf_op jit(solution)/shard_map/ppermute | solution.py:267
  59.3 5.1 %collective-permute-start.4 = (bf16[96,512]{1,0:T(8,128)(2,1)S(1)}, bf16[96,512]{1,0:T(8,128)(2,1)S(1)}, u32[]{:S(2)}, u32[]{:S(2)}) collective-permute-start(bf16[96,512]{1,0:T(8,128)(2,1)S(1)} %owner.1.refs_0_), channel_id=1, source_target_pairs={{0,2},{1,3},{2,0},{3,1},{4,6},{5,7},{6,4},{7,5},{8,10},{9,11},{10,... | collective-permute-start | bytes 294920 | tf_op jit(solution)/shard_map/ppermute | solution.py:267
  59.6 5.7 %collective-permute-start.3 = (bf16[96,512]{1,0:T(8,128)(2,1)S(1)}, bf16[96,512]{1,0:T(8,128)(2,1)S(1)}, u32[]{:S(2)}, u32[]{:S(2)}) collective-permute-start(bf16[96,512]{1,0:T(8,128)(2,1)S(1)} %owner.1.refs_0_), channel_id=1, source_target_pairs={{0,1},{1,2},{2,3},{3,0},{4,5},{5,6},{6,7},{7,4},{8,9},{9,10},{10,1... | collective-permute-start | bytes 294920 | tf_op jit(solution)/shard_map/ppermute | solution.py:267
  65.8 4.5 %collective-permute-start.6 = (bf16[256,512]{1,0:T(8,128)(2,1)S(1)}, bf16[256,512]{1,0:T(8,128)(2,1)S(1)}, u32[]{:S(2)}, u32[]{:S(2)}) collective-permute-start(bf16[256,512]{1,0:T(8,128)(2,1)S(1)} %get-tuple-element.40), channel_id=1, source_target_pairs={{0,4},{4,0},{1,5},{5,1},{2,6},{6,2},{3,7},{7,3},{8,12},{12,8},{9,1... | collective-permute-start | bytes 786440 | tf_op jit(solution)/shard_map/ppermute | solution.py:273
  70.3 4.8 %collective-permute-start.7 = (bf16[64,512]{1,0:T(8,128)(2,1)S(1)}, bf16[64,512]{1,0:T(8,128)(2,1)S(1)}, u32[]{:S(2)}, u32[]{:S(2)}) collective-permute-start(bf16[64,512]{1,0:T(8,128)(2,1)S(1)} %get-tuple-element.42), channel_id=1, source_target_pairs={{0,64},{64,128},{128,192},{192,0},{1,65},{65,129},{129,193},{193,1... | collective-permute-start | bytes 196616 | tf_op jit(solution)/shard_map/ppermute | solution.py:267
  72.1 5.6 %collective-permute-start.8 = (bf16[64,512]{1,0:T(8,128)(2,1)S(1)}, bf16[64,512]{1,0:T(8,128)(2,1)S(1)}, u32[]{:S(2)}, u32[]{:S(2)}) collective-permute-start(bf16[64,512]{1,0:T(8,128)(2,1)S(1)} %get-tuple-element.43), channel_id=1, source_target_pairs={{0,128},{64,192},{128,0},{192,64},{1,129},{65,193},{129,1},{193,65... | collective-permute-start | bytes 196616 | tf_op jit(solution)/shard_map/ppermute | solution.py:267
  74.1 3.6 %collective-permute-start.9 = (bf16[64,512]{1,0:T(8,128)(2,1)S(1)}, bf16[64,512]{1,0:T(8,128)(2,1)S(1)}, u32[]{:S(2)}, u32[]{:S(2)}) collective-permute-start(bf16[64,512]{1,0:T(8,128)(2,1)S(1)} %get-tuple-element.44), channel_id=1, source_target_pairs={{0,192},{64,0},{128,64},{192,128},{1,193},{65,1},{129,65},{193,129... | collective-permute-start | bytes 196616 | tf_op jit(solution)/shard_map/ppermute | solution.py:267
  77.8 3.2 %collective-permute-start.10 = (bf16[64,512]{1,0:T(8,128)(2,1)S(1)}, bf16[64,512]{1,0:T(8,128)(2,1)S(1)}, u32[]{:S(2)}, u32[]{:S(2)}) collective-permute-start(bf16[64,512]{1,0:T(8,128)(2,1)S(1)} %add.4.refs_0_), channel_id=1, source_target_pairs={{0,8},{8,0},{16,24},{24,16},{32,40},{40,32},{48,56},{56,48},{1,9},... | collective-permute-start | bytes 196616 | tf_op jit(solution)/shard_map/ppermute | solution.py:273
  81.0 4.8 %collective-permute-start.11 = (bf16[64,512]{1,0:T(8,128)(2,1)S(1)}, bf16[64,512]{1,0:T(8,128)(2,1)S(1)}, u32[]{:S(2)}, u32[]{:S(2)}) collective-permute-start(bf16[64,512]{1,0:T(8,128)(2,1)S(1)} %add.5.refs_0_), channel_id=1, source_target_pairs={{0,16},{8,24},{16,0},{24,8},{32,48},{40,56},{48,32},{56,40},{1,17}... | collective-permute-start | bytes 196616 | tf_op jit(solution)/shard_map/ppermute | solution.py:273
  85.8 7.8 %collective-permute-start.12 = (bf16[64,512]{1,0:T(8,128)(2,1)S(1)}, bf16[64,512]{1,0:T(8,128)(2,1)S(1)}, u32[]{:S(2)}, u32[]{:S(2)}) collective-permute-start(bf16[64,512]{1,0:T(8,128)(2,1)S(1)} %add.6.refs_0_), channel_id=1, source_target_pairs={{0,32},{8,40},{16,48},{24,56},{32,0},{40,8},{48,16},{56,24},{1,33}... | collective-permute-start | bytes 196616 | tf_op jit(solution)/shard_map/ppermute | solution.py:273
  93.7 8.6 %collective-permute-start.15 = (bf16[64,512]{1,0:T(8,128)(2,1)S(1)}, bf16[64,512]{1,0:T(8,128)(2,1)S(1)}, u32[]{:S(2)}, u32[]{:S(2)}) collective-permute-start(bf16[64,512]{1,0:T(8,128)(2,1)S(1)} %add.7.refs_0_), channel_id=1, source_target_pairs={{0,192},{64,0},{128,64},{192,128},{1,193},{65,1},{129,65},{193,129... | collective-permute-start | bytes 196616 | tf_op jit(solution)/shard_map/ppermute | solution.py:267
  94.8 9.0 %collective-permute-start.14 = (bf16[64,512]{1,0:T(8,128)(2,1)S(1)}, bf16[64,512]{1,0:T(8,128)(2,1)S(1)}, u32[]{:S(2)}, u32[]{:S(2)}) collective-permute-start(bf16[64,512]{1,0:T(8,128)(2,1)S(1)} %add.7.refs_0_), channel_id=1, source_target_pairs={{0,128},{64,192},{128,0},{192,64},{1,129},{65,193},{129,1},{193,65... | collective-permute-start | bytes 196616 | tf_op jit(solution)/shard_map/ppermute | solution.py:267
  95.1 12.1 %collective-permute-start.13 = (bf16[64,512]{1,0:T(8,128)(2,1)S(1)}, bf16[64,512]{1,0:T(8,128)(2,1)S(1)}, u32[]{:S(2)}, u32[]{:S(2)}) collective-permute-start(bf16[64,512]{1,0:T(8,128)(2,1)S(1)} %add.7.refs_0_), channel_id=1, source_target_pairs={{0,64},{64,128},{128,192},{192,0},{1,65},{65,129},{129,193},{193,1... | collective-permute-start | bytes 196616 | tf_op jit(solution)/shard_map/ppermute | solution.py:267
  95.8 12.6 %collective-permute-start.16 = (bf16[64,512]{1,0:T(8,128)(2,1)S(1)}, bf16[64,512]{1,0:T(8,128)(2,1)S(1)}, u32[]{:S(2)}, u32[]{:S(2)}) collective-permute-start(bf16[64,512]{1,0:T(8,128)(2,1)S(1)} %add.7.refs_0_), channel_id=1, source_target_pairs={{0,4},{4,0},{1,5},{5,1},{2,6},{6,2},{3,7},{7,3},{8,12},{12,8},{9,1... | collective-permute-start | bytes 196616 | tf_op jit(solution)/shard_map/ppermute | solution.py:273
  102.3 6.2 %collective-permute-start.19 = (bf16[64,512]{1,0:T(8,128)(2,1)S(1)}, bf16[64,512]{1,0:T(8,128)(2,1)S(1)}, u32[]{:S(2)}, u32[]{:S(2)}) collective-permute-start(bf16[64,512]{1,0:T(8,128)(2,1)S(1)} %collective-permute-done.15.refs_3_), channel_id=1, source_target_pairs={{0,4},{4,0},{1,5},{5,1},{2,6},{6,2},{3,7},{7,3},{8,12},{12,8},{9,1... | collective-permute-start | bytes 196616 | tf_op jit(solution)/shard_map/ppermute | solution.py:273
  103.8 4.6 %collective-permute-start.18 = (bf16[64,512]{1,0:T(8,128)(2,1)S(1)}, bf16[64,512]{1,0:T(8,128)(2,1)S(1)}, u32[]{:S(2)}, u32[]{:S(2)}) collective-permute-start(bf16[64,512]{1,0:T(8,128)(2,1)S(1)} %collective-permute-done.14.refs_2_), channel_id=1, source_target_pairs={{0,4},{4,0},{1,5},{5,1},{2,6},{6,2},{3,7},{7,3},{8,12},{12,8},{9,1... | collective-permute-start | bytes 196616 | tf_op jit(solution)/shard_map/ppermute | solution.py:273
  107.2 1.3 %collective-permute-start.17 = (bf16[64,512]{1,0:T(8,128)(2,1)S(1)}, bf16[64,512]{1,0:T(8,128)(2,1)S(1)}, u32[]{:S(2)}, u32[]{:S(2)}) collective-permute-start(bf16[64,512]{1,0:T(8,128)(2,1)S(1)} %collective-permute-done.13.refs_1_), channel_id=1, source_target_pairs={{0,4},{4,0},{1,5},{5,1},{2,6},{6,2},{3,7},{7,3},{8,12},{12,8},{9,1... | collective-permute-start | bytes 196616 | tf_op jit(solution)/shard_map/ppermute | solution.py:273

commit v12 on v11

--- a/solution.py
+++ b/solution.py
@@ -371,18 +371,21 @@
     (mixed,) = call(
         add_body, [(shard, BF16)], shifted(parts, "x", count_x), "add", 0, 4 * tall * hidden
     )
-    stride = 1
-    while stride < count_z:
-        (mixed,) = call(
-            add_body, [(shard, BF16)], (mixed, swapped(mixed, "z", count_z, stride)), "add",
-            0, 2 * tall * hidden,
-        )
-        stride *= 2
     (seed_embedding,) = call(
         functools.partial(embed_body, half=half), [((seeds, out_cols), BF16)],
         (at_feat, second_self, second_neighbor, *grads), "embed",
         4 * seeds * hidden * out_cols, 8 * seeds * hidden, scalars=1,
     )
+    stride = 1
+    while stride < count_z:
+        got = swapped(mixed, "z", count_z, stride)
+        if 2 * stride == count_z:
+            got, seed_embedding = lax.optimization_barrier((got, seed_embedding))
+        (mixed,) = call(
+            add_body, [(shard, BF16)], (mixed, got), "add",
+            0, 2 * tall * hidden,
+        )
+        stride *= 2
     mine = shifted([mixed] * count_x, "x", count_x)
     other = [swapped(piece, "core", cores, 1) for piece in mine]
     grad_first_self, grad_first_neighbor, grad_second_self, grad_second_neighbor = call(

time: 110 us -> 110 us (level)
  transfers between devices with their start and end apart: 21 -> 21, of which waited for: 10 -> 12; matrix products, arithmetic and copies ran while one was open for 1% -> 1% of each run, Pallas kernels for 11% -> 11%
where the time goes in v12:
time: 110 us
  starting transfers between devices  46.1 us (42%)
  waiting for transfers between devices  39.3 us (36%)
  Pallas kernels  21.2 us (19%)
  local copies, waits for them, and re-layouts  1.99 us (2%)
    pallas_call x12, Pallas kernels, call(): pl.pallas_call(body, out_shape=[jax.ShapeDtypeStruct(shape, dtype) for sh...  21.2 us
    ppermute x8, starting transfers between devices, swapped(): return lax.ppermute(value, axis, [(at, at ^ step) for at in range(count)])  18 us
    all_to_all x1, waiting for transfers between devices, exchange(): return lax.all_to_all(value, axis, split_axis=0, concat_axis=0, tiled=True)  15.4 us
    ppermute x12, starting transfers between devices, shifted(): lax.ppermute(piece, axis, [(at, (at + shift) % count) for at in range(cou...  15 us
    ppermute x8, waiting for transfers between devices, swapped(): return lax.ppermute(value, axis, [(at, at ^ step) for at in range(count)])  14 us
    all_to_all x1, starting transfers between devices, exchange(): return lax.all_to_all(value, axis, split_axis=0, concat_axis=0, tiled=True)  13.1 us
    ppermute x12, waiting for transfers between devices, shifted(): lax.ppermute(piece, axis, [(at, (at + shift) % count) for at in range(cou...  9.88 us
  transfers between devices with their start and end apart: 21, of which 12 were waited for; matrix products, arithmetic and copies ran while one was open for 1% of the time, Pallas kernels for 11%

profile of v12, /device:TPU:1, one launch (start us, length us, event | category | flops | bytes accessed | tf_op | source)
XLA Modules:
  0.0 109.5 jit_solution(13875729128767561159)
XLA Ops:
  0.6 4.0 %pick.1 = bf16[2048,256]{1,0:T(8,128)(2,1)} custom-call(s32[1,2048]{1,0:T(1,128)} %row_far.1, bf16[1536,256]{1,0:T(8,128)(2,1)} %x_far.1), custom_call_target="tpu_custom_call" | custom-call | flops 1610612736 | bytes 6291456 | tf_op jit(solution)/shard_map/pick/pallas_call | solution.py:31
  4.6 0.0 copy-start.3
  4.7 0.0 copy-start.4
  4.7 0.0 copy-start.8
  4.7 13.1 %all-to-all-start = ((bf16[64,32,256]{2,1,0:T(8,128)(2,1)}), bf16[64,32,256]{2,1,0:T(8,128)(2,1)S(1)}, u32[]{:S(2)}, u32[]{:S(2)}) async-start(bf16[64,32,256]{2,1,0:T(8,128)(2,1)} %bitcast.3), calls=%async_computation | async-start | bytes 2097152 | tf_op jit(solution)/shard_map/all_to_all | solution.py:260
  17.9 0.1 fusion
  18.0 0.1 reshape.59
  18.1 0.3 iota.10.mask_ref
  18.4 11.2 %count.1 = (bf16[2048,512]{1,0:T(8,128)(2,1)S(1)}, bf16[512,128]{1,0:T(8,128)(2,1)S(1)}, bf16[512,128]{1,0:T(8,128)(2,1)S(1)}) custom-call(s32[25,512]{1,0:T(8,128)S(1)} %bitcast.14, s32[1,512]{1,0:T(1,128)S(1)} %bitcast.16, bf16[2048,128]{1,0:T(8,128)(2,1)S(1)} %iota.10.mask_ref, s32[1,128]{1,0:T(1,128)S(1)} %bitcast.18, s32[10,128]{1,0:T(8,128)S(1)} %bitcast.15), custom_call_target="tpu_custom_call" | custom-call | bytes 16777216 | tf_op jit(solution)/shard_map/count/pallas_call | solution.py:31
  29.7 1.4 %copy-done.7 = bf16[2048,512]{1,0:T(8,128)(2,1)} copy-done((bf16[2048,512]{1,0:T(8,128)(2,1)}, bf16[2048,512]{1,0:T(8,128)(2,1)S(1)}, u32[]{:S(2)}) %copy-start.7) | copy-done | bytes 2097176
  31.0 15.4 %all-to-all-done = bf16[64,32,256]{2,1,0:T(8,128)(2,1)S(1)} async-done(((bf16[64,32,256]{2,1,0:T(8,128)(2,1)}), bf16[64,32,256]{2,1,0:T(8,128)(2,1)S(1)}, u32[]{:S(2)}, u32[]{:S(2)}) %all-to-all-start) | async-done | bytes 1048608 | tf_op jit(solution)/shard_map/all_to_all | solution.py:260
  46.4 3.0 %gather.1 = (bf16[256,512]{1,0:T(8,128)(2,1)S(1)}, bf16[256,512]{1,0:T(8,128)(2,1)S(1)}, bf16[64,512]{1,0:T(8,128)(2,1)S(1)}, bf16[64,512]{1,0:T(8,128)(2,1)S(1)...) custom-call(s32[1]{0:T(128)} %bitcast.1.place_ref, bf16[2048,256]{1,0:T(8,128)(2,1)S(1)} %bitcast.13, ...), custom_call_target="tpu_custom_call" | custom-call | flops 1073741824 | bytes 4194304 | tf_op jit(solution)/shard_map/gather/pallas_call | solution.py:31
  49.4 1.4 %collective-permute-start = (bf16[64,512]{1,0:T(8,128)(2,1)S(1)}, bf16[64,512]{1,0:T(8,128)(2,1)S(1)}, u32[]{:S(2)}, u32[]{:S(2)}) collective-permute-start(bf16[64,512]{1,0:T(8,128)(2,1)S(1)} %get-tuple-element.38), channel_id=1, source_target_pairs={{0,1},{1,2},{2,3},{3,0},{4,5},{5,6},{6,7},{7,4},{8,9},{9,10},{10,1... | collective-permute-start | bytes 196616 | tf_op jit(solution)/shard_map/ppermute | solution.py:267
  50.8 2.6 %collective-permute-start.1 = (bf16[64,512]{1,0:T(8,128)(2,1)S(1)}, bf16[64,512]{1,0:T(8,128)(2,1)S(1)}, u32[]{:S(2)}, u32[]{:S(2)}) collective-permute-start(bf16[64,512]{1,0:T(8,128)(2,1)S(1)} %get-tuple-element.39), channel_id=1, source_target_pairs={{0,2},{1,3},{2,0},{3,1},{4,6},{5,7},{6,4},{7,5},{8,10},{9,11},{10,... | collective-permute-start | bytes 196616 | tf_op jit(solution)/shard_map/ppermute | solution.py:267
  53.5 1.1 collective-permute-start.2
  54.5 0.1 copy.19.bias_ref
  54.7 2.4 %collective-permute-done.1.refs_2_ = bf16[64,512]{1,0:T(8,128)(2,1)S(1)} collective-permute-done((bf16[64,512]{1,0:T(8,128)(2,1)S(1)}, bf16[64,512]{1,0:T(8,128)(2,1)S(1)}, u32[]{:S(2)}, u32[]{:S(2)}) %collective-permute-start.1) | collective-permute-done | bytes 65568 | tf_op jit(solution)/shard_map/ppermute | solution.py:267
  57.1 0.4 owner.1.refs_0_
  57.5 1.9 %collective-permute-start.5 = (bf16[96,512]{1,0:T(8,128)(2,1)S(1)}, bf16[96,512]{1,0:T(8,128)(2,1)S(1)}, u32[]{:S(2)}, u32[]{:S(2)}) collective-permute-start(bf16[96,512]{1,0:T(8,128)(2,1)S(1)} %owner.1.refs_0_), channel_id=1, source_target_pairs={{0,3},{1,0},{2,1},{3,2},{4,7},{5,4},{6,5},{7,6},{8,11},{9,8},{10,9... | collective-permute-start | bytes 294920 | tf_op jit(solution)/shard_map/ppermute | solution.py:267
  59.3 0.2 collective-permute-start.4
  59.6 0.8 collective-permute-start.3
  60.3 1.1 %collective-permute-done.5.refs_3_ = bf16[96,512]{1,0:T(8,128)(2,1)S(1)} collective-permute-done((bf16[96,512]{1,0:T(8,128)(2,1)S(1)}, bf16[96,512]{1,0:T(8,128)(2,1)S(1)}, u32[]{:S(2)}, u32[]{:S(2)}) %collective-permute-start.5) | collective-permute-done | bytes 98336 | tf_op jit(solution)/shard_map/ppermute | solution.py:267
  61.5 3.0 %collective-permute-done.4.refs_2_ = bf16[96,512]{1,0:T(8,128)(2,1)S(1)} collective-permute-done((bf16[96,512]{1,0:T(8,128)(2,1)S(1)}, bf16[96,512]{1,0:T(8,128)(2,1)S(1)}, u32[]{:S(2)}, u32[]{:S(2)}) %collective-permute-start.4) | collective-permute-done | bytes 98336 | tf_op jit(solution)/shard_map/ppermute | solution.py:267
  64.4 0.9 collective-permute-done.3.refs_1_
  65.3 0.5 weight.1
  65.8 3.4 %collective-permute-start.6 = (bf16[256,512]{1,0:T(8,128)(2,1)S(1)}, bf16[256,512]{1,0:T(8,128)(2,1)S(1)}, u32[]{:S(2)}, u32[]{:S(2)}) collective-permute-start(bf16[256,512]{1,0:T(8,128)(2,1)S(1)} %get-tuple-element.42), channel_id=1, source_target_pairs={{0,4},{4,0},{1,5},{5,1},{2,6},{6,2},{3,7},{7,3},{8,12},{12,8},{9,1... | collective-permute-start | bytes 786440 | tf_op jit(solution)/shard_map/ppermute | solution.py:273
  69.1 1.2 %collective-permute-done.6.got_ref = bf16[256,512]{1,0:T(8,128)(2,1)S(1)} collective-permute-done((bf16[256,512]{1,0:T(8,128)(2,1)S(1)}, bf16[256,512]{1,0:T(8,128)(2,1)S(1)}, u32[]{:S(2)}, u32[]{:S(2)}) %collective-permute-start.6) | collective-permute-done | bytes 262176 | tf_op jit(solution)/shard_map/ppermute | solution.py:273
  70.3 1.8 %collective-permute-start.7 = (bf16[64,512]{1,0:T(8,128)(2,1)S(1)}, bf16[64,512]{1,0:T(8,128)(2,1)S(1)}, u32[]{:S(2)}, u32[]{:S(2)}) collective-permute-start(bf16[64,512]{1,0:T(8,128)(2,1)S(1)} %get-tuple-element.44), channel_id=1, source_target_pairs={{0,64},{64,128},{128,192},{192,0},{1,65},{65,129},{129,193},{193,1... | collective-permute-start | bytes 196616 | tf_op jit(solution)/shard_map/ppermute | solution.py:267
  72.1 2.0 %collective-permute-start.8 = (bf16[64,512]{1,0:T(8,128)(2,1)S(1)}, bf16[64,512]{1,0:T(8,128)(2,1)S(1)}, u32[]{:S(2)}, u32[]{:S(2)}) collective-permute-start(bf16[64,512]{1,0:T(8,128)(2,1)S(1)} %get-tuple-element.45), channel_id=1, source_target_pairs={{0,128},{64,192},{128,0},{192,64},{1,129},{65,193},{129,1},{193,65... | collective-permute-start | bytes 196616 | tf_op jit(solution)/shard_map/ppermute | solution.py:267
  74.1 1.1 collective-permute-start.9
  75.2 2.5 %collective-permute-done.8.refs_2_ = bf16[64,512]{1,0:T(8,128)(2,1)S(1)} collective-permute-done((bf16[64,512]{1,0:T(8,128)(2,1)S(1)}, bf16[64,512]{1,0:T(8,128)(2,1)S(1)}, u32[]{:S(2)}, u32[]{:S(2)}) %collective-permute-start.8) | collective-permute-done | bytes 65568 | tf_op jit(solution)/shard_map/ppermute | solution.py:267
  77.8 0.5 collective-permute-start.10
  78.3 2.7 %collective-permute-done.10.refs_1_ = bf16[64,512]{1,0:T(8,128)(2,1)S(1)} collective-permute-done((bf16[64,512]{1,0:T(8,128)(2,1)S(1)}, bf16[64,512]{1,0:T(8,128)(2,1)S(1)}, u32[]{:S(2)}, u32[]{:S(2)}) %collective-permute-start.10) | collective-permute-done | bytes 65568 | tf_op jit(solution)/shard_map/ppermute | solution.py:273
  81.0 0.7 collective-permute-start.11
  81.7 4.1 %collective-permute-done.11.refs_1_ = bf16[64,512]{1,0:T(8,128)(2,1)S(1)} collective-permute-done((bf16[64,512]{1,0:T(8,128)(2,1)S(1)}, bf16[64,512]{1,0:T(8,128)(2,1)S(1)}, u32[]{:S(2)}, u32[]{:S(2)}) %collective-permute-start.11) | collective-permute-done | bytes 65568 | tf_op jit(solution)/shard_map/ppermute | solution.py:273
  85.8 1.8 %collective-permute-start.12 = (bf16[64,512]{1,0:T(8,128)(2,1)S(1)}, bf16[64,512]{1,0:T(8,128)(2,1)S(1)}, u32[]{:S(2)}, u32[]{:S(2)}) collective-permute-start(bf16[64,512]{1,0:T(8,128)(2,1)S(1)} %add.6.refs_0_), channel_id=1, source_target_pairs={{0,32},{8,40},{16,48},{24,56},{32,0},{40,8},{48,16},{56,24},{1,33}... | collective-permute-start | bytes 196616 | tf_op jit(solution)/shard_map/ppermute | solution.py:273
  87.6 1.0 embed.1
  88.6 5.1 %collective-permute-done.12.refs_1_ = bf16[64,512]{1,0:T(8,128)(2,1)S(1)} collective-permute-done((bf16[64,512]{1,0:T(8,128)(2,1)S(1)}, bf16[64,512]{1,0:T(8,128)(2,1)S(1)}, u32[]{:S(2)}, u32[]{:S(2)}) %collective-permute-start.12) | collective-permute-done | bytes 65568 | tf_op jit(solution)/shard_map/ppermute | solution.py:273
  93.7 1.2 %collective-permute-start.15 = (bf16[64,512]{1,0:T(8,128)(2,1)S(1)}, bf16[64,512]{1,0:T(8,128)(2,1)S(1)}, u32[]{:S(2)}, u32[]{:S(2)}) collective-permute-start(bf16[64,512]{1,0:T(8,128)(2,1)S(1)} %add.7.refs_0_), channel_id=1, source_target_pairs={{0,192},{64,0},{128,64},{192,128},{1,193},{65,1},{129,65},{193,129... | collective-permute-start | bytes 196616 | tf_op jit(solution)/shard_map/ppermute | solution.py:267
  94.8 0.2 collective-permute-start.14
  95.1 0.8 collective-permute-start.13
  95.8 6.5 %collective-permute-start.16 = (bf16[64,512]{1,0:T(8,128)(2,1)S(1)}, bf16[64,512]{1,0:T(8,128)(2,1)S(1)}, u32[]{:S(2)}, u32[]{:S(2)}) collective-permute-start(bf16[64,512]{1,0:T(8,128)(2,1)S(1)} %add.7.refs_0_), channel_id=1, source_target_pairs={{0,4},{4,0},{1,5},{5,1},{2,6},{6,2},{3,7},{7,3},{8,12},{12,8},{9,1... | collective-permute-start | bytes 196616 | tf_op jit(solution)/shard_map/ppermute | solution.py:273
  102.3 1.6 %collective-permute-start.19 = (bf16[64,512]{1,0:T(8,128)(2,1)S(1)}, bf16[64,512]{1,0:T(8,128)(2,1)S(1)}, u32[]{:S(2)}, u32[]{:S(2)}) collective-permute-start(bf16[64,512]{1,0:T(8,128)(2,1)S(1)} %collective-permute-done.15.refs_3_), channel_id=1, source_target_pairs={{0,4},{4,0},{1,5},{5,1},{2,6},{6,2},{3,7},{7,3},{8,12},{12,8},{9,1... | collective-permute-start | bytes 196616 | tf_op jit(solution)/shard_map/ppermute | solution.py:273
  103.8 3.4 %collective-permute-start.18 = (bf16[64,512]{1,0:T(8,128)(2,1)S(1)}, bf16[64,512]{1,0:T(8,128)(2,1)S(1)}, u32[]{:S(2)}, u32[]{:S(2)}) collective-permute-start(bf16[64,512]{1,0:T(8,128)(2,1)S(1)} %collective-permute-done.14.refs_2_), channel_id=1, source_target_pairs={{0,4},{4,0},{1,5},{5,1},{2,6},{6,2},{3,7},{7,3},{8,12},{12,8},{9,1... | collective-permute-start | bytes 196616 | tf_op jit(solution)/shard_map/ppermute | solution.py:273
  107.2 0.3 collective-permute-start.17
  107.5 0.6 collective-permute-done.18.refs_6_
  108.1 0.4 collective-permute-done.17.refs_5_
  108.5 1.0 finish.1
  (36 shorter events, 0.2 us)
Async XLA Ops:
  4.6 13.2 %copy-start.12 = (s32[1,64]{1,0:T(1,128)S(1)}, s32[1,64]{1,0:T(1,128)}, u32[]{:S(2)}) copy-start(s32[1,64]{1,0:T(1,128)} %param.21) | copy-start | bytes 772
  4.6 13.8 %copy-start.3 = (s32[512,25]{0,1:T(8,128)S(1)}, s32[512,25]{0,1:T(8,128)}, u32[]{:S(2)}) copy-start(s32[512,25]{0,1:T(8,128)} %param.23) | copy-start | bytes 153604
  4.7 13.8 %copy-start.4 = (s32[128,10]{0,1:T(8,128)S(1)}, s32[128,10]{0,1:T(8,128)}, u32[]{:S(2)}) copy-start(s32[128,10]{0,1:T(8,128)} %param.26) | copy-start | bytes 15364
  4.7 13.8 %copy-start.5 = (s32[512]{0:T(512)S(1)}, s32[512]{0:T(512)}, u32[]{:S(2)}) copy-start(s32[512]{0:T(512)} %param.24) | copy-start | bytes 6148
  4.7 13.7 %copy-start.6 = (s32[128]{0:T(128)S(1)}, s32[128]{0:T(128)}, u32[]{:S(2)}) copy-start(s32[128]{0:T(128)} %param.25) | copy-start | bytes 1540
  4.7 41.7 %copy-start.8 = (bf16[256,256]{1,0:T(8,128)(2,1)S(1)}, bf16[256,256]{1,0:T(8,128)(2,1)}, u32[]{:S(2)}) copy-start(bf16[256,256]{1,0:T(8,128)(2,1)} %weight_self_ref.1) | copy-start | bytes 393220
  4.7 41.7 %copy-start.9 = (bf16[256,256]{1,0:T(8,128)(2,1)S(1)}, bf16[256,256]{1,0:T(8,128)(2,1)}, u32[]{:S(2)}) copy-start(bf16[256,256]{1,0:T(8,128)(2,1)} %weight_near_ref.1) | copy-start | bytes 393220
  4.7 41.7 %copy-start.10 = (s32[512]{0:T(512)S(1)}, s32[512]{0:T(512)}, u32[]{:S(2)}) copy-start(s32[512]{0:T(512)} %param.22) | copy-start | bytes 6148
  4.7 41.7 %all-to-all-start = ((bf16[64,32,256]{2,1,0:T(8,128)(2,1)}), bf16[64,32,256]{2,1,0:T(8,128)(2,1)S(1)}, u32[]{:S(2)}, u32[]{:S(2)}) async-start(bf16[64,32,256]{2,1,0:T(8,128)(2,1)} %bitcast.3), calls=%async_computation | async-start | bytes 2097152 | tf_op jit(solution)/shard_map/all_to_all | solution.py:260
  29.7 1.4 %copy-start.7 = (bf16[2048,512]{1,0:T(8,128)(2,1)}, bf16[2048,512]{1,0:T(8,128)(2,1)S(1)}, u32[]{:S(2)}) copy-start(bf16[2048,512]{1,0:T(8,128)(2,1)S(1)} %get-tuple-element.31) | copy-start | bytes 6291460
  31.0 23.5 %copy-start.11 = (f32[256]{0:T(256)S(1)}, f32[256]{0:T(256)}, u32[]{:S(2)}) copy-start(f32[256]{0:T(256)} %param.17) | copy-start | bytes 3076
  31.0 26.0 %copy-start = (bf16[256,256]{1,0:T(8,128)(2,1)S(1)}, bf16[256,256]{1,0:T(8,128)(2,1)}, u32[]{:S(2)}) copy-start(bf16[256,256]{1,0:T(8,128)(2,1)} %second_self_ref.3) | copy-start | bytes 393220
  31.0 26.0 %copy-start.1 = (bf16[256,256]{1,0:T(8,128)(2,1)S(1)}, bf16[256,256]{1,0:T(8,128)(2,1)}, u32[]{:S(2)}) copy-start(bf16[256,256]{1,0:T(8,128)(2,1)} %second_near_ref.3) | copy-start | bytes 393220
  31.0 26.0 %copy-start.2 = (bf16[128,256]{1,0:T(8,128)(2,1)S(1)}, bf16[128,256]{1,0:T(8,128)(2,1)}, u32[]{:S(2)}) copy-start(bf16[128,256]{1,0:T(8,128)(2,1)} %cotangent_ref.3) | copy-start | bytes 196612
  49.4 5.2 %collective-permute-start = (bf16[64,512]{1,0:T(8,128)(2,1)S(1)}, bf16[64,512]{1,0:T(8,128)(2,1)S(1)}, u32[]{:S(2)}, u32[]{:S(2)}) collective-permute-start(bf16[64,512]{1,0:T(8,128)(2,1)S(1)} %get-tuple-element.38), channel_id=1, source_target_pairs={{0,1},{1,2},{2,3},{3,0},{4,5},{5,6},{6,7},{7,4},{8,9},{9,10},{10,1... | collective-permute-start | bytes 196616 | tf_op jit(solution)/shard_map/ppermute | solution.py:267
  50.8 6.2 %collective-permute-start.1 = (bf16[64,512]{1,0:T(8,128)(2,1)S(1)}, bf16[64,512]{1,0:T(8,128)(2,1)S(1)}, u32[]{:S(2)}, u32[]{:S(2)}) collective-permute-start(bf16[64,512]{1,0:T(8,128)(2,1)S(1)} %get-tuple-element.39), channel_id=1, source_target_pairs={{0,2},{1,3},{2,0},{3,1},{4,6},{5,7},{6,4},{7,5},{8,10},{9,11},{10,... | collective-permute-start | bytes 196616 | tf_op jit(solution)/shard_map/ppermute | solution.py:267
  53.5 3.6 %collective-permute-start.2 = (bf16[64,512]{1,0:T(8,128)(2,1)S(1)}, bf16[64,512]{1,0:T(8,128)(2,1)S(1)}, u32[]{:S(2)}, u32[]{:S(2)}) collective-permute-start(bf16[64,512]{1,0:T(8,128)(2,1)S(1)} %get-tuple-element.40), channel_id=1, source_target_pairs={{0,3},{1,0},{2,1},{3,2},{4,7},{5,4},{6,5},{7,6},{8,11},{9,8},{10,9... | collective-permute-start | bytes 196616 | tf_op jit(solution)/shard_map/ppermute | solution.py:267
  57.5 4.0 %collective-permute-start.5 = (bf16[96,512]{1,0:T(8,128)(2,1)S(1)}, bf16[96,512]{1,0:T(8,128)(2,1)S(1)}, u32[]{:S(2)}, u32[]{:S(2)}) collective-permute-start(bf16[96,512]{1,0:T(8,128)(2,1)S(1)} %owner.1.refs_0_), channel_id=1, source_target_pairs={{0,3},{1,0},{2,1},{3,2},{4,7},{5,4},{6,5},{7,6},{8,11},{9,8},{10,9... | collective-permute-start | bytes 294920 | tf_op jit(solution)/shard_map/ppermute | solution.py:267
  59.3 5.1 %collective-permute-start.4 = (bf16[96,512]{1,0:T(8,128)(2,1)S(1)}, bf16[96,512]{1,0:T(8,128)(2,1)S(1)}, u32[]{:S(2)}, u32[]{:S(2)}) collective-permute-start(bf16[96,512]{1,0:T(8,128)(2,1)S(1)} %owner.1.refs_0_), channel_id=1, source_target_pairs={{0,2},{1,3},{2,0},{3,1},{4,6},{5,7},{6,4},{7,5},{8,10},{9,11},{10,... | collective-permute-start | bytes 294920 | tf_op jit(solution)/shard_map/ppermute | solution.py:267
  59.6 5.7 %collective-permute-start.3 = (bf16[96,512]{1,0:T(8,128)(2,1)S(1)}, bf16[96,512]{1,0:T(8,128)(2,1)S(1)}, u32[]{:S(2)}, u32[]{:S(2)}) collective-permute-start(bf16[96,512]{1,0:T(8,128)(2,1)S(1)} %owner.1.refs_0_), channel_id=1, source_target_pairs={{0,1},{1,2},{2,3},{3,0},{4,5},{5,6},{6,7},{7,4},{8,9},{9,10},{10,1... | collective-permute-start | bytes 294920 | tf_op jit(solution)/shard_map/ppermute | solution.py:267
  65.8 4.5 %collective-permute-start.6 = (bf16[256,512]{1,0:T(8,128)(2,1)S(1)}, bf16[256,512]{1,0:T(8,128)(2,1)S(1)}, u32[]{:S(2)}, u32[]{:S(2)}) collective-permute-start(bf16[256,512]{1,0:T(8,128)(2,1)S(1)} %get-tuple-element.42), channel_id=1, source_target_pairs={{0,4},{4,0},{1,5},{5,1},{2,6},{6,2},{3,7},{7,3},{8,12},{12,8},{9,1... | collective-permute-start | bytes 786440 | tf_op jit(solution)/shard_map/ppermute | solution.py:273
  70.3 4.8 %collective-permute-start.7 = (bf16[64,512]{1,0:T(8,128)(2,1)S(1)}, bf16[64,512]{1,0:T(8,128)(2,1)S(1)}, u32[]{:S(2)}, u32[]{:S(2)}) collective-permute-start(bf16[64,512]{1,0:T(8,128)(2,1)S(1)} %get-tuple-element.44), channel_id=1, source_target_pairs={{0,64},{64,128},{128,192},{192,0},{1,65},{65,129},{129,193},{193,1... | collective-permute-start | bytes 196616 | tf_op jit(solution)/shard_map/ppermute | solution.py:267
  72.1 5.6 %collective-permute-start.8 = (bf16[64,512]{1,0:T(8,128)(2,1)S(1)}, bf16[64,512]{1,0:T(8,128)(2,1)S(1)}, u32[]{:S(2)}, u32[]{:S(2)}) collective-permute-start(bf16[64,512]{1,0:T(8,128)(2,1)S(1)} %get-tuple-element.45), channel_id=1, source_target_pairs={{0,128},{64,192},{128,0},{192,64},{1,129},{65,193},{129,1},{193,65... | collective-permute-start | bytes 196616 | tf_op jit(solution)/shard_map/ppermute | solution.py:267
  74.1 3.6 %collective-permute-start.9 = (bf16[64,512]{1,0:T(8,128)(2,1)S(1)}, bf16[64,512]{1,0:T(8,128)(2,1)S(1)}, u32[]{:S(2)}, u32[]{:S(2)}) collective-permute-start(bf16[64,512]{1,0:T(8,128)(2,1)S(1)} %get-tuple-element.46), channel_id=1, source_target_pairs={{0,192},{64,0},{128,64},{192,128},{1,193},{65,1},{129,65},{193,129... | collective-permute-start | bytes 196616 | tf_op jit(solution)/shard_map/ppermute | solution.py:267
  77.8 3.2 %collective-permute-start.10 = (bf16[64,512]{1,0:T(8,128)(2,1)S(1)}, bf16[64,512]{1,0:T(8,128)(2,1)S(1)}, u32[]{:S(2)}, u32[]{:S(2)}) collective-permute-start(bf16[64,512]{1,0:T(8,128)(2,1)S(1)} %add.4.refs_0_), channel_id=1, source_target_pairs={{0,8},{8,0},{16,24},{24,16},{32,40},{40,32},{48,56},{56,48},{1,9},... | collective-permute-start | bytes 196616 | tf_op jit(solution)/shard_map/ppermute | solution.py:273
  81.0 4.8 %collective-permute-start.11 = (bf16[64,512]{1,0:T(8,128)(2,1)S(1)}, bf16[64,512]{1,0:T(8,128)(2,1)S(1)}, u32[]{:S(2)}, u32[]{:S(2)}) collective-permute-start(bf16[64,512]{1,0:T(8,128)(2,1)S(1)} %add.5.refs_0_), channel_id=1, source_target_pairs={{0,16},{8,24},{16,0},{24,8},{32,48},{40,56},{48,32},{56,40},{1,17}... | collective-permute-start | bytes 196616 | tf_op jit(solution)/shard_map/ppermute | solution.py:273
  85.8 7.8 %collective-permute-start.12 = (bf16[64,512]{1,0:T(8,128)(2,1)S(1)}, bf16[64,512]{1,0:T(8,128)(2,1)S(1)}, u32[]{:S(2)}, u32[]{:S(2)}) collective-permute-start(bf16[64,512]{1,0:T(8,128)(2,1)S(1)} %add.6.refs_0_), channel_id=1, source_target_pairs={{0,32},{8,40},{16,48},{24,56},{32,0},{40,8},{48,16},{56,24},{1,33}... | collective-permute-start | bytes 196616 | tf_op jit(solution)/shard_map/ppermute | solution.py:273
  93.7 8.6 %collective-permute-start.15 = (bf16[64,512]{1,0:T(8,128)(2,1)S(1)}, bf16[64,512]{1,0:T(8,128)(2,1)S(1)}, u32[]{:S(2)}, u32[]{:S(2)}) collective-permute-start(bf16[64,512]{1,0:T(8,128)(2,1)S(1)} %add.7.refs_0_), channel_id=1, source_target_pairs={{0,192},{64,0},{128,64},{192,128},{1,193},{65,1},{129,65},{193,129... | collective-permute-start | bytes 196616 | tf_op jit(solution)/shard_map/ppermute | solution.py:267
  94.8 9.0 %collective-permute-start.14 = (bf16[64,512]{1,0:T(8,128)(2,1)S(1)}, bf16[64,512]{1,0:T(8,128)(2,1)S(1)}, u32[]{:S(2)}, u32[]{:S(2)}) collective-permute-start(bf16[64,512]{1,0:T(8,128)(2,1)S(1)} %add.7.refs_0_), channel_id=1, source_target_pairs={{0,128},{64,192},{128,0},{192,64},{1,129},{65,193},{129,1},{193,65... | collective-permute-start | bytes 196616 | tf_op jit(solution)/shard_map/ppermute | solution.py:267
  95.1 12.1 %collective-permute-start.13 = (bf16[64,512]{1,0:T(8,128)(2,1)S(1)}, bf16[64,512]{1,0:T(8,128)(2,1)S(1)}, u32[]{:S(2)}, u32[]{:S(2)}) collective-permute-start(bf16[64,512]{1,0:T(8,128)(2,1)S(1)} %add.7.refs_0_), channel_id=1, source_target_pairs={{0,64},{64,128},{128,192},{192,0},{1,65},{65,129},{129,193},{193,1... | collective-permute-start | bytes 196616 | tf_op jit(solution)/shard_map/ppermute | solution.py:267
  95.8 11.7 %collective-permute-start.16 = (bf16[64,512]{1,0:T(8,128)(2,1)S(1)}, bf16[64,512]{1,0:T(8,128)(2,1)S(1)}, u32[]{:S(2)}, u32[]{:S(2)}) collective-permute-start(bf16[64,512]{1,0:T(8,128)(2,1)S(1)} %add.7.refs_0_), channel_id=1, source_target_pairs={{0,4},{4,0},{1,5},{5,1},{2,6},{6,2},{3,7},{7,3},{8,12},{12,8},{9,1... | collective-permute-start | bytes 196616 | tf_op jit(solution)/shard_map/ppermute | solution.py:273
  102.3 5.2 %collective-permute-start.19 = (bf16[64,512]{1,0:T(8,128)(2,1)S(1)}, bf16[64,512]{1,0:T(8,128)(2,1)S(1)}, u32[]{:S(2)}, u32[]{:S(2)}) collective-permute-start(bf16[64,512]{1,0:T(8,128)(2,1)S(1)} %collective-permute-done.15.refs_3_), channel_id=1, source_target_pairs={{0,4},{4,0},{1,5},{5,1},{2,6},{6,2},{3,7},{7,3},{8,12},{12,8},{9,1... | collective-permute-start | bytes 196616 | tf_op jit(solution)/shard_map/ppermute | solution.py:273
  103.8 4.3 %collective-permute-start.18 = (bf16[64,512]{1,0:T(8,128)(2,1)S(1)}, bf16[64,512]{1,0:T(8,128)(2,1)S(1)}, u32[]{:S(2)}, u32[]{:S(2)}) collective-permute-start(bf16[64,512]{1,0:T(8,128)(2,1)S(1)} %collective-permute-done.14.refs_2_), channel_id=1, source_target_pairs={{0,4},{4,0},{1,5},{5,1},{2,6},{6,2},{3,7},{7,3},{8,12},{12,8},{9,1... | collective-permute-start | bytes 196616 | tf_op jit(solution)/shard_map/ppermute | solution.py:273
  107.2 1.3 %collective-permute-start.17 = (bf16[64,512]{1,0:T(8,128)(2,1)S(1)}, bf16[64,512]{1,0:T(8,128)(2,1)S(1)}, u32[]{:S(2)}, u32[]{:S(2)}) collective-permute-start(bf16[64,512]{1,0:T(8,128)(2,1)S(1)} %collective-permute-done.13.refs_1_), channel_id=1, source_target_pairs={{0,4},{4,0},{1,5},{5,1},{2,6},{6,2},{3,7},{7,3},{8,12},{12,8},{9,1... | collective-permute-start | bytes 196616 | tf_op jit(solution)/shard_map/ppermute | solution.py:273
